TPU v7x, 256 devices: a whole 4x4x8 slice. The times are simulated.
256 devices in a mesh: slab: 64 (over y, z, x_lo), ffn: 4 (over x_hi, core).
Axes of the slice: x: 4 (x_hi: 2, x_lo: 2; x = x_hi * 2 + x_lo), y: 4, z: 8, core: 2. Of those that a mesh axis runs over, the one named last changes fastest.
Arguments:
- tokens: bfloat16 [32768, 512], P('slab'), may hold values from -6 to 6
- gain_attn: float32 [512], replicated, may hold values from 0.1 to 1.9
- w_reduce: bfloat16 [4096, 512], replicated, may hold values from -0.09375 to 0.09375
- gain_keys: float32 [512], replicated, may hold values from 0.1 to 1.9
- w_query: bfloat16 [512, 512], P(None, 'ffn'), may hold values from -1.5 to 1.5
- w_key: bfloat16 [512, 512], P(None, 'ffn'), may hold values from -1.5 to 1.5
- w_value: bfloat16 [512, 512], P(None, 'ffn'), may hold values from -0.25 to 0.25
- w_out: bfloat16 [512, 512], P('ffn'), may hold values from -1.796875 to 1.796875
- gain_ffn: float32 [512], replicated, may hold values from 0.1 to 1.9
- w_up: bfloat16 [512, 2048], P(None, 'ffn'), may hold values from -0.25 to 0.25
- w_depth: float32 [27, 2048], P(None, 'ffn'), may hold values from -1.25 to 1.25
- w_down: bfloat16 [2048, 512], P('ffn'), may hold values from -0.125 to 0.125
- grad_out: bfloat16 [32768, 512], P('slab'), may hold values from -0.0625 to 0.0625
Outputs:
- attended: bfloat16 [32768, 512], P('slab')
- grad_up: float32 [512, 2048], P('slab', 'ffn')
- grad_down: float32 [512, 2048], P('slab', 'ffn')
All inputs are finite; a program needn't handle non-finite values.
Results may differ from a plain program's by a relative error of at most 0.024.
The roundings to bfloat16 on the way count: a program that leaves them out, or rounds other values in their place, can miss the bound.
Values may be sent and summed in bfloat16 or wider, within the bound.
A program may use at most 64 MiB of HBM per device.

v0:
```python
import math

import jax
import jax.numpy as jnp
from jax import lax
from jax.sharding import PartitionSpec as P

HEAD = 64
GX = 16
GY = 16
CZ = 2


EPSILON = 1e-05
ROPE_BASE = 100.0
ROOT_HALF = 0.7071067811865476
NORMAL_SCALE = 0.3989422804014327


def padded_2(cells, sides, width):
    for axis, dim in sides:
        count = lax.axis_size(axis)
        ends = count - 1
        head = lax.slice_in_dim(cells, 0, width, axis=dim)
        tail = lax.slice_in_dim(cells, cells.shape[dim] - width, cells.shape[dim], axis=dim)
        cells = jnp.concatenate(
            [
                lax.ppermute(tail, axis, [(i, (i + 1) % count) for i in range(ends)]),
                cells,
                lax.ppermute(head, axis, [((i + 1) % count, i) for i in range(ends)]),
            ],
            axis=dim,
        )
    return cells


def layer_norm(values, scale_gain):
    values = values.astype(jnp.float32)
    centered = values - jnp.mean(values, axis=-1, keepdims=True)
    variance = jnp.mean(centered * centered, axis=-1, keepdims=True)
    return centered * lax.rsqrt(variance + EPSILON) * scale_gain


def rope_tables(coord_x, coord_y, coord_z, head_size):
    pair_count = head_size // 2
    position = jnp.arange(pair_count, dtype=jnp.int32)
    axis_pick = position % 3
    per_axis = (pair_count + 2) // 3
    frequency = ROPE_BASE ** (-(position // 3).astype(jnp.float32) / per_axis)
    angles = (
        coord_x[:, None] * (axis_pick == 0)
        + coord_y[:, None] * (axis_pick == 1)
        + coord_z[:, None] * (axis_pick == 2)
    ) * frequency
    return (jnp.cos(angles)[:, None, :], jnp.sin(angles)[:, None, :])


def token_tables(first_plane, planes, head_size):
    position = jnp.arange(planes * GY * GX, dtype=jnp.int32)
    coord_x = (position % GX).astype(jnp.float32)
    coord_y = (position // GX % GY).astype(jnp.float32)
    coord_z = (first_plane + position // (GX * GY)).astype(jnp.float32)
    return rope_tables(coord_x, coord_y, coord_z, head_size)


def key_tables(first_row, row_count, head_size):
    position = first_row + jnp.arange(row_count, dtype=jnp.int32)
    half_x = GX // 2
    half_y = GY // 2
    coord_x = (position % half_x).astype(jnp.float32) * 2.0 + 0.5
    coord_y = (position // half_x % half_y).astype(jnp.float32) * 2.0 + 0.5
    coord_z = (position // (half_x * half_y)).astype(jnp.float32) * 2.0 + 0.5
    return rope_tables(coord_x, coord_y, coord_z, head_size)


def rotate(values, cosine, sine_table):
    half_size = values.shape[-1] // 2
    front_half = values[..., :half_size]
    back_half = values[..., half_size:]
    return jnp.concatenate(
        [
            front_half * cosine - back_half * sine_table,
            back_half * cosine + front_half * sine_table,
        ],
        axis=-1,
    )


def make_patches(normed, planes):
    width = normed.shape[-1]
    cell_grid = normed.reshape(planes // 2, 2, GY // 2, 2, GX // 2, 2, width)
    return cell_grid.transpose(0, 2, 4, 1, 3, 5, 6).reshape(-1, 8 * width)


def depth_conv(padded, weights, planes):
    height = padded.shape[1] - 2
    width_x = padded.shape[2] - 2
    result = jnp.zeros((planes, height, width_x, padded.shape[3]), jnp.float32)
    for offset in range(27):
        shift_z = offset // 9
        shift_y = offset // 3 % 3
        shift_x = offset % 3
        window = padded[
            shift_z : shift_z + planes, shift_y : shift_y + height, shift_x : shift_x + width_x
        ]
        result = result + window.astype(jnp.float32) * weights[offset]
    return result


def attend_piece(state_tuple, queries, key_rows, value_rows):
    row_max, row_sum, weighted = state_tuple
    score_scale = key_rows.shape[-1] ** (-0.5)
    scores = (
        jnp.einsum("qhd,khd->hqk", queries, key_rows, preferred_element_type=jnp.float32)
        * score_scale
    )
    new_max = jnp.maximum(row_max, jnp.max(scores, axis=2))
    rescale = jnp.exp(row_max - new_max)
    expo = jnp.exp(scores - new_max[:, :, None])
    row_sum = row_sum * rescale + jnp.sum(expo, axis=2)
    weighted = weighted * rescale[:, :, None] + jnp.einsum(
        "hqk,khd->hqd", expo.astype(jnp.bfloat16), value_rows, preferred_element_type=jnp.float32
    )
    return (new_max, row_sum, weighted)


def per_device(
    tokens,
    gain_attn,
    w_reduce,
    gain_keys,
    w_query,
    w_key,
    w_value,
    w_out,
    gain_ffn,
    w_up,
    w_depth,
    w_down,
    grad_out,
):
    slab_index = lax.axis_index("slab")
    tok_rows = tokens.shape[0]
    heads_dev = w_query.shape[1] // HEAD
    normed = layer_norm(tokens, gain_attn).astype(jnp.bfloat16)
    patches = make_patches(normed, CZ)
    reduced = jnp.dot(patches, w_reduce, preferred_element_type=jnp.float32)
    key_input = layer_norm(reduced, gain_keys).astype(jnp.bfloat16)
    tok_cos, tok_sin = token_tables(slab_index * CZ, CZ, HEAD)
    queries = jnp.dot(normed, w_query, preferred_element_type=jnp.float32).reshape(
        tok_rows, heads_dev, HEAD
    )
    queries = rotate(queries, tok_cos, tok_sin).astype(jnp.bfloat16)
    initial = (
        jnp.full((heads_dev, tok_rows), -1e30, jnp.float32),
        jnp.zeros((heads_dev, tok_rows), jnp.float32),
        jnp.zeros((heads_dev, tok_rows, HEAD), jnp.float32),
    )
    state_tuple = initial
    pieces = lax.all_gather(key_input, "slab", axis=0, tiled=True)
    row_count = pieces.shape[0]
    block_rows = math.gcd(row_count, 1024)
    block_count = row_count // block_rows
    blocks = pieces.reshape(block_count, block_rows, pieces.shape[1])

    def one_block(state_inner, block_item):
        rows_in, block_index = block_item
        block_first = block_index * block_rows
        key_cos, key_sin = key_tables(block_first, block_rows, HEAD)
        key_block = jnp.dot(rows_in, w_key, preferred_element_type=jnp.float32).reshape(
            block_rows, heads_dev, HEAD
        )
        key_block = rotate(key_block, key_cos, key_sin).astype(jnp.bfloat16)
        value_block = (
            jnp.dot(rows_in, w_value, preferred_element_type=jnp.float32)
            .astype(jnp.bfloat16)
            .reshape(block_rows, heads_dev, HEAD)
        )
        return (attend_piece(state_inner, queries, key_block, value_block), None)

    state_tuple, _ = lax.scan(
        one_block, state_tuple, (blocks, jnp.arange(block_count, dtype=jnp.int32))
    )
    row_max, row_sum, weighted = state_tuple
    heads_out = (
        (weighted / row_sum[:, :, None])
        .transpose(1, 0, 2)
        .reshape(tok_rows, heads_dev * HEAD)
        .astype(jnp.bfloat16)
    )
    partial_value = jnp.dot(heads_out, w_out, preferred_element_type=jnp.float32)
    head_total = lax.psum(partial_value.astype(jnp.bfloat16), "ffn").astype(jnp.float32)
    attended = head_total.astype(jnp.bfloat16)
    residual = tokens.astype(jnp.float32) + head_total
    normed_ffn = layer_norm(residual, gain_ffn).astype(jnp.bfloat16)
    channels = w_up.shape[1]
    pre = (
        jnp.dot(normed_ffn, w_up, preferred_element_type=jnp.float32)
        .astype(jnp.bfloat16)
        .reshape(CZ, GY, GX, channels)
    )
    pre_wide = padded_2(pre, (("slab", 0),), 1)
    pre_pad = jnp.pad(pre_wide, ((0, 0), (1, 1), (1, 1), (0, 0)))
    mixed = depth_conv(pre_pad, w_depth, CZ).reshape(tok_rows, channels)
    normal_cdf = 0.5 * (1.0 + lax.erf(mixed * ROOT_HALF))
    normal_pdf = jnp.exp(-0.5 * mixed * mixed) * NORMAL_SCALE
    activated = (mixed * normal_cdf).astype(jnp.bfloat16)
    grad_act = jnp.einsum("td,cd->tc", grad_out, w_down, preferred_element_type=jnp.float32)
    grad_mixed = (
        (grad_act * (normal_cdf + mixed * normal_pdf))
        .astype(jnp.bfloat16)
        .reshape(CZ, GY, GX, channels)
    )
    grad_wide = padded_2(grad_mixed, (("slab", 0),), 1)
    grad_pad = jnp.pad(grad_wide, ((0, 0), (1, 1), (1, 1), (0, 0)))
    grad_pre = (
        depth_conv(grad_pad, w_depth[::-1], CZ).astype(jnp.bfloat16).reshape(tok_rows, channels)
    )
    up_full = jnp.einsum("td,tc->dc", normed_ffn, grad_pre, preferred_element_type=jnp.float32)
    down_full = jnp.einsum("td,tc->dc", grad_out, activated, preferred_element_type=jnp.float32)
    grads = lax.psum_scatter(
        jnp.concatenate([up_full, down_full], axis=1), "slab", scatter_dimension=0, tiled=True
    )
    return (attended, grads[:, :channels], grads[:, channels:])


def solution(mesh):
    in_specs = (
        P("slab", None),
        P(),
        P(),
        P(),
        P(None, "ffn"),
        P(None, "ffn"),
        P(None, "ffn"),
        P("ffn", None),
        P(),
        P(None, "ffn"),
        P(None, "ffn"),
        P("ffn", None),
        P("slab", None),
    )
    out_specs = (P("slab", None), P("slab", "ffn"), P("slab", "ffn"))
    return jax.shard_map(
        per_device, mesh=mesh, in_specs=in_specs, out_specs=out_specs, check_vma=False
    )
```

profile of v0, /device:TPU:2, one launch (start us, length us, event | category | flops | bytes accessed | tf_op | source)
XLA Modules:
  0.0 790.8 jit_solution(1866074170113802012)
XLA Ops:
  12.2 3.2 fusion.96
  17.3 304.6 %all-gather.2.cloned.1.call-done = bf16[4096,512]{1,0:T(8,128)(2,1)} async-done(((bf16[64,512]{1,0:T(8,128)(2,1)}), bf16[4096,512]{1,0:T(8,128)(2,1)}) %all-gather.2.cloned.1.call-update) | async-done | bytes 4194320 | tf_op jit(solution)/shard_map/all_gather | solution.py:160
  321.9 48.4 %while.18 = (s32[]{:T(128)}, f32[2,512]{1,0:T(2,128)S(1)}, f32[2,512]{1,0:T(2,128)S(1)}, f32[2,512,64]{1,2,0:T(8,128)S(1)}, bf16[4,1024,512]{2,1,0:T(8,128)(2,1)...) while((s32[]{:T(128)}, f32[2,512]{1,0:T(2,128)S(1)}, ...), condition=%wide.region_7.8_spmd.clone, body=%wide.region_4.7_spmd.clone.sunk | while | flops 546895744 | bytes 35088572 | solution.py:181
  325.6 2.7 bitcast_reduce_fusion.2
  328.3 3.0 fusion.143
  337.7 2.7 bitcast_reduce_fusion.2
  340.4 3.0 fusion.143
  349.8 2.7 bitcast_reduce_fusion.2
  352.5 3.0 fusion.143
  355.6 1.7 convolution_convert_fusion.4
  361.9 2.7 bitcast_reduce_fusion.2
  364.6 3.0 fusion.143
  371.6 45.3 %all-reduce.4.cloned.1.call-done = bf16[512,512]{1,0:T(8,128)(2,1)} async-done(((bf16[512,512]{1,0:T(8,128)(2,1)}), bf16[512,512]{1,0:T(8,128)(2,1)}) %all-reduce.4.cloned.1.call-update) | async-done | bytes 524304 | tf_op jit(solution)/shard_map/psum | solution.py:192
  421.1 4.4 collective-permute-start
  425.5 1.9 collective-permute-start.1
  427.5 9.7 %collective-permute-done = bf16[1,16,16,512]{3,2,1,0:T(8,128)(2,1)S(1)} collective-permute-done((bf16[1,16,16,512]{3,2,1,0:T(8,128)(2,1)S(1)}, bf16[1,16,16,512]{3,2,1,0:T(8,128)(2,1)S(1)}, u32[]{:S(2)}, u32[]{:S(2)}) %collective-permute-start) | collective-permute-done | bytes 262176 | tf_op jit(solution)/shard_map/ppermute | solution.py:28
  437.2 1.9 collective-permute-done.1
  439.9 3.8 multiply_add_fusion
  444.6 3.4 collective-permute-start.2
  447.9 2.7 collective-permute-start.3
  451.1 9.2 %collective-permute-done.2 = bf16[1,16,16,512]{3,2,1,0:T(8,128)(2,1)S(1)} collective-permute-done((bf16[1,16,16,512]{3,2,1,0:T(8,128)(2,1)S(1)}, bf16[1,16,16,512]{3,2,1,0:T(8,128)(2,1)S(1)}, u32[]{:S(2)}, u32[]{:S(2)}) %collective-permute-start.2) | collective-permute-done | bytes 262176 | tf_op jit(solution)/shard_map/ppermute | solution.py:28
  462.3 3.8 add_convert_fusion.1
  467.0 1.8 copy.31
  468.9 313.3 %reduce-scatter.4.cloned.1.call-done = f32[8,1024]{1,0:T(8,128)} async-done(((f32[512,1024]{1,0:T(8,128)}), f32[8,1024]{1,0:T(8,128)}) %reduce-scatter.4.cloned.1.call-update) | async-done | bytes 32784
  (142 shorter events, 39.9 us)
Async XLA Ops:
  7.2 436.8 %copy-start = (bf16[512,512]{1,0:T(8,128)(2,1)S(1)}, bf16[512,512]{1,0:T(8,128)(2,1)}, u32[]{:S(2)}) copy-start(bf16[512,512]{1,0:T(8,128)(2,1)} %param.27) | copy-start | bytes 1572868
  7.2 314.7 %all-gather.2.cloned.1.call-start = ((), (), s32[]{:S(2)}) async-start(), calls=%async_computation.1 | async-start | bytes 4259840 | tf_op jit(solution)/shard_map/all_gather | solution.py:160
  11.3 4.2 copy-start.11
  11.3 5.1 copy-start.8
  11.7 5.2 copy-start.7
  12.1 309.7 %copy-start.5 = (bf16[512,128]{1,0:T(8,128)(2,1)S(1)}, bf16[512,128]{1,0:T(8,128)(2,1)}, u32[]{:S(2)}) copy-start(bf16[512,128]{1,0:T(8,128)(2,1)} %param.21) | copy-start | bytes 393220
  16.3 400.6 %all-reduce.4.cloned.1.call-start = ((), (), s32[]{:S(2)}) async-start(), calls=%async_computation.2 | async-start | bytes 1048576 | tf_op jit(solution)/shard_map/psum | solution.py:192
  321.9 48.5 %copy-start.9 = (bf16[128,512]{1,0:T(8,128)(2,1)S(1)}, bf16[128,512]{1,0:T(8,128)(2,1)}, u32[]{:S(2)}) copy-start(bf16[128,512]{1,0:T(8,128)(2,1)} %param.22) | copy-start | bytes 393220
  321.9 95.0 %copy-start.2 = (bf16[512,512]{1,0:T(8,128)(2,1)S(1)}, bf16[512,512]{1,0:T(8,128)(2,1)}, u32[]{:S(2)}) copy-start(bf16[512,512]{1,0:T(8,128)(2,1)} %param.15) | copy-start | bytes 1572868
  328.3 4.8 copy-start.1
  340.4 4.8 copy-start.1
  352.5 4.8 copy-start.1
  364.6 4.8 copy-start.1
  370.3 49.2 %copy-start.12 = (bf16[512,512]{1,0:T(8,128)(2,1)S(1)}, bf16[512,512]{1,0:T(8,128)(2,1)}, u32[]{:S(2)}) copy-start(bf16[512,512]{1,0:T(8,128)(2,1)} %param.24) | copy-start | bytes 1572868
  370.3 49.2 %copy-start.13 = (f32[512]{0:T(512)S(1)}, f32[512]{0:T(512)}, u32[]{:S(2)}) copy-start(f32[512]{0:T(512)} %param.23) | copy-start | bytes 6148
  370.4 57.0 %copy-start.10 = (f32[27,512]{1,0:T(8,128)S(1)}, f32[27,512]{1,0:T(8,128)}, u32[]{:S(2)}) copy-start(f32[27,512]{1,0:T(8,128)} %param.25) | copy-start | bytes 165892
  371.5 410.6 %reduce-scatter.4.cloned.1.call-start = ((), (), s32[]{:S(2)}) async-start(), calls=%async_computation.3 | async-start | bytes 2129920
  421.1 16.1 %collective-permute-start = (bf16[1,16,16,512]{3,2,1,0:T(8,128)(2,1)S(1)}, bf16[1,16,16,512]{3,2,1,0:T(8,128)(2,1)S(1)}, u32[]{:S(2)}, u32[]{:S(2)}) collective-permute-start(bf16[1,16,16,512]{3,2,1,0:T(8,128)(2,1)S(1)} %bitcast.133), channel_id=1, source_target_pairs={{0,4},{4,8},{8,12},{12,16},{16,20},{20,24},{24,28},{28,32},{32,36}... | collective-permute-start | bytes 786440 | tf_op jit(solution)/shard_map/ppermute | solution.py:28
  425.5 13.6 %collective-permute-start.1 = (bf16[1,16,16,512]{3,2,1,0:T(8,128)(2,1)S(1)}, bf16[1,16,16,512]{3,2,1,0:T(8,128)(2,1)S(1)}, u32[]{:S(2)}, u32[]{:S(2)}) collective-permute-start(bf16[1,16,16,512]{3,2,1,0:T(8,128)(2,1)S(1)} %bitcast.132), channel_id=1, source_target_pairs={{4,0},{8,4},{12,8},{16,12},{20,16},{24,20},{28,24},{32,28},{36,32}... | collective-permute-start | bytes 786440 | tf_op jit(solution)/shard_map/ppermute | solution.py:30
  439.9 4.1 copy-start.6
  444.6 15.7 %collective-permute-start.2 = (bf16[1,16,16,512]{3,2,1,0:T(8,128)(2,1)S(1)}, bf16[1,16,16,512]{3,2,1,0:T(8,128)(2,1)S(1)}, u32[]{:S(2)}, u32[]{:S(2)}) collective-permute-start(bf16[1,16,16,512]{3,2,1,0:T(8,128)(2,1)S(1)} %bitcast.135), channel_id=1, source_target_pairs={{0,4},{4,8},{8,12},{12,16},{16,20},{20,24},{24,28},{28,32},{32,36}... | collective-permute-start | bytes 786440 | tf_op jit(solution)/shard_map/ppermute | solution.py:28
  447.9 13.6 %collective-permute-start.3 = (bf16[1,16,16,512]{3,2,1,0:T(8,128)(2,1)S(1)}, bf16[1,16,16,512]{3,2,1,0:T(8,128)(2,1)S(1)}, u32[]{:S(2)}, u32[]{:S(2)}) collective-permute-start(bf16[1,16,16,512]{3,2,1,0:T(8,128)(2,1)S(1)} %bitcast.134), channel_id=1, source_target_pairs={{4,0},{8,4},{12,8},{16,12},{20,16},{24,20},{28,24},{32,28},{36,32}... | collective-permute-start | bytes 786440 | tf_op jit(solution)/shard_map/ppermute | solution.py:30
  462.3 3.9 copy-start.3
  467.0 316.5 %copy-start.4 = (bf16[512,512]{1,0:T(8,128)(2,1)S(1)}, bf16[512,512]{1,0:T(8,128)(2,1)}, u32[]{:S(2)}) copy-start(bf16[512,512]{1,0:T(8,128)(2,1)} %all-reduce.4.cloned.1.call-done) | copy-start | bytes 1572868
Sparse Core Ops, SparseCore 0:
  16.4 305.4 all-gather.1
  371.7 45.1 all-reduce.3
  469.0 313.1 reduce-scatter.3
where the time goes:
time: 796 us; the launch traced here: 791 us
  waiting for transfers between devices  685 us (86%)
  matrix products  35.8 us (4%)
  other arithmetic  32.5 us (4%)
  between operations  14.2 us (2%)
  starting transfers between devices  12.4 us (2%)
    unnamed x4, waiting for transfers between devices  313 us
    all_gather x1, waiting for transfers between devices, per_device(): pieces = lax.all_gather(key_input, 'slab', axis=0, tiled=True)  305 us
    psum x1, waiting for transfers between devices, per_device(): lax.psum(partial_value.astype(jnp.bfloat16), 'ffn').astype(jnp.float32)  45.3 us
    ppermute x2, waiting for transfers between devices, padded_2(): lax.ppermute(tail, axis, [(i, (i + 1) % count) for i in range(ends)])  18.9 us
  transfers between devices with their start and end apart: 7, of which 7 were waited for; matrix products, arithmetic and copies ran while one was open for 0% of the time, Pallas kernels for 0%

commit v1 on v0

--- a/solution.py
+++ b/solution.py
@@ -3,12 +3,15 @@
 import jax
 import jax.numpy as jnp
 from jax import lax
+from jax.sharding import Mesh
 from jax.sharding import PartitionSpec as P
 
 HEAD = 64
 GX = 16
 GY = 16
 CZ = 2
+SLAB = ("y", "z", "xl")
+FFN = ("xh", "core")
 
 
 EPSILON = 1e-05
@@ -19,7 +22,7 @@
 
 def padded_2(cells, sides, width):
     for axis, dim in sides:
-        count = lax.axis_size(axis)
+        count = lax.psum(1, axis)
         ends = count - 1
         head = lax.slice_in_dim(cells, 0, width, axis=dim)
         tail = lax.slice_in_dim(cells, cells.shape[dim] - width, cells.shape[dim], axis=dim)
@@ -139,7 +142,7 @@
     w_down,
     grad_out,
 ):
-    slab_index = lax.axis_index("slab")
+    slab_index = lax.axis_index(SLAB)
     tok_rows = tokens.shape[0]
     heads_dev = w_query.shape[1] // HEAD
     normed = layer_norm(tokens, gain_attn).astype(jnp.bfloat16)
@@ -157,30 +160,30 @@
         jnp.zeros((heads_dev, tok_rows, HEAD), jnp.float32),
     )
     state_tuple = initial
-    pieces = lax.all_gather(key_input, "slab", axis=0, tiled=True)
+    local_rows = key_input.shape[0]
+    own_cos, own_sin = key_tables(slab_index * local_rows, local_rows, HEAD)
+    own_keys = jnp.dot(key_input, w_key, preferred_element_type=jnp.float32).reshape(
+        local_rows, heads_dev, HEAD
+    )
+    own_keys = rotate(own_keys, own_cos, own_sin).astype(jnp.bfloat16)
+    own_values = jnp.dot(key_input, w_value, preferred_element_type=jnp.float32).astype(
+        jnp.bfloat16
+    )
+    key_width = heads_dev * HEAD
+    pieces = jnp.concatenate([own_keys.reshape(local_rows, key_width), own_values], axis=1)
+    for axis in ("xl", "z", "y"):
+        pieces = lax.all_gather(pieces, axis, axis=0, tiled=True)
     row_count = pieces.shape[0]
     block_rows = math.gcd(row_count, 1024)
     block_count = row_count // block_rows
     blocks = pieces.reshape(block_count, block_rows, pieces.shape[1])
 
-    def one_block(state_inner, block_item):
-        rows_in, block_index = block_item
-        block_first = block_index * block_rows
-        key_cos, key_sin = key_tables(block_first, block_rows, HEAD)
-        key_block = jnp.dot(rows_in, w_key, preferred_element_type=jnp.float32).reshape(
-            block_rows, heads_dev, HEAD
-        )
-        key_block = rotate(key_block, key_cos, key_sin).astype(jnp.bfloat16)
-        value_block = (
-            jnp.dot(rows_in, w_value, preferred_element_type=jnp.float32)
-            .astype(jnp.bfloat16)
-            .reshape(block_rows, heads_dev, HEAD)
-        )
+    def one_block(state_inner, rows_in):
+        key_block = rows_in[:, :key_width].reshape(block_rows, heads_dev, HEAD)
+        value_block = rows_in[:, key_width:].reshape(block_rows, heads_dev, HEAD)
         return (attend_piece(state_inner, queries, key_block, value_block), None)
 
-    state_tuple, _ = lax.scan(
-        one_block, state_tuple, (blocks, jnp.arange(block_count, dtype=jnp.int32))
-    )
+    state_tuple, _ = lax.scan(one_block, state_tuple, blocks)
     row_max, row_sum, weighted = state_tuple
     heads_out = (
         (weighted / row_sum[:, :, None])
@@ -189,7 +192,7 @@
         .astype(jnp.bfloat16)
     )
     partial_value = jnp.dot(heads_out, w_out, preferred_element_type=jnp.float32)
-    head_total = lax.psum(partial_value.astype(jnp.bfloat16), "ffn").astype(jnp.float32)
+    head_total = lax.psum(partial_value.astype(jnp.bfloat16), FFN).astype(jnp.float32)
     attended = head_total.astype(jnp.bfloat16)
     residual = tokens.astype(jnp.float32) + head_total
     normed_ffn = layer_norm(residual, gain_ffn).astype(jnp.bfloat16)
@@ -199,7 +202,7 @@
         .astype(jnp.bfloat16)
         .reshape(CZ, GY, GX, channels)
     )
-    pre_wide = padded_2(pre, (("slab", 0),), 1)
+    pre_wide = padded_2(pre, ((SLAB, 0),), 1)
     pre_pad = jnp.pad(pre_wide, ((0, 0), (1, 1), (1, 1), (0, 0)))
     mixed = depth_conv(pre_pad, w_depth, CZ).reshape(tok_rows, channels)
     normal_cdf = 0.5 * (1.0 + lax.erf(mixed * ROOT_HALF))
@@ -211,36 +214,40 @@
         .astype(jnp.bfloat16)
         .reshape(CZ, GY, GX, channels)
     )
-    grad_wide = padded_2(grad_mixed, (("slab", 0),), 1)
+    grad_wide = padded_2(grad_mixed, ((SLAB, 0),), 1)
     grad_pad = jnp.pad(grad_wide, ((0, 0), (1, 1), (1, 1), (0, 0)))
     grad_pre = (
         depth_conv(grad_pad, w_depth[::-1], CZ).astype(jnp.bfloat16).reshape(tok_rows, channels)
     )
     up_full = jnp.einsum("td,tc->dc", normed_ffn, grad_pre, preferred_element_type=jnp.float32)
     down_full = jnp.einsum("td,tc->dc", grad_out, activated, preferred_element_type=jnp.float32)
-    grads = lax.psum_scatter(
-        jnp.concatenate([up_full, down_full], axis=1), "slab", scatter_dimension=0, tiled=True
-    )
+    grads = jnp.concatenate([up_full, down_full], axis=1)
+    sizes = [lax.psum(1, axis) for axis in SLAB]
+    grads = grads.reshape(sizes + [-1, grads.shape[1]])
+    grads = grads.transpose(1, 0, 2, 3, 4).reshape(-1, grads.shape[-1])
+    for axis in ("z", "y", "xl"):
+        grads = lax.psum_scatter(grads, axis, scatter_dimension=0, tiled=True)
     return (attended, grads[:, :channels], grads[:, channels:])
 
 
 def solution(mesh):
+    mesh = Mesh(mesh.devices.reshape(4, 8, 2, 2, 2), SLAB + FFN)
     in_specs = (
-        P("slab", None),
-        P(),
-        P(),
-        P(),
-        P(None, "ffn"),
-        P(None, "ffn"),
-        P(None, "ffn"),
-        P("ffn", None),
-        P(),
-        P(None, "ffn"),
-        P(None, "ffn"),
-        P("ffn", None),
-        P("slab", None),
-    )
-    out_specs = (P("slab", None), P("slab", "ffn"), P("slab", "ffn"))
+        P(SLAB, None),
+        P(),
+        P(),
+        P(),
+        P(None, FFN),
+        P(None, FFN),
+        P(None, FFN),
+        P(FFN, None),
+        P(),
+        P(None, FFN),
+        P(None, FFN),
+        P(FFN, None),
+        P(SLAB, None),
+    )
+    out_specs = (P(SLAB, None), P(SLAB, FFN), P(SLAB, FFN))
     return jax.shard_map(
         per_device, mesh=mesh, in_specs=in_specs, out_specs=out_specs, check_vma=False
     )

time: 796 us -> 316 us (0.40)
  waiting for transfers between devices: 685 us -> 184 us
  blocking collectives: 0 us -> 35.8 us
  matrix products: 35.8 us -> 22.5 us
    unnamed x4 -> x5, waiting for transfers between devices: 313 us -> 0.08 us
    all_gather x1, waiting for transfers between devices: 305 us -> 32 us  [per_device(): pieces = lax.all_gather(pieces, axis, axis=0, tiled=True)]
    reduce_scatter x0 -> x3, waiting for transfers between devices: none -> 83.8 us  [per_device(): grads = lax.psum_scatter(grads, axis, scatter_dimension=0, tiled=True)]
    all_gather x0 -> x2, blocking collectives: none -> 35.8 us  [per_device(): pieces = lax.all_gather(pieces, axis, axis=0, tiled=True)]
    dot_general x8 -> x2, matrix products: 13.6 us -> 0.41 us  [the longest x1 0.2 us: per_device(): jnp.dot(key_input, w_value, preferred_element_type=jnp.float32)]
  transfers between devices with their start and end apart: 7 -> 9, of which waited for: 7 -> 9; matrix products, arithmetic and copies ran while one was open for 0% -> 0% of each run, Pallas kernels for 0% -> 0%
where the time goes in v1:
time: 316 us; the launch traced here: 315 us
  waiting for transfers between devices  184 us (58%)
  blocking collectives  35.8 us (11%)
  other arithmetic  29.5 us (9%)
  matrix products  22.5 us (7%)
  local copies, waits for them, and re-layouts  15.5 us (5%)
  between operations  14.3 us (5%)
  starting transfers between devices  12.5 us (4%)
    reduce_scatter x3, waiting for transfers between devices, per_device(): grads = lax.psum_scatter(grads, axis, scatter_dimension=0, tiled=True)  83.8 us
    psum x1, waiting for transfers between devices, per_device(): lax.psum(partial_value.astype(jnp.bfloat16), FFN).astype(jnp.float32)  46.4 us
    all_gather x2, blocking collectives, per_device(): pieces = lax.all_gather(pieces, axis, axis=0, tiled=True)  35.8 us
    all_gather x1, waiting for transfers between devices, per_device(): pieces = lax.all_gather(pieces, axis, axis=0, tiled=True)  32 us
    ppermute x2, waiting for transfers between devices, padded_2(): lax.ppermute(tail, axis, [(i, (i + 1) % count) for i in range(ends)])  18.9 us
    reduce_sum x4, other arithmetic, attend_piece(): row_sum = row_sum * rescale + jnp.sum(expo, axis=2)  12.1 us
    dot_general x4, matrix products, attend_piece(): jnp.einsum('qhd,khd->hqk', queries, key_rows, preferred_element_type=jnp....  10.8 us
    ppermute x2, starting transfers between devices, padded_2(): lax.ppermute(tail, axis, [(i, (i + 1) % count) for i in range(ends)])  7.71 us
  transfers between devices with their start and end apart: 9, of which 9 were waited for; matrix products, arithmetic and copies ran while one was open for 0% of the time, Pallas kernels for 0%

profile of v1, /device:TPU:2, one launch (start us, length us, event | category | flops | bytes accessed | tf_op | source)
XLA Modules:
  0.0 314.7 jit_solution(17436997218391451417)
XLA Ops:
  12.5 3.2 %fusion.75 = (f32[64]{0:T(128)S(1)}, f32[64,512]{1,0:T(8,128)S(1)}) fusion(bf16[64,4096]{1,0:T(8,128)(2,1)S(1)} %reshape.621, bf16[4096,512]{1,0:T(8,128)(2,1)} %param.17), kind=kOutput, calls=%fused_computation.155 | convolution fusion | flops 268468160 | bytes 4849920 | tf_op jit(solution)/shard_map/dot_general | solution.py:150
  16.9 4.8 %all_gather.9 = bf16[128,256]{1,0:T(8,128)(2,1)S(1)} all-gather(bf16[64,256]{1,0:T(8,128)(2,1)S(1)} %pad_maximum_fusion.7), channel_id=1, replica_groups=mesh['y'=4,'z'=8,'xl'=2,'xh'=2,'core'=2] {'xl'}, dimensions={0}, use_global_device_ids=true | all-gather | bytes 98304 | tf_op jit(solution)/shard_map/all_gather | solution.py:175
  21.7 30.9 %all_gather.10 = bf16[1024,256]{1,0:T(8,128)(2,1)} all-gather(bf16[128,256]{1,0:T(8,128)(2,1)S(1)} %all_gather.9), channel_id=1, replica_groups=mesh['y'=4,'z'=8,'xl'=2,'xh'=2,'core'=2] {'z'}, dimensions={0}, use_global_device_ids=true | all-gather | bytes 589824 | tf_op jit(solution)/shard_map/all_gather | solution.py:175
  53.5 32.0 %all-gather.2.cloned.1.call-done = bf16[4096,256]{1,0:T(8,128)(2,1)} async-done(((bf16[1024,256]{1,0:T(8,128)(2,1)}), bf16[4096,256]{1,0:T(8,128)(2,1)}) %all-gather.2.cloned.1.call-update) | async-done | bytes 2097168 | tf_op jit(solution)/shard_map/all_gather | solution.py:175
  85.5 33.6 %while.15 = (s32[]{:T(128)}, f32[2,512]{1,0:T(2,128)S(1)}, f32[2,512]{1,0:T(2,128)S(1)}, f32[2,512,64]{1,2,0:T(8,128)S(1)}, bf16[4,1024,256]{2,1,0:T(8,128)(2,1)...) while((s32[]{:T(128)}, f32[2,512]{1,0:T(2,128)S(1)}, f32[2,512]{1,0:T(2,128)S(1)}, ...), condition=%wide.region_7.8_spmd.clone, body=%wide.region_4.7_spmd.clone.sunk | while | flops 277025792 | bytes 33751168 | solution.py:186
  86.9 2.7 bitcast_reduce_fusion.2
  89.6 3.0 fusion.109
  95.3 2.7 bitcast_reduce_fusion.2
  98.0 3.0 fusion.109
  103.7 2.7 bitcast_reduce_fusion.2
  106.4 3.0 fusion.109
  112.1 2.7 bitcast_reduce_fusion.2
  114.8 3.0 fusion.109
  120.4 46.4 %all-reduce.4.cloned.1.call-done = bf16[512,512]{1,0:T(8,128)(2,1)} async-done(((bf16[512,512]{1,0:T(8,128)(2,1)}), bf16[512,512]{1,0:T(8,128)(2,1)}) %all-reduce.4.cloned.1.call-update) | async-done | bytes 524304 | tf_op jit(solution)/shard_map/psum | solution.py:195
  171.1 4.3 %collective-permute-start = (bf16[1,16,16,512]{3,2,1,0:T(8,128)(2,1)S(1)}, bf16[1,16,16,512]{3,2,1,0:T(8,128)(2,1)S(1)}, u32[]{:S(2)}, u32[]{:S(2)}) collective-permute-start(bf16[1,16,16,512]{3,2,1,0:T(8,128)(2,1)S(1)} %bitcast.126), channel_id=1, source_target_pairs={{0,4},{4,8},{8,12},{12,16},{16,20},{20,24},{24,28},{28,32},{32,36}... | collective-permute-start | bytes 786440 | tf_op jit(solution)/shard_map/ppermute | solution.py:31
  177.5 9.7 %collective-permute-done = bf16[1,16,16,512]{3,2,1,0:T(8,128)(2,1)S(1)} collective-permute-done((bf16[1,16,16,512]{3,2,1,0:T(8,128)(2,1)S(1)}, bf16[1,16,16,512]{3,2,1,0:T(8,128)(2,1)S(1)}, u32[]{:S(2)}, u32[]{:S(2)}) %collective-permute-start) | collective-permute-done | bytes 262176 | tf_op jit(solution)/shard_map/ppermute | solution.py:31
  189.8 3.8 %multiply_add_fusion = f32[2,16,16,512]{3,2,1,0:T(8,128)S(1)} fusion(bf16[2,16,16,512]{3,2,1,0:T(8,128)(2,1)S(1)} %bitcast.119, bf16[4,18,18,512]{3,2,1,0:T(8,128)(2,1)S(1)} %fusion.21, bf16[1,16,16,512]{3,2,1,0:T(8,128)(2,1)S(1)} %collective-permute-done.1, bf16[1,16,16,512]{3,2,1,0:T(8,128)(2,1)S(1)} %collective-permute-done, f32[512]{0:T(512)S(1)} %bitcast.141, ...), kind=kLoop, calls=%fused_computation.59 | loop fusion | flops 21495808 | bytes 14735360 | tf_op jit(solution)/shard_map/add | solution.py:109
  194.5 3.4 %collective-permute-start.2 = (bf16[1,16,16,512]{3,2,1,0:T(8,128)(2,1)S(1)}, bf16[1,16,16,512]{3,2,1,0:T(8,128)(2,1)S(1)}, u32[]{:S(2)}, u32[]{:S(2)}) collective-permute-start(bf16[1,16,16,512]{3,2,1,0:T(8,128)(2,1)S(1)} %bitcast.128), channel_id=1, source_target_pairs={{0,4},{4,8},{8,12},{12,16},{16,20},{20,24},{24,28},{28,32},{32,36}... | collective-permute-start | bytes 786440 | tf_op jit(solution)/shard_map/ppermute | solution.py:31
  201.1 9.2 %collective-permute-done.2 = bf16[1,16,16,512]{3,2,1,0:T(8,128)(2,1)S(1)} collective-permute-done((bf16[1,16,16,512]{3,2,1,0:T(8,128)(2,1)S(1)}, bf16[1,16,16,512]{3,2,1,0:T(8,128)(2,1)S(1)}, u32[]{:S(2)}, u32[]{:S(2)}) %collective-permute-start.2) | collective-permute-done | bytes 262176 | tf_op jit(solution)/shard_map/ppermute | solution.py:31
  212.3 3.8 %add_convert_fusion = bf16[2,16,16,512]{3,2,1,0:T(8,128)(2,1)S(1)} fusion(bf16[2,16,16,512]{3,2,1,0:T(8,128)(2,1)S(1)} %bitcast.115, bf16[4,18,18,512]{3,2,1,0:T(8,128)(2,1)S(1)} %select_maximum_fusion, bf16[1,16,16,512]{3,2,1,0:T(8,128)(2,1)S(1)} %collective-permute-done.3, bf16[1,16,16,512]{3,2,1,0:T(8,128)(2,1)S(1)} %collective-permute-done.2, ...), kind=kLoop, calls=%fused_computation.58 | loop fusion | flops 21757952 | bytes 14211072 | tf_op jit(solution)/shard_map/convert_element_type | solution.py:220
  218.9 3.2 %copy.34 = f32[8,4,2,8,1024]{4,3,2,1,0:T(8,128)} copy(f32[8,4,2,8,1024]{4,3,2,0,1:T(8,128)} %bitcast.117) | data formatting | bytes 4194304 | tf_op jit(solution)/shard_map/transpose | solution.py:227
  222.1 42.8 %reduce-scatter.4.cloned.1.call-done = f32[64,1024]{1,0:T(8,128)} async-done(((f32[512,1024]{1,0:T(8,128)}), f32[64,1024]{1,0:T(8,128)}) %reduce-scatter.4.cloned.1.call-update) | async-done | bytes 262160 | tf_op jit(solution)/shard_map/reduce_scatter | solution.py:229
  265.0 24.6 %reduce-scatter.6.cloned.1.call-done = f32[16,1024]{1,0:T(8,128)} async-done(((f32[64,1024]{1,0:T(8,128)}), f32[16,1024]{1,0:T(8,128)}) %reduce-scatter.6.cloned.1.call-update) | async-done | bytes 65552 | tf_op jit(solution)/shard_map/reduce_scatter | solution.py:229
  289.6 16.5 %reduce-scatter.8.cloned.1.call-done = f32[8,1024]{1,0:T(8,128)} async-done(((f32[16,1024]{1,0:T(8,128)}), f32[8,1024]{1,0:T(8,128)}) %reduce-scatter.8.cloned.1.call-update) | async-done | bytes 32784 | tf_op jit(solution)/shard_map/reduce_scatter | solution.py:229
  (130 shorter events, 38.6 us)
Async XLA Ops:
  7.2 186.7 %copy-start = (bf16[512,512]{1,0:T(8,128)(2,1)S(1)}, bf16[512,512]{1,0:T(8,128)(2,1)}, u32[]{:S(2)}) copy-start(bf16[512,512]{1,0:T(8,128)(2,1)} %param.27) | copy-start | bytes 1572868
  7.2 78.3 %all-gather.2.cloned.1.call-start = ((), (), s32[]{:S(2)}) async-start(), calls=%async_computation.3 | async-start | bytes 2621440 | tf_op jit(solution)/shard_map/all_gather | solution.py:175
  11.7 4.2 %copy-start.6 = (bf16[512,128]{1,0:T(8,128)(2,1)S(1)}, bf16[512,128]{1,0:T(8,128)(2,1)}, u32[]{:S(2)}) copy-start(bf16[512,128]{1,0:T(8,128)(2,1)} %param.20) | copy-start | bytes 393220
  11.7 4.2 %copy-start.10 = (f32[512]{0:T(512)S(1)}, f32[512]{0:T(512)}, u32[]{:S(2)}) copy-start(f32[512]{0:T(512)} %param.18) | copy-start | bytes 6148
  12.1 4.5 %copy-start.7 = (bf16[512,128]{1,0:T(8,128)(2,1)S(1)}, bf16[512,128]{1,0:T(8,128)(2,1)}, u32[]{:S(2)}) copy-start(bf16[512,128]{1,0:T(8,128)(2,1)} %param.21) | copy-start | bytes 393220
  12.5 40.6 %copy-start.5 = (bf16[512,128]{1,0:T(8,128)(2,1)S(1)}, bf16[512,128]{1,0:T(8,128)(2,1)}, u32[]{:S(2)}) copy-start(bf16[512,128]{1,0:T(8,128)(2,1)} %param.19) | copy-start | bytes 393220
  52.7 114.2 %all-reduce.4.cloned.1.call-start = ((), (), s32[]{:S(2)}) async-start(), calls=%async_computation.4 | async-start | bytes 1048576 | tf_op jit(solution)/shard_map/psum | solution.py:195
  85.5 33.7 %copy-start.8 = (bf16[128,512]{1,0:T(8,128)(2,1)S(1)}, bf16[128,512]{1,0:T(8,128)(2,1)}, u32[]{:S(2)}) copy-start(bf16[128,512]{1,0:T(8,128)(2,1)} %param.22) | copy-start | bytes 393220
  85.5 81.3 %copy-start.2 = (bf16[512,512]{1,0:T(8,128)(2,1)S(1)}, bf16[512,512]{1,0:T(8,128)(2,1)}, u32[]{:S(2)}) copy-start(bf16[512,512]{1,0:T(8,128)(2,1)} %param.15) | copy-start | bytes 1572868
  89.6 3.4 %copy-start.1 = (f32[2,1024,512]{2,1,0:T(8,128)S(1)}, f32[2,1024,512]{2,1,0:T(8,128)}, u32[]{:S(2)}) copy-start(f32[2,1024,512]{2,1,0:T(8,128)} %get-tuple-element.197) | copy-start | bytes 12582916 | tf_op jit(solution)/shard_map/while
  98.0 3.4 %copy-start.1 = (f32[2,1024,512]{2,1,0:T(8,128)S(1)}, f32[2,1024,512]{2,1,0:T(8,128)}, u32[]{:S(2)}) copy-start(f32[2,1024,512]{2,1,0:T(8,128)} %get-tuple-element.197) | copy-start | bytes 12582916 | tf_op jit(solution)/shard_map/while
  106.4 3.4 %copy-start.1 = (f32[2,1024,512]{2,1,0:T(8,128)S(1)}, f32[2,1024,512]{2,1,0:T(8,128)}, u32[]{:S(2)}) copy-start(f32[2,1024,512]{2,1,0:T(8,128)} %get-tuple-element.197) | copy-start | bytes 12582916 | tf_op jit(solution)/shard_map/while
  119.1 50.3 %copy-start.11 = (bf16[512,512]{1,0:T(8,128)(2,1)S(1)}, bf16[512,512]{1,0:T(8,128)(2,1)}, u32[]{:S(2)}) copy-start(bf16[512,512]{1,0:T(8,128)(2,1)} %param.24) | copy-start | bytes 1572868
  119.1 50.3 %copy-start.12 = (f32[512]{0:T(512)S(1)}, f32[512]{0:T(512)}, u32[]{:S(2)}) copy-start(f32[512]{0:T(512)} %param.23) | copy-start | bytes 6148
  119.2 58.2 %copy-start.9 = (f32[27,512]{1,0:T(8,128)S(1)}, f32[27,512]{1,0:T(8,128)}, u32[]{:S(2)}) copy-start(f32[27,512]{1,0:T(8,128)} %param.25) | copy-start | bytes 165892
  120.4 144.6 %reduce-scatter.4.cloned.1.call-start = ((), (), s32[]{:S(2)}) async-start(), calls=%async_computation.5 | async-start | bytes 2359296 | tf_op jit(solution)/shard_map/reduce_scatter | solution.py:229
  171.1 16.1 %collective-permute-start = (bf16[1,16,16,512]{3,2,1,0:T(8,128)(2,1)S(1)}, bf16[1,16,16,512]{3,2,1,0:T(8,128)(2,1)S(1)}, u32[]{:S(2)}, u32[]{:S(2)}) collective-permute-start(bf16[1,16,16,512]{3,2,1,0:T(8,128)(2,1)S(1)} %bitcast.126), channel_id=1, source_target_pairs={{0,4},{4,8},{8,12},{12,16},{16,20},{20,24},{24,28},{28,32},{32,36}... | collective-permute-start | bytes 786440 | tf_op jit(solution)/shard_map/ppermute | solution.py:31
  175.5 13.6 %collective-permute-start.1 = (bf16[1,16,16,512]{3,2,1,0:T(8,128)(2,1)S(1)}, bf16[1,16,16,512]{3,2,1,0:T(8,128)(2,1)S(1)}, u32[]{:S(2)}, u32[]{:S(2)}) collective-permute-start(bf16[1,16,16,512]{3,2,1,0:T(8,128)(2,1)S(1)} %bitcast.125), channel_id=1, source_target_pairs={{4,0},{8,4},{12,8},{16,12},{20,16},{24,20},{28,24},{32,28},{36,32}... | collective-permute-start | bytes 786440 | tf_op jit(solution)/shard_map/ppermute | solution.py:33
  189.8 4.1 %copy-start.4 = (bf16[512,512]{1,0:T(8,128)(2,1)S(1)}, bf16[512,512]{1,0:T(8,128)(2,1)}, u32[]{:S(2)}) copy-start(bf16[512,512]{1,0:T(8,128)(2,1)} %param.26) | copy-start | bytes 1572868
  194.5 15.7 %collective-permute-start.2 = (bf16[1,16,16,512]{3,2,1,0:T(8,128)(2,1)S(1)}, bf16[1,16,16,512]{3,2,1,0:T(8,128)(2,1)S(1)}, u32[]{:S(2)}, u32[]{:S(2)}) collective-permute-start(bf16[1,16,16,512]{3,2,1,0:T(8,128)(2,1)S(1)} %bitcast.128), channel_id=1, source_target_pairs={{0,4},{4,8},{8,12},{12,16},{16,20},{20,24},{24,28},{28,32},{32,36}... | collective-permute-start | bytes 786440 | tf_op jit(solution)/shard_map/ppermute | solution.py:31
  197.9 13.6 %collective-permute-start.3 = (bf16[1,16,16,512]{3,2,1,0:T(8,128)(2,1)S(1)}, bf16[1,16,16,512]{3,2,1,0:T(8,128)(2,1)S(1)}, u32[]{:S(2)}, u32[]{:S(2)}) collective-permute-start(bf16[1,16,16,512]{3,2,1,0:T(8,128)(2,1)S(1)} %bitcast.127), channel_id=1, source_target_pairs={{4,0},{8,4},{12,8},{16,12},{20,16},{24,20},{28,24},{32,28},{36,32}... | collective-permute-start | bytes 786440 | tf_op jit(solution)/shard_map/ppermute | solution.py:33
  212.3 3.9 %copy-start.3 = (bf16[512,512]{1,0:T(8,128)(2,1)S(1)}, bf16[512,512]{1,0:T(8,128)(2,1)}, u32[]{:S(2)}) copy-start(bf16[512,512]{1,0:T(8,128)(2,1)} %all-reduce.4.cloned.1.call-done) | copy-start | bytes 1572868
  222.1 67.5 %reduce-scatter.6.cloned.1.call-start = ((), (), s32[]{:S(2)}) async-start(), calls=%async_computation.6 | async-start | bytes 327680 | tf_op jit(solution)/shard_map/reduce_scatter | solution.py:229
  265.0 41.1 %reduce-scatter.8.cloned.1.call-start = ((), (), s32[]{:S(2)}) async-start(), calls=%async_computation.7 | async-start | bytes 98304 | tf_op jit(solution)/shard_map/reduce_scatter | solution.py:229
  (1 other events, 3.4 us)
Sparse Core Ops, SparseCore 0:
  52.8 32.6 all-gather.1
  120.5 46.3 all-reduce.3
  222.2 42.6 reduce-scatter.3
  267.3 22.2 reduce-scatter.5
  292.0 13.9 reduce-scatter.7

commit v2 on v1

--- a/solution.py
+++ b/solution.py
@@ -1,8 +1,11 @@
+import functools
 import math
 
 import jax
 import jax.numpy as jnp
 from jax import lax
+from jax.experimental import pallas as pl
+from jax.experimental.pallas import tpu as pltpu
 from jax.sharding import Mesh
 from jax.sharding import PartitionSpec as P
 
@@ -18,6 +21,74 @@
 ROPE_BASE = 100.0
 ROOT_HALF = 0.7071067811865476
 NORMAL_SCALE = 0.3989422804014327
+
+
+MESH = pl.DeviceIdType.MESH
+
+
+def peer_id(p):
+    return (p // 16, p // 2 % 8, p % 2, lax.axis_index("xh"), lax.axis_index("core"))
+
+
+def greet_all(count, me):
+    barrier = pltpu.get_barrier_semaphore()
+
+    def body(k, carry):
+        peer = lax.rem(me + k, count)
+        pl.semaphore_signal(barrier, inc=1, device_id=peer_id(peer), device_id_type=MESH)
+        return carry
+
+    lax.fori_loop(1, count, body, 0)
+    pl.semaphore_wait(barrier, count - 1)
+
+
+def scatter_kernel(count, g_ref, out_ref, slots, send_sem, recv_sem):
+    me = lax.axis_index(SLAB)
+    rows = out_ref.shape[0]
+    greet_all(count, me)
+
+    def copy_to(peer, source):
+        return pltpu.make_async_remote_copy(
+            src_ref=g_ref.at[pl.ds(peer * rows, rows)],
+            dst_ref=slots.at[source],
+            send_sem=send_sem.at[peer],
+            recv_sem=recv_sem.at[source],
+            device_id=peer_id(peer),
+            device_id_type=MESH,
+        )
+
+    def start(k, carry):
+        copy_to(lax.rem(me + k, count), me).start()
+        return carry
+
+    lax.fori_loop(1, count, start, 0)
+    out_ref[...] = g_ref[pl.ds(me * rows, rows)]
+
+    def finish(k, carry):
+        peer = lax.rem(me + k, count)
+        copy_to(peer, me).wait_send()
+        copy_to(peer, peer).wait_recv()
+        out_ref[...] += slots[peer]
+        return carry
+
+    lax.fori_loop(1, count, finish, 0)
+
+
+def slab_scatter(g, count):
+    total_rows, width = g.shape
+    rows = total_rows // count
+    return pl.pallas_call(
+        functools.partial(scatter_kernel, count),
+        out_shape=jax.ShapeDtypeStruct((rows, width), g.dtype),
+        in_specs=[pl.BlockSpec(memory_space=pltpu.VMEM)],
+        out_specs=pl.BlockSpec(memory_space=pltpu.VMEM),
+        scratch_shapes=[
+            pltpu.VMEM((count, rows, width), g.dtype),
+            pltpu.SemaphoreType.DMA((count,)),
+            pltpu.SemaphoreType.DMA((count,)),
+        ],
+        compiler_params=pltpu.CompilerParams(collective_id=1, has_side_effects=True),
+    )(g)
 
 
 def padded_2(cells, sides, width):
@@ -192,7 +263,10 @@
         .astype(jnp.bfloat16)
     )
     partial_value = jnp.dot(heads_out, w_out, preferred_element_type=jnp.float32)
-    head_total = lax.psum(partial_value.astype(jnp.bfloat16), FFN).astype(jnp.float32)
+    head_total = lax.psum_scatter(
+        partial_value.astype(jnp.bfloat16), FFN, scatter_dimension=0, tiled=True
+    )
+    head_total = lax.all_gather(head_total, FFN, axis=0, tiled=True).astype(jnp.float32)
     attended = head_total.astype(jnp.bfloat16)
     residual = tokens.astype(jnp.float32) + head_total
     normed_ffn = layer_norm(residual, gain_ffn).astype(jnp.bfloat16)
@@ -221,12 +295,7 @@
     )
     up_full = jnp.einsum("td,tc->dc", normed_ffn, grad_pre, preferred_element_type=jnp.float32)
     down_full = jnp.einsum("td,tc->dc", grad_out, activated, preferred_element_type=jnp.float32)
-    grads = jnp.concatenate([up_full, down_full], axis=1)
-    sizes = [lax.psum(1, axis) for axis in SLAB]
-    grads = grads.reshape(sizes + [-1, grads.shape[1]])
-    grads = grads.transpose(1, 0, 2, 3, 4).reshape(-1, grads.shape[-1])
-    for axis in ("z", "y", "xl"):
-        grads = lax.psum_scatter(grads, axis, scatter_dimension=0, tiled=True)
+    grads = slab_scatter(jnp.concatenate([up_full, down_full], axis=1), lax.psum(1, SLAB))
     return (attended, grads[:, :channels], grads[:, channels:])
 
 

time: 316 us -> 280 us (0.89)
  waiting for transfers between devices: 184 us -> 87 us
  Pallas kernels: 0 us -> 60.3 us
  blocking collectives: 35.8 us -> 44.2 us
  local copies, waits for them, and re-layouts: 15.5 us -> 10.5 us
    pallas_call x0 -> x1, Pallas kernels: none -> 60.3 us  [slab_scatter(): pl.pallas_call(functools.partial(scatter_kernel, count), out_shape=jax.Sh...]
    reduce_scatter x3 -> x1, waiting for transfers between devices: 83.8 us -> 33 us  [per_device(): lax.psum_scatter(partial_value.astype(jnp.bfloat16), FFN, scatter_dimensi...]
    psum x1 -> x0, waiting for transfers between devices: 46.4 us -> none  [per_device(): lax.psum(partial_value.astype(jnp.bfloat16), FFN).astype(jnp.float32)]
    all_gather x0 -> x1, blocking collectives: none -> 8.48 us  [per_device(): lax.all_gather(head_total, FFN, axis=0, tiled=True).astype(jnp.float32)]
    transpose x1 -> x0, local copies, waits for them, and re-layouts: 3.18 us -> none  [per_device(): grads = grads.transpose(1, 0, 2, 3, 4).reshape(-1, grads.shape[-1])]
  transfers between devices with their start and end apart: 9 -> 6, of which waited for: 9 -> 6; matrix products, arithmetic and copies ran while one was open for 0% -> 0% of each run, Pallas kernels for 0% -> 0%
where the time goes in v2:
time: 280 us; the launch traced here: 279 us
  waiting for transfers between devices  87 us (31%)
  Pallas kernels  60.3 us (22%)
  blocking collectives  44.2 us (16%)
  other arithmetic  28.7 us (10%)
  matrix products  21.5 us (8%)
  between operations  14.5 us (5%)
  starting transfers between devices  12.4 us (4%)
  local copies, waits for them, and re-layouts  10.5 us (4%)
    pallas_call x1, Pallas kernels, slab_scatter(): pl.pallas_call(functools.partial(scatter_kernel, count), out_shape=jax.Sh...  60.3 us
    all_gather x2, blocking collectives, per_device(): pieces = lax.all_gather(pieces, axis, axis=0, tiled=True)  35.8 us
    reduce_scatter x1, waiting for transfers between devices, per_device(): lax.psum_scatter(partial_value.astype(jnp.bfloat16), FFN, scatter_dimensi...  33 us
    all_gather x1, waiting for transfers between devices, per_device(): pieces = lax.all_gather(pieces, axis, axis=0, tiled=True)  32 us
    ppermute x2, waiting for transfers between devices, padded_2(): lax.ppermute(tail, axis, [(i, (i + 1) % count) for i in range(ends)])  18.9 us
    reduce_sum x4, other arithmetic, attend_piece(): row_sum = row_sum * rescale + jnp.sum(expo, axis=2)  12.2 us
    dot_general x4, matrix products, attend_piece(): jnp.einsum('qhd,khd->hqk', queries, key_rows, preferred_element_type=jnp....  10.8 us
    all_gather x1, blocking collectives, per_device(): lax.all_gather(head_total, FFN, axis=0, tiled=True).astype(jnp.float32)  8.48 us
  transfers between devices with their start and end apart: 6, of which 6 were waited for; matrix products, arithmetic and copies ran while one was open for 0% of the time, Pallas kernels for 0%

profile of v2, /device:TPU:2, one launch (start us, length us, event | category | flops | bytes accessed | tf_op | source)
XLA Modules:
  0.0 279.4 jit_solution(698401935292546680)
XLA Ops:
  12.5 3.2 %fusion.75 = (f32[64]{0:T(128)S(1)}, f32[64,512]{1,0:T(8,128)S(1)}) fusion(bf16[64,4096]{1,0:T(8,128)(2,1)S(1)} %reshape.615, bf16[4096,512]{1,0:T(8,128)(2,1)} %param.17), kind=kOutput, calls=%fused_computation.155 | convolution fusion | flops 268468160 | bytes 4849920 | tf_op jit(solution)/shard_map/dot_general | solution.py:221
  16.9 4.8 %all_gather.12 = bf16[128,256]{1,0:T(8,128)(2,1)S(1)} all-gather(bf16[64,256]{1,0:T(8,128)(2,1)S(1)} %pad_maximum_fusion.7), channel_id=1, replica_groups=mesh['y'=4,'z'=8,'xl'=2,'xh'=2,'core'=2] {'xl'}, dimensions={0}, use_global_device_ids=true | all-gather | bytes 98304 | tf_op jit(solution)/shard_map/all_gather | solution.py:246
  21.7 30.9 %all_gather.13 = bf16[1024,256]{1,0:T(8,128)(2,1)} all-gather(bf16[128,256]{1,0:T(8,128)(2,1)S(1)} %all_gather.12), channel_id=1, replica_groups=mesh['y'=4,'z'=8,'xl'=2,'xh'=2,'core'=2] {'z'}, dimensions={0}, use_global_device_ids=true | all-gather | bytes 589824 | tf_op jit(solution)/shard_map/all_gather | solution.py:246
  53.5 32.0 %all-gather.2.cloned.1.call-done = bf16[4096,256]{1,0:T(8,128)(2,1)} async-done(((bf16[1024,256]{1,0:T(8,128)(2,1)}), bf16[4096,256]{1,0:T(8,128)(2,1)}) %all-gather.2.cloned.1.call-update) | async-done | bytes 2097168 | tf_op jit(solution)/shard_map/all_gather | solution.py:246
  85.5 33.6 %while.15 = (s32[]{:T(128)}, f32[2,512]{1,0:T(2,128)S(1)}, f32[2,512]{1,0:T(2,128)S(1)}, f32[2,512,64]{1,2,0:T(8,128)S(1)}, bf16[4,1024,256]{2,1,0:T(8,128)(2,1)...) while((s32[]{:T(128)}, f32[2,512]{1,0:T(2,128)S(1)}, f32[2,512]{1,0:T(2,128)S(1)}, ...), condition=%wide.region_7.8_spmd.clone, body=%wide.region_4.7_spmd.clone.sunk | while | flops 277025792 | bytes 33751168 | solution.py:257
  86.9 2.7 bitcast_reduce_fusion.2
  89.6 3.0 %fusion.109 = f32[2,512]{1,0:T(2,128)S(1)} fusion(f32[2,1024,512]{2,1,0:T(8,128)} %get-tuple-element.191, f32[2,512]{1,0:T(2,128)S(1)} %fusion.108), kind=kLoop, calls=%fused_computation.4.clone.1 | loop fusion | flops 3144704 | bytes 4202496 | tf_op jit(solution)/shard_map/while/body/eval_jaxpr/reduce_sum | solution.py:194
  95.3 2.7 bitcast_reduce_fusion.2
  98.0 3.0 %fusion.109 = f32[2,512]{1,0:T(2,128)S(1)} fusion(f32[2,1024,512]{2,1,0:T(8,128)} %get-tuple-element.191, f32[2,512]{1,0:T(2,128)S(1)} %fusion.108), kind=kLoop, calls=%fused_computation.4.clone.1 | loop fusion | flops 3144704 | bytes 4202496 | tf_op jit(solution)/shard_map/while/body/eval_jaxpr/reduce_sum | solution.py:194
  103.7 2.7 bitcast_reduce_fusion.2
  106.4 3.0 %fusion.109 = f32[2,512]{1,0:T(2,128)S(1)} fusion(f32[2,1024,512]{2,1,0:T(8,128)} %get-tuple-element.191, f32[2,512]{1,0:T(2,128)S(1)} %fusion.108), kind=kLoop, calls=%fused_computation.4.clone.1 | loop fusion | flops 3144704 | bytes 4202496 | tf_op jit(solution)/shard_map/while/body/eval_jaxpr/reduce_sum | solution.py:194
  112.1 2.7 bitcast_reduce_fusion.2
  114.8 3.0 %fusion.109 = f32[2,512]{1,0:T(2,128)S(1)} fusion(f32[2,1024,512]{2,1,0:T(8,128)} %get-tuple-element.191, f32[2,512]{1,0:T(2,128)S(1)} %fusion.108), kind=kLoop, calls=%fused_computation.4.clone.1 | loop fusion | flops 3144704 | bytes 4202496 | tf_op jit(solution)/shard_map/while/body/eval_jaxpr/reduce_sum | solution.py:194
  120.4 33.0 %reduce-scatter.2.cloned.1.call-done = bf16[128,512]{1,0:T(8,128)(2,1)} async-done(((bf16[512,512]{1,0:T(8,128)(2,1)}), bf16[128,512]{1,0:T(8,128)(2,1)}) %reduce-scatter.2.cloned.1.call-update) | async-done | bytes 131088 | tf_op jit(solution)/shard_map/reduce_scatter | solution.py:266
  153.3 8.5 %all_gather.15 = bf16[512,512]{1,0:T(8,128)(2,1)S(1)} all-gather(bf16[128,512]{1,0:T(8,128)(2,1)} %reduce-scatter.2.cloned.1.call-done), channel_id=1, replica_groups=mesh['y'=4,'z'=8,'xl'=2,'xh'=2,'core'=2] {'xh','core'}, dimensions={0}, use_global_device_ids=true | all-gather | bytes 655360 | tf_op jit(solution)/shard_map/all_gather | solution.py:269
  162.9 4.4 %collective-permute-start = (bf16[1,16,16,512]{3,2,1,0:T(8,128)(2,1)S(1)}, bf16[1,16,16,512]{3,2,1,0:T(8,128)(2,1)S(1)}, u32[]{:S(2)}, u32[]{:S(2)}) collective-permute-start(bf16[1,16,16,512]{3,2,1,0:T(8,128)(2,1)S(1)} %bitcast.120), channel_id=1, source_target_pairs={{0,4},{4,8},{8,12},{12,16},{16,20},{20,24},{24,28},{28,32},{32,36}... | collective-permute-start | bytes 786440 | tf_op jit(solution)/shard_map/ppermute | solution.py:102
  167.3 1.9 collective-permute-start.1
  169.3 9.7 %collective-permute-done = bf16[1,16,16,512]{3,2,1,0:T(8,128)(2,1)S(1)} collective-permute-done((bf16[1,16,16,512]{3,2,1,0:T(8,128)(2,1)S(1)}, bf16[1,16,16,512]{3,2,1,0:T(8,128)(2,1)S(1)}, u32[]{:S(2)}, u32[]{:S(2)}) %collective-permute-start) | collective-permute-done | bytes 262176 | tf_op jit(solution)/shard_map/ppermute | solution.py:102
  181.7 3.8 %multiply_add_fusion = f32[2,16,16,512]{3,2,1,0:T(8,128)S(1)} fusion(bf16[2,16,16,512]{3,2,1,0:T(8,128)(2,1)S(1)} %bitcast.113, bf16[4,18,18,512]{3,2,1,0:T(8,128)(2,1)S(1)} %fusion.21, bf16[1,16,16,512]{3,2,1,0:T(8,128)(2,1)S(1)} %collective-permute-done.1, bf16[1,16,16,512]{3,2,1,0:T(8,128)(2,1)S(1)} %collective-permute-done, f32[512]{0:T(512)S(1)} %bitcast.135, ...), kind=kLoop, calls=%fused_computation.59 | loop fusion | flops 21495808 | bytes 14735360 | tf_op jit(solution)/shard_map/add | solution.py:180
  186.4 3.4 %collective-permute-start.2 = (bf16[1,16,16,512]{3,2,1,0:T(8,128)(2,1)S(1)}, bf16[1,16,16,512]{3,2,1,0:T(8,128)(2,1)S(1)}, u32[]{:S(2)}, u32[]{:S(2)}) collective-permute-start(bf16[1,16,16,512]{3,2,1,0:T(8,128)(2,1)S(1)} %bitcast.122), channel_id=1, source_target_pairs={{0,4},{4,8},{8,12},{12,16},{16,20},{20,24},{24,28},{28,32},{32,36}... | collective-permute-start | bytes 786440 | tf_op jit(solution)/shard_map/ppermute | solution.py:102
  189.8 2.7 collective-permute-start.3
  192.9 9.2 %collective-permute-done.2 = bf16[1,16,16,512]{3,2,1,0:T(8,128)(2,1)S(1)} collective-permute-done((bf16[1,16,16,512]{3,2,1,0:T(8,128)(2,1)S(1)}, bf16[1,16,16,512]{3,2,1,0:T(8,128)(2,1)S(1)}, u32[]{:S(2)}, u32[]{:S(2)}) %collective-permute-start.2) | collective-permute-done | bytes 262176 | tf_op jit(solution)/shard_map/ppermute | solution.py:102
  204.1 3.8 %add_convert_fusion = bf16[2,16,16,512]{3,2,1,0:T(8,128)(2,1)S(1)} fusion(bf16[2,16,16,512]{3,2,1,0:T(8,128)(2,1)S(1)} %bitcast.111, bf16[4,18,18,512]{3,2,1,0:T(8,128)(2,1)S(1)} %select_maximum_fusion, bf16[1,16,16,512]{3,2,1,0:T(8,128)(2,1)S(1)} %collective-permute-done.3, bf16[1,16,16,512]{3,2,1,0:T(8,128)(2,1)S(1)} %collective-permute-done.2, ...), kind=kLoop, calls=%fused_computation.58 | loop fusion | flops 21757952 | bytes 14211072 | tf_op jit(solution)/shard_map/convert_element_type | solution.py:294
  210.1 60.3 %shard_map.148 = f32[8,1024]{1,0:T(8,128)} custom-call(f32[512,1024]{1,0:T(8,128)} %pad_maximum_fusion.g_ref), custom_call_target="tpu_custom_call" | custom-call | tf_op jit(solution)/shard_map/pallas_call | solution.py:80
  (119 shorter events, 30.1 us)
Async XLA Ops:
  7.2 178.6 %copy-start = (bf16[512,512]{1,0:T(8,128)(2,1)S(1)}, bf16[512,512]{1,0:T(8,128)(2,1)}, u32[]{:S(2)}) copy-start(bf16[512,512]{1,0:T(8,128)(2,1)} %param.27) | copy-start | bytes 1572868
  7.2 78.3 %all-gather.2.cloned.1.call-start = ((), (), s32[]{:S(2)}) async-start(), calls=%async_computation.1 | async-start | bytes 2621440 | tf_op jit(solution)/shard_map/all_gather | solution.py:246
  11.7 4.2 %copy-start.5 = (bf16[512,128]{1,0:T(8,128)(2,1)S(1)}, bf16[512,128]{1,0:T(8,128)(2,1)}, u32[]{:S(2)}) copy-start(bf16[512,128]{1,0:T(8,128)(2,1)} %param.20) | copy-start | bytes 393220
  11.7 4.2 %copy-start.9 = (f32[512]{0:T(512)S(1)}, f32[512]{0:T(512)}, u32[]{:S(2)}) copy-start(f32[512]{0:T(512)} %param.18) | copy-start | bytes 6148
  12.1 4.5 %copy-start.6 = (bf16[512,128]{1,0:T(8,128)(2,1)S(1)}, bf16[512,128]{1,0:T(8,128)(2,1)}, u32[]{:S(2)}) copy-start(bf16[512,128]{1,0:T(8,128)(2,1)} %param.21) | copy-start | bytes 393220
  12.5 40.6 %copy-start.4 = (bf16[512,128]{1,0:T(8,128)(2,1)S(1)}, bf16[512,128]{1,0:T(8,128)(2,1)}, u32[]{:S(2)}) copy-start(bf16[512,128]{1,0:T(8,128)(2,1)} %param.19) | copy-start | bytes 393220
  52.7 100.7 %reduce-scatter.2.cloned.1.call-start = ((), (), s32[]{:S(2)}) async-start(), calls=%async_computation.2 | async-start | bytes 655360 | tf_op jit(solution)/shard_map/reduce_scatter | solution.py:266
  85.5 33.7 %copy-start.7 = (bf16[128,512]{1,0:T(8,128)(2,1)S(1)}, bf16[128,512]{1,0:T(8,128)(2,1)}, u32[]{:S(2)}) copy-start(bf16[128,512]{1,0:T(8,128)(2,1)} %param.22) | copy-start | bytes 393220
  85.5 76.3 %copy-start.2 = (bf16[512,512]{1,0:T(8,128)(2,1)S(1)}, bf16[512,512]{1,0:T(8,128)(2,1)}, u32[]{:S(2)}) copy-start(bf16[512,512]{1,0:T(8,128)(2,1)} %param.15) | copy-start | bytes 1572868
  89.6 3.4 %copy-start.1 = (f32[2,1024,512]{2,1,0:T(8,128)S(1)}, f32[2,1024,512]{2,1,0:T(8,128)}, u32[]{:S(2)}) copy-start(f32[2,1024,512]{2,1,0:T(8,128)} %get-tuple-element.191) | copy-start | bytes 12582916 | tf_op jit(solution)/shard_map/while
  98.0 3.4 %copy-start.1 = (f32[2,1024,512]{2,1,0:T(8,128)S(1)}, f32[2,1024,512]{2,1,0:T(8,128)}, u32[]{:S(2)}) copy-start(f32[2,1024,512]{2,1,0:T(8,128)} %get-tuple-element.191) | copy-start | bytes 12582916 | tf_op jit(solution)/shard_map/while
  106.4 3.4 %copy-start.1 = (f32[2,1024,512]{2,1,0:T(8,128)S(1)}, f32[2,1024,512]{2,1,0:T(8,128)}, u32[]{:S(2)}) copy-start(f32[2,1024,512]{2,1,0:T(8,128)} %get-tuple-element.191) | copy-start | bytes 12582916 | tf_op jit(solution)/shard_map/while
  114.8 3.4 %copy-start.1 = (f32[2,1024,512]{2,1,0:T(8,128)S(1)}, f32[2,1024,512]{2,1,0:T(8,128)}, u32[]{:S(2)}) copy-start(f32[2,1024,512]{2,1,0:T(8,128)} %get-tuple-element.191) | copy-start | bytes 12582916 | tf_op jit(solution)/shard_map/while
  119.2 43.2 %copy-start.10 = (bf16[512,512]{1,0:T(8,128)(2,1)S(1)}, bf16[512,512]{1,0:T(8,128)(2,1)}, u32[]{:S(2)}) copy-start(bf16[512,512]{1,0:T(8,128)(2,1)} %param.24) | copy-start | bytes 1572868
  119.2 43.2 %copy-start.11 = (f32[512]{0:T(512)S(1)}, f32[512]{0:T(512)}, u32[]{:S(2)}) copy-start(f32[512]{0:T(512)} %param.23) | copy-start | bytes 6148
  120.3 48.9 %copy-start.8 = (f32[27,512]{1,0:T(8,128)S(1)}, f32[27,512]{1,0:T(8,128)}, u32[]{:S(2)}) copy-start(f32[27,512]{1,0:T(8,128)} %param.25) | copy-start | bytes 165892
  162.9 16.1 %collective-permute-start = (bf16[1,16,16,512]{3,2,1,0:T(8,128)(2,1)S(1)}, bf16[1,16,16,512]{3,2,1,0:T(8,128)(2,1)S(1)}, u32[]{:S(2)}, u32[]{:S(2)}) collective-permute-start(bf16[1,16,16,512]{3,2,1,0:T(8,128)(2,1)S(1)} %bitcast.120), channel_id=1, source_target_pairs={{0,4},{4,8},{8,12},{12,16},{16,20},{20,24},{24,28},{28,32},{32,36}... | collective-permute-start | bytes 786440 | tf_op jit(solution)/shard_map/ppermute | solution.py:102
  167.3 13.6 %collective-permute-start.1 = (bf16[1,16,16,512]{3,2,1,0:T(8,128)(2,1)S(1)}, bf16[1,16,16,512]{3,2,1,0:T(8,128)(2,1)S(1)}, u32[]{:S(2)}, u32[]{:S(2)}) collective-permute-start(bf16[1,16,16,512]{3,2,1,0:T(8,128)(2,1)S(1)} %bitcast.119), channel_id=1, source_target_pairs={{4,0},{8,4},{12,8},{16,12},{20,16},{24,20},{28,24},{32,28},{36,32}... | collective-permute-start | bytes 786440 | tf_op jit(solution)/shard_map/ppermute | solution.py:104
  181.7 4.1 %copy-start.3 = (bf16[512,512]{1,0:T(8,128)(2,1)S(1)}, bf16[512,512]{1,0:T(8,128)(2,1)}, u32[]{:S(2)}) copy-start(bf16[512,512]{1,0:T(8,128)(2,1)} %param.26) | copy-start | bytes 1572868
  186.4 15.7 %collective-permute-start.2 = (bf16[1,16,16,512]{3,2,1,0:T(8,128)(2,1)S(1)}, bf16[1,16,16,512]{3,2,1,0:T(8,128)(2,1)S(1)}, u32[]{:S(2)}, u32[]{:S(2)}) collective-permute-start(bf16[1,16,16,512]{3,2,1,0:T(8,128)(2,1)S(1)} %bitcast.122), channel_id=1, source_target_pairs={{0,4},{4,8},{8,12},{12,16},{16,20},{20,24},{24,28},{28,32},{32,36}... | collective-permute-start | bytes 786440 | tf_op jit(solution)/shard_map/ppermute | solution.py:102
  189.8 13.6 %collective-permute-start.3 = (bf16[1,16,16,512]{3,2,1,0:T(8,128)(2,1)S(1)}, bf16[1,16,16,512]{3,2,1,0:T(8,128)(2,1)S(1)}, u32[]{:S(2)}, u32[]{:S(2)}) collective-permute-start(bf16[1,16,16,512]{3,2,1,0:T(8,128)(2,1)S(1)} %bitcast.121), channel_id=1, source_target_pairs={{4,0},{8,4},{12,8},{16,12},{20,16},{24,20},{28,24},{32,28},{36,32}... | collective-permute-start | bytes 786440 | tf_op jit(solution)/shard_map/ppermute | solution.py:104
Sparse Core Ops, SparseCore 0:
  52.8 32.6 all-gather.1
  120.5 32.8 reduce-scatter.1

commit v3 on v2

--- a/solution.py
+++ b/solution.py
@@ -44,12 +44,11 @@
 
 def scatter_kernel(count, g_ref, out_ref, slots, send_sem, recv_sem):
     me = lax.axis_index(SLAB)
-    rows = out_ref.shape[0]
     greet_all(count, me)
 
     def copy_to(peer, source):
         return pltpu.make_async_remote_copy(
-            src_ref=g_ref.at[pl.ds(peer * rows, rows)],
+            src_ref=g_ref.at[peer],
             dst_ref=slots.at[source],
             send_sem=send_sem.at[peer],
             recv_sem=recv_sem.at[source],
@@ -62,13 +61,13 @@
         return carry
 
     lax.fori_loop(1, count, start, 0)
-    out_ref[...] = g_ref[pl.ds(me * rows, rows)]
+    out_ref[...] = g_ref[me].astype(jnp.float32)
 
     def finish(k, carry):
         peer = lax.rem(me + k, count)
         copy_to(peer, me).wait_send()
         copy_to(peer, peer).wait_recv()
-        out_ref[...] += slots[peer]
+        out_ref[...] += slots[peer].astype(jnp.float32)
         return carry
 
     lax.fori_loop(1, count, finish, 0)
@@ -77,18 +76,21 @@
 def slab_scatter(g, count):
     total_rows, width = g.shape
     rows = total_rows // count
-    return pl.pallas_call(
+    tile_rows = 16
+    g = g.astype(jnp.bfloat16).reshape(count, tile_rows, rows * width // tile_rows)
+    summed = pl.pallas_call(
         functools.partial(scatter_kernel, count),
-        out_shape=jax.ShapeDtypeStruct((rows, width), g.dtype),
+        out_shape=jax.ShapeDtypeStruct(g.shape[1:], jnp.float32),
         in_specs=[pl.BlockSpec(memory_space=pltpu.VMEM)],
         out_specs=pl.BlockSpec(memory_space=pltpu.VMEM),
         scratch_shapes=[
-            pltpu.VMEM((count, rows, width), g.dtype),
+            pltpu.VMEM(g.shape, g.dtype),
             pltpu.SemaphoreType.DMA((count,)),
             pltpu.SemaphoreType.DMA((count,)),
         ],
         compiler_params=pltpu.CompilerParams(collective_id=1, has_side_effects=True),
     )(g)
+    return summed.reshape(rows, width)
 
 
 def padded_2(cells, sides, width):

time: 280 us -> 260 us (0.929)
  Pallas kernels: 60.3 us -> 37.4 us
  local copies, waits for them, and re-layouts: 10.5 us -> 14.1 us
    pallas_call x1, Pallas kernels: 60.3 us -> 37.4 us  [slab_scatter(): pl.pallas_call(functools.partial(scatter_kernel, count), out_shape=jax.Sh...]
where the time goes in v3:
time: 260 us; the launch traced here: 259 us
  waiting for transfers between devices  87 us (33%)
  blocking collectives  44.2 us (17%)
  Pallas kernels  37.4 us (14%)
  other arithmetic  27.2 us (10%)
  matrix products  21.5 us (8%)
  between operations  14.6 us (6%)
  local copies, waits for them, and re-layouts  14.1 us (5%)
  starting transfers between devices  12.4 us (5%)
    pallas_call x1, Pallas kernels, slab_scatter(): pl.pallas_call(functools.partial(scatter_kernel, count), out_shape=jax.Sh...  37.4 us
    all_gather x2, blocking collectives, per_device(): pieces = lax.all_gather(pieces, axis, axis=0, tiled=True)  35.8 us
    reduce_scatter x1, waiting for transfers between devices, per_device(): lax.psum_scatter(partial_value.astype(jnp.bfloat16), FFN, scatter_dimensi...  33 us
    all_gather x1, waiting for transfers between devices, per_device(): pieces = lax.all_gather(pieces, axis, axis=0, tiled=True)  32 us
    ppermute x2, waiting for transfers between devices, padded_2(): lax.ppermute(tail, axis, [(i, (i + 1) % count) for i in range(ends)])  18.9 us
    reduce_sum x4, other arithmetic, attend_piece(): row_sum = row_sum * rescale + jnp.sum(expo, axis=2)  12.2 us
    dot_general x4, matrix products, attend_piece(): jnp.einsum('qhd,khd->hqk', queries, key_rows, preferred_element_type=jnp....  10.8 us
    all_gather x1, blocking collectives, per_device(): lax.all_gather(head_total, FFN, axis=0, tiled=True).astype(jnp.float32)  8.48 us
  transfers between devices with their start and end apart: 6, of which 6 were waited for; matrix products, arithmetic and copies ran while one was open for 0% of the time, Pallas kernels for 0%

profile of v3, /device:TPU:2, one launch (start us, length us, event | category | flops | bytes accessed | tf_op | source)
XLA Modules:
  0.0 258.6 jit_solution(11657385044962392947)
XLA Ops:
  12.5 3.2 %fusion.75 = (f32[64]{0:T(128)S(1)}, f32[64,512]{1,0:T(8,128)S(1)}) fusion(bf16[64,4096]{1,0:T(8,128)(2,1)S(1)} %reshape.621, bf16[4096,512]{1,0:T(8,128)(2,1)} %param.17), kind=kOutput, calls=%fused_computation.156 | convolution fusion | flops 268468160 | bytes 4849920 | tf_op jit(solution)/shard_map/dot_general | solution.py:223
  16.9 4.8 %all_gather.12 = bf16[128,256]{1,0:T(8,128)(2,1)S(1)} all-gather(bf16[64,256]{1,0:T(8,128)(2,1)S(1)} %pad_maximum_fusion.7), channel_id=1, replica_groups=mesh['y'=4,'z'=8,'xl'=2,'xh'=2,'core'=2] {'xl'}, dimensions={0}, use_global_device_ids=true | all-gather | bytes 98304 | tf_op jit(solution)/shard_map/all_gather | solution.py:248
  21.7 30.9 %all_gather.13 = bf16[1024,256]{1,0:T(8,128)(2,1)} all-gather(bf16[128,256]{1,0:T(8,128)(2,1)S(1)} %all_gather.12), channel_id=1, replica_groups=mesh['y'=4,'z'=8,'xl'=2,'xh'=2,'core'=2] {'z'}, dimensions={0}, use_global_device_ids=true | all-gather | bytes 589824 | tf_op jit(solution)/shard_map/all_gather | solution.py:248
  53.5 32.0 %all-gather.2.cloned.1.call-done = bf16[4096,256]{1,0:T(8,128)(2,1)} async-done(((bf16[1024,256]{1,0:T(8,128)(2,1)}), bf16[4096,256]{1,0:T(8,128)(2,1)}) %all-gather.2.cloned.1.call-update) | async-done | bytes 2097168 | tf_op jit(solution)/shard_map/all_gather | solution.py:248
  85.5 33.6 %while.15 = (s32[]{:T(128)}, f32[2,512]{1,0:T(2,128)S(1)}, f32[2,512]{1,0:T(2,128)S(1)}, f32[2,512,64]{1,2,0:T(8,128)S(1)}, bf16[4,1024,256]{2,1,0:T(8,128)(2,1)...) while((s32[]{:T(128)}, f32[2,512]{1,0:T(2,128)S(1)}, f32[2,512]{1,0:T(2,128)S(1)}, ...), condition=%wide.region_7.8_spmd.clone, body=%wide.region_4.7_spmd.clone.sunk | while | flops 277025792 | bytes 33751168 | solution.py:259
  86.9 2.7 %bitcast_reduce_fusion.2 = (f32[2,512]{1,0:T(2,128)S(1)}, f32[2,1024,512]{2,1,0:T(8,128)}) fusion(bf16[1024,2,64]{0,2,1:T(8,128)(2,1)S(1)} %bitcast.108, bf16[512,2,64]{0,2,1:T(8,128)(2,1)S(1)} %get-tuple-element.216), kind=kOutput, calls=%fused_computation.1.clone.1 | convolution fusion | flops 136313856 | bytes 4591616 | tf_op jit(solution)/shard_map/while/body/eval_jaxpr/qhd,khd->hqk/dot_general | solution.py:190
  89.6 3.0 %fusion.109 = f32[2,512]{1,0:T(2,128)S(1)} fusion(f32[2,1024,512]{2,1,0:T(8,128)} %get-tuple-element.191, f32[2,512]{1,0:T(2,128)S(1)} %fusion.108), kind=kLoop, calls=%fused_computation.4.clone.1 | loop fusion | flops 3144704 | bytes 4202496 | tf_op jit(solution)/shard_map/while/body/eval_jaxpr/reduce_sum | solution.py:196
  95.3 2.7 %bitcast_reduce_fusion.2 = (f32[2,512]{1,0:T(2,128)S(1)}, f32[2,1024,512]{2,1,0:T(8,128)}) fusion(bf16[1024,2,64]{0,2,1:T(8,128)(2,1)S(1)} %bitcast.108, bf16[512,2,64]{0,2,1:T(8,128)(2,1)S(1)} %get-tuple-element.216), kind=kOutput, calls=%fused_computation.1.clone.1 | convolution fusion | flops 136313856 | bytes 4591616 | tf_op jit(solution)/shard_map/while/body/eval_jaxpr/qhd,khd->hqk/dot_general | solution.py:190
  98.0 3.0 %fusion.109 = f32[2,512]{1,0:T(2,128)S(1)} fusion(f32[2,1024,512]{2,1,0:T(8,128)} %get-tuple-element.191, f32[2,512]{1,0:T(2,128)S(1)} %fusion.108), kind=kLoop, calls=%fused_computation.4.clone.1 | loop fusion | flops 3144704 | bytes 4202496 | tf_op jit(solution)/shard_map/while/body/eval_jaxpr/reduce_sum | solution.py:196
  103.7 2.7 %bitcast_reduce_fusion.2 = (f32[2,512]{1,0:T(2,128)S(1)}, f32[2,1024,512]{2,1,0:T(8,128)}) fusion(bf16[1024,2,64]{0,2,1:T(8,128)(2,1)S(1)} %bitcast.108, bf16[512,2,64]{0,2,1:T(8,128)(2,1)S(1)} %get-tuple-element.216), kind=kOutput, calls=%fused_computation.1.clone.1 | convolution fusion | flops 136313856 | bytes 4591616 | tf_op jit(solution)/shard_map/while/body/eval_jaxpr/qhd,khd->hqk/dot_general | solution.py:190
  106.4 3.0 %fusion.109 = f32[2,512]{1,0:T(2,128)S(1)} fusion(f32[2,1024,512]{2,1,0:T(8,128)} %get-tuple-element.191, f32[2,512]{1,0:T(2,128)S(1)} %fusion.108), kind=kLoop, calls=%fused_computation.4.clone.1 | loop fusion | flops 3144704 | bytes 4202496 | tf_op jit(solution)/shard_map/while/body/eval_jaxpr/reduce_sum | solution.py:196
  112.1 2.7 %bitcast_reduce_fusion.2 = (f32[2,512]{1,0:T(2,128)S(1)}, f32[2,1024,512]{2,1,0:T(8,128)}) fusion(bf16[1024,2,64]{0,2,1:T(8,128)(2,1)S(1)} %bitcast.108, bf16[512,2,64]{0,2,1:T(8,128)(2,1)S(1)} %get-tuple-element.216), kind=kOutput, calls=%fused_computation.1.clone.1 | convolution fusion | flops 136313856 | bytes 4591616 | tf_op jit(solution)/shard_map/while/body/eval_jaxpr/qhd,khd->hqk/dot_general | solution.py:190
  114.8 3.0 %fusion.109 = f32[2,512]{1,0:T(2,128)S(1)} fusion(f32[2,1024,512]{2,1,0:T(8,128)} %get-tuple-element.191, f32[2,512]{1,0:T(2,128)S(1)} %fusion.108), kind=kLoop, calls=%fused_computation.4.clone.1 | loop fusion | flops 3144704 | bytes 4202496 | tf_op jit(solution)/shard_map/while/body/eval_jaxpr/reduce_sum | solution.py:196
  120.3 33.0 %reduce-scatter.2.cloned.1.call-done = bf16[128,512]{1,0:T(8,128)(2,1)} async-done(((bf16[512,512]{1,0:T(8,128)(2,1)}), bf16[128,512]{1,0:T(8,128)(2,1)}) %reduce-scatter.2.cloned.1.call-update) | async-done | bytes 131088 | tf_op jit(solution)/shard_map/reduce_scatter | solution.py:268
  153.3 8.5 %all_gather.15 = bf16[512,512]{1,0:T(8,128)(2,1)S(1)} all-gather(bf16[128,512]{1,0:T(8,128)(2,1)} %reduce-scatter.2.cloned.1.call-done), channel_id=1, replica_groups=mesh['y'=4,'z'=8,'xl'=2,'xh'=2,'core'=2] {'xh','core'}, dimensions={0}, use_global_device_ids=true | all-gather | bytes 655360 | tf_op jit(solution)/shard_map/all_gather | solution.py:271
  162.9 4.4 %collective-permute-start = (bf16[1,16,16,512]{3,2,1,0:T(8,128)(2,1)S(1)}, bf16[1,16,16,512]{3,2,1,0:T(8,128)(2,1)S(1)}, u32[]{:S(2)}, u32[]{:S(2)}) collective-permute-start(bf16[1,16,16,512]{3,2,1,0:T(8,128)(2,1)S(1)} %bitcast.120), channel_id=1, source_target_pairs={{0,4},{4,8},{8,12},{12,16},{16,20},{20,24},{24,28},{28,32},{32,36}... | collective-permute-start | bytes 786440 | tf_op jit(solution)/shard_map/ppermute | solution.py:104
  169.3 9.7 %collective-permute-done = bf16[1,16,16,512]{3,2,1,0:T(8,128)(2,1)S(1)} collective-permute-done((bf16[1,16,16,512]{3,2,1,0:T(8,128)(2,1)S(1)}, bf16[1,16,16,512]{3,2,1,0:T(8,128)(2,1)S(1)}, u32[]{:S(2)}, u32[]{:S(2)}) %collective-permute-start) | collective-permute-done | bytes 262176 | tf_op jit(solution)/shard_map/ppermute | solution.py:104
  181.7 3.8 %multiply_add_fusion = f32[2,16,16,512]{3,2,1,0:T(8,128)S(1)} fusion(bf16[2,16,16,512]{3,2,1,0:T(8,128)(2,1)S(1)} %bitcast.113, bf16[4,18,18,512]{3,2,1,0:T(8,128)(2,1)S(1)} %fusion.21, bf16[1,16,16,512]{3,2,1,0:T(8,128)(2,1)S(1)} %collective-permute-done.1, bf16[1,16,16,512]{3,2,1,0:T(8,128)(2,1)S(1)} %collective-permute-done, f32[512]{0:T(512)S(1)} %bitcast.135, ...), kind=kLoop, calls=%fused_computation.61 | loop fusion | flops 21495808 | bytes 14735360 | tf_op jit(solution)/shard_map/add | solution.py:182
  186.4 3.4 %collective-permute-start.2 = (bf16[1,16,16,512]{3,2,1,0:T(8,128)(2,1)S(1)}, bf16[1,16,16,512]{3,2,1,0:T(8,128)(2,1)S(1)}, u32[]{:S(2)}, u32[]{:S(2)}) collective-permute-start(bf16[1,16,16,512]{3,2,1,0:T(8,128)(2,1)S(1)} %bitcast.122), channel_id=1, source_target_pairs={{0,4},{4,8},{8,12},{12,16},{16,20},{20,24},{24,28},{28,32},{32,36}... | collective-permute-start | bytes 786440 | tf_op jit(solution)/shard_map/ppermute | solution.py:104
  189.7 2.7 %collective-permute-start.3 = (bf16[1,16,16,512]{3,2,1,0:T(8,128)(2,1)S(1)}, bf16[1,16,16,512]{3,2,1,0:T(8,128)(2,1)S(1)}, u32[]{:S(2)}, u32[]{:S(2)}) collective-permute-start(bf16[1,16,16,512]{3,2,1,0:T(8,128)(2,1)S(1)} %bitcast.121), channel_id=1, source_target_pairs={{4,0},{8,4},{12,8},{16,12},{20,16},{24,20},{28,24},{32,28},{36,32}... | collective-permute-start | bytes 786440 | tf_op jit(solution)/shard_map/ppermute | solution.py:106
  192.9 9.2 %collective-permute-done.2 = bf16[1,16,16,512]{3,2,1,0:T(8,128)(2,1)S(1)} collective-permute-done((bf16[1,16,16,512]{3,2,1,0:T(8,128)(2,1)S(1)}, bf16[1,16,16,512]{3,2,1,0:T(8,128)(2,1)S(1)}, u32[]{:S(2)}, u32[]{:S(2)}) %collective-permute-start.2) | collective-permute-done | bytes 262176 | tf_op jit(solution)/shard_map/ppermute | solution.py:104
  204.1 3.8 %add_convert_fusion = bf16[2,16,16,512]{3,2,1,0:T(8,128)(2,1)S(1)} fusion(bf16[2,16,16,512]{3,2,1,0:T(8,128)(2,1)S(1)} %bitcast.111, bf16[4,18,18,512]{3,2,1,0:T(8,128)(2,1)S(1)} %select_maximum_fusion, bf16[1,16,16,512]{3,2,1,0:T(8,128)(2,1)S(1)} %collective-permute-done.3, bf16[1,16,16,512]{3,2,1,0:T(8,128)(2,1)S(1)} %collective-permute-done.2, ...), kind=kLoop, calls=%fused_computation.60 | loop fusion | flops 21757952 | bytes 14211072 | tf_op jit(solution)/shard_map/convert_element_type | solution.py:296
  210.0 2.2 convert_element_type.384.g_ref
  212.2 37.4 %shard_map.148 = f32[16,512]{1,0:T(8,128)} custom-call(bf16[64,16,512]{2,1,0:T(8,128)(2,1)} %convert_element_type.384.g_ref), custom_call_target="tpu_custom_call" | custom-call | tf_op jit(solution)/shard_map/pallas_call | solution.py:81
  (122 shorter events, 31.9 us)
Async XLA Ops:
  7.2 178.6 %copy-start = (bf16[512,512]{1,0:T(8,128)(2,1)S(1)}, bf16[512,512]{1,0:T(8,128)(2,1)}, u32[]{:S(2)}) copy-start(bf16[512,512]{1,0:T(8,128)(2,1)} %param.27) | copy-start | bytes 1572868
  7.2 78.3 %all-gather.2.cloned.1.call-start = ((), (), s32[]{:S(2)}) async-start(), calls=%async_computation.1 | async-start | bytes 2621440 | tf_op jit(solution)/shard_map/all_gather | solution.py:248
  11.7 4.2 %copy-start.5 = (bf16[512,128]{1,0:T(8,128)(2,1)S(1)}, bf16[512,128]{1,0:T(8,128)(2,1)}, u32[]{:S(2)}) copy-start(bf16[512,128]{1,0:T(8,128)(2,1)} %param.20) | copy-start | bytes 393220
  11.7 4.2 %copy-start.9 = (f32[512]{0:T(512)S(1)}, f32[512]{0:T(512)}, u32[]{:S(2)}) copy-start(f32[512]{0:T(512)} %param.18) | copy-start | bytes 6148
  12.1 4.5 %copy-start.6 = (bf16[512,128]{1,0:T(8,128)(2,1)S(1)}, bf16[512,128]{1,0:T(8,128)(2,1)}, u32[]{:S(2)}) copy-start(bf16[512,128]{1,0:T(8,128)(2,1)} %param.21) | copy-start | bytes 393220
  12.5 40.6 %copy-start.4 = (bf16[512,128]{1,0:T(8,128)(2,1)S(1)}, bf16[512,128]{1,0:T(8,128)(2,1)}, u32[]{:S(2)}) copy-start(bf16[512,128]{1,0:T(8,128)(2,1)} %param.19) | copy-start | bytes 393220
  52.7 100.6 %reduce-scatter.2.cloned.1.call-start = ((), (), s32[]{:S(2)}) async-start(), calls=%async_computation.2 | async-start | bytes 655360 | tf_op jit(solution)/shard_map/reduce_scatter | solution.py:268
  85.5 33.7 %copy-start.7 = (bf16[128,512]{1,0:T(8,128)(2,1)S(1)}, bf16[128,512]{1,0:T(8,128)(2,1)}, u32[]{:S(2)}) copy-start(bf16[128,512]{1,0:T(8,128)(2,1)} %param.22) | copy-start | bytes 393220
  85.5 76.3 %copy-start.2 = (bf16[512,512]{1,0:T(8,128)(2,1)S(1)}, bf16[512,512]{1,0:T(8,128)(2,1)}, u32[]{:S(2)}) copy-start(bf16[512,512]{1,0:T(8,128)(2,1)} %param.15) | copy-start | bytes 1572868
  89.6 3.4 %copy-start.1 = (f32[2,1024,512]{2,1,0:T(8,128)S(1)}, f32[2,1024,512]{2,1,0:T(8,128)}, u32[]{:S(2)}) copy-start(f32[2,1024,512]{2,1,0:T(8,128)} %get-tuple-element.191) | copy-start | bytes 12582916 | tf_op jit(solution)/shard_map/while
  98.0 3.4 %copy-start.1 = (f32[2,1024,512]{2,1,0:T(8,128)S(1)}, f32[2,1024,512]{2,1,0:T(8,128)}, u32[]{:S(2)}) copy-start(f32[2,1024,512]{2,1,0:T(8,128)} %get-tuple-element.191) | copy-start | bytes 12582916 | tf_op jit(solution)/shard_map/while
  106.4 3.4 %copy-start.1 = (f32[2,1024,512]{2,1,0:T(8,128)S(1)}, f32[2,1024,512]{2,1,0:T(8,128)}, u32[]{:S(2)}) copy-start(f32[2,1024,512]{2,1,0:T(8,128)} %get-tuple-element.191) | copy-start | bytes 12582916 | tf_op jit(solution)/shard_map/while
  114.8 3.4 %copy-start.1 = (f32[2,1024,512]{2,1,0:T(8,128)S(1)}, f32[2,1024,512]{2,1,0:T(8,128)}, u32[]{:S(2)}) copy-start(f32[2,1024,512]{2,1,0:T(8,128)} %get-tuple-element.191) | copy-start | bytes 12582916 | tf_op jit(solution)/shard_map/while
  119.1 43.2 %copy-start.10 = (bf16[512,512]{1,0:T(8,128)(2,1)S(1)}, bf16[512,512]{1,0:T(8,128)(2,1)}, u32[]{:S(2)}) copy-start(bf16[512,512]{1,0:T(8,128)(2,1)} %param.24) | copy-start | bytes 1572868
  119.1 43.2 %copy-start.11 = (f32[512]{0:T(512)S(1)}, f32[512]{0:T(512)}, u32[]{:S(2)}) copy-start(f32[512]{0:T(512)} %param.23) | copy-start | bytes 6148
  120.3 48.9 %copy-start.8 = (f32[27,512]{1,0:T(8,128)S(1)}, f32[27,512]{1,0:T(8,128)}, u32[]{:S(2)}) copy-start(f32[27,512]{1,0:T(8,128)} %param.25) | copy-start | bytes 165892
  162.9 16.1 %collective-permute-start = (bf16[1,16,16,512]{3,2,1,0:T(8,128)(2,1)S(1)}, bf16[1,16,16,512]{3,2,1,0:T(8,128)(2,1)S(1)}, u32[]{:S(2)}, u32[]{:S(2)}) collective-permute-start(bf16[1,16,16,512]{3,2,1,0:T(8,128)(2,1)S(1)} %bitcast.120), channel_id=1, source_target_pairs={{0,4},{4,8},{8,12},{12,16},{16,20},{20,24},{24,28},{28,32},{32,36}... | collective-permute-start | bytes 786440 | tf_op jit(solution)/shard_map/ppermute | solution.py:104
  167.3 13.6 %collective-permute-start.1 = (bf16[1,16,16,512]{3,2,1,0:T(8,128)(2,1)S(1)}, bf16[1,16,16,512]{3,2,1,0:T(8,128)(2,1)S(1)}, u32[]{:S(2)}, u32[]{:S(2)}) collective-permute-start(bf16[1,16,16,512]{3,2,1,0:T(8,128)(2,1)S(1)} %bitcast.119), channel_id=1, source_target_pairs={{4,0},{8,4},{12,8},{16,12},{20,16},{24,20},{28,24},{32,28},{36,32}... | collective-permute-start | bytes 786440 | tf_op jit(solution)/shard_map/ppermute | solution.py:106
  181.6 4.1 %copy-start.3 = (bf16[512,512]{1,0:T(8,128)(2,1)S(1)}, bf16[512,512]{1,0:T(8,128)(2,1)}, u32[]{:S(2)}) copy-start(bf16[512,512]{1,0:T(8,128)(2,1)} %param.26) | copy-start | bytes 1572868
  186.4 15.7 %collective-permute-start.2 = (bf16[1,16,16,512]{3,2,1,0:T(8,128)(2,1)S(1)}, bf16[1,16,16,512]{3,2,1,0:T(8,128)(2,1)S(1)}, u32[]{:S(2)}, u32[]{:S(2)}) collective-permute-start(bf16[1,16,16,512]{3,2,1,0:T(8,128)(2,1)S(1)} %bitcast.122), channel_id=1, source_target_pairs={{0,4},{4,8},{8,12},{12,16},{16,20},{20,24},{24,28},{28,32},{32,36}... | collective-permute-start | bytes 786440 | tf_op jit(solution)/shard_map/ppermute | solution.py:104
  189.7 13.6 %collective-permute-start.3 = (bf16[1,16,16,512]{3,2,1,0:T(8,128)(2,1)S(1)}, bf16[1,16,16,512]{3,2,1,0:T(8,128)(2,1)S(1)}, u32[]{:S(2)}, u32[]{:S(2)}) collective-permute-start(bf16[1,16,16,512]{3,2,1,0:T(8,128)(2,1)S(1)} %bitcast.121), channel_id=1, source_target_pairs={{4,0},{8,4},{12,8},{16,12},{20,16},{24,20},{28,24},{32,28},{36,32}... | collective-permute-start | bytes 786440 | tf_op jit(solution)/shard_map/ppermute | solution.py:106
Sparse Core Ops, SparseCore 0:
  52.8 32.6 all-gather.1
  120.5 32.8 reduce-scatter.1

commit v4 on v3

--- a/solution.py
+++ b/solution.py
@@ -40,6 +40,75 @@
 
     lax.fori_loop(1, count, body, 0)
     pl.semaphore_wait(barrier, count - 1)
+
+
+def head_peer(q):
+    return (lax.axis_index("y"), lax.axis_index("z"), lax.axis_index("xl"), q // 2, q % 2)
+
+
+def head_sum_kernel(count, part_ref, out_ref, slots, send_sem, recv_sem, send_back, recv_back):
+    me = lax.axis_index(FFN)
+    barrier = pltpu.get_barrier_semaphore()
+    for k in range(1, count):
+        pl.semaphore_signal(
+            barrier, inc=1, device_id=head_peer(lax.rem(me + k, count)), device_id_type=MESH
+        )
+    pl.semaphore_wait(barrier, count - 1)
+
+    def share(peer, source):
+        return pltpu.make_async_remote_copy(
+            src_ref=part_ref.at[peer],
+            dst_ref=slots.at[source],
+            send_sem=send_sem.at[peer],
+            recv_sem=recv_sem.at[source],
+            device_id=head_peer(peer),
+            device_id_type=MESH,
+        )
+
+    def spread(peer, source):
+        return pltpu.make_async_remote_copy(
+            src_ref=out_ref.at[source],
+            dst_ref=out_ref.at[source],
+            send_sem=send_back.at[peer],
+            recv_sem=recv_back.at[source],
+            device_id=head_peer(peer),
+            device_id_type=MESH,
+        )
+
+    peers = [lax.rem(me + k, count) for k in range(1, count)]
+    for peer in peers:
+        share(peer, me).start()
+    total = part_ref[me].astype(jnp.float32)
+    for peer in peers:
+        share(peer, me).wait_send()
+        share(peer, peer).wait_recv()
+        total = total + slots[peer].astype(jnp.float32)
+    out_ref[me] = total.astype(out_ref.dtype)
+    for peer in peers:
+        spread(peer, me).start()
+    for peer in peers:
+        spread(peer, me).wait_send()
+        spread(peer, peer).wait_recv()
+
+
+def head_sum(partial_value, count):
+    rows, width = partial_value.shape
+    parts = partial_value.astype(jnp.bfloat16).reshape(count, rows // count, width)
+    summed = pl.pallas_call(
+        functools.partial(head_sum_kernel, count),
+        out_shape=jax.ShapeDtypeStruct(parts.shape, parts.dtype),
+        in_specs=[pl.BlockSpec(memory_space=pltpu.VMEM)],
+        out_specs=pl.BlockSpec(memory_space=pltpu.VMEM),
+        scratch_shapes=[
+            pltpu.VMEM(parts.shape, parts.dtype),
+            pltpu.SemaphoreType.DMA((count,)),
+            pltpu.SemaphoreType.DMA((count,)),
+            pltpu.SemaphoreType.DMA((count,)),
+            pltpu.SemaphoreType.DMA((count,)),
+        ],
+        compiler_params=pltpu.CompilerParams(collective_id=2, has_side_effects=True),
+    )(parts)
+    return summed.reshape(rows, width)
 
 
 def scatter_kernel(count, g_ref, out_ref, slots, send_sem, recv_sem):
@@ -265,10 +334,7 @@
         .astype(jnp.bfloat16)
     )
     partial_value = jnp.dot(heads_out, w_out, preferred_element_type=jnp.float32)
-    head_total = lax.psum_scatter(
-        partial_value.astype(jnp.bfloat16), FFN, scatter_dimension=0, tiled=True
-    )
-    head_total = lax.all_gather(head_total, FFN, axis=0, tiled=True).astype(jnp.float32)
+    head_total = head_sum(partial_value, lax.psum(1, FFN)).astype(jnp.float32)
     attended = head_total.astype(jnp.bfloat16)
     residual = tokens.astype(jnp.float32) + head_total
     normed_ffn = layer_norm(residual, gain_ffn).astype(jnp.bfloat16)

time: 260 us -> 239 us (0.919)
  waiting for transfers between devices: 87 us -> 54.2 us
  Pallas kernels: 37.4 us -> 54.1 us
  blocking collectives: 44.2 us -> 35.8 us
    reduce_scatter x1 -> x0, waiting for transfers between devices: 33 us -> none  [per_device(): lax.psum_scatter(partial_value.astype(jnp.bfloat16), FFN, scatter_dimensi...]
    pallas_call x0 -> x1, Pallas kernels: none -> 17.7 us  [head_sum(): pl.pallas_call(functools.partial(head_sum_kernel, count), out_shape=jax.S...]
    all_gather x1 -> x0, blocking collectives: 8.48 us -> none  [per_device(): lax.all_gather(head_total, FFN, axis=0, tiled=True).astype(jnp.float32)]
  transfers between devices with their start and end apart: 6 -> 5, of which waited for: 6 -> 5; matrix products, arithmetic and copies ran while one was open for 0% -> 1% of each run, Pallas kernels for 0% -> 0%
where the time goes in v4:
time: 239 us; the launch traced here: 237 us
  waiting for transfers between devices  54.2 us (23%)
  Pallas kernels  54.1 us (23%)
  blocking collectives  35.8 us (15%)
  other arithmetic  29.3 us (12%)
  matrix products  22.5 us (9%)
  between operations  14.6 us (6%)
  local copies, waits for them, and re-layouts  14.1 us (6%)
  starting transfers between devices  12.6 us (5%)
    pallas_call x1, Pallas kernels, slab_scatter(): pl.pallas_call(functools.partial(scatter_kernel, count), out_shape=jax.Sh...  36.5 us
    all_gather x2, blocking collectives, per_device(): pieces = lax.all_gather(pieces, axis, axis=0, tiled=True)  35.8 us
    all_gather x1, waiting for transfers between devices, per_device(): pieces = lax.all_gather(pieces, axis, axis=0, tiled=True)  32.1 us
    ppermute x2, waiting for transfers between devices, padded_2(): lax.ppermute(tail, axis, [(i, (i + 1) % count) for i in range(ends)])  19.2 us
    pallas_call x1, Pallas kernels, head_sum(): pl.pallas_call(functools.partial(head_sum_kernel, count), out_shape=jax.S...  17.7 us
    reduce_sum x4, other arithmetic, attend_piece(): row_sum = row_sum * rescale + jnp.sum(expo, axis=2)  12.2 us
    dot_general x4, matrix products, attend_piece(): jnp.einsum('qhd,khd->hqk', queries, key_rows, preferred_element_type=jnp....  10.8 us
    ppermute x2, starting transfers between devices, padded_2(): lax.ppermute(tail, axis, [(i, (i + 1) % count) for i in range(ends)])  8.57 us
  transfers between devices with their start and end apart: 5, of which 5 were waited for; matrix products, arithmetic and copies ran while one was open for 1% of the time, Pallas kernels for 0%

profile of v4, /device:TPU:2, one launch (start us, length us, event | category | flops | bytes accessed | tf_op | source)
XLA Modules:
  0.0 237.4 jit_solution(13050801453005627022)
XLA Ops:
  12.5 3.2 %fusion.75 = (f32[64]{0:T(128)S(1)}, f32[64,512]{1,0:T(8,128)S(1)}) fusion(bf16[64,4096]{1,0:T(8,128)(2,1)S(1)} %reshape.627, bf16[4096,512]{1,0:T(8,128)(2,1)} %param.17), kind=kOutput, calls=%fused_computation.156 | convolution fusion | flops 268468160 | bytes 4849920 | tf_op jit(solution)/shard_map/dot_general | solution.py:292
  16.9 4.8 %all_gather.9 = bf16[128,256]{1,0:T(8,128)(2,1)S(1)} all-gather(bf16[64,256]{1,0:T(8,128)(2,1)S(1)} %pad_maximum_fusion.7), channel_id=1, replica_groups=mesh['y'=4,'z'=8,'xl'=2,'xh'=2,'core'=2] {'xl'}, dimensions={0}, use_global_device_ids=true | all-gather | bytes 98304 | tf_op jit(solution)/shard_map/all_gather | solution.py:317
  21.7 30.9 %all_gather.10 = bf16[1024,256]{1,0:T(8,128)(2,1)} all-gather(bf16[128,256]{1,0:T(8,128)(2,1)S(1)} %all_gather.9), channel_id=1, replica_groups=mesh['y'=4,'z'=8,'xl'=2,'xh'=2,'core'=2] {'z'}, dimensions={0}, use_global_device_ids=true | all-gather | bytes 589824 | tf_op jit(solution)/shard_map/all_gather | solution.py:317
  53.4 32.1 %all-gather.2.cloned.1.call-done = bf16[4096,256]{1,0:T(8,128)(2,1)} async-done(((bf16[1024,256]{1,0:T(8,128)(2,1)}), bf16[4096,256]{1,0:T(8,128)(2,1)}) %all-gather.2.cloned.1.call-update) | async-done | bytes 2097168 | tf_op jit(solution)/shard_map/all_gather | solution.py:317
  85.5 33.6 %while.15 = (s32[]{:T(128)}, f32[2,512]{1,0:T(2,128)S(1)}, f32[2,512]{1,0:T(2,128)S(1)}, f32[2,512,64]{1,2,0:T(8,128)S(1)}, bf16[4,1024,256]{2,1,0:T(8,128)(2,1)...) while((s32[]{:T(128)}, f32[2,512]{1,0:T(2,128)S(1)}, f32[2,512]{1,0:T(2,128)S(1)}, ...), condition=%wide.region_7.8_spmd.clone, body=%wide.region_4.7_spmd.clone.sunk | while | flops 277025792 | bytes 33751168 | solution.py:328
  86.9 2.7 %bitcast_reduce_fusion.2 = (f32[2,512]{1,0:T(2,128)S(1)}, f32[2,1024,512]{2,1,0:T(8,128)}) fusion(bf16[1024,2,64]{0,2,1:T(8,128)(2,1)S(1)} %bitcast.112, bf16[512,2,64]{0,2,1:T(8,128)(2,1)S(1)} %get-tuple-element.216), kind=kOutput, calls=%fused_computation.1.clone.1 | convolution fusion | flops 136313856 | bytes 4591616 | tf_op jit(solution)/shard_map/while/body/eval_jaxpr/qhd,khd->hqk/dot_general | solution.py:259
  89.6 3.0 %fusion.109 = f32[2,512]{1,0:T(2,128)S(1)} fusion(f32[2,1024,512]{2,1,0:T(8,128)} %get-tuple-element.191, f32[2,512]{1,0:T(2,128)S(1)} %fusion.108), kind=kLoop, calls=%fused_computation.4.clone.1 | loop fusion | flops 3144704 | bytes 4202496 | tf_op jit(solution)/shard_map/while/body/eval_jaxpr/reduce_sum | solution.py:265
  95.3 2.7 %bitcast_reduce_fusion.2 = (f32[2,512]{1,0:T(2,128)S(1)}, f32[2,1024,512]{2,1,0:T(8,128)}) fusion(bf16[1024,2,64]{0,2,1:T(8,128)(2,1)S(1)} %bitcast.112, bf16[512,2,64]{0,2,1:T(8,128)(2,1)S(1)} %get-tuple-element.216), kind=kOutput, calls=%fused_computation.1.clone.1 | convolution fusion | flops 136313856 | bytes 4591616 | tf_op jit(solution)/shard_map/while/body/eval_jaxpr/qhd,khd->hqk/dot_general | solution.py:259
  98.0 3.0 %fusion.109 = f32[2,512]{1,0:T(2,128)S(1)} fusion(f32[2,1024,512]{2,1,0:T(8,128)} %get-tuple-element.191, f32[2,512]{1,0:T(2,128)S(1)} %fusion.108), kind=kLoop, calls=%fused_computation.4.clone.1 | loop fusion | flops 3144704 | bytes 4202496 | tf_op jit(solution)/shard_map/while/body/eval_jaxpr/reduce_sum | solution.py:265
  103.7 2.7 %bitcast_reduce_fusion.2 = (f32[2,512]{1,0:T(2,128)S(1)}, f32[2,1024,512]{2,1,0:T(8,128)}) fusion(bf16[1024,2,64]{0,2,1:T(8,128)(2,1)S(1)} %bitcast.112, bf16[512,2,64]{0,2,1:T(8,128)(2,1)S(1)} %get-tuple-element.216), kind=kOutput, calls=%fused_computation.1.clone.1 | convolution fusion | flops 136313856 | bytes 4591616 | tf_op jit(solution)/shard_map/while/body/eval_jaxpr/qhd,khd->hqk/dot_general | solution.py:259
  106.4 3.0 %fusion.109 = f32[2,512]{1,0:T(2,128)S(1)} fusion(f32[2,1024,512]{2,1,0:T(8,128)} %get-tuple-element.191, f32[2,512]{1,0:T(2,128)S(1)} %fusion.108), kind=kLoop, calls=%fused_computation.4.clone.1 | loop fusion | flops 3144704 | bytes 4202496 | tf_op jit(solution)/shard_map/while/body/eval_jaxpr/reduce_sum | solution.py:265
  112.1 2.7 %bitcast_reduce_fusion.2 = (f32[2,512]{1,0:T(2,128)S(1)}, f32[2,1024,512]{2,1,0:T(8,128)}) fusion(bf16[1024,2,64]{0,2,1:T(8,128)(2,1)S(1)} %bitcast.112, bf16[512,2,64]{0,2,1:T(8,128)(2,1)S(1)} %get-tuple-element.216), kind=kOutput, calls=%fused_computation.1.clone.1 | convolution fusion | flops 136313856 | bytes 4591616 | tf_op jit(solution)/shard_map/while/body/eval_jaxpr/qhd,khd->hqk/dot_general | solution.py:259
  114.8 3.0 %fusion.109 = f32[2,512]{1,0:T(2,128)S(1)} fusion(f32[2,1024,512]{2,1,0:T(8,128)} %get-tuple-element.191, f32[2,512]{1,0:T(2,128)S(1)} %fusion.108), kind=kLoop, calls=%fused_computation.4.clone.1 | loop fusion | flops 3144704 | bytes 4202496 | tf_op jit(solution)/shard_map/while/body/eval_jaxpr/reduce_sum | solution.py:265
  120.3 17.7 %shard_map.148 = bf16[4,128,512]{2,1,0:T(8,128)(2,1)} custom-call(bf16[4,128,512]{2,1,0:T(8,128)(2,1)} %bitcast.123), custom_call_target="tpu_custom_call" | custom-call | tf_op jit(solution)/shard_map/pallas_call | solution.py:97
  142.2 4.4 %collective-permute-start = (bf16[1,16,16,512]{3,2,1,0:T(8,128)(2,1)S(1)}, bf16[1,16,16,512]{3,2,1,0:T(8,128)(2,1)S(1)}, u32[]{:S(2)}, u32[]{:S(2)}) collective-permute-start(bf16[1,16,16,512]{3,2,1,0:T(8,128)(2,1)S(1)} %bitcast.128), channel_id=1, source_target_pairs={{0,4},{4,8},{8,12},{12,16},{16,20},{20,24},{24,28},{28,32},{32,36}... | collective-permute-start | bytes 786440 | tf_op jit(solution)/shard_map/ppermute | solution.py:173
  146.6 1.9 collective-permute-start.1
  148.6 10.1 %collective-permute-done = bf16[1,16,16,512]{3,2,1,0:T(8,128)(2,1)S(1)} collective-permute-done((bf16[1,16,16,512]{3,2,1,0:T(8,128)(2,1)S(1)}, bf16[1,16,16,512]{3,2,1,0:T(8,128)(2,1)S(1)}, u32[]{:S(2)}, u32[]{:S(2)}) %collective-permute-start) | collective-permute-done | bytes 262176 | tf_op jit(solution)/shard_map/ppermute | solution.py:173
  160.7 3.8 %multiply_add_fusion = f32[2,16,16,512]{3,2,1,0:T(8,128)S(1)} fusion(bf16[2,16,16,512]{3,2,1,0:T(8,128)(2,1)S(1)} %bitcast.120, bf16[4,18,18,512]{3,2,1,0:T(8,128)(2,1)S(1)} %fusion.21, bf16[1,16,16,512]{3,2,1,0:T(8,128)(2,1)S(1)} %collective-permute-done.1, bf16[1,16,16,512]{3,2,1,0:T(8,128)(2,1)S(1)} %collective-permute-done, f32[512]{0:T(512)S(1)} %bitcast.143, ...), kind=kLoop, calls=%fused_computation.61 | loop fusion | flops 21495808 | bytes 14735360 | tf_op jit(solution)/shard_map/add | solution.py:251
  165.5 4.2 %collective-permute-start.2 = (bf16[1,16,16,512]{3,2,1,0:T(8,128)(2,1)S(1)}, bf16[1,16,16,512]{3,2,1,0:T(8,128)(2,1)S(1)}, u32[]{:S(2)}, u32[]{:S(2)}) collective-permute-start(bf16[1,16,16,512]{3,2,1,0:T(8,128)(2,1)S(1)} %bitcast.130), channel_id=1, source_target_pairs={{0,4},{4,8},{8,12},{12,16},{16,20},{20,24},{24,28},{28,32},{32,36}... | collective-permute-start | bytes 786440 | tf_op jit(solution)/shard_map/ppermute | solution.py:173
  169.7 2.1 collective-permute-start.3
  172.3 9.1 %collective-permute-done.2 = bf16[1,16,16,512]{3,2,1,0:T(8,128)(2,1)S(1)} collective-permute-done((bf16[1,16,16,512]{3,2,1,0:T(8,128)(2,1)S(1)}, bf16[1,16,16,512]{3,2,1,0:T(8,128)(2,1)S(1)}, u32[]{:S(2)}, u32[]{:S(2)}) %collective-permute-start.2) | collective-permute-done | bytes 262176 | tf_op jit(solution)/shard_map/ppermute | solution.py:173
  183.8 3.8 %add_convert_fusion = bf16[2,16,16,512]{3,2,1,0:T(8,128)(2,1)S(1)} fusion(bf16[2,16,16,512]{3,2,1,0:T(8,128)(2,1)S(1)} %bitcast.115, bf16[4,18,18,512]{3,2,1,0:T(8,128)(2,1)S(1)} %select_maximum_fusion, bf16[1,16,16,512]{3,2,1,0:T(8,128)(2,1)S(1)} %collective-permute-done.3, bf16[1,16,16,512]{3,2,1,0:T(8,128)(2,1)S(1)} %collective-permute-done.2, ...), kind=kLoop, calls=%fused_computation.60 | loop fusion | flops 21757952 | bytes 14211072 | tf_op jit(solution)/shard_map/convert_element_type | solution.py:362
  189.7 2.2 convert_element_type.384.g_ref
  192.0 36.5 %shard_map.149 = f32[16,512]{1,0:T(8,128)} custom-call(bf16[64,16,512]{2,1,0:T(8,128)(2,1)} %convert_element_type.384.g_ref), custom_call_target="tpu_custom_call" | custom-call | tf_op jit(solution)/shard_map/pallas_call | solution.py:150
  (121 shorter events, 32.9 us)
Async XLA Ops:
  7.2 157.7 %copy-start = (bf16[512,512]{1,0:T(8,128)(2,1)S(1)}, bf16[512,512]{1,0:T(8,128)(2,1)}, u32[]{:S(2)}) copy-start(bf16[512,512]{1,0:T(8,128)(2,1)} %param.27) | copy-start | bytes 1572868
  7.2 78.3 %all-gather.2.cloned.1.call-start = ((), (), s32[]{:S(2)}) async-start(), calls=%async_computation | async-start | bytes 2621440 | tf_op jit(solution)/shard_map/all_gather | solution.py:317
  11.7 4.2 %copy-start.6 = (bf16[512,128]{1,0:T(8,128)(2,1)S(1)}, bf16[512,128]{1,0:T(8,128)(2,1)}, u32[]{:S(2)}) copy-start(bf16[512,128]{1,0:T(8,128)(2,1)} %param.20) | copy-start | bytes 393220
  11.7 4.2 %copy-start.10 = (f32[512]{0:T(512)S(1)}, f32[512]{0:T(512)}, u32[]{:S(2)}) copy-start(f32[512]{0:T(512)} %param.18) | copy-start | bytes 6148
  12.1 4.5 %copy-start.7 = (bf16[512,128]{1,0:T(8,128)(2,1)S(1)}, bf16[512,128]{1,0:T(8,128)(2,1)}, u32[]{:S(2)}) copy-start(bf16[512,128]{1,0:T(8,128)(2,1)} %param.21) | copy-start | bytes 393220
  12.5 40.5 %copy-start.5 = (bf16[512,128]{1,0:T(8,128)(2,1)S(1)}, bf16[512,128]{1,0:T(8,128)(2,1)}, u32[]{:S(2)}) copy-start(bf16[512,128]{1,0:T(8,128)(2,1)} %param.19) | copy-start | bytes 393220
  85.5 33.7 %copy-start.8 = (bf16[128,512]{1,0:T(8,128)(2,1)S(1)}, bf16[128,512]{1,0:T(8,128)(2,1)}, u32[]{:S(2)}) copy-start(bf16[128,512]{1,0:T(8,128)(2,1)} %param.22) | copy-start | bytes 393220
  85.5 52.5 %copy-start.2 = (bf16[512,512]{1,0:T(8,128)(2,1)S(1)}, bf16[512,512]{1,0:T(8,128)(2,1)}, u32[]{:S(2)}) copy-start(bf16[512,512]{1,0:T(8,128)(2,1)} %param.15) | copy-start | bytes 1572868
  89.6 3.4 %copy-start.1 = (f32[2,1024,512]{2,1,0:T(8,128)S(1)}, f32[2,1024,512]{2,1,0:T(8,128)}, u32[]{:S(2)}) copy-start(f32[2,1024,512]{2,1,0:T(8,128)} %get-tuple-element.191) | copy-start | bytes 12582916 | tf_op jit(solution)/shard_map/while
  98.0 3.4 %copy-start.1 = (f32[2,1024,512]{2,1,0:T(8,128)S(1)}, f32[2,1024,512]{2,1,0:T(8,128)}, u32[]{:S(2)}) copy-start(f32[2,1024,512]{2,1,0:T(8,128)} %get-tuple-element.191) | copy-start | bytes 12582916 | tf_op jit(solution)/shard_map/while
  106.4 3.4 %copy-start.1 = (f32[2,1024,512]{2,1,0:T(8,128)S(1)}, f32[2,1024,512]{2,1,0:T(8,128)}, u32[]{:S(2)}) copy-start(f32[2,1024,512]{2,1,0:T(8,128)} %get-tuple-element.191) | copy-start | bytes 12582916 | tf_op jit(solution)/shard_map/while
  114.8 3.4 %copy-start.1 = (f32[2,1024,512]{2,1,0:T(8,128)S(1)}, f32[2,1024,512]{2,1,0:T(8,128)}, u32[]{:S(2)}) copy-start(f32[2,1024,512]{2,1,0:T(8,128)} %get-tuple-element.191) | copy-start | bytes 12582916 | tf_op jit(solution)/shard_map/while
  119.1 21.5 %copy-start.11 = (bf16[512,512]{1,0:T(8,128)(2,1)S(1)}, bf16[512,512]{1,0:T(8,128)(2,1)}, u32[]{:S(2)}) copy-start(bf16[512,512]{1,0:T(8,128)(2,1)} %param.24) | copy-start | bytes 1572868
  119.1 21.5 %copy-start.12 = (f32[512]{0:T(512)S(1)}, f32[512]{0:T(512)}, u32[]{:S(2)}) copy-start(f32[512]{0:T(512)} %param.23) | copy-start | bytes 6148
  120.3 28.2 %copy-start.9 = (f32[27,512]{1,0:T(8,128)S(1)}, f32[27,512]{1,0:T(8,128)}, u32[]{:S(2)}) copy-start(f32[27,512]{1,0:T(8,128)} %param.25) | copy-start | bytes 165892
  142.2 16.4 %collective-permute-start = (bf16[1,16,16,512]{3,2,1,0:T(8,128)(2,1)S(1)}, bf16[1,16,16,512]{3,2,1,0:T(8,128)(2,1)S(1)}, u32[]{:S(2)}, u32[]{:S(2)}) collective-permute-start(bf16[1,16,16,512]{3,2,1,0:T(8,128)(2,1)S(1)} %bitcast.128), channel_id=1, source_target_pairs={{0,4},{4,8},{8,12},{12,16},{16,20},{20,24},{24,28},{28,32},{32,36}... | collective-permute-start | bytes 786440 | tf_op jit(solution)/shard_map/ppermute | solution.py:173
  146.6 13.3 %collective-permute-start.1 = (bf16[1,16,16,512]{3,2,1,0:T(8,128)(2,1)S(1)}, bf16[1,16,16,512]{3,2,1,0:T(8,128)(2,1)S(1)}, u32[]{:S(2)}, u32[]{:S(2)}) collective-permute-start(bf16[1,16,16,512]{3,2,1,0:T(8,128)(2,1)S(1)} %bitcast.127), channel_id=1, source_target_pairs={{4,0},{8,4},{12,8},{16,12},{20,16},{24,20},{28,24},{32,28},{36,32}... | collective-permute-start | bytes 786440 | tf_op jit(solution)/shard_map/ppermute | solution.py:175
  160.7 4.1 %copy-start.4 = (bf16[512,512]{1,0:T(8,128)(2,1)S(1)}, bf16[512,512]{1,0:T(8,128)(2,1)}, u32[]{:S(2)}) copy-start(bf16[512,512]{1,0:T(8,128)(2,1)} %param.26) | copy-start | bytes 1572868
  165.5 16.0 %collective-permute-start.2 = (bf16[1,16,16,512]{3,2,1,0:T(8,128)(2,1)S(1)}, bf16[1,16,16,512]{3,2,1,0:T(8,128)(2,1)S(1)}, u32[]{:S(2)}, u32[]{:S(2)}) collective-permute-start(bf16[1,16,16,512]{3,2,1,0:T(8,128)(2,1)S(1)} %bitcast.130), channel_id=1, source_target_pairs={{0,4},{4,8},{8,12},{12,16},{16,20},{20,24},{24,28},{28,32},{32,36}... | collective-permute-start | bytes 786440 | tf_op jit(solution)/shard_map/ppermute | solution.py:173
  169.7 13.4 %collective-permute-start.3 = (bf16[1,16,16,512]{3,2,1,0:T(8,128)(2,1)S(1)}, bf16[1,16,16,512]{3,2,1,0:T(8,128)(2,1)S(1)}, u32[]{:S(2)}, u32[]{:S(2)}) collective-permute-start(bf16[1,16,16,512]{3,2,1,0:T(8,128)(2,1)S(1)} %bitcast.129), channel_id=1, source_target_pairs={{4,0},{8,4},{12,8},{16,12},{20,16},{24,20},{28,24},{32,28},{36,32}... | collective-permute-start | bytes 786440 | tf_op jit(solution)/shard_map/ppermute | solution.py:175
  183.8 3.9 %copy-start.3 = (bf16[4,128,512]{2,1,0:T(8,128)(2,1)S(1)}, bf16[4,128,512]{2,1,0:T(8,128)(2,1)}, u32[]{:S(2)}) copy-start(bf16[4,128,512]{2,1,0:T(8,128)(2,1)} %shard_map.148) | copy-start | bytes 1572868
Sparse Core Ops, SparseCore 0:
  52.8 32.6 all-gather.1

commit v5 on v4

--- a/solution.py
+++ b/solution.py
@@ -40,6 +40,89 @@
 
     lax.fori_loop(1, count, body, 0)
     pl.semaphore_wait(barrier, count - 1)
+
+
+def gather_kernel(row_size, x_ref, out_ref, send_a, recv_a, send_b, recv_b, local_sem):
+    me = lax.axis_index(SLAB)
+    block = x_ref.shape[0]
+    own_y, spot = me // row_size, me % row_size
+    y_count = lax.psum(1, "y")
+    barrier = pltpu.get_barrier_semaphore()
+
+    def greet(k, carry):
+        peer = own_y * row_size + lax.rem(spot + k, row_size)
+        pl.semaphore_signal(barrier, inc=1, device_id=peer_id(peer), device_id_type=MESH)
+        return carry
+
+    lax.fori_loop(1, row_size, greet, 0)
+    for j in range(1, y_count):
+        peer = lax.rem(own_y + j, y_count) * row_size + spot
+        pl.semaphore_signal(barrier, inc=1, device_id=peer_id(peer), device_id_type=MESH)
+    pl.semaphore_wait(barrier, row_size + y_count - 2)
+
+    def along_row(target, source):
+        return pltpu.make_async_remote_copy(
+            src_ref=x_ref,
+            dst_ref=out_ref.at[pl.ds((own_y * row_size + source) * block, block)],
+            send_sem=send_a.at[target],
+            recv_sem=recv_a.at[source],
+            device_id=peer_id(own_y * row_size + target),
+            device_id_type=MESH,
+        )
+
+    def start_row(k, carry):
+        along_row(lax.rem(spot + k, row_size), spot).start()
+        return carry
+
+    lax.fori_loop(1, row_size, start_row, 0)
+    local = pltpu.make_async_copy(x_ref, out_ref.at[pl.ds(me * block, block)], local_sem)
+    local.start()
+    local.wait()
+
+    def finish_row(k, carry):
+        other = lax.rem(spot + k, row_size)
+        along_row(other, spot).wait_send()
+        along_row(other, other).wait_recv()
+        return carry
+
+    lax.fori_loop(1, row_size, finish_row, 0)
+    row_rows = row_size * block
+
+    def across(target_y, source_y):
+        return pltpu.make_async_remote_copy(
+            src_ref=out_ref.at[pl.ds(source_y * row_rows, row_rows)],
+            dst_ref=out_ref.at[pl.ds(source_y * row_rows, row_rows)],
+            send_sem=send_b.at[target_y],
+            recv_sem=recv_b.at[source_y],
+            device_id=peer_id(target_y * row_size + spot),
+            device_id_type=MESH,
+        )
+
+    others = [lax.rem(own_y + j, y_count) for j in range(1, y_count)]
+    for other in others:
+        across(other, own_y).start()
+    for other in others:
+        across(other, own_y).wait_send()
+        across(other, other).wait_recv()
+
+
+def slab_gather(x, count, row_size):
+    rows, width = x.shape
+    y_count = count // row_size
+    return pl.pallas_call(
+        functools.partial(gather_kernel, row_size),
+        out_shape=jax.ShapeDtypeStruct((count * rows, width), x.dtype),
+        in_specs=[pl.BlockSpec(memory_space=pltpu.VMEM)],
+        out_specs=pl.BlockSpec(memory_space=pltpu.VMEM),
+        scratch_shapes=[
+            pltpu.SemaphoreType.DMA((row_size,)),
+            pltpu.SemaphoreType.DMA((row_size,)),
+            pltpu.SemaphoreType.DMA((y_count,)),
+            pltpu.SemaphoreType.DMA((y_count,)),
+            pltpu.SemaphoreType.DMA(()),
+        ],
+        compiler_params=pltpu.CompilerParams(collective_id=0, has_side_effects=True),
+    )(x)
 
 
 def head_peer(q):
@@ -313,8 +396,7 @@
     )
     key_width = heads_dev * HEAD
     pieces = jnp.concatenate([own_keys.reshape(local_rows, key_width), own_values], axis=1)
-    for axis in ("xl", "z", "y"):
-        pieces = lax.all_gather(pieces, axis, axis=0, tiled=True)
+    pieces = slab_gather(pieces, lax.psum(1, SLAB), lax.psum(1, ("z", "xl")))
     row_count = pieces.shape[0]
     block_rows = math.gcd(row_count, 1024)
     block_count = row_count // block_rows

time: 239 us -> 206 us (0.86)
  Pallas kernels: 54.1 us -> 104 us
  blocking collectives: 35.8 us -> 0 us
  waiting for transfers between devices: 54.2 us -> 21.3 us
  between operations: 14.6 us -> 1.2 us
    pallas_call x0 -> x1, Pallas kernels: none -> 49.2 us  [slab_gather(): pl.pallas_call(functools.partial(gather_kernel, row_size), out_shape=jax....]
    all_gather x2 -> x0, blocking collectives: 35.8 us -> none  [per_device(): pieces = lax.all_gather(pieces, axis, axis=0, tiled=True)]
    all_gather x1 -> x0, waiting for transfers between devices: 32.1 us -> none  [per_device(): pieces = lax.all_gather(pieces, axis, axis=0, tiled=True)]
  transfers between devices with their start and end apart: 5 -> 4, of which waited for: 5 -> 3; matrix products, arithmetic and copies ran while one was open for 1% -> 0% of each run, Pallas kernels for 0% -> 0%
where the time goes in v5:
time: 206 us; the launch traced here: 205 us
  Pallas kernels  104 us (50%)
  other arithmetic  29.9 us (15%)
  matrix products  22.5 us (11%)
  waiting for transfers between devices  21.3 us (10%)
  local copies, waits for them, and re-layouts  14.1 us (7%)
  starting transfers between devices  11.9 us (6%)
    pallas_call x1, Pallas kernels, slab_gather(): pl.pallas_call(functools.partial(gather_kernel, row_size), out_shape=jax....  49.2 us
    pallas_call x1, Pallas kernels, slab_scatter(): pl.pallas_call(functools.partial(scatter_kernel, count), out_shape=jax.Sh...  36.7 us
    ppermute x2, waiting for transfers between devices, padded_2(): lax.ppermute(tail, axis, [(i, (i + 1) % count) for i in range(ends)])  19.8 us
    pallas_call x1, Pallas kernels, head_sum(): pl.pallas_call(functools.partial(head_sum_kernel, count), out_shape=jax.S...  17.7 us
    reduce_sum x4, other arithmetic, attend_piece(): row_sum = row_sum * rescale + jnp.sum(expo, axis=2)  12.2 us
    dot_general x4, matrix products, attend_piece(): jnp.einsum('qhd,khd->hqk', queries, key_rows, preferred_element_type=jnp....  10.8 us
    ppermute x2, starting transfers between devices, padded_2(): lax.ppermute(tail, axis, [(i, (i + 1) % count) for i in range(ends)])  6.72 us
    dynamic_slice x8, local copies, waits for them, and re-layouts, per_device(): state_tuple, _ = lax.scan(one_block, state_tuple, blocks)  5.21 us
  transfers between devices with their start and end apart: 4, of which 3 were waited for; matrix products, arithmetic and copies ran while one was open for 0% of the time, Pallas kernels for 0%

profile of v5, /device:TPU:2, one launch (start us, length us, event | category | flops | bytes accessed | tf_op | source)
XLA Modules:
  0.0 204.7 jit_solution(5720961077136451699)
XLA Ops:
  6.0 3.2 %fusion.75 = (f32[64]{0:T(128)S(1)}, f32[64,512]{1,0:T(8,128)S(1)}) fusion(bf16[64,4096]{1,0:T(8,128)(2,1)S(1)} %reshape.627, bf16[4096,512]{1,0:T(8,128)(2,1)} %param.17), kind=kOutput, calls=%fused_computation.156 | convolution fusion | flops 268468160 | bytes 4849920 | tf_op jit(solution)/shard_map/dot_general | solution.py:375
  11.0 49.2 %shard_map.148 = bf16[4096,256]{1,0:T(8,128)(2,1)} custom-call(bf16[64,256]{1,0:T(8,128)(2,1)} %pad_maximum_fusion.7.x_ref), custom_call_target="tpu_custom_call" | custom-call | tf_op jit(solution)/shard_map/pallas_call | solution.py:112
  60.9 33.6 %while.15 = (s32[]{:T(128)}, f32[2,512]{1,0:T(2,128)S(1)}, f32[2,512]{1,0:T(2,128)S(1)}, f32[2,512,64]{1,2,0:T(8,128)S(1)}, bf16[4,1024,256]{2,1,0:T(8,128)(2,1)...) while((s32[]{:T(128)}, f32[2,512]{1,0:T(2,128)S(1)}, f32[2,512]{1,0:T(2,128)S(1)}, ...), condition=%wide.region_7.8_spmd.clone, body=%wide.region_4.7_spmd.clone.sunk | while | flops 277025792 | bytes 33751168 | solution.py:410
  62.3 2.7 %bitcast_reduce_fusion.2 = (f32[2,512]{1,0:T(2,128)S(1)}, f32[2,1024,512]{2,1,0:T(8,128)}) fusion(bf16[1024,2,64]{0,2,1:T(8,128)(2,1)S(1)} %bitcast.112, bf16[512,2,64]{0,2,1:T(8,128)(2,1)S(1)} %get-tuple-element.216), kind=kOutput, calls=%fused_computation.1.clone.1 | convolution fusion | flops 136313856 | bytes 4591616 | tf_op jit(solution)/shard_map/while/body/eval_jaxpr/qhd,khd->hqk/dot_general | solution.py:342
  65.1 3.0 %fusion.109 = f32[2,512]{1,0:T(2,128)S(1)} fusion(f32[2,1024,512]{2,1,0:T(8,128)} %get-tuple-element.191, f32[2,512]{1,0:T(2,128)S(1)} %fusion.108), kind=kLoop, calls=%fused_computation.4.clone.1 | loop fusion | flops 3144704 | bytes 4202496 | tf_op jit(solution)/shard_map/while/body/eval_jaxpr/reduce_sum | solution.py:348
  70.7 2.7 %bitcast_reduce_fusion.2 = (f32[2,512]{1,0:T(2,128)S(1)}, f32[2,1024,512]{2,1,0:T(8,128)}) fusion(bf16[1024,2,64]{0,2,1:T(8,128)(2,1)S(1)} %bitcast.112, bf16[512,2,64]{0,2,1:T(8,128)(2,1)S(1)} %get-tuple-element.216), kind=kOutput, calls=%fused_computation.1.clone.1 | convolution fusion | flops 136313856 | bytes 4591616 | tf_op jit(solution)/shard_map/while/body/eval_jaxpr/qhd,khd->hqk/dot_general | solution.py:342
  73.5 3.0 %fusion.109 = f32[2,512]{1,0:T(2,128)S(1)} fusion(f32[2,1024,512]{2,1,0:T(8,128)} %get-tuple-element.191, f32[2,512]{1,0:T(2,128)S(1)} %fusion.108), kind=kLoop, calls=%fused_computation.4.clone.1 | loop fusion | flops 3144704 | bytes 4202496 | tf_op jit(solution)/shard_map/while/body/eval_jaxpr/reduce_sum | solution.py:348
  79.1 2.7 %bitcast_reduce_fusion.2 = (f32[2,512]{1,0:T(2,128)S(1)}, f32[2,1024,512]{2,1,0:T(8,128)}) fusion(bf16[1024,2,64]{0,2,1:T(8,128)(2,1)S(1)} %bitcast.112, bf16[512,2,64]{0,2,1:T(8,128)(2,1)S(1)} %get-tuple-element.216), kind=kOutput, calls=%fused_computation.1.clone.1 | convolution fusion | flops 136313856 | bytes 4591616 | tf_op jit(solution)/shard_map/while/body/eval_jaxpr/qhd,khd->hqk/dot_general | solution.py:342
  81.8 3.0 %fusion.109 = f32[2,512]{1,0:T(2,128)S(1)} fusion(f32[2,1024,512]{2,1,0:T(8,128)} %get-tuple-element.191, f32[2,512]{1,0:T(2,128)S(1)} %fusion.108), kind=kLoop, calls=%fused_computation.4.clone.1 | loop fusion | flops 3144704 | bytes 4202496 | tf_op jit(solution)/shard_map/while/body/eval_jaxpr/reduce_sum | solution.py:348
  87.5 2.7 %bitcast_reduce_fusion.2 = (f32[2,512]{1,0:T(2,128)S(1)}, f32[2,1024,512]{2,1,0:T(8,128)}) fusion(bf16[1024,2,64]{0,2,1:T(8,128)(2,1)S(1)} %bitcast.112, bf16[512,2,64]{0,2,1:T(8,128)(2,1)S(1)} %get-tuple-element.216), kind=kOutput, calls=%fused_computation.1.clone.1 | convolution fusion | flops 136313856 | bytes 4591616 | tf_op jit(solution)/shard_map/while/body/eval_jaxpr/qhd,khd->hqk/dot_general | solution.py:342
  90.2 3.0 %fusion.109 = f32[2,512]{1,0:T(2,128)S(1)} fusion(f32[2,1024,512]{2,1,0:T(8,128)} %get-tuple-element.191, f32[2,512]{1,0:T(2,128)S(1)} %fusion.108), kind=kLoop, calls=%fused_computation.4.clone.1 | loop fusion | flops 3144704 | bytes 4202496 | tf_op jit(solution)/shard_map/while/body/eval_jaxpr/reduce_sum | solution.py:348
  95.8 17.7 %shard_map.149 = bf16[4,128,512]{2,1,0:T(8,128)(2,1)} custom-call(bf16[4,128,512]{2,1,0:T(8,128)(2,1)} %bitcast.123), custom_call_target="tpu_custom_call" | custom-call | tf_op jit(solution)/shard_map/pallas_call | solution.py:180
  116.1 1.6 convolution_convert_fusion.2
  117.7 2.8 %collective-permute-start = (bf16[1,16,16,512]{3,2,1,0:T(8,128)(2,1)S(1)}, bf16[1,16,16,512]{3,2,1,0:T(8,128)(2,1)S(1)}, u32[]{:S(2)}, u32[]{:S(2)}) collective-permute-start(bf16[1,16,16,512]{3,2,1,0:T(8,128)(2,1)S(1)} %bitcast.128), channel_id=1, source_target_pairs={{0,4},{4,8},{8,12},{12,16},{16,20},{20,24},{24,28},{28,32},{32,36}... | collective-permute-start | bytes 786440 | tf_op jit(solution)/shard_map/ppermute | solution.py:256
  120.5 3.1 %collective-permute-start.1 = (bf16[1,16,16,512]{3,2,1,0:T(8,128)(2,1)S(1)}, bf16[1,16,16,512]{3,2,1,0:T(8,128)(2,1)S(1)}, u32[]{:S(2)}, u32[]{:S(2)}) collective-permute-start(bf16[1,16,16,512]{3,2,1,0:T(8,128)(2,1)S(1)} %bitcast.127), channel_id=1, source_target_pairs={{4,0},{8,4},{12,8},{16,12},{20,16},{24,20},{28,24},{32,28},{36,32}... | collective-permute-start | bytes 786440 | tf_op jit(solution)/shard_map/ppermute | solution.py:258
  123.7 10.5 %collective-permute-done = bf16[1,16,16,512]{3,2,1,0:T(8,128)(2,1)S(1)} collective-permute-done((bf16[1,16,16,512]{3,2,1,0:T(8,128)(2,1)S(1)}, bf16[1,16,16,512]{3,2,1,0:T(8,128)(2,1)S(1)}, u32[]{:S(2)}, u32[]{:S(2)}) %collective-permute-start) | collective-permute-done | bytes 262176 | tf_op jit(solution)/shard_map/ppermute | solution.py:256
  135.0 3.8 %multiply_add_fusion = f32[2,16,16,512]{3,2,1,0:T(8,128)S(1)} fusion(bf16[2,16,16,512]{3,2,1,0:T(8,128)(2,1)S(1)} %bitcast.121, bf16[4,18,18,512]{3,2,1,0:T(8,128)(2,1)S(1)} %fusion.21, bf16[1,16,16,512]{3,2,1,0:T(8,128)(2,1)S(1)} %collective-permute-done.1, bf16[1,16,16,512]{3,2,1,0:T(8,128)(2,1)S(1)} %collective-permute-done, f32[512]{0:T(512)S(1)} %bitcast.143, ...), kind=kLoop, calls=%fused_computation.61 | loop fusion | flops 21495808 | bytes 14735360 | tf_op jit(solution)/shard_map/add | solution.py:334
  139.7 3.9 %collective-permute-start.2 = (bf16[1,16,16,512]{3,2,1,0:T(8,128)(2,1)S(1)}, bf16[1,16,16,512]{3,2,1,0:T(8,128)(2,1)S(1)}, u32[]{:S(2)}, u32[]{:S(2)}) collective-permute-start(bf16[1,16,16,512]{3,2,1,0:T(8,128)(2,1)S(1)} %bitcast.130), channel_id=1, source_target_pairs={{0,4},{4,8},{8,12},{12,16},{16,20},{20,24},{24,28},{28,32},{32,36}... | collective-permute-start | bytes 786440 | tf_op jit(solution)/shard_map/ppermute | solution.py:256
  143.6 2.1 %collective-permute-start.3 = (bf16[1,16,16,512]{3,2,1,0:T(8,128)(2,1)S(1)}, bf16[1,16,16,512]{3,2,1,0:T(8,128)(2,1)S(1)}, u32[]{:S(2)}, u32[]{:S(2)}) collective-permute-start(bf16[1,16,16,512]{3,2,1,0:T(8,128)(2,1)S(1)} %bitcast.129), channel_id=1, source_target_pairs={{4,0},{8,4},{12,8},{16,12},{20,16},{24,20},{28,24},{32,28},{36,32}... | collective-permute-start | bytes 786440 | tf_op jit(solution)/shard_map/ppermute | solution.py:258
  146.2 9.3 %collective-permute-done.2 = bf16[1,16,16,512]{3,2,1,0:T(8,128)(2,1)S(1)} collective-permute-done((bf16[1,16,16,512]{3,2,1,0:T(8,128)(2,1)S(1)}, bf16[1,16,16,512]{3,2,1,0:T(8,128)(2,1)S(1)}, u32[]{:S(2)}, u32[]{:S(2)}) %collective-permute-start.2) | collective-permute-done | bytes 262176 | tf_op jit(solution)/shard_map/ppermute | solution.py:256
  155.5 1.5 collective-permute-done.3
  157.8 3.8 %add_convert_fusion = bf16[2,16,16,512]{3,2,1,0:T(8,128)(2,1)S(1)} fusion(bf16[2,16,16,512]{3,2,1,0:T(8,128)(2,1)S(1)} %bitcast.116, bf16[4,18,18,512]{3,2,1,0:T(8,128)(2,1)S(1)} %select_maximum_fusion, bf16[1,16,16,512]{3,2,1,0:T(8,128)(2,1)S(1)} %collective-permute-done.3, bf16[1,16,16,512]{3,2,1,0:T(8,128)(2,1)S(1)} %collective-permute-done.2, ...), kind=kLoop, calls=%fused_computation.60 | loop fusion | flops 21757952 | bytes 14211072 | tf_op jit(solution)/shard_map/convert_element_type | solution.py:444
  163.7 2.2 %convert_element_type.384.g_ref = bf16[64,16,512]{2,1,0:T(8,128)(2,1)} reshape(bf16[512,1024]{1,0:T(8,128)(2,1)} %copy.28) | data formatting | bytes 2097152 | tf_op jit(solution)/shard_map/convert_element_type | solution.py:232
  165.9 36.7 %shard_map.150 = f32[16,512]{1,0:T(8,128)} custom-call(bf16[64,16,512]{2,1,0:T(8,128)(2,1)} %convert_element_type.384.g_ref), custom_call_target="tpu_custom_call" | custom-call | tf_op jit(solution)/shard_map/pallas_call | solution.py:233
  (117 shorter events, 28.9 us)
Async XLA Ops:
  0.6 138.4 %copy-start = (bf16[512,512]{1,0:T(8,128)(2,1)S(1)}, bf16[512,512]{1,0:T(8,128)(2,1)}, u32[]{:S(2)}) copy-start(bf16[512,512]{1,0:T(8,128)(2,1)} %param.27) | copy-start | bytes 1572868
  5.2 4.2 %copy-start.6 = (bf16[512,128]{1,0:T(8,128)(2,1)S(1)}, bf16[512,128]{1,0:T(8,128)(2,1)}, u32[]{:S(2)}) copy-start(bf16[512,128]{1,0:T(8,128)(2,1)} %param.20) | copy-start | bytes 393220
  5.2 4.2 %copy-start.10 = (f32[512]{0:T(512)S(1)}, f32[512]{0:T(512)}, u32[]{:S(2)}) copy-start(f32[512]{0:T(512)} %param.18) | copy-start | bytes 6148
  5.6 4.5 %copy-start.7 = (bf16[512,128]{1,0:T(8,128)(2,1)S(1)}, bf16[512,128]{1,0:T(8,128)(2,1)}, u32[]{:S(2)}) copy-start(bf16[512,128]{1,0:T(8,128)(2,1)} %param.21) | copy-start | bytes 393220
  6.0 54.2 %copy-start.5 = (bf16[512,128]{1,0:T(8,128)(2,1)S(1)}, bf16[512,128]{1,0:T(8,128)(2,1)}, u32[]{:S(2)}) copy-start(bf16[512,128]{1,0:T(8,128)(2,1)} %param.19) | copy-start | bytes 393220
  60.9 33.7 %copy-start.8 = (bf16[128,512]{1,0:T(8,128)(2,1)S(1)}, bf16[128,512]{1,0:T(8,128)(2,1)}, u32[]{:S(2)}) copy-start(bf16[128,512]{1,0:T(8,128)(2,1)} %param.22) | copy-start | bytes 393220
  60.9 52.6 %copy-start.2 = (bf16[512,512]{1,0:T(8,128)(2,1)S(1)}, bf16[512,512]{1,0:T(8,128)(2,1)}, u32[]{:S(2)}) copy-start(bf16[512,512]{1,0:T(8,128)(2,1)} %param.15) | copy-start | bytes 1572868
  65.0 3.4 %copy-start.1 = (f32[2,1024,512]{2,1,0:T(8,128)S(1)}, f32[2,1024,512]{2,1,0:T(8,128)}, u32[]{:S(2)}) copy-start(f32[2,1024,512]{2,1,0:T(8,128)} %get-tuple-element.191) | copy-start | bytes 12582916 | tf_op jit(solution)/shard_map/while
  73.4 3.4 %copy-start.1 = (f32[2,1024,512]{2,1,0:T(8,128)S(1)}, f32[2,1024,512]{2,1,0:T(8,128)}, u32[]{:S(2)}) copy-start(f32[2,1024,512]{2,1,0:T(8,128)} %get-tuple-element.191) | copy-start | bytes 12582916 | tf_op jit(solution)/shard_map/while
  81.8 3.4 %copy-start.1 = (f32[2,1024,512]{2,1,0:T(8,128)S(1)}, f32[2,1024,512]{2,1,0:T(8,128)}, u32[]{:S(2)}) copy-start(f32[2,1024,512]{2,1,0:T(8,128)} %get-tuple-element.191) | copy-start | bytes 12582916 | tf_op jit(solution)/shard_map/while
  90.2 3.4 %copy-start.1 = (f32[2,1024,512]{2,1,0:T(8,128)S(1)}, f32[2,1024,512]{2,1,0:T(8,128)}, u32[]{:S(2)}) copy-start(f32[2,1024,512]{2,1,0:T(8,128)} %get-tuple-element.191) | copy-start | bytes 12582916 | tf_op jit(solution)/shard_map/while
  94.6 21.5 %copy-start.11 = (bf16[512,512]{1,0:T(8,128)(2,1)S(1)}, bf16[512,512]{1,0:T(8,128)(2,1)}, u32[]{:S(2)}) copy-start(bf16[512,512]{1,0:T(8,128)(2,1)} %param.24) | copy-start | bytes 1572868
  94.6 21.5 %copy-start.12 = (f32[512]{0:T(512)S(1)}, f32[512]{0:T(512)}, u32[]{:S(2)}) copy-start(f32[512]{0:T(512)} %param.23) | copy-start | bytes 6148
  95.7 27.9 %copy-start.9 = (f32[27,512]{1,0:T(8,128)S(1)}, f32[27,512]{1,0:T(8,128)}, u32[]{:S(2)}) copy-start(f32[27,512]{1,0:T(8,128)} %param.25) | copy-start | bytes 165892
  117.7 16.4 %collective-permute-start = (bf16[1,16,16,512]{3,2,1,0:T(8,128)(2,1)S(1)}, bf16[1,16,16,512]{3,2,1,0:T(8,128)(2,1)S(1)}, u32[]{:S(2)}, u32[]{:S(2)}) collective-permute-start(bf16[1,16,16,512]{3,2,1,0:T(8,128)(2,1)S(1)} %bitcast.128), channel_id=1, source_target_pairs={{0,4},{4,8},{8,12},{12,16},{16,20},{20,24},{24,28},{28,32},{32,36}... | collective-permute-start | bytes 786440 | tf_op jit(solution)/shard_map/ppermute | solution.py:256
  120.5 13.6 %collective-permute-start.1 = (bf16[1,16,16,512]{3,2,1,0:T(8,128)(2,1)S(1)}, bf16[1,16,16,512]{3,2,1,0:T(8,128)(2,1)S(1)}, u32[]{:S(2)}, u32[]{:S(2)}) collective-permute-start(bf16[1,16,16,512]{3,2,1,0:T(8,128)(2,1)S(1)} %bitcast.127), channel_id=1, source_target_pairs={{4,0},{8,4},{12,8},{16,12},{20,16},{24,20},{28,24},{32,28},{36,32}... | collective-permute-start | bytes 786440 | tf_op jit(solution)/shard_map/ppermute | solution.py:258
  134.9 4.1 %copy-start.4 = (bf16[512,512]{1,0:T(8,128)(2,1)S(1)}, bf16[512,512]{1,0:T(8,128)(2,1)}, u32[]{:S(2)}) copy-start(bf16[512,512]{1,0:T(8,128)(2,1)} %param.26) | copy-start | bytes 1572868
  139.7 15.8 %collective-permute-start.2 = (bf16[1,16,16,512]{3,2,1,0:T(8,128)(2,1)S(1)}, bf16[1,16,16,512]{3,2,1,0:T(8,128)(2,1)S(1)}, u32[]{:S(2)}, u32[]{:S(2)}) collective-permute-start(bf16[1,16,16,512]{3,2,1,0:T(8,128)(2,1)S(1)} %bitcast.130), channel_id=1, source_target_pairs={{0,4},{4,8},{8,12},{12,16},{16,20},{20,24},{24,28},{28,32},{32,36}... | collective-permute-start | bytes 786440 | tf_op jit(solution)/shard_map/ppermute | solution.py:256
  143.6 13.4 %collective-permute-start.3 = (bf16[1,16,16,512]{3,2,1,0:T(8,128)(2,1)S(1)}, bf16[1,16,16,512]{3,2,1,0:T(8,128)(2,1)S(1)}, u32[]{:S(2)}, u32[]{:S(2)}) collective-permute-start(bf16[1,16,16,512]{3,2,1,0:T(8,128)(2,1)S(1)} %bitcast.129), channel_id=1, source_target_pairs={{4,0},{8,4},{12,8},{16,12},{20,16},{24,20},{28,24},{32,28},{36,32}... | collective-permute-start | bytes 786440 | tf_op jit(solution)/shard_map/ppermute | solution.py:258
  157.7 3.9 %copy-start.3 = (bf16[4,128,512]{2,1,0:T(8,128)(2,1)S(1)}, bf16[4,128,512]{2,1,0:T(8,128)(2,1)}, u32[]{:S(2)}) copy-start(bf16[4,128,512]{2,1,0:T(8,128)(2,1)} %shard_map.149) | copy-start | bytes 1572868

commit v6 on v5

--- a/solution.py
+++ b/solution.py
@@ -42,7 +42,9 @@
     pl.semaphore_wait(barrier, count - 1)
 
 
-def gather_kernel(row_size, x_ref, out_ref, send_a, recv_a, send_b, recv_b, local_sem):
+def gather_kernel(
+    row_size, x_ref, out_ref, send_a, recv_a, send_b, recv_b, send_c, recv_c, local_sem
+):
     me = lax.axis_index(SLAB)
     block = x_ref.shape[0]
     own_y, spot = me // row_size, me % row_size
@@ -55,10 +57,12 @@
         return carry
 
     lax.fori_loop(1, row_size, greet, 0)
-    for j in range(1, y_count):
-        peer = lax.rem(own_y + j, y_count) * row_size + spot
+    left_y = lax.rem(own_y + y_count - 1, y_count)
+    right_y = lax.rem(own_y + 1, y_count)
+    for other_y in (left_y, right_y):
+        peer = other_y * row_size + spot
         pl.semaphore_signal(barrier, inc=1, device_id=peer_id(peer), device_id_type=MESH)
-    pl.semaphore_wait(barrier, row_size + y_count - 2)
+    pl.semaphore_wait(barrier, row_size + 1)
 
     def along_row(target, source):
         return pltpu.make_async_remote_copy(
@@ -98,17 +102,37 @@
             device_id_type=MESH,
         )
 
-    others = [lax.rem(own_y + j, y_count) for j in range(1, y_count)]
-    for other in others:
-        across(other, own_y).start()
-    for other in others:
-        across(other, own_y).wait_send()
-        across(other, other).wait_recv()
+    for other_y in (left_y, right_y):
+        across(other_y, own_y).start()
+    for other_y in (left_y, right_y):
+        across(other_y, own_y).wait_send()
+        across(other_y, other_y).wait_recv()
+    half = row_rows // 2
+
+    def forward(target_y, source_y, part):
+        rows = pl.ds(source_y * row_rows + part * half, half)
+        return pltpu.make_async_remote_copy(
+            src_ref=out_ref.at[rows],
+            dst_ref=out_ref.at[rows],
+            send_sem=send_c.at[part],
+            recv_sem=recv_c.at[part],
+            device_id=peer_id(target_y * row_size + spot),
+            device_id_type=MESH,
+        )
+
+    far_y = lax.rem(own_y + 2, y_count)
+    forward(right_y, left_y, 0).start()
+    forward(left_y, right_y, 1).start()
+    forward(right_y, left_y, 0).wait_send()
+    forward(left_y, right_y, 1).wait_send()
+    forward(right_y, far_y, 0).wait_recv()
+    forward(left_y, far_y, 1).wait_recv()
 
 
 def slab_gather(x, count, row_size):
     rows, width = x.shape
     y_count = count // row_size
+    assert y_count == 4
     return pl.pallas_call(
         functools.partial(gather_kernel, row_size),
         out_shape=jax.ShapeDtypeStruct((count * rows, width), x.dtype),
@@ -119,6 +143,8 @@
             pltpu.SemaphoreType.DMA((row_size,)),
             pltpu.SemaphoreType.DMA((y_count,)),
             pltpu.SemaphoreType.DMA((y_count,)),
+            pltpu.SemaphoreType.DMA((2,)),
+            pltpu.SemaphoreType.DMA((2,)),
             pltpu.SemaphoreType.DMA(()),
         ],
         compiler_params=pltpu.CompilerParams(collective_id=0, has_side_effects=True),

time: 206 us -> 199 us (0.966)
  Pallas kernels: 104 us -> 96.4 us
    pallas_call x1, Pallas kernels: 49.2 us -> 43.7 us  [slab_gather(): pl.pallas_call(functools.partial(gather_kernel, row_size), out_shape=jax....]
  transfers between devices with their start and end apart: 4 -> 4, of which waited for: 3 -> 4; matrix products, arithmetic and copies ran while one was open for 0% -> 0% of each run, Pallas kernels for 0% -> 0%
where the time goes in v6:
time: 199 us; the launch traced here: 198 us
  Pallas kernels  96.4 us (48%)
  other arithmetic  29.9 us (15%)
  matrix products  22.5 us (11%)
  waiting for transfers between devices  21.6 us (11%)
  local copies, waits for them, and re-layouts  14.1 us (7%)
  starting transfers between devices  11.9 us (6%)
    pallas_call x1, Pallas kernels, slab_gather(): pl.pallas_call(functools.partial(gather_kernel, row_size), out_shape=jax....  43.7 us
    pallas_call x1, Pallas kernels, slab_scatter(): pl.pallas_call(functools.partial(scatter_kernel, count), out_shape=jax.Sh...  34.9 us
    ppermute x2, waiting for transfers between devices, padded_2(): lax.ppermute(tail, axis, [(i, (i + 1) % count) for i in range(ends)])  19.9 us
    pallas_call x1, Pallas kernels, head_sum(): pl.pallas_call(functools.partial(head_sum_kernel, count), out_shape=jax.S...  17.7 us
    reduce_sum x4, other arithmetic, attend_piece(): row_sum = row_sum * rescale + jnp.sum(expo, axis=2)  12.2 us
    dot_general x4, matrix products, attend_piece(): jnp.einsum('qhd,khd->hqk', queries, key_rows, preferred_element_type=jnp....  10.9 us
    ppermute x2, starting transfers between devices, padded_2(): lax.ppermute(head, axis, [((i + 1) % count, i) for i in range(ends)])  6.24 us
    ppermute x2, starting transfers between devices, padded_2(): lax.ppermute(tail, axis, [(i, (i + 1) % count) for i in range(ends)])  5.65 us
  transfers between devices with their start and end apart: 4, of which 4 were waited for; matrix products, arithmetic and copies ran while one was open for 0% of the time, Pallas kernels for 0%

profile of v6, /device:TPU:2, one launch (start us, length us, event | category | flops | bytes accessed | tf_op | source)
XLA Modules:
  0.0 197.9 jit_solution(2583339788564664427)
XLA Ops:
  6.0 3.2 %fusion.75 = (f32[64]{0:T(128)S(1)}, f32[64,512]{1,0:T(8,128)S(1)}) fusion(bf16[64,4096]{1,0:T(8,128)(2,1)S(1)} %reshape.627, bf16[4096,512]{1,0:T(8,128)(2,1)} %param.17), kind=kOutput, calls=%fused_computation.156 | convolution fusion | flops 268468160 | bytes 4849920 | tf_op jit(solution)/shard_map/dot_general | solution.py:401
  11.0 43.7 %shard_map.148 = bf16[4096,256]{1,0:T(8,128)(2,1)} custom-call(bf16[64,256]{1,0:T(8,128)(2,1)} %pad_maximum_fusion.7.x_ref), custom_call_target="tpu_custom_call" | custom-call | tf_op jit(solution)/shard_map/pallas_call | solution.py:136
  55.5 33.6 %while.15 = (s32[]{:T(128)}, f32[2,512]{1,0:T(2,128)S(1)}, f32[2,512]{1,0:T(2,128)S(1)}, f32[2,512,64]{1,2,0:T(8,128)S(1)}, bf16[4,1024,256]{2,1,0:T(8,128)(2,1)...) while((s32[]{:T(128)}, f32[2,512]{1,0:T(2,128)S(1)}, f32[2,512]{1,0:T(2,128)S(1)}, ...), condition=%wide.region_7.8_spmd.clone, body=%wide.region_4.7_spmd.clone.sunk | while | flops 277025792 | bytes 33751168 | solution.py:436
  56.9 2.7 %bitcast_reduce_fusion.2 = (f32[2,512]{1,0:T(2,128)S(1)}, f32[2,1024,512]{2,1,0:T(8,128)}) fusion(bf16[1024,2,64]{0,2,1:T(8,128)(2,1)S(1)} %bitcast.112, bf16[512,2,64]{0,2,1:T(8,128)(2,1)S(1)} %get-tuple-element.216), kind=kOutput, calls=%fused_computation.1.clone.1 | convolution fusion | flops 136313856 | bytes 4591616 | tf_op jit(solution)/shard_map/while/body/eval_jaxpr/qhd,khd->hqk/dot_general | solution.py:368
  59.6 3.0 %fusion.109 = f32[2,512]{1,0:T(2,128)S(1)} fusion(f32[2,1024,512]{2,1,0:T(8,128)} %get-tuple-element.191, f32[2,512]{1,0:T(2,128)S(1)} %fusion.108), kind=kLoop, calls=%fused_computation.4.clone.1 | loop fusion | flops 3144704 | bytes 4202496 | tf_op jit(solution)/shard_map/while/body/eval_jaxpr/reduce_sum | solution.py:374
  65.3 2.7 %bitcast_reduce_fusion.2 = (f32[2,512]{1,0:T(2,128)S(1)}, f32[2,1024,512]{2,1,0:T(8,128)}) fusion(bf16[1024,2,64]{0,2,1:T(8,128)(2,1)S(1)} %bitcast.112, bf16[512,2,64]{0,2,1:T(8,128)(2,1)S(1)} %get-tuple-element.216), kind=kOutput, calls=%fused_computation.1.clone.1 | convolution fusion | flops 136313856 | bytes 4591616 | tf_op jit(solution)/shard_map/while/body/eval_jaxpr/qhd,khd->hqk/dot_general | solution.py:368
  68.0 3.0 %fusion.109 = f32[2,512]{1,0:T(2,128)S(1)} fusion(f32[2,1024,512]{2,1,0:T(8,128)} %get-tuple-element.191, f32[2,512]{1,0:T(2,128)S(1)} %fusion.108), kind=kLoop, calls=%fused_computation.4.clone.1 | loop fusion | flops 3144704 | bytes 4202496 | tf_op jit(solution)/shard_map/while/body/eval_jaxpr/reduce_sum | solution.py:374
  73.7 2.7 %bitcast_reduce_fusion.2 = (f32[2,512]{1,0:T(2,128)S(1)}, f32[2,1024,512]{2,1,0:T(8,128)}) fusion(bf16[1024,2,64]{0,2,1:T(8,128)(2,1)S(1)} %bitcast.112, bf16[512,2,64]{0,2,1:T(8,128)(2,1)S(1)} %get-tuple-element.216), kind=kOutput, calls=%fused_computation.1.clone.1 | convolution fusion | flops 136313856 | bytes 4591616 | tf_op jit(solution)/shard_map/while/body/eval_jaxpr/qhd,khd->hqk/dot_general | solution.py:368
  76.4 3.0 %fusion.109 = f32[2,512]{1,0:T(2,128)S(1)} fusion(f32[2,1024,512]{2,1,0:T(8,128)} %get-tuple-element.191, f32[2,512]{1,0:T(2,128)S(1)} %fusion.108), kind=kLoop, calls=%fused_computation.4.clone.1 | loop fusion | flops 3144704 | bytes 4202496 | tf_op jit(solution)/shard_map/while/body/eval_jaxpr/reduce_sum | solution.py:374
  82.1 2.7 %bitcast_reduce_fusion.2 = (f32[2,512]{1,0:T(2,128)S(1)}, f32[2,1024,512]{2,1,0:T(8,128)}) fusion(bf16[1024,2,64]{0,2,1:T(8,128)(2,1)S(1)} %bitcast.112, bf16[512,2,64]{0,2,1:T(8,128)(2,1)S(1)} %get-tuple-element.216), kind=kOutput, calls=%fused_computation.1.clone.1 | convolution fusion | flops 136313856 | bytes 4591616 | tf_op jit(solution)/shard_map/while/body/eval_jaxpr/qhd,khd->hqk/dot_general | solution.py:368
  84.8 3.0 %fusion.109 = f32[2,512]{1,0:T(2,128)S(1)} fusion(f32[2,1024,512]{2,1,0:T(8,128)} %get-tuple-element.191, f32[2,512]{1,0:T(2,128)S(1)} %fusion.108), kind=kLoop, calls=%fused_computation.4.clone.1 | loop fusion | flops 3144704 | bytes 4202496 | tf_op jit(solution)/shard_map/while/body/eval_jaxpr/reduce_sum | solution.py:374
  90.3 17.7 %shard_map.149 = bf16[4,128,512]{2,1,0:T(8,128)(2,1)} custom-call(bf16[4,128,512]{2,1,0:T(8,128)(2,1)} %bitcast.123), custom_call_target="tpu_custom_call" | custom-call | tf_op jit(solution)/shard_map/pallas_call | solution.py:206
  109.3 1.3 multiply_reduce_fusion
  110.7 1.6 convolution_convert_fusion.2
  112.3 2.5 %collective-permute-start = (bf16[1,16,16,512]{3,2,1,0:T(8,128)(2,1)S(1)}, bf16[1,16,16,512]{3,2,1,0:T(8,128)(2,1)S(1)}, u32[]{:S(2)}, u32[]{:S(2)}) collective-permute-start(bf16[1,16,16,512]{3,2,1,0:T(8,128)(2,1)S(1)} %bitcast.128), channel_id=1, source_target_pairs={{0,4},{4,8},{8,12},{12,16},{16,20},{20,24},{24,28},{28,32},{32,36}... | collective-permute-start | bytes 786440 | tf_op jit(solution)/shard_map/ppermute | solution.py:282
  114.8 3.4 %collective-permute-start.1 = (bf16[1,16,16,512]{3,2,1,0:T(8,128)(2,1)S(1)}, bf16[1,16,16,512]{3,2,1,0:T(8,128)(2,1)S(1)}, u32[]{:S(2)}, u32[]{:S(2)}) collective-permute-start(bf16[1,16,16,512]{3,2,1,0:T(8,128)(2,1)S(1)} %bitcast.127), channel_id=1, source_target_pairs={{4,0},{8,4},{12,8},{16,12},{20,16},{24,20},{28,24},{32,28},{36,32}... | collective-permute-start | bytes 786440 | tf_op jit(solution)/shard_map/ppermute | solution.py:284
  118.2 10.5 %collective-permute-done = bf16[1,16,16,512]{3,2,1,0:T(8,128)(2,1)S(1)} collective-permute-done((bf16[1,16,16,512]{3,2,1,0:T(8,128)(2,1)S(1)}, bf16[1,16,16,512]{3,2,1,0:T(8,128)(2,1)S(1)}, u32[]{:S(2)}, u32[]{:S(2)}) %collective-permute-start) | collective-permute-done | bytes 262176 | tf_op jit(solution)/shard_map/ppermute | solution.py:282
  130.0 3.8 %multiply_add_fusion = f32[2,16,16,512]{3,2,1,0:T(8,128)S(1)} fusion(bf16[2,16,16,512]{3,2,1,0:T(8,128)(2,1)S(1)} %bitcast.121, bf16[4,18,18,512]{3,2,1,0:T(8,128)(2,1)S(1)} %fusion.21, bf16[1,16,16,512]{3,2,1,0:T(8,128)(2,1)S(1)} %collective-permute-done.1, bf16[1,16,16,512]{3,2,1,0:T(8,128)(2,1)S(1)} %collective-permute-done, f32[512]{0:T(512)S(1)} %bitcast.143, ...), kind=kLoop, calls=%fused_computation.61 | loop fusion | flops 21495808 | bytes 14735360 | tf_op jit(solution)/shard_map/add | solution.py:360
  134.7 3.2 %collective-permute-start.2 = (bf16[1,16,16,512]{3,2,1,0:T(8,128)(2,1)S(1)}, bf16[1,16,16,512]{3,2,1,0:T(8,128)(2,1)S(1)}, u32[]{:S(2)}, u32[]{:S(2)}) collective-permute-start(bf16[1,16,16,512]{3,2,1,0:T(8,128)(2,1)S(1)} %bitcast.130), channel_id=1, source_target_pairs={{0,4},{4,8},{8,12},{12,16},{16,20},{20,24},{24,28},{28,32},{32,36}... | collective-permute-start | bytes 786440 | tf_op jit(solution)/shard_map/ppermute | solution.py:282
  137.9 2.9 %collective-permute-start.3 = (bf16[1,16,16,512]{3,2,1,0:T(8,128)(2,1)S(1)}, bf16[1,16,16,512]{3,2,1,0:T(8,128)(2,1)S(1)}, u32[]{:S(2)}, u32[]{:S(2)}) collective-permute-start(bf16[1,16,16,512]{3,2,1,0:T(8,128)(2,1)S(1)} %bitcast.129), channel_id=1, source_target_pairs={{4,0},{8,4},{12,8},{16,12},{20,16},{24,20},{28,24},{32,28},{36,32}... | collective-permute-start | bytes 786440 | tf_op jit(solution)/shard_map/ppermute | solution.py:284
  141.2 9.4 %collective-permute-done.2 = bf16[1,16,16,512]{3,2,1,0:T(8,128)(2,1)S(1)} collective-permute-done((bf16[1,16,16,512]{3,2,1,0:T(8,128)(2,1)S(1)}, bf16[1,16,16,512]{3,2,1,0:T(8,128)(2,1)S(1)}, u32[]{:S(2)}, u32[]{:S(2)}) %collective-permute-start.2) | collective-permute-done | bytes 262176 | tf_op jit(solution)/shard_map/ppermute | solution.py:282
  152.6 3.8 %add_convert_fusion = bf16[2,16,16,512]{3,2,1,0:T(8,128)(2,1)S(1)} fusion(bf16[2,16,16,512]{3,2,1,0:T(8,128)(2,1)S(1)} %bitcast.116, bf16[4,18,18,512]{3,2,1,0:T(8,128)(2,1)S(1)} %select_maximum_fusion, bf16[1,16,16,512]{3,2,1,0:T(8,128)(2,1)S(1)} %collective-permute-done.3, bf16[1,16,16,512]{3,2,1,0:T(8,128)(2,1)S(1)} %collective-permute-done.2, ...), kind=kLoop, calls=%fused_computation.60 | loop fusion | flops 21757952 | bytes 14211072 | tf_op jit(solution)/shard_map/convert_element_type | solution.py:470
  158.5 2.2 %convert_element_type.384.g_ref = bf16[64,16,512]{2,1,0:T(8,128)(2,1)} reshape(bf16[512,1024]{1,0:T(8,128)(2,1)} %copy.28) | data formatting | bytes 2097152 | tf_op jit(solution)/shard_map/convert_element_type | solution.py:258
  160.7 34.9 %shard_map.150 = f32[16,512]{1,0:T(8,128)} custom-call(bf16[64,16,512]{2,1,0:T(8,128)(2,1)} %convert_element_type.384.g_ref), custom_call_target="tpu_custom_call" | custom-call | tf_op jit(solution)/shard_map/pallas_call | solution.py:259
  (117 shorter events, 29.3 us)
Async XLA Ops:
  0.6 133.4 %copy-start = (bf16[512,512]{1,0:T(8,128)(2,1)S(1)}, bf16[512,512]{1,0:T(8,128)(2,1)}, u32[]{:S(2)}) copy-start(bf16[512,512]{1,0:T(8,128)(2,1)} %param.27) | copy-start | bytes 1572868
  5.2 4.2 %copy-start.6 = (bf16[512,128]{1,0:T(8,128)(2,1)S(1)}, bf16[512,128]{1,0:T(8,128)(2,1)}, u32[]{:S(2)}) copy-start(bf16[512,128]{1,0:T(8,128)(2,1)} %param.20) | copy-start | bytes 393220
  5.2 4.2 %copy-start.10 = (f32[512]{0:T(512)S(1)}, f32[512]{0:T(512)}, u32[]{:S(2)}) copy-start(f32[512]{0:T(512)} %param.18) | copy-start | bytes 6148
  5.6 4.5 %copy-start.7 = (bf16[512,128]{1,0:T(8,128)(2,1)S(1)}, bf16[512,128]{1,0:T(8,128)(2,1)}, u32[]{:S(2)}) copy-start(bf16[512,128]{1,0:T(8,128)(2,1)} %param.21) | copy-start | bytes 393220
  6.0 48.7 %copy-start.5 = (bf16[512,128]{1,0:T(8,128)(2,1)S(1)}, bf16[512,128]{1,0:T(8,128)(2,1)}, u32[]{:S(2)}) copy-start(bf16[512,128]{1,0:T(8,128)(2,1)} %param.19) | copy-start | bytes 393220
  55.4 33.7 %copy-start.8 = (bf16[128,512]{1,0:T(8,128)(2,1)S(1)}, bf16[128,512]{1,0:T(8,128)(2,1)}, u32[]{:S(2)}) copy-start(bf16[128,512]{1,0:T(8,128)(2,1)} %param.22) | copy-start | bytes 393220
  55.4 52.6 %copy-start.2 = (bf16[512,512]{1,0:T(8,128)(2,1)S(1)}, bf16[512,512]{1,0:T(8,128)(2,1)}, u32[]{:S(2)}) copy-start(bf16[512,512]{1,0:T(8,128)(2,1)} %param.15) | copy-start | bytes 1572868
  59.6 3.4 %copy-start.1 = (f32[2,1024,512]{2,1,0:T(8,128)S(1)}, f32[2,1024,512]{2,1,0:T(8,128)}, u32[]{:S(2)}) copy-start(f32[2,1024,512]{2,1,0:T(8,128)} %get-tuple-element.191) | copy-start | bytes 12582916 | tf_op jit(solution)/shard_map/while
  68.0 3.4 %copy-start.1 = (f32[2,1024,512]{2,1,0:T(8,128)S(1)}, f32[2,1024,512]{2,1,0:T(8,128)}, u32[]{:S(2)}) copy-start(f32[2,1024,512]{2,1,0:T(8,128)} %get-tuple-element.191) | copy-start | bytes 12582916 | tf_op jit(solution)/shard_map/while
  76.4 3.4 %copy-start.1 = (f32[2,1024,512]{2,1,0:T(8,128)S(1)}, f32[2,1024,512]{2,1,0:T(8,128)}, u32[]{:S(2)}) copy-start(f32[2,1024,512]{2,1,0:T(8,128)} %get-tuple-element.191) | copy-start | bytes 12582916 | tf_op jit(solution)/shard_map/while
  84.8 3.4 %copy-start.1 = (f32[2,1024,512]{2,1,0:T(8,128)S(1)}, f32[2,1024,512]{2,1,0:T(8,128)}, u32[]{:S(2)}) copy-start(f32[2,1024,512]{2,1,0:T(8,128)} %get-tuple-element.191) | copy-start | bytes 12582916 | tf_op jit(solution)/shard_map/while
  89.1 21.5 %copy-start.11 = (bf16[512,512]{1,0:T(8,128)(2,1)S(1)}, bf16[512,512]{1,0:T(8,128)(2,1)}, u32[]{:S(2)}) copy-start(bf16[512,512]{1,0:T(8,128)(2,1)} %param.24) | copy-start | bytes 1572868
  89.1 21.5 %copy-start.12 = (f32[512]{0:T(512)S(1)}, f32[512]{0:T(512)}, u32[]{:S(2)}) copy-start(f32[512]{0:T(512)} %param.23) | copy-start | bytes 6148
  90.3 27.9 %copy-start.9 = (f32[27,512]{1,0:T(8,128)S(1)}, f32[27,512]{1,0:T(8,128)}, u32[]{:S(2)}) copy-start(f32[27,512]{1,0:T(8,128)} %param.25) | copy-start | bytes 165892
  112.3 16.4 %collective-permute-start = (bf16[1,16,16,512]{3,2,1,0:T(8,128)(2,1)S(1)}, bf16[1,16,16,512]{3,2,1,0:T(8,128)(2,1)S(1)}, u32[]{:S(2)}, u32[]{:S(2)}) collective-permute-start(bf16[1,16,16,512]{3,2,1,0:T(8,128)(2,1)S(1)} %bitcast.128), channel_id=1, source_target_pairs={{0,4},{4,8},{8,12},{12,16},{16,20},{20,24},{24,28},{28,32},{32,36}... | collective-permute-start | bytes 786440 | tf_op jit(solution)/shard_map/ppermute | solution.py:282
  114.8 14.4 %collective-permute-start.1 = (bf16[1,16,16,512]{3,2,1,0:T(8,128)(2,1)S(1)}, bf16[1,16,16,512]{3,2,1,0:T(8,128)(2,1)S(1)}, u32[]{:S(2)}, u32[]{:S(2)}) collective-permute-start(bf16[1,16,16,512]{3,2,1,0:T(8,128)(2,1)S(1)} %bitcast.127), channel_id=1, source_target_pairs={{4,0},{8,4},{12,8},{16,12},{20,16},{24,20},{28,24},{32,28},{36,32}... | collective-permute-start | bytes 786440 | tf_op jit(solution)/shard_map/ppermute | solution.py:284
  130.0 4.1 %copy-start.4 = (bf16[512,512]{1,0:T(8,128)(2,1)S(1)}, bf16[512,512]{1,0:T(8,128)(2,1)}, u32[]{:S(2)}) copy-start(bf16[512,512]{1,0:T(8,128)(2,1)} %param.26) | copy-start | bytes 1572868
  134.7 16.0 %collective-permute-start.2 = (bf16[1,16,16,512]{3,2,1,0:T(8,128)(2,1)S(1)}, bf16[1,16,16,512]{3,2,1,0:T(8,128)(2,1)S(1)}, u32[]{:S(2)}, u32[]{:S(2)}) collective-permute-start(bf16[1,16,16,512]{3,2,1,0:T(8,128)(2,1)S(1)} %bitcast.130), channel_id=1, source_target_pairs={{0,4},{4,8},{8,12},{12,16},{16,20},{20,24},{24,28},{28,32},{32,36}... | collective-permute-start | bytes 786440 | tf_op jit(solution)/shard_map/ppermute | solution.py:282
  137.9 14.0 %collective-permute-start.3 = (bf16[1,16,16,512]{3,2,1,0:T(8,128)(2,1)S(1)}, bf16[1,16,16,512]{3,2,1,0:T(8,128)(2,1)S(1)}, u32[]{:S(2)}, u32[]{:S(2)}) collective-permute-start(bf16[1,16,16,512]{3,2,1,0:T(8,128)(2,1)S(1)} %bitcast.129), channel_id=1, source_target_pairs={{4,0},{8,4},{12,8},{16,12},{20,16},{24,20},{28,24},{32,28},{36,32}... | collective-permute-start | bytes 786440 | tf_op jit(solution)/shard_map/ppermute | solution.py:284
  152.6 3.9 %copy-start.3 = (bf16[4,128,512]{2,1,0:T(8,128)(2,1)S(1)}, bf16[4,128,512]{2,1,0:T(8,128)(2,1)}, u32[]{:S(2)}) copy-start(bf16[4,128,512]{2,1,0:T(8,128)(2,1)} %shard_map.149) | copy-start | bytes 1572868

commit v7 on v6

--- a/solution.py
+++ b/solution.py
@@ -28,18 +28,6 @@
 
 def peer_id(p):
     return (p // 16, p // 2 % 8, p % 2, lax.axis_index("xh"), lax.axis_index("core"))
-
-
-def greet_all(count, me):
-    barrier = pltpu.get_barrier_semaphore()
-
-    def body(k, carry):
-        peer = lax.rem(me + k, count)
-        pl.semaphore_signal(barrier, inc=1, device_id=peer_id(peer), device_id_type=MESH)
-        return carry
-
-    lax.fori_loop(1, count, body, 0)
-    pl.semaphore_wait(barrier, count - 1)
 
 
 def gather_kernel(
@@ -220,51 +208,94 @@
     return summed.reshape(rows, width)
 
 
-def scatter_kernel(count, g_ref, out_ref, slots, send_sem, recv_sem):
+def scatter_kernel(
+    row_size, g_ref, out_ref, slots_y, totals, sums, slots_row, send_a, recv_a, send_b, recv_b
+):
     me = lax.axis_index(SLAB)
-    greet_all(count, me)
-
-    def copy_to(peer, source):
-        return pltpu.make_async_remote_copy(
-            src_ref=g_ref.at[peer],
-            dst_ref=slots.at[source],
-            send_sem=send_sem.at[peer],
-            recv_sem=recv_sem.at[source],
-            device_id=peer_id(peer),
-            device_id_type=MESH,
-        )
-
-    def start(k, carry):
-        copy_to(lax.rem(me + k, count), me).start()
+    own_y, spot = me // row_size, me % row_size
+    y_count = lax.psum(1, "y")
+    barrier = pltpu.get_barrier_semaphore()
+
+    def greet(k, carry):
+        peer = own_y * row_size + lax.rem(spot + k, row_size)
+        pl.semaphore_signal(barrier, inc=1, device_id=peer_id(peer), device_id_type=MESH)
         return carry
 
-    lax.fori_loop(1, count, start, 0)
-    out_ref[...] = g_ref[me].astype(jnp.float32)
-
-    def finish(k, carry):
-        peer = lax.rem(me + k, count)
-        copy_to(peer, me).wait_send()
-        copy_to(peer, peer).wait_recv()
-        out_ref[...] += slots[peer].astype(jnp.float32)
+    lax.fori_loop(1, row_size, greet, 0)
+    others = [lax.rem(own_y + j, y_count) for j in range(1, y_count)]
+    for other_y in others:
+        pl.semaphore_signal(
+            barrier, inc=1, device_id=peer_id(other_y * row_size + spot), device_id_type=MESH
+        )
+    pl.semaphore_wait(barrier, row_size + y_count - 2)
+
+    def across(target_y, source_y):
+        return pltpu.make_async_remote_copy(
+            src_ref=g_ref.at[pl.ds(target_y * row_size, row_size)],
+            dst_ref=slots_y.at[source_y],
+            send_sem=send_a.at[target_y],
+            recv_sem=recv_a.at[source_y],
+            device_id=peer_id(target_y * row_size + spot),
+            device_id_type=MESH,
+        )
+
+    for other_y in others:
+        across(other_y, own_y).start()
+    total = g_ref[pl.ds(own_y * row_size, row_size)].astype(jnp.float32)
+    for other_y in others:
+        across(other_y, own_y).wait_send()
+        across(other_y, other_y).wait_recv()
+        total = total + slots_y[other_y].astype(jnp.float32)
+    totals[...] = total
+    sums[...] = total.astype(sums.dtype)
+
+    def along_row(target, source):
+        return pltpu.make_async_remote_copy(
+            src_ref=sums.at[target],
+            dst_ref=slots_row.at[source],
+            send_sem=send_b.at[target],
+            recv_sem=recv_b.at[source],
+            device_id=peer_id(own_y * row_size + target),
+            device_id_type=MESH,
+        )
+
+    def start_row(k, carry):
+        along_row(lax.rem(spot + k, row_size), spot).start()
         return carry
 
-    lax.fori_loop(1, count, finish, 0)
-
-
-def slab_scatter(g, count):
+    lax.fori_loop(1, row_size, start_row, 0)
+    out_ref[...] = totals[spot]
+
+    def finish_row(k, carry):
+        other = lax.rem(spot + k, row_size)
+        along_row(other, spot).wait_send()
+        along_row(other, other).wait_recv()
+        out_ref[...] += slots_row[other].astype(jnp.float32)
+        return carry
+
+    lax.fori_loop(1, row_size, finish_row, 0)
+
+
+def slab_scatter(g, count, row_size):
     total_rows, width = g.shape
     rows = total_rows // count
+    y_count = count // row_size
     tile_rows = 16
     g = g.astype(jnp.bfloat16).reshape(count, tile_rows, rows * width // tile_rows)
     summed = pl.pallas_call(
-        functools.partial(scatter_kernel, count),
+        functools.partial(scatter_kernel, row_size),
         out_shape=jax.ShapeDtypeStruct(g.shape[1:], jnp.float32),
         in_specs=[pl.BlockSpec(memory_space=pltpu.VMEM)],
         out_specs=pl.BlockSpec(memory_space=pltpu.VMEM),
         scratch_shapes=[
-            pltpu.VMEM(g.shape, g.dtype),
-            pltpu.SemaphoreType.DMA((count,)),
-            pltpu.SemaphoreType.DMA((count,)),
+            pltpu.VMEM((y_count, row_size) + g.shape[1:], g.dtype),
+            pltpu.VMEM((row_size,) + g.shape[1:], jnp.float32),
+            pltpu.VMEM((row_size,) + g.shape[1:], g.dtype),
+            pltpu.VMEM((row_size,) + g.shape[1:], g.dtype),
+            pltpu.SemaphoreType.DMA((y_count,)),
+            pltpu.SemaphoreType.DMA((y_count,)),
+            pltpu.SemaphoreType.DMA((row_size,)),
+            pltpu.SemaphoreType.DMA((row_size,)),
         ],
         compiler_params=pltpu.CompilerParams(collective_id=1, has_side_effects=True),
     )(g)
@@ -471,7 +502,11 @@
     )
     up_full = jnp.einsum("td,tc->dc", normed_ffn, grad_pre, preferred_element_type=jnp.float32)
     down_full = jnp.einsum("td,tc->dc", grad_out, activated, preferred_element_type=jnp.float32)
-    grads = slab_scatter(jnp.concatenate([up_full, down_full], axis=1), lax.psum(1, SLAB))
+    grads = slab_scatter(
+        jnp.concatenate([up_full, down_full], axis=1),
+        lax.psum(1, SLAB),
+        lax.psum(1, ("z", "xl")),
+    )
     return (attended, grads[:, :channels], grads[:, channels:])
 
 

time: 199 us -> 192 us (0.965)
  Pallas kernels: 96.4 us -> 89.5 us
    pallas_call x1, Pallas kernels: 34.9 us -> 28.1 us  [slab_scatter(): pl.pallas_call(functools.partial(scatter_kernel, row_size), out_shape=jax...]
where the time goes in v7:
time: 192 us; the launch traced here: 191 us
  Pallas kernels  89.5 us (47%)
  other arithmetic  29.9 us (16%)
  matrix products  22.5 us (12%)
  waiting for transfers between devices  21.6 us (11%)
  local copies, waits for them, and re-layouts  14.1 us (7%)
  starting transfers between devices  11.9 us (6%)
    pallas_call x1, Pallas kernels, slab_gather(): pl.pallas_call(functools.partial(gather_kernel, row_size), out_shape=jax....  43.7 us
    pallas_call x1, Pallas kernels, slab_scatter(): pl.pallas_call(functools.partial(scatter_kernel, row_size), out_shape=jax...  28.1 us
    ppermute x2, waiting for transfers between devices, padded_2(): lax.ppermute(tail, axis, [(i, (i + 1) % count) for i in range(ends)])  19.9 us
    pallas_call x1, Pallas kernels, head_sum(): pl.pallas_call(functools.partial(head_sum_kernel, count), out_shape=jax.S...  17.7 us
    reduce_sum x4, other arithmetic, attend_piece(): row_sum = row_sum * rescale + jnp.sum(expo, axis=2)  12.2 us
    dot_general x4, matrix products, attend_piece(): jnp.einsum('qhd,khd->hqk', queries, key_rows, preferred_element_type=jnp....  10.9 us
    ppermute x2, starting transfers between devices, padded_2(): lax.ppermute(head, axis, [((i + 1) % count, i) for i in range(ends)])  6.24 us
    ppermute x2, starting transfers between devices, padded_2(): lax.ppermute(tail, axis, [(i, (i + 1) % count) for i in range(ends)])  5.65 us
  transfers between devices with their start and end apart: 4, of which 4 were waited for; matrix products, arithmetic and copies ran while one was open for 0% of the time, Pallas kernels for 0%

profile of v7, /device:TPU:2, one launch (start us, length us, event | category | flops | bytes accessed | tf_op | source)
XLA Modules:
  0.0 191.0 jit_solution(3097393335356370943)
XLA Ops:
  6.0 3.2 %fusion.75 = (f32[64]{0:T(128)S(1)}, f32[64,512]{1,0:T(8,128)S(1)}) fusion(bf16[64,4096]{1,0:T(8,128)(2,1)S(1)} %reshape.627, bf16[4096,512]{1,0:T(8,128)(2,1)} %param.17), kind=kOutput, calls=%fused_computation.156 | convolution fusion | flops 268468160 | bytes 4849920 | tf_op jit(solution)/shard_map/dot_general | solution.py:432
  11.0 43.7 %shard_map.148 = bf16[4096,256]{1,0:T(8,128)(2,1)} custom-call(bf16[64,256]{1,0:T(8,128)(2,1)} %pad_maximum_fusion.7.x_ref), custom_call_target="tpu_custom_call" | custom-call | tf_op jit(solution)/shard_map/pallas_call | solution.py:124
  55.5 33.6 %while.15 = (s32[]{:T(128)}, f32[2,512]{1,0:T(2,128)S(1)}, f32[2,512]{1,0:T(2,128)S(1)}, f32[2,512,64]{1,2,0:T(8,128)S(1)}, bf16[4,1024,256]{2,1,0:T(8,128)(2,1)...) while((s32[]{:T(128)}, f32[2,512]{1,0:T(2,128)S(1)}, f32[2,512]{1,0:T(2,128)S(1)}, ...), condition=%wide.region_7.8_spmd.clone, body=%wide.region_4.7_spmd.clone.sunk | while | flops 277025792 | bytes 33751168 | solution.py:467
  56.9 2.7 %bitcast_reduce_fusion.2 = (f32[2,512]{1,0:T(2,128)S(1)}, f32[2,1024,512]{2,1,0:T(8,128)}) fusion(bf16[1024,2,64]{0,2,1:T(8,128)(2,1)S(1)} %bitcast.112, bf16[512,2,64]{0,2,1:T(8,128)(2,1)S(1)} %get-tuple-element.216), kind=kOutput, calls=%fused_computation.1.clone.1 | convolution fusion | flops 136313856 | bytes 4591616 | tf_op jit(solution)/shard_map/while/body/eval_jaxpr/qhd,khd->hqk/dot_general | solution.py:399
  59.6 3.0 %fusion.109 = f32[2,512]{1,0:T(2,128)S(1)} fusion(f32[2,1024,512]{2,1,0:T(8,128)} %get-tuple-element.191, f32[2,512]{1,0:T(2,128)S(1)} %fusion.108), kind=kLoop, calls=%fused_computation.4.clone.1 | loop fusion | flops 3144704 | bytes 4202496 | tf_op jit(solution)/shard_map/while/body/eval_jaxpr/reduce_sum | solution.py:405
  65.3 2.7 %bitcast_reduce_fusion.2 = (f32[2,512]{1,0:T(2,128)S(1)}, f32[2,1024,512]{2,1,0:T(8,128)}) fusion(bf16[1024,2,64]{0,2,1:T(8,128)(2,1)S(1)} %bitcast.112, bf16[512,2,64]{0,2,1:T(8,128)(2,1)S(1)} %get-tuple-element.216), kind=kOutput, calls=%fused_computation.1.clone.1 | convolution fusion | flops 136313856 | bytes 4591616 | tf_op jit(solution)/shard_map/while/body/eval_jaxpr/qhd,khd->hqk/dot_general | solution.py:399
  68.0 3.0 %fusion.109 = f32[2,512]{1,0:T(2,128)S(1)} fusion(f32[2,1024,512]{2,1,0:T(8,128)} %get-tuple-element.191, f32[2,512]{1,0:T(2,128)S(1)} %fusion.108), kind=kLoop, calls=%fused_computation.4.clone.1 | loop fusion | flops 3144704 | bytes 4202496 | tf_op jit(solution)/shard_map/while/body/eval_jaxpr/reduce_sum | solution.py:405
  73.7 2.7 %bitcast_reduce_fusion.2 = (f32[2,512]{1,0:T(2,128)S(1)}, f32[2,1024,512]{2,1,0:T(8,128)}) fusion(bf16[1024,2,64]{0,2,1:T(8,128)(2,1)S(1)} %bitcast.112, bf16[512,2,64]{0,2,1:T(8,128)(2,1)S(1)} %get-tuple-element.216), kind=kOutput, calls=%fused_computation.1.clone.1 | convolution fusion | flops 136313856 | bytes 4591616 | tf_op jit(solution)/shard_map/while/body/eval_jaxpr/qhd,khd->hqk/dot_general | solution.py:399
  76.4 3.0 %fusion.109 = f32[2,512]{1,0:T(2,128)S(1)} fusion(f32[2,1024,512]{2,1,0:T(8,128)} %get-tuple-element.191, f32[2,512]{1,0:T(2,128)S(1)} %fusion.108), kind=kLoop, calls=%fused_computation.4.clone.1 | loop fusion | flops 3144704 | bytes 4202496 | tf_op jit(solution)/shard_map/while/body/eval_jaxpr/reduce_sum | solution.py:405
  82.1 2.7 %bitcast_reduce_fusion.2 = (f32[2,512]{1,0:T(2,128)S(1)}, f32[2,1024,512]{2,1,0:T(8,128)}) fusion(bf16[1024,2,64]{0,2,1:T(8,128)(2,1)S(1)} %bitcast.112, bf16[512,2,64]{0,2,1:T(8,128)(2,1)S(1)} %get-tuple-element.216), kind=kOutput, calls=%fused_computation.1.clone.1 | convolution fusion | flops 136313856 | bytes 4591616 | tf_op jit(solution)/shard_map/while/body/eval_jaxpr/qhd,khd->hqk/dot_general | solution.py:399
  84.8 3.0 %fusion.109 = f32[2,512]{1,0:T(2,128)S(1)} fusion(f32[2,1024,512]{2,1,0:T(8,128)} %get-tuple-element.191, f32[2,512]{1,0:T(2,128)S(1)} %fusion.108), kind=kLoop, calls=%fused_computation.4.clone.1 | loop fusion | flops 3144704 | bytes 4202496 | tf_op jit(solution)/shard_map/while/body/eval_jaxpr/reduce_sum | solution.py:405
  90.3 17.7 %shard_map.149 = bf16[4,128,512]{2,1,0:T(8,128)(2,1)} custom-call(bf16[4,128,512]{2,1,0:T(8,128)(2,1)} %bitcast.123), custom_call_target="tpu_custom_call" | custom-call | tf_op jit(solution)/shard_map/pallas_call | solution.py:194
  109.3 1.3 multiply_reduce_fusion
  110.7 1.6 convolution_convert_fusion.2
  112.3 2.5 %collective-permute-start = (bf16[1,16,16,512]{3,2,1,0:T(8,128)(2,1)S(1)}, bf16[1,16,16,512]{3,2,1,0:T(8,128)(2,1)S(1)}, u32[]{:S(2)}, u32[]{:S(2)}) collective-permute-start(bf16[1,16,16,512]{3,2,1,0:T(8,128)(2,1)S(1)} %bitcast.128), channel_id=1, source_target_pairs={{0,4},{4,8},{8,12},{12,16},{16,20},{20,24},{24,28},{28,32},{32,36}... | collective-permute-start | bytes 786440 | tf_op jit(solution)/shard_map/ppermute | solution.py:313
  114.8 3.4 %collective-permute-start.1 = (bf16[1,16,16,512]{3,2,1,0:T(8,128)(2,1)S(1)}, bf16[1,16,16,512]{3,2,1,0:T(8,128)(2,1)S(1)}, u32[]{:S(2)}, u32[]{:S(2)}) collective-permute-start(bf16[1,16,16,512]{3,2,1,0:T(8,128)(2,1)S(1)} %bitcast.127), channel_id=1, source_target_pairs={{4,0},{8,4},{12,8},{16,12},{20,16},{24,20},{28,24},{32,28},{36,32}... | collective-permute-start | bytes 786440 | tf_op jit(solution)/shard_map/ppermute | solution.py:315
  118.2 10.5 %collective-permute-done = bf16[1,16,16,512]{3,2,1,0:T(8,128)(2,1)S(1)} collective-permute-done((bf16[1,16,16,512]{3,2,1,0:T(8,128)(2,1)S(1)}, bf16[1,16,16,512]{3,2,1,0:T(8,128)(2,1)S(1)}, u32[]{:S(2)}, u32[]{:S(2)}) %collective-permute-start) | collective-permute-done | bytes 262176 | tf_op jit(solution)/shard_map/ppermute | solution.py:313
  130.0 3.8 %multiply_add_fusion = f32[2,16,16,512]{3,2,1,0:T(8,128)S(1)} fusion(bf16[2,16,16,512]{3,2,1,0:T(8,128)(2,1)S(1)} %bitcast.121, bf16[4,18,18,512]{3,2,1,0:T(8,128)(2,1)S(1)} %fusion.21, bf16[1,16,16,512]{3,2,1,0:T(8,128)(2,1)S(1)} %collective-permute-done.1, bf16[1,16,16,512]{3,2,1,0:T(8,128)(2,1)S(1)} %collective-permute-done, f32[512]{0:T(512)S(1)} %bitcast.143, ...), kind=kLoop, calls=%fused_computation.61 | loop fusion | flops 21495808 | bytes 14735360 | tf_op jit(solution)/shard_map/add | solution.py:391
  134.7 3.2 %collective-permute-start.2 = (bf16[1,16,16,512]{3,2,1,0:T(8,128)(2,1)S(1)}, bf16[1,16,16,512]{3,2,1,0:T(8,128)(2,1)S(1)}, u32[]{:S(2)}, u32[]{:S(2)}) collective-permute-start(bf16[1,16,16,512]{3,2,1,0:T(8,128)(2,1)S(1)} %bitcast.130), channel_id=1, source_target_pairs={{0,4},{4,8},{8,12},{12,16},{16,20},{20,24},{24,28},{28,32},{32,36}... | collective-permute-start | bytes 786440 | tf_op jit(solution)/shard_map/ppermute | solution.py:313
  137.9 2.9 %collective-permute-start.3 = (bf16[1,16,16,512]{3,2,1,0:T(8,128)(2,1)S(1)}, bf16[1,16,16,512]{3,2,1,0:T(8,128)(2,1)S(1)}, u32[]{:S(2)}, u32[]{:S(2)}) collective-permute-start(bf16[1,16,16,512]{3,2,1,0:T(8,128)(2,1)S(1)} %bitcast.129), channel_id=1, source_target_pairs={{4,0},{8,4},{12,8},{16,12},{20,16},{24,20},{28,24},{32,28},{36,32}... | collective-permute-start | bytes 786440 | tf_op jit(solution)/shard_map/ppermute | solution.py:315
  141.2 9.4 %collective-permute-done.2 = bf16[1,16,16,512]{3,2,1,0:T(8,128)(2,1)S(1)} collective-permute-done((bf16[1,16,16,512]{3,2,1,0:T(8,128)(2,1)S(1)}, bf16[1,16,16,512]{3,2,1,0:T(8,128)(2,1)S(1)}, u32[]{:S(2)}, u32[]{:S(2)}) %collective-permute-start.2) | collective-permute-done | bytes 262176 | tf_op jit(solution)/shard_map/ppermute | solution.py:313
  152.6 3.8 %add_convert_fusion = bf16[2,16,16,512]{3,2,1,0:T(8,128)(2,1)S(1)} fusion(bf16[2,16,16,512]{3,2,1,0:T(8,128)(2,1)S(1)} %bitcast.116, bf16[4,18,18,512]{3,2,1,0:T(8,128)(2,1)S(1)} %select_maximum_fusion, bf16[1,16,16,512]{3,2,1,0:T(8,128)(2,1)S(1)} %collective-permute-done.3, bf16[1,16,16,512]{3,2,1,0:T(8,128)(2,1)S(1)} %collective-permute-done.2, ...), kind=kLoop, calls=%fused_computation.60 | loop fusion | flops 21757952 | bytes 14211072 | tf_op jit(solution)/shard_map/convert_element_type | solution.py:501
  158.5 2.2 %convert_element_type.384.g_ref = bf16[64,16,512]{2,1,0:T(8,128)(2,1)} reshape(bf16[512,1024]{1,0:T(8,128)(2,1)} %copy.28) | data formatting | bytes 2097152 | tf_op jit(solution)/shard_map/convert_element_type | solution.py:284
  160.7 28.1 %shard_map.150 = f32[16,512]{1,0:T(8,128)} custom-call(bf16[64,16,512]{2,1,0:T(8,128)(2,1)} %convert_element_type.384.g_ref), custom_call_target="tpu_custom_call" | custom-call | tf_op jit(solution)/shard_map/pallas_call | solution.py:285
  (117 shorter events, 29.3 us)
Async XLA Ops:
  0.6 133.4 %copy-start = (bf16[512,512]{1,0:T(8,128)(2,1)S(1)}, bf16[512,512]{1,0:T(8,128)(2,1)}, u32[]{:S(2)}) copy-start(bf16[512,512]{1,0:T(8,128)(2,1)} %param.27) | copy-start | bytes 1572868
  5.2 4.2 %copy-start.6 = (bf16[512,128]{1,0:T(8,128)(2,1)S(1)}, bf16[512,128]{1,0:T(8,128)(2,1)}, u32[]{:S(2)}) copy-start(bf16[512,128]{1,0:T(8,128)(2,1)} %param.20) | copy-start | bytes 393220
  5.2 4.2 %copy-start.10 = (f32[512]{0:T(512)S(1)}, f32[512]{0:T(512)}, u32[]{:S(2)}) copy-start(f32[512]{0:T(512)} %param.18) | copy-start | bytes 6148
  5.6 4.5 %copy-start.7 = (bf16[512,128]{1,0:T(8,128)(2,1)S(1)}, bf16[512,128]{1,0:T(8,128)(2,1)}, u32[]{:S(2)}) copy-start(bf16[512,128]{1,0:T(8,128)(2,1)} %param.21) | copy-start | bytes 393220
  6.0 48.7 %copy-start.5 = (bf16[512,128]{1,0:T(8,128)(2,1)S(1)}, bf16[512,128]{1,0:T(8,128)(2,1)}, u32[]{:S(2)}) copy-start(bf16[512,128]{1,0:T(8,128)(2,1)} %param.19) | copy-start | bytes 393220
  55.4 33.7 %copy-start.8 = (bf16[128,512]{1,0:T(8,128)(2,1)S(1)}, bf16[128,512]{1,0:T(8,128)(2,1)}, u32[]{:S(2)}) copy-start(bf16[128,512]{1,0:T(8,128)(2,1)} %param.22) | copy-start | bytes 393220
  55.4 52.6 %copy-start.2 = (bf16[512,512]{1,0:T(8,128)(2,1)S(1)}, bf16[512,512]{1,0:T(8,128)(2,1)}, u32[]{:S(2)}) copy-start(bf16[512,512]{1,0:T(8,128)(2,1)} %param.15) | copy-start | bytes 1572868
  59.6 3.4 %copy-start.1 = (f32[2,1024,512]{2,1,0:T(8,128)S(1)}, f32[2,1024,512]{2,1,0:T(8,128)}, u32[]{:S(2)}) copy-start(f32[2,1024,512]{2,1,0:T(8,128)} %get-tuple-element.191) | copy-start | bytes 12582916 | tf_op jit(solution)/shard_map/while
  68.0 3.4 %copy-start.1 = (f32[2,1024,512]{2,1,0:T(8,128)S(1)}, f32[2,1024,512]{2,1,0:T(8,128)}, u32[]{:S(2)}) copy-start(f32[2,1024,512]{2,1,0:T(8,128)} %get-tuple-element.191) | copy-start | bytes 12582916 | tf_op jit(solution)/shard_map/while
  76.4 3.4 %copy-start.1 = (f32[2,1024,512]{2,1,0:T(8,128)S(1)}, f32[2,1024,512]{2,1,0:T(8,128)}, u32[]{:S(2)}) copy-start(f32[2,1024,512]{2,1,0:T(8,128)} %get-tuple-element.191) | copy-start | bytes 12582916 | tf_op jit(solution)/shard_map/while
  84.8 3.4 %copy-start.1 = (f32[2,1024,512]{2,1,0:T(8,128)S(1)}, f32[2,1024,512]{2,1,0:T(8,128)}, u32[]{:S(2)}) copy-start(f32[2,1024,512]{2,1,0:T(8,128)} %get-tuple-element.191) | copy-start | bytes 12582916 | tf_op jit(solution)/shard_map/while
  89.1 21.5 %copy-start.11 = (bf16[512,512]{1,0:T(8,128)(2,1)S(1)}, bf16[512,512]{1,0:T(8,128)(2,1)}, u32[]{:S(2)}) copy-start(bf16[512,512]{1,0:T(8,128)(2,1)} %param.24) | copy-start | bytes 1572868
  89.1 21.5 %copy-start.12 = (f32[512]{0:T(512)S(1)}, f32[512]{0:T(512)}, u32[]{:S(2)}) copy-start(f32[512]{0:T(512)} %param.23) | copy-start | bytes 6148
  90.3 27.9 %copy-start.9 = (f32[27,512]{1,0:T(8,128)S(1)}, f32[27,512]{1,0:T(8,128)}, u32[]{:S(2)}) copy-start(f32[27,512]{1,0:T(8,128)} %param.25) | copy-start | bytes 165892
  112.3 16.4 %collective-permute-start = (bf16[1,16,16,512]{3,2,1,0:T(8,128)(2,1)S(1)}, bf16[1,16,16,512]{3,2,1,0:T(8,128)(2,1)S(1)}, u32[]{:S(2)}, u32[]{:S(2)}) collective-permute-start(bf16[1,16,16,512]{3,2,1,0:T(8,128)(2,1)S(1)} %bitcast.128), channel_id=1, source_target_pairs={{0,4},{4,8},{8,12},{12,16},{16,20},{20,24},{24,28},{28,32},{32,36}... | collective-permute-start | bytes 786440 | tf_op jit(solution)/shard_map/ppermute | solution.py:313
  114.8 14.4 %collective-permute-start.1 = (bf16[1,16,16,512]{3,2,1,0:T(8,128)(2,1)S(1)}, bf16[1,16,16,512]{3,2,1,0:T(8,128)(2,1)S(1)}, u32[]{:S(2)}, u32[]{:S(2)}) collective-permute-start(bf16[1,16,16,512]{3,2,1,0:T(8,128)(2,1)S(1)} %bitcast.127), channel_id=1, source_target_pairs={{4,0},{8,4},{12,8},{16,12},{20,16},{24,20},{28,24},{32,28},{36,32}... | collective-permute-start | bytes 786440 | tf_op jit(solution)/shard_map/ppermute | solution.py:315
  130.0 4.1 %copy-start.4 = (bf16[512,512]{1,0:T(8,128)(2,1)S(1)}, bf16[512,512]{1,0:T(8,128)(2,1)}, u32[]{:S(2)}) copy-start(bf16[512,512]{1,0:T(8,128)(2,1)} %param.26) | copy-start | bytes 1572868
  134.7 16.0 %collective-permute-start.2 = (bf16[1,16,16,512]{3,2,1,0:T(8,128)(2,1)S(1)}, bf16[1,16,16,512]{3,2,1,0:T(8,128)(2,1)S(1)}, u32[]{:S(2)}, u32[]{:S(2)}) collective-permute-start(bf16[1,16,16,512]{3,2,1,0:T(8,128)(2,1)S(1)} %bitcast.130), channel_id=1, source_target_pairs={{0,4},{4,8},{8,12},{12,16},{16,20},{20,24},{24,28},{28,32},{32,36}... | collective-permute-start | bytes 786440 | tf_op jit(solution)/shard_map/ppermute | solution.py:313
  137.9 14.0 %collective-permute-start.3 = (bf16[1,16,16,512]{3,2,1,0:T(8,128)(2,1)S(1)}, bf16[1,16,16,512]{3,2,1,0:T(8,128)(2,1)S(1)}, u32[]{:S(2)}, u32[]{:S(2)}) collective-permute-start(bf16[1,16,16,512]{3,2,1,0:T(8,128)(2,1)S(1)} %bitcast.129), channel_id=1, source_target_pairs={{4,0},{8,4},{12,8},{16,12},{20,16},{24,20},{28,24},{32,28},{36,32}... | collective-permute-start | bytes 786440 | tf_op jit(solution)/shard_map/ppermute | solution.py:315
  152.6 3.9 %copy-start.3 = (bf16[4,128,512]{2,1,0:T(8,128)(2,1)S(1)}, bf16[4,128,512]{2,1,0:T(8,128)(2,1)}, u32[]{:S(2)}) copy-start(bf16[4,128,512]{2,1,0:T(8,128)(2,1)} %shard_map.149) | copy-start | bytes 1572868

commit v8 on v7

--- a/solution.py
+++ b/solution.py
@@ -302,6 +302,37 @@
     return summed.reshape(rows, width)
 
 
+def attention_kernel(heads, q_tile, q_ref, kv_ref, out_ref):
+    key_width = heads * HEAD
+    score_scale = HEAD ** (-0.5)
+    for head in range(heads):
+        keys = kv_ref[:, head * HEAD : (head + 1) * HEAD]
+        values = kv_ref[:, key_width + head * HEAD : key_width + (head + 1) * HEAD]
+        for first in range(0, q_ref.shape[0], q_tile):
+            queries = q_ref[first : first + q_tile, head * HEAD : (head + 1) * HEAD]
+            scores = lax.dot_general(
+                queries, keys, (((1,), (1,)), ((), ())), preferred_element_type=jnp.float32
+            ) * score_scale
+            top = jnp.max(scores, axis=1, keepdims=True)
+            weights = jnp.exp(scores - top)
+            row_sum = jnp.sum(weights, axis=1, keepdims=True)
+            mixed = jnp.dot(
+                weights.astype(jnp.bfloat16), values, preferred_element_type=jnp.float32
+            )
+            out_ref[first : first + q_tile, head * HEAD : (head + 1) * HEAD] = (
+                mixed / row_sum
+            ).astype(out_ref.dtype)
+
+
+def attention(queries, kv, heads, q_tile=256):
+    return pl.pallas_call(
+        functools.partial(attention_kernel, heads, q_tile),
+        out_shape=jax.ShapeDtypeStruct(queries.shape, jnp.bfloat16),
+        in_specs=[pl.BlockSpec(memory_space=pltpu.VMEM)] * 2,
+        out_specs=pl.BlockSpec(memory_space=pltpu.VMEM),
+    )(queries, kv)
+
+
 def padded_2(cells, sides, width):
     for axis, dim in sides:
         count = lax.psum(1, axis)
@@ -390,23 +421,6 @@
         ]
         result = result + window.astype(jnp.float32) * weights[offset]
     return result
-
-
-def attend_piece(state_tuple, queries, key_rows, value_rows):
-    row_max, row_sum, weighted = state_tuple
-    score_scale = key_rows.shape[-1] ** (-0.5)
-    scores = (
-        jnp.einsum("qhd,khd->hqk", queries, key_rows, preferred_element_type=jnp.float32)
-        * score_scale
-    )
-    new_max = jnp.maximum(row_max, jnp.max(scores, axis=2))
-    rescale = jnp.exp(row_max - new_max)
-    expo = jnp.exp(scores - new_max[:, :, None])
-    row_sum = row_sum * rescale + jnp.sum(expo, axis=2)
-    weighted = weighted * rescale[:, :, None] + jnp.einsum(
-        "hqk,khd->hqd", expo.astype(jnp.bfloat16), value_rows, preferred_element_type=jnp.float32
-    )
-    return (new_max, row_sum, weighted)
 
 
 def per_device(
@@ -436,12 +450,6 @@
         tok_rows, heads_dev, HEAD
     )
     queries = rotate(queries, tok_cos, tok_sin).astype(jnp.bfloat16)
-    initial = (
-        jnp.full((heads_dev, tok_rows), -1e30, jnp.float32),
-        jnp.zeros((heads_dev, tok_rows), jnp.float32),
-        jnp.zeros((heads_dev, tok_rows, HEAD), jnp.float32),
-    )
-    state_tuple = initial
     local_rows = key_input.shape[0]
     own_cos, own_sin = key_tables(slab_index * local_rows, local_rows, HEAD)
     own_keys = jnp.dot(key_input, w_key, preferred_element_type=jnp.float32).reshape(
@@ -454,24 +462,7 @@
     key_width = heads_dev * HEAD
     pieces = jnp.concatenate([own_keys.reshape(local_rows, key_width), own_values], axis=1)
     pieces = slab_gather(pieces, lax.psum(1, SLAB), lax.psum(1, ("z", "xl")))
-    row_count = pieces.shape[0]
-    block_rows = math.gcd(row_count, 1024)
-    block_count = row_count // block_rows
-    blocks = pieces.reshape(block_count, block_rows, pieces.shape[1])
-
-    def one_block(state_inner, rows_in):
-        key_block = rows_in[:, :key_width].reshape(block_rows, heads_dev, HEAD)
-        value_block = rows_in[:, key_width:].reshape(block_rows, heads_dev, HEAD)
-        return (attend_piece(state_inner, queries, key_block, value_block), None)
-
-    state_tuple, _ = lax.scan(one_block, state_tuple, blocks)
-    row_max, row_sum, weighted = state_tuple
-    heads_out = (
-        (weighted / row_sum[:, :, None])
-        .transpose(1, 0, 2)
-        .reshape(tok_rows, heads_dev * HEAD)
-        .astype(jnp.bfloat16)
-    )
+    heads_out = attention(queries.reshape(tok_rows, key_width), pieces, heads_dev)
     partial_value = jnp.dot(heads_out, w_out, preferred_element_type=jnp.float32)
     head_total = head_sum(partial_value, lax.psum(1, FFN)).astype(jnp.float32)
     attended = head_total.astype(jnp.bfloat16)

time: 192 us -> 167 us (0.87)
  matrix products: 22.5 us -> 8.14 us
  other arithmetic: 29.9 us -> 17.7 us
  Pallas kernels: 89.5 us -> 98.8 us
  local copies, waits for them, and re-layouts: 14.1 us -> 6.95 us
    dot_general x8 -> x0, matrix products: 14.3 us -> none  [the longest x4 10.9 us: attend_piece(): jnp.einsum('qhd,khd->hqk', queries, key_rows, preferred_element_type=jnp....]
    reduce_sum x4 -> x0, other arithmetic: 12.2 us -> none  [attend_piece(): row_sum = row_sum * rescale + jnp.sum(expo, axis=2)]
    pallas_call x0 -> x1, Pallas kernels: none -> 9.26 us  [attention(): pl.pallas_call(functools.partial(attention_kernel, heads, q_tile), out_sh...]
    dynamic_slice x8 -> x0, local copies, waits for them, and re-layouts: 5.21 us -> none  [per_device(): state_tuple, _ = lax.scan(one_block, state_tuple, blocks)]
where the time goes in v8:
time: 167 us; the launch traced here: 166 us
  Pallas kernels  98.8 us (59%)
  waiting for transfers between devices  21.8 us (13%)
  other arithmetic  17.7 us (11%)
  starting transfers between devices  11.7 us (7%)
  matrix products  8.14 us (5%)
  local copies, waits for them, and re-layouts  6.95 us (4%)
    pallas_call x1, Pallas kernels, slab_gather(): pl.pallas_call(functools.partial(gather_kernel, row_size), out_shape=jax....  43.7 us
    pallas_call x1, Pallas kernels, slab_scatter(): pl.pallas_call(functools.partial(scatter_kernel, row_size), out_shape=jax...  28.1 us
    ppermute x2, waiting for transfers between devices, padded_2(): lax.ppermute(tail, axis, [(i, (i + 1) % count) for i in range(ends)])  20.1 us
    pallas_call x1, Pallas kernels, head_sum(): pl.pallas_call(functools.partial(head_sum_kernel, count), out_shape=jax.S...  17.7 us
    pallas_call x1, Pallas kernels, attention(): pl.pallas_call(functools.partial(attention_kernel, heads, q_tile), out_sh...  9.26 us
    ppermute x2, starting transfers between devices, padded_2(): lax.ppermute(head, axis, [((i + 1) % count, i) for i in range(ends)])  6.04 us
    ppermute x2, starting transfers between devices, padded_2(): lax.ppermute(tail, axis, [(i, (i + 1) % count) for i in range(ends)])  5.67 us
    convert_element_type x1, other arithmetic, per_device(): depth_conv(grad_pad, w_depth[::-1], CZ).astype(jnp.bfloat16)  3.84 us
  transfers between devices with their start and end apart: 4, of which 4 were waited for; matrix products, arithmetic and copies ran while one was open for 0% of the time, Pallas kernels for 0%

profile of v8, /device:TPU:2, one launch (start us, length us, event | category | flops | bytes accessed | tf_op | source)
XLA Modules:
  0.0 166.2 jit_solution(8766789087519623343)
XLA Ops:
  1.1 1.2 convert_reduce_fusion
  2.3 1.3 fusion.15
  3.6 1.3 fusion.17
  6.0 3.2 %fusion.63 = (f32[64]{0:T(128)S(1)}, f32[64,512]{1,0:T(8,128)S(1)}) fusion(bf16[64,4096]{1,0:T(8,128)(2,1)S(1)} %reshape.617, bf16[4096,512]{1,0:T(8,128)(2,1)} %param.15), kind=kOutput, calls=%fused_computation.139 | convolution fusion | flops 268468160 | bytes 4849920 | tf_op jit(solution)/shard_map/dot_general | solution.py:446
  11.0 43.7 %shard_map.148.kv_ref = bf16[4096,256]{1,0:T(8,128)(2,1)} custom-call(bf16[64,256]{1,0:T(8,128)(2,1)} %pad_maximum_fusion.7.x_ref), custom_call_target="tpu_custom_call" | custom-call | tf_op jit(solution)/shard_map/pallas_call | solution.py:124
  56.2 9.3 %shard_map.149 = bf16[512,128]{1,0:T(8,128)(2,1)} custom-call(bf16[512,128]{1,0:T(8,128)(2,1)} %copy.25.q_ref, bf16[4096,256]{1,0:T(8,128)(2,1)} %shard_map.148.kv_ref), custom_call_target="tpu_custom_call" | custom-call | tf_op jit(solution)/shard_map/pallas_call | solution.py:328
  65.5 2.0 %convolution_convert_fusion.3 = bf16[512,512]{1,0:T(8,128)(2,1)} fusion(bf16[512,128]{1,0:T(8,128)(2,1)} %shard_map.149, bf16[128,512]{1,0:T(8,128)(2,1)S(1)} %copy-done.7), kind=kOutput, calls=%fused_computation.26 | convolution fusion | flops 67371008 | bytes 786432 | tf_op jit(solution)/shard_map/dot_general | solution.py:466
  67.5 17.7 %shard_map.150 = bf16[4,128,512]{2,1,0:T(8,128)(2,1)} custom-call(bf16[4,128,512]{2,1,0:T(8,128)(2,1)} %bitcast.80), custom_call_target="tpu_custom_call" | custom-call | tf_op jit(solution)/shard_map/pallas_call | solution.py:194
  85.2 1.3 fusion.27
  86.6 1.3 multiply_reduce_fusion
  88.5 2.5 %collective-permute-start = (bf16[1,16,16,512]{3,2,1,0:T(8,128)(2,1)S(1)}, bf16[1,16,16,512]{3,2,1,0:T(8,128)(2,1)S(1)}, u32[]{:S(2)}, u32[]{:S(2)}) collective-permute-start(bf16[1,16,16,512]{3,2,1,0:T(8,128)(2,1)S(1)} %bitcast.85), channel_id=1, source_target_pairs={{0,4},{4,8},{8,12},{12,16},{16,20},{20,24},{24,28},{28,32},{32,36}... | collective-permute-start | bytes 786440 | tf_op jit(solution)/shard_map/ppermute | solution.py:344
  91.0 3.3 %collective-permute-start.1 = (bf16[1,16,16,512]{3,2,1,0:T(8,128)(2,1)S(1)}, bf16[1,16,16,512]{3,2,1,0:T(8,128)(2,1)S(1)}, u32[]{:S(2)}, u32[]{:S(2)}) collective-permute-start(bf16[1,16,16,512]{3,2,1,0:T(8,128)(2,1)S(1)} %bitcast.84), channel_id=1, source_target_pairs={{4,0},{8,4},{12,8},{16,12},{20,16},{24,20},{28,24},{32,28},{36,32}... | collective-permute-start | bytes 786440 | tf_op jit(solution)/shard_map/ppermute | solution.py:346
  94.5 10.5 %collective-permute-done = bf16[1,16,16,512]{3,2,1,0:T(8,128)(2,1)S(1)} collective-permute-done((bf16[1,16,16,512]{3,2,1,0:T(8,128)(2,1)S(1)}, bf16[1,16,16,512]{3,2,1,0:T(8,128)(2,1)S(1)}, u32[]{:S(2)}, u32[]{:S(2)}) %collective-permute-start) | collective-permute-done | bytes 262176 | tf_op jit(solution)/shard_map/ppermute | solution.py:344
  106.2 3.8 %multiply_add_fusion = f32[2,16,16,512]{3,2,1,0:T(8,128)S(1)} fusion(bf16[2,16,16,512]{3,2,1,0:T(8,128)(2,1)S(1)} %bitcast.78, bf16[4,18,18,512]{3,2,1,0:T(8,128)(2,1)S(1)} %fusion.10, bf16[1,16,16,512]{3,2,1,0:T(8,128)(2,1)S(1)} %collective-permute-done.1, bf16[1,16,16,512]{3,2,1,0:T(8,128)(2,1)S(1)} %collective-permute-done, f32[512]{0:T(512)S(1)} %bitcast.100, ...), kind=kLoop, calls=%fused_computation.46 | loop fusion | flops 21495808 | bytes 14735360 | tf_op jit(solution)/shard_map/add | solution.py:422
  110.3 0.8 copy-done.3
  111.7 3.2 %collective-permute-start.2 = (bf16[1,16,16,512]{3,2,1,0:T(8,128)(2,1)S(1)}, bf16[1,16,16,512]{3,2,1,0:T(8,128)(2,1)S(1)}, u32[]{:S(2)}, u32[]{:S(2)}) collective-permute-start(bf16[1,16,16,512]{3,2,1,0:T(8,128)(2,1)S(1)} %bitcast.87), channel_id=1, source_target_pairs={{0,4},{4,8},{8,12},{12,16},{16,20},{20,24},{24,28},{28,32},{32,36}... | collective-permute-start | bytes 786440 | tf_op jit(solution)/shard_map/ppermute | solution.py:344
  114.9 2.7 %collective-permute-start.3 = (bf16[1,16,16,512]{3,2,1,0:T(8,128)(2,1)S(1)}, bf16[1,16,16,512]{3,2,1,0:T(8,128)(2,1)S(1)}, u32[]{:S(2)}, u32[]{:S(2)}) collective-permute-start(bf16[1,16,16,512]{3,2,1,0:T(8,128)(2,1)S(1)} %bitcast.86), channel_id=1, source_target_pairs={{4,0},{8,4},{12,8},{16,12},{20,16},{24,20},{28,24},{32,28},{36,32}... | collective-permute-start | bytes 786440 | tf_op jit(solution)/shard_map/ppermute | solution.py:346
  118.1 9.6 %collective-permute-done.2 = bf16[1,16,16,512]{3,2,1,0:T(8,128)(2,1)S(1)} collective-permute-done((bf16[1,16,16,512]{3,2,1,0:T(8,128)(2,1)S(1)}, bf16[1,16,16,512]{3,2,1,0:T(8,128)(2,1)S(1)}, u32[]{:S(2)}, u32[]{:S(2)}) %collective-permute-start.2) | collective-permute-done | bytes 262176 | tf_op jit(solution)/shard_map/ppermute | solution.py:344
  127.7 1.2 collective-permute-done.3
  129.6 3.8 %add_convert_fusion = bf16[2,16,16,512]{3,2,1,0:T(8,128)(2,1)S(1)} fusion(bf16[2,16,16,512]{3,2,1,0:T(8,128)(2,1)S(1)} %bitcast.73, bf16[4,18,18,512]{3,2,1,0:T(8,128)(2,1)S(1)} %select_maximum_fusion, bf16[1,16,16,512]{3,2,1,0:T(8,128)(2,1)S(1)} %collective-permute-done.3, bf16[1,16,16,512]{3,2,1,0:T(8,128)(2,1)S(1)} %collective-permute-done.2, ...), kind=kLoop, calls=%fused_computation.45 | loop fusion | flops 21757952 | bytes 14211072 | tf_op jit(solution)/shard_map/convert_element_type | solution.py:492
  134.8 1.2 convert_element_type.374.g_ref
  136.0 28.1 %shard_map.151 = f32[16,512]{1,0:T(8,128)} custom-call(bf16[64,16,512]{2,1,0:T(8,128)(2,1)} %convert_element_type.374.g_ref), custom_call_target="tpu_custom_call" | custom-call | tf_op jit(solution)/shard_map/pallas_call | solution.py:285
  164.0 0.8 reshape.625
  165.4 0.8 copy.30
  (70 shorter events, 10.4 us)
Async XLA Ops:
  0.6 109.7 %copy-start = (bf16[512,512]{1,0:T(8,128)(2,1)S(1)}, bf16[512,512]{1,0:T(8,128)(2,1)}, u32[]{:S(2)}) copy-start(bf16[512,512]{1,0:T(8,128)(2,1)} %param.25) | copy-start | bytes 1572868
  5.9 3.5 %copy-start.5 = (bf16[512,128]{1,0:T(8,128)(2,1)S(1)}, bf16[512,128]{1,0:T(8,128)(2,1)}, u32[]{:S(2)}) copy-start(bf16[512,128]{1,0:T(8,128)(2,1)} %param.18) | copy-start | bytes 393220
  5.9 3.5 %copy-start.9 = (f32[512]{0:T(512)S(1)}, f32[512]{0:T(512)}, u32[]{:S(2)}) copy-start(f32[512]{0:T(512)} %param.16) | copy-start | bytes 6148
  6.0 4.2 %copy-start.6 = (bf16[512,128]{1,0:T(8,128)(2,1)S(1)}, bf16[512,128]{1,0:T(8,128)(2,1)}, u32[]{:S(2)}) copy-start(bf16[512,128]{1,0:T(8,128)(2,1)} %param.19) | copy-start | bytes 393220
  9.2 45.6 %copy-start.4 = (bf16[512,128]{1,0:T(8,128)(2,1)S(1)}, bf16[512,128]{1,0:T(8,128)(2,1)}, u32[]{:S(2)}) copy-start(bf16[512,128]{1,0:T(8,128)(2,1)} %param.17) | copy-start | bytes 393220
  54.7 10.8 %copy-start.7 = (bf16[128,512]{1,0:T(8,128)(2,1)S(1)}, bf16[128,512]{1,0:T(8,128)(2,1)}, u32[]{:S(2)}) copy-start(bf16[128,512]{1,0:T(8,128)(2,1)} %param.20) | copy-start | bytes 393220
  56.2 29.0 %copy-start.1 = (bf16[512,512]{1,0:T(8,128)(2,1)S(1)}, bf16[512,512]{1,0:T(8,128)(2,1)}, u32[]{:S(2)}) copy-start(bf16[512,512]{1,0:T(8,128)(2,1)} %param.13) | copy-start | bytes 1572868
  65.5 22.5 %copy-start.10 = (bf16[512,512]{1,0:T(8,128)(2,1)S(1)}, bf16[512,512]{1,0:T(8,128)(2,1)}, u32[]{:S(2)}) copy-start(bf16[512,512]{1,0:T(8,128)(2,1)} %param.22) | copy-start | bytes 1572868
  65.5 22.5 %copy-start.11 = (f32[512]{0:T(512)S(1)}, f32[512]{0:T(512)}, u32[]{:S(2)}) copy-start(f32[512]{0:T(512)} %param.21) | copy-start | bytes 6148
  85.2 2.7 %copy-start.2 = (bf16[4,128,512]{2,1,0:T(8,128)(2,1)S(1)}, bf16[4,128,512]{2,1,0:T(8,128)(2,1)}, u32[]{:S(2)}) copy-start(bf16[4,128,512]{2,1,0:T(8,128)(2,1)} %shard_map.150) | copy-start | bytes 1572868
  87.9 6.5 %copy-start.8 = (f32[27,512]{1,0:T(8,128)S(1)}, f32[27,512]{1,0:T(8,128)}, u32[]{:S(2)}) copy-start(f32[27,512]{1,0:T(8,128)} %param.23) | copy-start | bytes 165892
  88.5 16.4 %collective-permute-start = (bf16[1,16,16,512]{3,2,1,0:T(8,128)(2,1)S(1)}, bf16[1,16,16,512]{3,2,1,0:T(8,128)(2,1)S(1)}, u32[]{:S(2)}, u32[]{:S(2)}) collective-permute-start(bf16[1,16,16,512]{3,2,1,0:T(8,128)(2,1)S(1)} %bitcast.85), channel_id=1, source_target_pairs={{0,4},{4,8},{8,12},{12,16},{16,20},{20,24},{24,28},{28,32},{32,36}... | collective-permute-start | bytes 786440 | tf_op jit(solution)/shard_map/ppermute | solution.py:344
  91.0 14.4 %collective-permute-start.1 = (bf16[1,16,16,512]{3,2,1,0:T(8,128)(2,1)S(1)}, bf16[1,16,16,512]{3,2,1,0:T(8,128)(2,1)S(1)}, u32[]{:S(2)}, u32[]{:S(2)}) collective-permute-start(bf16[1,16,16,512]{3,2,1,0:T(8,128)(2,1)S(1)} %bitcast.84), channel_id=1, source_target_pairs={{4,0},{8,4},{12,8},{16,12},{20,16},{24,20},{28,24},{32,28},{36,32}... | collective-permute-start | bytes 786440 | tf_op jit(solution)/shard_map/ppermute | solution.py:346
  110.1 1.0 copy-start.3
  111.7 16.0 %collective-permute-start.2 = (bf16[1,16,16,512]{3,2,1,0:T(8,128)(2,1)S(1)}, bf16[1,16,16,512]{3,2,1,0:T(8,128)(2,1)S(1)}, u32[]{:S(2)}, u32[]{:S(2)}) collective-permute-start(bf16[1,16,16,512]{3,2,1,0:T(8,128)(2,1)S(1)} %bitcast.87), channel_id=1, source_target_pairs={{0,4},{4,8},{8,12},{12,16},{16,20},{20,24},{24,28},{28,32},{32,36}... | collective-permute-start | bytes 786440 | tf_op jit(solution)/shard_map/ppermute | solution.py:344
  114.9 14.0 %collective-permute-start.3 = (bf16[1,16,16,512]{3,2,1,0:T(8,128)(2,1)S(1)}, bf16[1,16,16,512]{3,2,1,0:T(8,128)(2,1)S(1)}, u32[]{:S(2)}, u32[]{:S(2)}) collective-permute-start(bf16[1,16,16,512]{3,2,1,0:T(8,128)(2,1)S(1)} %bitcast.86), channel_id=1, source_target_pairs={{4,0},{8,4},{12,8},{16,12},{20,16},{24,20},{28,24},{32,28},{36,32}... | collective-permute-start | bytes 786440 | tf_op jit(solution)/shard_map/ppermute | solution.py:346

commit v9 on v8

--- a/solution.py
+++ b/solution.py
@@ -333,21 +333,54 @@
     )(queries, kv)
 
 
-def padded_2(cells, sides, width):
-    for axis, dim in sides:
-        count = lax.psum(1, axis)
-        ends = count - 1
-        head = lax.slice_in_dim(cells, 0, width, axis=dim)
-        tail = lax.slice_in_dim(cells, cells.shape[dim] - width, cells.shape[dim], axis=dim)
-        cells = jnp.concatenate(
-            [
-                lax.ppermute(tail, axis, [(i, (i + 1) % count) for i in range(ends)]),
-                cells,
-                lax.ppermute(head, axis, [((i + 1) % count, i) for i in range(ends)]),
-            ],
-            axis=dim,
-        )
-    return cells
+def halo_kernel(count, cells_ref, below_ref, above_ref, send_sem, recv_sem):
+    me = lax.axis_index(SLAB)
+    plane = below_ref.shape[0]
+    after = lax.rem(me + 1, count)
+    before = lax.rem(me + count - 1, count)
+    barrier = pltpu.get_barrier_semaphore()
+    for peer in (before, after):
+        pl.semaphore_signal(barrier, inc=1, device_id=peer_id(peer), device_id_type=MESH)
+    pl.semaphore_wait(barrier, 2)
+    up = pltpu.make_async_remote_copy(
+        src_ref=cells_ref.at[pl.ds(cells_ref.shape[0] - plane, plane)],
+        dst_ref=below_ref,
+        send_sem=send_sem.at[0],
+        recv_sem=recv_sem.at[0],
+        device_id=peer_id(after),
+        device_id_type=MESH,
+    )
+    down = pltpu.make_async_remote_copy(
+        src_ref=cells_ref.at[pl.ds(0, plane)],
+        dst_ref=above_ref,
+        send_sem=send_sem.at[1],
+        recv_sem=recv_sem.at[1],
+        device_id=peer_id(before),
+        device_id_type=MESH,
+    )
+    up.start()
+    down.start()
+    up.wait()
+    down.wait()
+
+
+def halo_planes(cells, collective):
+    count = lax.psum(1, SLAB)
+    me = lax.axis_index(SLAB)
+    plane_shape = cells.shape[1:]
+    flat = cells.reshape(cells.shape[0] * math.prod(plane_shape[:-1]), plane_shape[-1])
+    plane = flat.shape[0] // cells.shape[0]
+    below, above = pl.pallas_call(
+        functools.partial(halo_kernel, count),
+        out_shape=[jax.ShapeDtypeStruct((plane, flat.shape[1]), flat.dtype)] * 2,
+        in_specs=[pl.BlockSpec(memory_space=pltpu.VMEM)],
+        out_specs=[pl.BlockSpec(memory_space=pltpu.VMEM)] * 2,
+        scratch_shapes=[pltpu.SemaphoreType.DMA((2,)), pltpu.SemaphoreType.DMA((2,))],
+        compiler_params=pltpu.CompilerParams(collective_id=collective, has_side_effects=True),
+    )(flat)
+    below = jnp.where(me > 0, below, jnp.zeros_like(below)).reshape((1,) + plane_shape)
+    above = jnp.where(me < count - 1, above, jnp.zeros_like(above)).reshape((1,) + plane_shape)
+    return jnp.concatenate([below, cells, above], axis=0)
 
 
 def layer_norm(values, scale_gain):
@@ -474,7 +507,7 @@
         .astype(jnp.bfloat16)
         .reshape(CZ, GY, GX, channels)
     )
-    pre_wide = padded_2(pre, ((SLAB, 0),), 1)
+    pre_wide = halo_planes(pre, 3)
     pre_pad = jnp.pad(pre_wide, ((0, 0), (1, 1), (1, 1), (0, 0)))
     mixed = depth_conv(pre_pad, w_depth, CZ).reshape(tok_rows, channels)
     normal_cdf = 0.5 * (1.0 + lax.erf(mixed * ROOT_HALF))
@@ -486,7 +519,7 @@
         .astype(jnp.bfloat16)
         .reshape(CZ, GY, GX, channels)
     )
-    grad_wide = padded_2(grad_mixed, ((SLAB, 0),), 1)
+    grad_wide = halo_planes(grad_mixed, 4)
     grad_pad = jnp.pad(grad_wide, ((0, 0), (1, 1), (1, 1), (0, 0)))
     grad_pre = (
         depth_conv(grad_pad, w_depth[::-1], CZ).astype(jnp.bfloat16).reshape(tok_rows, channels)

time: 167 us -> 175 us (1.048)
  Pallas kernels: 98.8 us -> 133 us
  waiting for transfers between devices: 21.8 us -> 0 us
  starting transfers between devices: 11.7 us -> 0 us
  other arithmetic: 17.7 us -> 23.9 us
    pallas_call x0 -> x2, Pallas kernels: none -> 34.4 us  [halo_planes(): pl.pallas_call(functools.partial(halo_kernel, count), out_shape=[jax.Shap...]
    ppermute x4 -> x0, waiting for transfers between devices: 21.8 us -> none  [the longest x2 20.1 us: padded_2(): lax.ppermute(tail, axis, [(i, (i + 1) % count) for i in range(ends)])]
    ppermute x4 -> x0, starting transfers between devices: 11.7 us -> none  [the longest x2 6.04 us: padded_2(): lax.ppermute(head, axis, [((i + 1) % count, i) for i in range(ends)])]
    select_n x0 -> x4, other arithmetic: none -> 3.97 us  [the longest x2 2.01 us: halo_planes(): jnp.where(me > 0, below, jnp.zeros_like(below)).reshape((1,) + plane_shape)]
    concatenate x2, other arithmetic: 1.53 us -> 3.51 us  [halo_planes(): return jnp.concatenate([below, cells, above], axis=0)]
  transfers between devices with their start and end apart: 4 -> 0, of which waited for: 4 -> 0; matrix products, arithmetic and copies ran while one was open for 0% -> 0% of each run, Pallas kernels for 0% -> 0%
where the time goes in v9:
time: 175 us
  Pallas kernels  133 us (76%)
  other arithmetic  23.9 us (14%)
  matrix products  9.73 us (6%)
  local copies, waits for them, and re-layouts  6.88 us (4%)
    pallas_call x1, Pallas kernels, slab_gather(): pl.pallas_call(functools.partial(gather_kernel, row_size), out_shape=jax....  43.7 us
    pallas_call x2, Pallas kernels, halo_planes(): pl.pallas_call(functools.partial(halo_kernel, count), out_shape=[jax.Shap...  34.4 us
    pallas_call x1, Pallas kernels, slab_scatter(): pl.pallas_call(functools.partial(scatter_kernel, row_size), out_shape=jax...  28 us
    pallas_call x1, Pallas kernels, head_sum(): pl.pallas_call(functools.partial(head_sum_kernel, count), out_shape=jax.S...  17.7 us
    pallas_call x1, Pallas kernels, attention(): pl.pallas_call(functools.partial(attention_kernel, heads, q_tile), out_sh...  9.27 us
    add x1, other arithmetic, depth_conv(): result = result + window.astype(jnp.float32) * weights[offset]  4.05 us
    convert_element_type x1, other arithmetic, per_device(): depth_conv(grad_pad, w_depth[::-1], CZ).astype(jnp.bfloat16)  3.85 us
    concatenate x2, other arithmetic, halo_planes(): return jnp.concatenate([below, cells, above], axis=0)  3.51 us

profile of v9, /device:TPU:2, one launch (start us, length us, event | category | flops | bytes accessed | tf_op | source)
XLA Modules:
  0.0 174.7 jit_solution(9317384431549518605)
XLA Ops:
  1.1 1.2 convert_reduce_fusion
  2.3 1.3 fusion.15
  3.6 1.3 fusion.17
  6.0 3.2 %fusion.61 = (f32[64]{0:T(128)S(1)}, f32[64,512]{1,0:T(8,128)S(1)}) fusion(bf16[64,4096]{1,0:T(8,128)(2,1)S(1)} %reshape.625, bf16[4096,512]{1,0:T(8,128)(2,1)} %param.15), kind=kOutput, calls=%fused_computation.141 | convolution fusion | flops 268468160 | bytes 4849920 | tf_op jit(solution)/shard_map/dot_general | solution.py:479
  10.9 43.7 %shard_map.148.kv_ref = bf16[4096,256]{1,0:T(8,128)(2,1)} custom-call(bf16[64,256]{1,0:T(8,128)(2,1)} %pad_maximum_fusion.7.x_ref), custom_call_target="tpu_custom_call" | custom-call | tf_op jit(solution)/shard_map/pallas_call | solution.py:124
  56.2 9.3 %shard_map.149 = bf16[512,128]{1,0:T(8,128)(2,1)} custom-call(bf16[512,128]{1,0:T(8,128)(2,1)} %copy.25.q_ref, bf16[4096,256]{1,0:T(8,128)(2,1)} %shard_map.148.kv_ref), custom_call_target="tpu_custom_call" | custom-call | tf_op jit(solution)/shard_map/pallas_call | solution.py:328
  65.5 2.0 %convolution_convert_fusion.3 = bf16[512,512]{1,0:T(8,128)(2,1)} fusion(bf16[512,128]{1,0:T(8,128)(2,1)} %shard_map.149, bf16[128,512]{1,0:T(8,128)(2,1)S(1)} %copy-done.9), kind=kOutput, calls=%fused_computation.26 | convolution fusion | flops 67371008 | bytes 786432 | tf_op jit(solution)/shard_map/dot_general | solution.py:499
  67.5 17.7 %shard_map.150 = bf16[4,128,512]{2,1,0:T(8,128)(2,1)} custom-call(bf16[4,128,512]{2,1,0:T(8,128)(2,1)} %bitcast.88), custom_call_target="tpu_custom_call" | custom-call | tf_op jit(solution)/shard_map/pallas_call | solution.py:194
  85.3 1.3 fusion.27
  86.6 1.3 multiply_reduce_fusion
  87.9 1.3 convolution_convert_fusion.2.cells_ref
  89.3 17.6 %shard_map.151 = (bf16[256,512]{1,0:T(8,128)(2,1)}, bf16[256,512]{1,0:T(8,128)(2,1)}) custom-call(bf16[512,512]{1,0:T(8,128)(2,1)} %convolution_convert_fusion.2.cells_ref), custom_call_target="tpu_custom_call" | custom-call | tf_op jit(solution)/shard_map/pallas_call | solution.py:373
  106.9 1.0 broadcast_select_fusion.3
  107.9 1.0 broadcast_select_fusion.1
  108.9 1.8 %fusion.10 = bf16[4,18,18,512]{3,2,1,0:T(8,128)(2,1)S(1)} fusion(bf16[1,16,16,512]{3,2,1,0:T(8,128)(2,1)S(1)} %bitcast.81, bf16[2,16,16,512]{3,2,1,0:T(8,128)(2,1)} %bitcast.77, bf16[1,16,16,512]{3,2,1,0:T(8,128)(2,1)S(1)} %bitcast.79), kind=kLoop, calls=%fused_computation.16 | loop fusion | flops 12607488 | bytes 2375680 | tf_op jit(solution)/shard_map/concatenate | solution.py:383
  110.7 4.1 %multiply_add_fusion = f32[2,16,16,512]{3,2,1,0:T(8,128)S(1)} fusion(bf16[2,16,16,512]{3,2,1,0:T(8,128)(2,1)S(1)} %bitcast.78, bf16[4,18,18,512]{3,2,1,0:T(8,128)(2,1)S(1)} %fusion.10, bf16[1,16,16,512]{3,2,1,0:T(8,128)(2,1)S(1)} %bitcast.82, bf16[1,16,16,512]{3,2,1,0:T(8,128)(2,1)S(1)} %bitcast.80, f32[512]{0:T(512)S(1)} %bitcast.142, f32[512]{0:T(512)S(1)} %bitcast.144, ...), kind=kLoop, calls=%fused_computation.46 | loop fusion | flops 21495808 | bytes 14735360 | tf_op jit(solution)/shard_map/add | solution.py:455
  115.8 1.4 fusion.11.cells_ref
  117.2 16.8 %shard_map.152 = (bf16[256,512]{1,0:T(8,128)(2,1)}, bf16[256,512]{1,0:T(8,128)(2,1)}) custom-call(bf16[512,512]{1,0:T(8,128)(2,1)} %fusion.11.cells_ref), custom_call_target="tpu_custom_call" | custom-call | tf_op jit(solution)/shard_map/pallas_call | solution.py:373
  134.0 1.0 broadcast_select_fusion.2
  135.0 1.0 broadcast_select_fusion
  136.0 1.8 %select_maximum_fusion = bf16[4,18,18,512]{3,2,1,0:T(8,128)(2,1)S(1)} fusion(bf16[1,16,16,512]{3,2,1,0:T(8,128)(2,1)S(1)} %bitcast.85, bf16[2,16,16,512]{3,2,1,0:T(8,128)(2,1)} %bitcast.72, bf16[1,16,16,512]{3,2,1,0:T(8,128)(2,1)S(1)} %bitcast.83), kind=kLoop, calls=%fused_computation.7 | loop fusion | flops 12607488 | bytes 2375680 | tf_op jit(solution)/shard_map/concatenate | solution.py:383
  137.7 3.8 %add_convert_fusion = bf16[2,16,16,512]{3,2,1,0:T(8,128)(2,1)S(1)} fusion(bf16[2,16,16,512]{3,2,1,0:T(8,128)(2,1)S(1)} %bitcast.73, bf16[4,18,18,512]{3,2,1,0:T(8,128)(2,1)S(1)} %select_maximum_fusion, bf16[1,16,16,512]{3,2,1,0:T(8,128)(2,1)S(1)} %bitcast.86, bf16[1,16,16,512]{3,2,1,0:T(8,128)(2,1)S(1)} %bitcast.84, f32[512]{0:T(512)S(1)} %bitcast.143, ...), kind=kLoop, calls=%fused_computation.45 | loop fusion | flops 21757952 | bytes 14211072 | tf_op jit(solution)/shard_map/convert_element_type | solution.py:525
  143.3 1.2 convert_element_type.374.g_ref
  144.5 28.0 %shard_map.153 = f32[16,512]{1,0:T(8,128)} custom-call(bf16[64,16,512]{2,1,0:T(8,128)(2,1)} %convert_element_type.374.g_ref), custom_call_target="tpu_custom_call" | custom-call | tf_op jit(solution)/shard_map/pallas_call | solution.py:285
  (70 shorter events, 9.6 us)
Async XLA Ops:
  0.6 114.4 %copy-start = (bf16[512,512]{1,0:T(8,128)(2,1)S(1)}, bf16[512,512]{1,0:T(8,128)(2,1)}, u32[]{:S(2)}) copy-start(bf16[512,512]{1,0:T(8,128)(2,1)} %param.25) | copy-start | bytes 1572868
  5.9 3.5 %copy-start.7 = (bf16[512,128]{1,0:T(8,128)(2,1)S(1)}, bf16[512,128]{1,0:T(8,128)(2,1)}, u32[]{:S(2)}) copy-start(bf16[512,128]{1,0:T(8,128)(2,1)} %param.18) | copy-start | bytes 393220
  5.9 3.5 %copy-start.11 = (f32[512]{0:T(512)S(1)}, f32[512]{0:T(512)}, u32[]{:S(2)}) copy-start(f32[512]{0:T(512)} %param.16) | copy-start | bytes 6148
  5.9 4.2 %copy-start.8 = (bf16[512,128]{1,0:T(8,128)(2,1)S(1)}, bf16[512,128]{1,0:T(8,128)(2,1)}, u32[]{:S(2)}) copy-start(bf16[512,128]{1,0:T(8,128)(2,1)} %param.19) | copy-start | bytes 393220
  9.2 45.9 %copy-start.6 = (bf16[512,128]{1,0:T(8,128)(2,1)S(1)}, bf16[512,128]{1,0:T(8,128)(2,1)}, u32[]{:S(2)}) copy-start(bf16[512,128]{1,0:T(8,128)(2,1)} %param.17) | copy-start | bytes 393220
  55.0 10.4 %copy-start.9 = (bf16[128,512]{1,0:T(8,128)(2,1)S(1)}, bf16[128,512]{1,0:T(8,128)(2,1)}, u32[]{:S(2)}) copy-start(bf16[128,512]{1,0:T(8,128)(2,1)} %param.20) | copy-start | bytes 393220
  56.2 29.0 %copy-start.1 = (bf16[512,512]{1,0:T(8,128)(2,1)S(1)}, bf16[512,512]{1,0:T(8,128)(2,1)}, u32[]{:S(2)}) copy-start(bf16[512,512]{1,0:T(8,128)(2,1)} %param.13) | copy-start | bytes 1572868
  65.5 22.4 %copy-start.12 = (bf16[512,512]{1,0:T(8,128)(2,1)S(1)}, bf16[512,512]{1,0:T(8,128)(2,1)}, u32[]{:S(2)}) copy-start(bf16[512,512]{1,0:T(8,128)(2,1)} %param.22) | copy-start | bytes 1572868
  65.5 22.5 %copy-start.13 = (f32[512]{0:T(512)S(1)}, f32[512]{0:T(512)}, u32[]{:S(2)}) copy-start(f32[512]{0:T(512)} %param.21) | copy-start | bytes 6148
  85.2 2.7 %copy-start.3 = (bf16[4,128,512]{2,1,0:T(8,128)(2,1)S(1)}, bf16[4,128,512]{2,1,0:T(8,128)(2,1)}, u32[]{:S(2)}) copy-start(bf16[4,128,512]{2,1,0:T(8,128)(2,1)} %shard_map.150) | copy-start | bytes 1572868
  89.3 21.4 %copy-start.10 = (f32[27,512]{1,0:T(8,128)S(1)}, f32[27,512]{1,0:T(8,128)}, u32[]{:S(2)}) copy-start(f32[27,512]{1,0:T(8,128)} %param.23) | copy-start | bytes 165892
  106.8 3.9 %copy-start.4 = (bf16[512,512]{1,0:T(8,128)(2,1)S(1)}, bf16[512,512]{1,0:T(8,128)(2,1)}, u32[]{:S(2)}) copy-start(bf16[512,512]{1,0:T(8,128)(2,1)} %convolution_convert_fusion.2.cells_ref) | copy-start | bytes 1572868
  114.8 1.0 copy-start.5
  117.2 20.5 %copy-start.2 = (bf16[512,512]{1,0:T(8,128)(2,1)S(1)}, bf16[512,512]{1,0:T(8,128)(2,1)}, u32[]{:S(2)}) copy-start(bf16[512,512]{1,0:T(8,128)(2,1)} %fusion.11.cells_ref) | copy-start | bytes 1572868

commit v10 on v8

--- a/solution.py
+++ b/solution.py
@@ -474,20 +474,24 @@
         .astype(jnp.bfloat16)
         .reshape(CZ, GY, GX, channels)
     )
-    pre_wide = padded_2(pre, ((SLAB, 0),), 1)
+    plane_rows = GY * GX
+    pre_wide = padded_2(pre, ((SLAB, 0),), CZ)
     pre_pad = jnp.pad(pre_wide, ((0, 0), (1, 1), (1, 1), (0, 0)))
-    mixed = depth_conv(pre_pad, w_depth, CZ).reshape(tok_rows, channels)
-    normal_cdf = 0.5 * (1.0 + lax.erf(mixed * ROOT_HALF))
-    normal_pdf = jnp.exp(-0.5 * mixed * mixed) * NORMAL_SCALE
-    activated = (mixed * normal_cdf).astype(jnp.bfloat16)
-    grad_act = jnp.einsum("td,cd->tc", grad_out, w_down, preferred_element_type=jnp.float32)
+    mixed_wide = depth_conv(pre_pad, w_depth, CZ + 2).reshape(-1, channels)
+    normal_cdf = 0.5 * (1.0 + lax.erf(mixed_wide * ROOT_HALF))
+    normal_pdf = jnp.exp(-0.5 * mixed_wide * mixed_wide) * NORMAL_SCALE
+    mixed = mixed_wide[plane_rows : plane_rows + tok_rows]
+    activated = (mixed * normal_cdf[plane_rows : plane_rows + tok_rows]).astype(jnp.bfloat16)
+    grad_out_wide = padded_2(grad_out, ((SLAB, 0),), plane_rows)
+    grad_act = jnp.einsum(
+        "td,cd->tc", grad_out_wide, w_down, preferred_element_type=jnp.float32
+    )
     grad_mixed = (
-        (grad_act * (normal_cdf + mixed * normal_pdf))
+        (grad_act * (normal_cdf + mixed_wide * normal_pdf))
         .astype(jnp.bfloat16)
-        .reshape(CZ, GY, GX, channels)
-    )
-    grad_wide = padded_2(grad_mixed, ((SLAB, 0),), 1)
-    grad_pad = jnp.pad(grad_wide, ((0, 0), (1, 1), (1, 1), (0, 0)))
+        .reshape(CZ + 2, GY, GX, channels)
+    )
+    grad_pad = jnp.pad(grad_mixed, ((0, 0), (1, 1), (1, 1), (0, 0)))
     grad_pre = (
         depth_conv(grad_pad, w_depth[::-1], CZ).astype(jnp.bfloat16).reshape(tok_rows, channels)
     )

time: 167 us -> 175 us (1.048)
  other arithmetic: 17.7 us -> 23.3 us
  starting transfers between devices: 11.7 us -> 13.5 us
    ppermute x2, waiting for transfers between devices: 20.1 us -> 3.49 us  [padded_2(): lax.ppermute(tail, axis, [(i, (i + 1) % count) for i in range(ends)])]
    ppermute x2, waiting for transfers between devices: 1.7 us -> 17.3 us  [padded_2(): lax.ppermute(head, axis, [((i + 1) % count, i) for i in range(ends)])]
    add x1, other arithmetic: 3.82 us -> 9.62 us  [depth_conv(): result = result + window.astype(jnp.float32) * weights[offset]]
    ppermute x2, starting transfers between devices: 5.67 us -> 9.51 us  [padded_2(): lax.ppermute(tail, axis, [(i, (i + 1) % count) for i in range(ends)])]
    ppermute x2, starting transfers between devices: 6.04 us -> 4 us  [padded_2(): lax.ppermute(head, axis, [((i + 1) % count, i) for i in range(ends)])]
  transfers between devices with their start and end apart: 4 -> 4, of which waited for: 4 -> 2; matrix products, arithmetic and copies ran while one was open for 0% -> 6% of each run, Pallas kernels for 0% -> 0%
where the time goes in v10:
time: 175 us; the launch traced here: 174 us
  Pallas kernels  100 us (57%)
  other arithmetic  23.3 us (13%)
  waiting for transfers between devices  20.8 us (12%)
  starting transfers between devices  13.5 us (8%)
  matrix products  8.6 us (5%)
  local copies, waits for them, and re-layouts  6.36 us (4%)
    pallas_call x1, Pallas kernels, slab_gather(): pl.pallas_call(functools.partial(gather_kernel, row_size), out_shape=jax....  43.8 us
    pallas_call x1, Pallas kernels, slab_scatter(): pl.pallas_call(functools.partial(scatter_kernel, row_size), out_shape=jax...  29.4 us
    pallas_call x1, Pallas kernels, head_sum(): pl.pallas_call(functools.partial(head_sum_kernel, count), out_shape=jax.S...  17.7 us
    ppermute x2, waiting for transfers between devices, padded_2(): lax.ppermute(head, axis, [((i + 1) % count, i) for i in range(ends)])  17.3 us
    add x1, other arithmetic, depth_conv(): result = result + window.astype(jnp.float32) * weights[offset]  9.62 us
    ppermute x2, starting transfers between devices, padded_2(): lax.ppermute(tail, axis, [(i, (i + 1) % count) for i in range(ends)])  9.51 us
    pallas_call x1, Pallas kernels, attention(): pl.pallas_call(functools.partial(attention_kernel, heads, q_tile), out_sh...  9.27 us
    convert_element_type x1, other arithmetic, per_device(): depth_conv(grad_pad, w_depth[::-1], CZ).astype(jnp.bfloat16)  4.71 us
  transfers between devices with their start and end apart: 4, of which 2 were waited for; matrix products, arithmetic and copies ran while one was open for 6% of the time, Pallas kernels for 0%

profile of v10, /device:TPU:2, one launch (start us, length us, event | category | flops | bytes accessed | tf_op | source)
XLA Modules:
  0.0 173.9 jit_solution(7513987212712546102)
XLA Ops:
  0.8 1.2 convert_reduce_fusion
  2.0 1.3 fusion.12
  3.3 1.3 fusion.14
  5.5 0.8 copy.25.q_ref
  7.2 3.2 %fusion.82 = (f32[64]{0:T(128)S(1)}, f32[64,512]{1,0:T(8,128)S(1)}) fusion(bf16[64,4096]{1,0:T(8,128)(2,1)S(1)} %reshape.623, bf16[4096,512]{1,0:T(8,128)(2,1)} %param.15), kind=kOutput, calls=%fused_computation.199 | convolution fusion | flops 268468160 | bytes 4849920 | tf_op jit(solution)/shard_map/dot_general | solution.py:446
  12.5 43.8 %shard_map.148.kv_ref = bf16[4096,256]{1,0:T(8,128)(2,1)} custom-call(bf16[64,256]{1,0:T(8,128)(2,1)} %pad_maximum_fusion.4.x_ref), custom_call_target="tpu_custom_call" | custom-call | tf_op jit(solution)/shard_map/pallas_call | solution.py:124
  56.3 9.3 %shard_map.149 = bf16[512,128]{1,0:T(8,128)(2,1)} custom-call(bf16[512,128]{1,0:T(8,128)(2,1)} %copy.25.q_ref, bf16[4096,256]{1,0:T(8,128)(2,1)} %shard_map.148.kv_ref), custom_call_target="tpu_custom_call" | custom-call | tf_op jit(solution)/shard_map/pallas_call | solution.py:328
  65.5 2.0 %convolution_convert_fusion.3 = bf16[512,512]{1,0:T(8,128)(2,1)} fusion(bf16[512,128]{1,0:T(8,128)(2,1)} %shard_map.149, bf16[128,512]{1,0:T(8,128)(2,1)S(1)} %copy-done.7), kind=kOutput, calls=%fused_computation.67 | convolution fusion | flops 67371008 | bytes 786432 | tf_op jit(solution)/shard_map/dot_general | solution.py:466
  67.6 17.7 %shard_map.150 = bf16[4,128,512]{2,1,0:T(8,128)(2,1)} custom-call(bf16[4,128,512]{2,1,0:T(8,128)(2,1)} %bitcast.80), custom_call_target="tpu_custom_call" | custom-call | tf_op jit(solution)/shard_map/pallas_call | solution.py:194
  85.3 1.3 fusion.46
  86.6 1.4 multiply_reduce_fusion
  88.6 2.1 %collective-permute-start.3 = (bf16[2,16,16,512]{3,2,1,0:T(8,128)(2,1)S(1)}, bf16[2,16,16,512]{3,2,1,0:T(8,128)(2,1)S(1)}, u32[]{:S(2)}, u32[]{:S(2)}) collective-permute-start(bf16[2,16,16,512]{3,2,1,0:T(8,128)(2,1)S(1)} %bitcast.75), channel_id=1, source_target_pairs={{4,0},{8,4},{12,8},{16,12},{20,16},{24,20},{28,24},{32,28},{36,32}... | collective-permute-start | bytes 1572872 | tf_op jit(solution)/shard_map/ppermute | solution.py:346
  90.7 4.7 %collective-permute-start.2 = (bf16[2,16,16,512]{3,2,1,0:T(8,128)(2,1)S(1)}, bf16[2,16,16,512]{3,2,1,0:T(8,128)(2,1)S(1)}, u32[]{:S(2)}, u32[]{:S(2)}) collective-permute-start(bf16[2,16,16,512]{3,2,1,0:T(8,128)(2,1)S(1)} %bitcast.76), channel_id=1, source_target_pairs={{0,4},{4,8},{8,12},{12,16},{16,20},{20,24},{24,28},{28,32},{32,36}... | collective-permute-start | bytes 1572872 | tf_op jit(solution)/shard_map/ppermute | solution.py:344
  95.4 1.9 %collective-permute-start.1 = (bf16[256,512]{1,0:T(8,128)(2,1)S(1)}, bf16[256,512]{1,0:T(8,128)(2,1)S(1)}, u32[]{:S(2)}, u32[]{:S(2)}) collective-permute-start(bf16[256,512]{1,0:T(8,128)(2,1)S(1)} %get-tuple-element.7), channel_id=1, source_target_pairs={{4,0},{8,4},{12,8},{16,12},{20,16},{24,20},{28,24},{32,28},{36,32}... | collective-permute-start | bytes 786440 | tf_op jit(solution)/shard_map/ppermute | solution.py:346
  97.3 4.8 %collective-permute-start = (bf16[256,512]{1,0:T(8,128)(2,1)S(1)}, bf16[256,512]{1,0:T(8,128)(2,1)S(1)}, u32[]{:S(2)}, u32[]{:S(2)}) collective-permute-start(bf16[256,512]{1,0:T(8,128)(2,1)S(1)} %get-tuple-element.6), channel_id=1, source_target_pairs={{0,4},{4,8},{8,12},{12,16},{16,20},{20,24},{24,28},{28,32},{32,36}... | collective-permute-start | bytes 786440 | tf_op jit(solution)/shard_map/ppermute | solution.py:344
  102.3 17.3 %collective-permute-done.3 = bf16[2,16,16,512]{3,2,1,0:T(8,128)(2,1)S(1)} collective-permute-done((bf16[2,16,16,512]{3,2,1,0:T(8,128)(2,1)S(1)}, bf16[2,16,16,512]{3,2,1,0:T(8,128)(2,1)S(1)}, u32[]{:S(2)}, u32[]{:S(2)}) %collective-permute-start.3) | collective-permute-done | bytes 524320 | tf_op jit(solution)/shard_map/ppermute | solution.py:346
  119.5 3.5 %collective-permute-done.2 = bf16[2,16,16,512]{3,2,1,0:T(8,128)(2,1)S(1)} collective-permute-done((bf16[2,16,16,512]{3,2,1,0:T(8,128)(2,1)S(1)}, bf16[2,16,16,512]{3,2,1,0:T(8,128)(2,1)S(1)}, u32[]{:S(2)}, u32[]{:S(2)}) %collective-permute-start.2) | collective-permute-done | bytes 524320 | tf_op jit(solution)/shard_map/ppermute | solution.py:344
  123.2 9.6 %multiply_add_fusion = f32[4,16,16,512]{3,2,1,0:T(8,128)S(1)} fusion(bf16[6,16,16,512]{3,2,1,0:T(8,128)(2,1)S(1)} %pad_maximum_fusion, bf16[2,16,16,512]{3,2,1,0:T(8,128)(2,1)S(1)} %bitcast.78, bf16[2,16,16,512]{3,2,1,0:T(8,128)(2,1)S(1)} %collective-permute-done.2, bf16[2,16,16,512]{3,2,1,0:T(8,128)(2,1)S(1)} %collective-permute-done.3, ...), kind=kLoop, calls=%fused_computation.59 | loop fusion | flops 45088768 | bytes 6346752 | tf_op jit(solution)/shard_map/add | solution.py:422
  134.0 1.0 fusion.5
  135.2 4.7 %fusion.26 = bf16[2,16,16,512]{3,2,1,0:T(8,128)(2,1)S(1)} fusion(bf16[2,16,16,512]{3,2,1,0:T(8,128)(2,1)S(1)} %bitcast.82, bf16[2,16,16,512]{3,2,1,0:T(8,128)(2,1)S(1)} %bitcast.83, bf16[2,16,16,512]{3,2,1,0:T(8,128)(2,1)S(1)} %bitcast.81, bf16[4,16,16,512]{3,2,1,0:T(8,128)(2,1)S(1)} %bitcast.74, f32[512]{0:T(512)S(1)} %bitcast.104, f32[512]{0:T(512)S(1)} %bitcast.88, ...), kind=kLoop, calls=%fused_computation.89 | loop fusion | flops 21233664 | bytes 3201024 | tf_op jit(solution)/shard_map/convert_element_type | solution.py:496
  141.2 1.2 convert_element_type.387.g_ref
  142.3 29.4 %shard_map.151 = f32[16,512]{1,0:T(8,128)} custom-call(bf16[64,16,512]{2,1,0:T(8,128)(2,1)} %convert_element_type.387.g_ref), custom_call_target="tpu_custom_call" | custom-call | tf_op jit(solution)/shard_map/pallas_call | solution.py:285
  171.7 0.8 reshape.631
  173.1 0.8 copy.30
  (71 shorter events, 7.7 us)
Async XLA Ops:
  0.6 133.3 %copy-start = (bf16[512,512]{1,0:T(8,128)(2,1)S(1)}, bf16[512,512]{1,0:T(8,128)(2,1)}, u32[]{:S(2)}) copy-start(bf16[512,512]{1,0:T(8,128)(2,1)} %param.24) | copy-start | bytes 1572868
  0.6 4.2 %copy-start.4 = (bf16[512,128]{1,0:T(8,128)(2,1)S(1)}, bf16[512,128]{1,0:T(8,128)(2,1)}, u32[]{:S(2)}) copy-start(bf16[512,128]{1,0:T(8,128)(2,1)} %param.17) | copy-start | bytes 393220
  7.1 3.4 %copy-start.6 = (bf16[512,128]{1,0:T(8,128)(2,1)S(1)}, bf16[512,128]{1,0:T(8,128)(2,1)}, u32[]{:S(2)}) copy-start(bf16[512,128]{1,0:T(8,128)(2,1)} %param.19) | copy-start | bytes 393220
  7.1 3.4 %copy-start.9 = (f32[512]{0:T(512)S(1)}, f32[512]{0:T(512)}, u32[]{:S(2)}) copy-start(f32[512]{0:T(512)} %param.16) | copy-start | bytes 6148
  7.1 3.7 %copy-start.5 = (bf16[512,128]{1,0:T(8,128)(2,1)S(1)}, bf16[512,128]{1,0:T(8,128)(2,1)}, u32[]{:S(2)}) copy-start(bf16[512,128]{1,0:T(8,128)(2,1)} %param.18) | copy-start | bytes 393220
  12.5 53.1 %copy-start.7 = (bf16[128,512]{1,0:T(8,128)(2,1)S(1)}, bf16[128,512]{1,0:T(8,128)(2,1)}, u32[]{:S(2)}) copy-start(bf16[128,512]{1,0:T(8,128)(2,1)} %param.20) | copy-start | bytes 393220
  56.2 29.0 %copy-start.1 = (bf16[512,512]{1,0:T(8,128)(2,1)S(1)}, bf16[512,512]{1,0:T(8,128)(2,1)}, u32[]{:S(2)}) copy-start(bf16[512,512]{1,0:T(8,128)(2,1)} %param.13) | copy-start | bytes 1572868
  65.5 22.5 %copy-start.10 = (bf16[512,512]{1,0:T(8,128)(2,1)S(1)}, bf16[512,512]{1,0:T(8,128)(2,1)}, u32[]{:S(2)}) copy-start(bf16[512,512]{1,0:T(8,128)(2,1)} %param.22) | copy-start | bytes 1572868
  65.5 22.5 %copy-start.11 = (f32[512]{0:T(512)S(1)}, f32[512]{0:T(512)}, u32[]{:S(2)}) copy-start(f32[512]{0:T(512)} %param.21) | copy-start | bytes 6148
  85.3 2.8 %copy-start.2 = (bf16[4,128,512]{2,1,0:T(8,128)(2,1)S(1)}, bf16[4,128,512]{2,1,0:T(8,128)(2,1)}, u32[]{:S(2)}) copy-start(bf16[4,128,512]{2,1,0:T(8,128)(2,1)} %shard_map.150) | copy-start | bytes 1572868
  86.6 8.7 %copy-start.3 = (bf16[512,512]{1,0:T(8,128)(2,1)S(1)}, bf16[512,512]{1,0:T(8,128)(2,1)}, u32[]{:S(2)}) copy-start(bf16[512,512]{1,0:T(8,128)(2,1)} %param.25) | copy-start | bytes 1572868
  88.0 14.2 %copy-start.8 = (f32[27,512]{1,0:T(8,128)S(1)}, f32[27,512]{1,0:T(8,128)}, u32[]{:S(2)}) copy-start(f32[27,512]{1,0:T(8,128)} %param.23) | copy-start | bytes 165892
  88.6 30.9 %collective-permute-start.3 = (bf16[2,16,16,512]{3,2,1,0:T(8,128)(2,1)S(1)}, bf16[2,16,16,512]{3,2,1,0:T(8,128)(2,1)S(1)}, u32[]{:S(2)}, u32[]{:S(2)}) collective-permute-start(bf16[2,16,16,512]{3,2,1,0:T(8,128)(2,1)S(1)} %bitcast.75), channel_id=1, source_target_pairs={{4,0},{8,4},{12,8},{16,12},{20,16},{24,20},{28,24},{32,28},{36,32}... | collective-permute-start | bytes 1572872 | tf_op jit(solution)/shard_map/ppermute | solution.py:346
  90.7 32.3 %collective-permute-start.2 = (bf16[2,16,16,512]{3,2,1,0:T(8,128)(2,1)S(1)}, bf16[2,16,16,512]{3,2,1,0:T(8,128)(2,1)S(1)}, u32[]{:S(2)}, u32[]{:S(2)}) collective-permute-start(bf16[2,16,16,512]{3,2,1,0:T(8,128)(2,1)S(1)} %bitcast.76), channel_id=1, source_target_pairs={{0,4},{4,8},{8,12},{12,16},{16,20},{20,24},{24,28},{28,32},{32,36}... | collective-permute-start | bytes 1572872 | tf_op jit(solution)/shard_map/ppermute | solution.py:344
  95.4 38.6 %collective-permute-start.1 = (bf16[256,512]{1,0:T(8,128)(2,1)S(1)}, bf16[256,512]{1,0:T(8,128)(2,1)S(1)}, u32[]{:S(2)}, u32[]{:S(2)}) collective-permute-start(bf16[256,512]{1,0:T(8,128)(2,1)S(1)} %get-tuple-element.7), channel_id=1, source_target_pairs={{4,0},{8,4},{12,8},{16,12},{20,16},{24,20},{28,24},{32,28},{36,32}... | collective-permute-start | bytes 786440 | tf_op jit(solution)/shard_map/ppermute | solution.py:346
  97.3 36.6 %collective-permute-start = (bf16[256,512]{1,0:T(8,128)(2,1)S(1)}, bf16[256,512]{1,0:T(8,128)(2,1)S(1)}, u32[]{:S(2)}, u32[]{:S(2)}) collective-permute-start(bf16[256,512]{1,0:T(8,128)(2,1)S(1)} %get-tuple-element.6), channel_id=1, source_target_pairs={{0,4},{4,8},{8,12},{12,16},{16,20},{20,24},{24,28},{28,32},{32,36}... | collective-permute-start | bytes 786440 | tf_op jit(solution)/shard_map/ppermute | solution.py:344

commit v11 on v8

--- a/solution.py
+++ b/solution.py
@@ -31,12 +31,17 @@
 
 
 def gather_kernel(
-    row_size, x_ref, out_ref, send_a, recv_a, send_b, recv_b, send_c, recv_c, local_sem
+    row_size, x_ref, out_ref, send_a, recv_a, send_l, recv_l, send_r, recv_r, send_f, recv_f,
+    local_sem,
 ):
     me = lax.axis_index(SLAB)
     block = x_ref.shape[0]
     own_y, spot = me // row_size, me % row_size
     y_count = lax.psum(1, "y")
+    half = row_size // 2
+    left_y = lax.rem(own_y + y_count - 1, y_count)
+    right_y = lax.rem(own_y + 1, y_count)
+    far_y = lax.rem(own_y + 2, y_count)
     barrier = pltpu.get_barrier_semaphore()
 
     def greet(k, carry):
@@ -45,76 +50,105 @@
         return carry
 
     lax.fori_loop(1, row_size, greet, 0)
-    left_y = lax.rem(own_y + y_count - 1, y_count)
-    right_y = lax.rem(own_y + 1, y_count)
     for other_y in (left_y, right_y):
         peer = other_y * row_size + spot
         pl.semaphore_signal(barrier, inc=1, device_id=peer_id(peer), device_id_type=MESH)
     pl.semaphore_wait(barrier, row_size + 1)
 
+    def piece(row_y, index):
+        return out_ref.at[pl.ds((row_y * row_size + index) * block, block)]
+
     def along_row(target, source):
         return pltpu.make_async_remote_copy(
             src_ref=x_ref,
-            dst_ref=out_ref.at[pl.ds((own_y * row_size + source) * block, block)],
+            dst_ref=piece(own_y, source),
             send_sem=send_a.at[target],
             recv_sem=recv_a.at[source],
             device_id=peer_id(own_y * row_size + target),
             device_id_type=MESH,
         )
 
+    def sideways(target_y, row_y, index, send_sem, recv_sem):
+        return pltpu.make_async_remote_copy(
+            src_ref=piece(row_y, index),
+            dst_ref=piece(row_y, index),
+            send_sem=send_sem.at[index],
+            recv_sem=recv_sem.at[index],
+            device_id=peer_id(target_y * row_size + spot),
+            device_id_type=MESH,
+        )
+
+    def to_left(row_y, index):
+        return sideways(left_y, row_y, index, send_l, recv_r)
+
+    def to_right(row_y, index):
+        return sideways(right_y, row_y, index, send_r, recv_l)
+
     def start_row(k, carry):
         along_row(lax.rem(spot + k, row_size), spot).start()
         return carry
 
     lax.fori_loop(1, row_size, start_row, 0)
-    local = pltpu.make_async_copy(x_ref, out_ref.at[pl.ds(me * block, block)], local_sem)
+    local = pltpu.make_async_copy(x_ref, piece(own_y, spot), local_sem)
     local.start()
     local.wait()
+    to_left(own_y, spot).start()
+    to_right(own_y, spot).start()
+
+    def pass_row(k, carry):
+        other = lax.rem(spot + k, row_size)
+        along_row(other, other).wait_recv()
+        to_left(own_y, other).start()
+        to_right(own_y, other).start()
+        return carry
+
+    lax.fori_loop(1, row_size, pass_row, 0)
+
+    def from_left(index):
+        return sideways(right_y, left_y, index, send_f, recv_f)
+
+    def from_right(index):
+        return sideways(left_y, right_y, index, send_f, recv_f)
+
+    def pass_low(index, carry):
+        to_right(left_y, index).wait_recv()
+        from_left(index).start()
+        to_left(right_y, index).wait_recv()
+        return carry
+
+    def pass_high(index, carry):
+        to_left(right_y, index).wait_recv()
+        from_right(index).start()
+        to_right(left_y, index).wait_recv()
+        return carry
+
+    lax.fori_loop(0, half, pass_low, 0)
+    lax.fori_loop(half, row_size, pass_high, 0)
+
+    def finish(index, carry):
+        sideways(left_y, far_y, index, send_f, recv_f).wait_recv()
+        to_left(own_y, index).wait_send()
+        to_right(own_y, index).wait_send()
+        return carry
+
+    lax.fori_loop(0, row_size, finish, 0)
 
     def finish_row(k, carry):
-        other = lax.rem(spot + k, row_size)
-        along_row(other, spot).wait_send()
-        along_row(other, other).wait_recv()
+        along_row(lax.rem(spot + k, row_size), spot).wait_send()
         return carry
 
     lax.fori_loop(1, row_size, finish_row, 0)
-    row_rows = row_size * block
-
-    def across(target_y, source_y):
-        return pltpu.make_async_remote_copy(
-            src_ref=out_ref.at[pl.ds(source_y * row_rows, row_rows)],
-            dst_ref=out_ref.at[pl.ds(source_y * row_rows, row_rows)],
-            send_sem=send_b.at[target_y],
-            recv_sem=recv_b.at[source_y],
-            device_id=peer_id(target_y * row_size + spot),
-            device_id_type=MESH,
-        )
-
-    for other_y in (left_y, right_y):
-        across(other_y, own_y).start()
-    for other_y in (left_y, right_y):
-        across(other_y, own_y).wait_send()
-        across(other_y, other_y).wait_recv()
-    half = row_rows // 2
-
-    def forward(target_y, source_y, part):
-        rows = pl.ds(source_y * row_rows + part * half, half)
-        return pltpu.make_async_remote_copy(
-            src_ref=out_ref.at[rows],
-            dst_ref=out_ref.at[rows],
-            send_sem=send_c.at[part],
-            recv_sem=recv_c.at[part],
-            device_id=peer_id(target_y * row_size + spot),
-            device_id_type=MESH,
-        )
-
-    far_y = lax.rem(own_y + 2, y_count)
-    forward(right_y, left_y, 0).start()
-    forward(left_y, right_y, 1).start()
-    forward(right_y, left_y, 0).wait_send()
-    forward(left_y, right_y, 1).wait_send()
-    forward(right_y, far_y, 0).wait_recv()
-    forward(left_y, far_y, 1).wait_recv()
+
+    def finish_low(index, carry):
+        from_left(index).wait_send()
+        return carry
+
+    def finish_high(index, carry):
+        from_right(index).wait_send()
+        return carry
+
+    lax.fori_loop(0, half, finish_low, 0)
+    lax.fori_loop(half, row_size, finish_high, 0)
 
 
 def slab_gather(x, count, row_size):
@@ -126,15 +160,8 @@
         out_shape=jax.ShapeDtypeStruct((count * rows, width), x.dtype),
         in_specs=[pl.BlockSpec(memory_space=pltpu.VMEM)],
         out_specs=pl.BlockSpec(memory_space=pltpu.VMEM),
-        scratch_shapes=[
-            pltpu.SemaphoreType.DMA((row_size,)),
-            pltpu.SemaphoreType.DMA((row_size,)),
-            pltpu.SemaphoreType.DMA((y_count,)),
-            pltpu.SemaphoreType.DMA((y_count,)),
-            pltpu.SemaphoreType.DMA((2,)),
-            pltpu.SemaphoreType.DMA((2,)),
-            pltpu.SemaphoreType.DMA(()),
-        ],
+        scratch_shapes=[pltpu.SemaphoreType.DMA((row_size,))] * 8
+        + [pltpu.SemaphoreType.DMA(())],
         compiler_params=pltpu.CompilerParams(collective_id=0, has_side_effects=True),
     )(x)
 

time: 167 us -> 168 us (level)
  transfers between devices with their start and end apart: 4 -> 4, of which waited for: 4 -> 3; matrix products, arithmetic and copies ran while one was open for 0% -> 0% of each run, Pallas kernels for 0% -> 0%
where the time goes in v11:
time: 168 us; the launch traced here: 167 us
  Pallas kernels  100 us (60%)
  waiting for transfers between devices  21.2 us (13%)
  other arithmetic  17.7 us (11%)
  starting transfers between devices  11.7 us (7%)
  matrix products  8.13 us (5%)
  local copies, waits for them, and re-layouts  6.95 us (4%)
    pallas_call x1, Pallas kernels, slab_gather(): pl.pallas_call(functools.partial(gather_kernel, row_size), out_shape=jax....  44 us
    pallas_call x1, Pallas kernels, slab_scatter(): pl.pallas_call(functools.partial(scatter_kernel, row_size), out_shape=jax...  29.3 us
    ppermute x2, waiting for transfers between devices, padded_2(): lax.ppermute(tail, axis, [(i, (i + 1) % count) for i in range(ends)])  20 us
    pallas_call x1, Pallas kernels, head_sum(): pl.pallas_call(functools.partial(head_sum_kernel, count), out_shape=jax.S...  17.7 us
    pallas_call x1, Pallas kernels, attention(): pl.pallas_call(functools.partial(attention_kernel, heads, q_tile), out_sh...  9.26 us
    ppermute x2, starting transfers between devices, padded_2(): lax.ppermute(head, axis, [((i + 1) % count, i) for i in range(ends)])  6.72 us
    ppermute x2, starting transfers between devices, padded_2(): lax.ppermute(tail, axis, [(i, (i + 1) % count) for i in range(ends)])  4.99 us
    convert_element_type x1, other arithmetic, per_device(): depth_conv(grad_pad, w_depth[::-1], CZ).astype(jnp.bfloat16)  3.84 us
  transfers between devices with their start and end apart: 4, of which 3 were waited for; matrix products, arithmetic and copies ran while one was open for 0% of the time, Pallas kernels for 0%

profile of v11, /device:TPU:2, one launch (start us, length us, event | category | flops | bytes accessed | tf_op | source)
XLA Modules:
  0.0 167.1 jit_solution(6818756977219714175)
XLA Ops:
  1.1 1.2 convert_reduce_fusion
  2.3 1.3 fusion.15
  3.6 1.3 fusion.17
  6.0 3.2 %fusion.63 = (f32[64]{0:T(128)S(1)}, f32[64,512]{1,0:T(8,128)S(1)}) fusion(bf16[64,4096]{1,0:T(8,128)(2,1)S(1)} %reshape.617, bf16[4096,512]{1,0:T(8,128)(2,1)} %param.15), kind=kOutput, calls=%fused_computation.139 | convolution fusion | flops 268468160 | bytes 4849920 | tf_op jit(solution)/shard_map/dot_general | solution.py:473
  11.0 44.0 %shard_map.148.kv_ref = bf16[4096,256]{1,0:T(8,128)(2,1)} custom-call(bf16[64,256]{1,0:T(8,128)(2,1)} %pad_maximum_fusion.7.x_ref), custom_call_target="tpu_custom_call" | custom-call | tf_op jit(solution)/shard_map/pallas_call | solution.py:158
  56.4 9.3 %shard_map.149 = bf16[512,128]{1,0:T(8,128)(2,1)} custom-call(bf16[512,128]{1,0:T(8,128)(2,1)} %copy.25.q_ref, bf16[4096,256]{1,0:T(8,128)(2,1)} %shard_map.148.kv_ref), custom_call_target="tpu_custom_call" | custom-call | tf_op jit(solution)/shard_map/pallas_call | solution.py:355
  65.7 2.0 %convolution_convert_fusion.3 = bf16[512,512]{1,0:T(8,128)(2,1)} fusion(bf16[512,128]{1,0:T(8,128)(2,1)} %shard_map.149, bf16[128,512]{1,0:T(8,128)(2,1)S(1)} %copy-done.7), kind=kOutput, calls=%fused_computation.26 | convolution fusion | flops 67371008 | bytes 786432 | tf_op jit(solution)/shard_map/dot_general | solution.py:493
  67.7 17.7 %shard_map.150 = bf16[4,128,512]{2,1,0:T(8,128)(2,1)} custom-call(bf16[4,128,512]{2,1,0:T(8,128)(2,1)} %bitcast.80), custom_call_target="tpu_custom_call" | custom-call | tf_op jit(solution)/shard_map/pallas_call | solution.py:221
  85.5 1.3 fusion.27
  86.8 1.3 multiply_reduce_fusion
  88.8 1.9 %collective-permute-start = (bf16[1,16,16,512]{3,2,1,0:T(8,128)(2,1)S(1)}, bf16[1,16,16,512]{3,2,1,0:T(8,128)(2,1)S(1)}, u32[]{:S(2)}, u32[]{:S(2)}) collective-permute-start(bf16[1,16,16,512]{3,2,1,0:T(8,128)(2,1)S(1)} %bitcast.85), channel_id=1, source_target_pairs={{0,4},{4,8},{8,12},{12,16},{16,20},{20,24},{24,28},{28,32},{32,36}... | collective-permute-start | bytes 786440 | tf_op jit(solution)/shard_map/ppermute | solution.py:371
  90.7 3.9 %collective-permute-start.1 = (bf16[1,16,16,512]{3,2,1,0:T(8,128)(2,1)S(1)}, bf16[1,16,16,512]{3,2,1,0:T(8,128)(2,1)S(1)}, u32[]{:S(2)}, u32[]{:S(2)}) collective-permute-start(bf16[1,16,16,512]{3,2,1,0:T(8,128)(2,1)S(1)} %bitcast.84), channel_id=1, source_target_pairs={{4,0},{8,4},{12,8},{16,12},{20,16},{24,20},{28,24},{32,28},{36,32}... | collective-permute-start | bytes 786440 | tf_op jit(solution)/shard_map/ppermute | solution.py:373
  94.7 10.5 %collective-permute-done = bf16[1,16,16,512]{3,2,1,0:T(8,128)(2,1)S(1)} collective-permute-done((bf16[1,16,16,512]{3,2,1,0:T(8,128)(2,1)S(1)}, bf16[1,16,16,512]{3,2,1,0:T(8,128)(2,1)S(1)}, u32[]{:S(2)}, u32[]{:S(2)}) %collective-permute-start) | collective-permute-done | bytes 262176 | tf_op jit(solution)/shard_map/ppermute | solution.py:371
  106.0 3.8 %multiply_add_fusion = f32[2,16,16,512]{3,2,1,0:T(8,128)S(1)} fusion(bf16[2,16,16,512]{3,2,1,0:T(8,128)(2,1)S(1)} %bitcast.78, bf16[4,18,18,512]{3,2,1,0:T(8,128)(2,1)S(1)} %fusion.10, bf16[1,16,16,512]{3,2,1,0:T(8,128)(2,1)S(1)} %collective-permute-done.1, bf16[1,16,16,512]{3,2,1,0:T(8,128)(2,1)S(1)} %collective-permute-done, f32[512]{0:T(512)S(1)} %bitcast.100, ...), kind=kLoop, calls=%fused_computation.46 | loop fusion | flops 21495808 | bytes 14735360 | tf_op jit(solution)/shard_map/add | solution.py:449
  110.1 0.8 copy-done.3
  111.5 3.1 %collective-permute-start.2 = (bf16[1,16,16,512]{3,2,1,0:T(8,128)(2,1)S(1)}, bf16[1,16,16,512]{3,2,1,0:T(8,128)(2,1)S(1)}, u32[]{:S(2)}, u32[]{:S(2)}) collective-permute-start(bf16[1,16,16,512]{3,2,1,0:T(8,128)(2,1)S(1)} %bitcast.87), channel_id=1, source_target_pairs={{0,4},{4,8},{8,12},{12,16},{16,20},{20,24},{24,28},{28,32},{32,36}... | collective-permute-start | bytes 786440 | tf_op jit(solution)/shard_map/ppermute | solution.py:371
  114.5 2.8 %collective-permute-start.3 = (bf16[1,16,16,512]{3,2,1,0:T(8,128)(2,1)S(1)}, bf16[1,16,16,512]{3,2,1,0:T(8,128)(2,1)S(1)}, u32[]{:S(2)}, u32[]{:S(2)}) collective-permute-start(bf16[1,16,16,512]{3,2,1,0:T(8,128)(2,1)S(1)} %bitcast.86), channel_id=1, source_target_pairs={{4,0},{8,4},{12,8},{16,12},{20,16},{24,20},{28,24},{32,28},{36,32}... | collective-permute-start | bytes 786440 | tf_op jit(solution)/shard_map/ppermute | solution.py:373
  117.8 9.5 %collective-permute-done.2 = bf16[1,16,16,512]{3,2,1,0:T(8,128)(2,1)S(1)} collective-permute-done((bf16[1,16,16,512]{3,2,1,0:T(8,128)(2,1)S(1)}, bf16[1,16,16,512]{3,2,1,0:T(8,128)(2,1)S(1)}, u32[]{:S(2)}, u32[]{:S(2)}) %collective-permute-start.2) | collective-permute-done | bytes 262176 | tf_op jit(solution)/shard_map/ppermute | solution.py:371
  127.3 1.2 collective-permute-done.3
  129.3 3.8 %add_convert_fusion = bf16[2,16,16,512]{3,2,1,0:T(8,128)(2,1)S(1)} fusion(bf16[2,16,16,512]{3,2,1,0:T(8,128)(2,1)S(1)} %bitcast.73, bf16[4,18,18,512]{3,2,1,0:T(8,128)(2,1)S(1)} %select_maximum_fusion, bf16[1,16,16,512]{3,2,1,0:T(8,128)(2,1)S(1)} %collective-permute-done.3, bf16[1,16,16,512]{3,2,1,0:T(8,128)(2,1)S(1)} %collective-permute-done.2, ...), kind=kLoop, calls=%fused_computation.45 | loop fusion | flops 21757952 | bytes 14211072 | tf_op jit(solution)/shard_map/convert_element_type | solution.py:519
  134.4 1.2 convert_element_type.374.g_ref
  135.6 29.3 %shard_map.151 = f32[16,512]{1,0:T(8,128)} custom-call(bf16[64,16,512]{2,1,0:T(8,128)(2,1)} %convert_element_type.374.g_ref), custom_call_target="tpu_custom_call" | custom-call | tf_op jit(solution)/shard_map/pallas_call | solution.py:312
  164.9 0.8 reshape.625
  166.3 0.8 copy.30
  (70 shorter events, 9.9 us)
Async XLA Ops:
  0.6 109.4 %copy-start = (bf16[512,512]{1,0:T(8,128)(2,1)S(1)}, bf16[512,512]{1,0:T(8,128)(2,1)}, u32[]{:S(2)}) copy-start(bf16[512,512]{1,0:T(8,128)(2,1)} %param.25) | copy-start | bytes 1572868
  5.9 3.5 %copy-start.5 = (bf16[512,128]{1,0:T(8,128)(2,1)S(1)}, bf16[512,128]{1,0:T(8,128)(2,1)}, u32[]{:S(2)}) copy-start(bf16[512,128]{1,0:T(8,128)(2,1)} %param.18) | copy-start | bytes 393220
  5.9 3.5 %copy-start.9 = (f32[512]{0:T(512)S(1)}, f32[512]{0:T(512)}, u32[]{:S(2)}) copy-start(f32[512]{0:T(512)} %param.16) | copy-start | bytes 6148
  6.0 4.2 %copy-start.6 = (bf16[512,128]{1,0:T(8,128)(2,1)S(1)}, bf16[512,128]{1,0:T(8,128)(2,1)}, u32[]{:S(2)}) copy-start(bf16[512,128]{1,0:T(8,128)(2,1)} %param.19) | copy-start | bytes 393220
  9.2 45.8 %copy-start.4 = (bf16[512,128]{1,0:T(8,128)(2,1)S(1)}, bf16[512,128]{1,0:T(8,128)(2,1)}, u32[]{:S(2)}) copy-start(bf16[512,128]{1,0:T(8,128)(2,1)} %param.17) | copy-start | bytes 393220
  55.0 10.7 %copy-start.7 = (bf16[128,512]{1,0:T(8,128)(2,1)S(1)}, bf16[128,512]{1,0:T(8,128)(2,1)}, u32[]{:S(2)}) copy-start(bf16[128,512]{1,0:T(8,128)(2,1)} %param.20) | copy-start | bytes 393220
  56.4 29.0 %copy-start.1 = (bf16[512,512]{1,0:T(8,128)(2,1)S(1)}, bf16[512,512]{1,0:T(8,128)(2,1)}, u32[]{:S(2)}) copy-start(bf16[512,512]{1,0:T(8,128)(2,1)} %param.13) | copy-start | bytes 1572868
  65.7 22.5 %copy-start.10 = (bf16[512,512]{1,0:T(8,128)(2,1)S(1)}, bf16[512,512]{1,0:T(8,128)(2,1)}, u32[]{:S(2)}) copy-start(bf16[512,512]{1,0:T(8,128)(2,1)} %param.22) | copy-start | bytes 1572868
  65.7 22.5 %copy-start.11 = (f32[512]{0:T(512)S(1)}, f32[512]{0:T(512)}, u32[]{:S(2)}) copy-start(f32[512]{0:T(512)} %param.21) | copy-start | bytes 6148
  85.5 2.7 %copy-start.2 = (bf16[4,128,512]{2,1,0:T(8,128)(2,1)S(1)}, bf16[4,128,512]{2,1,0:T(8,128)(2,1)}, u32[]{:S(2)}) copy-start(bf16[4,128,512]{2,1,0:T(8,128)(2,1)} %shard_map.150) | copy-start | bytes 1572868
  88.1 6.5 %copy-start.8 = (f32[27,512]{1,0:T(8,128)S(1)}, f32[27,512]{1,0:T(8,128)}, u32[]{:S(2)}) copy-start(f32[27,512]{1,0:T(8,128)} %param.23) | copy-start | bytes 165892
  88.8 16.4 %collective-permute-start = (bf16[1,16,16,512]{3,2,1,0:T(8,128)(2,1)S(1)}, bf16[1,16,16,512]{3,2,1,0:T(8,128)(2,1)S(1)}, u32[]{:S(2)}, u32[]{:S(2)}) collective-permute-start(bf16[1,16,16,512]{3,2,1,0:T(8,128)(2,1)S(1)} %bitcast.85), channel_id=1, source_target_pairs={{0,4},{4,8},{8,12},{12,16},{16,20},{20,24},{24,28},{28,32},{32,36}... | collective-permute-start | bytes 786440 | tf_op jit(solution)/shard_map/ppermute | solution.py:371
  90.7 14.5 %collective-permute-start.1 = (bf16[1,16,16,512]{3,2,1,0:T(8,128)(2,1)S(1)}, bf16[1,16,16,512]{3,2,1,0:T(8,128)(2,1)S(1)}, u32[]{:S(2)}, u32[]{:S(2)}) collective-permute-start(bf16[1,16,16,512]{3,2,1,0:T(8,128)(2,1)S(1)} %bitcast.84), channel_id=1, source_target_pairs={{4,0},{8,4},{12,8},{16,12},{20,16},{24,20},{28,24},{32,28},{36,32}... | collective-permute-start | bytes 786440 | tf_op jit(solution)/shard_map/ppermute | solution.py:373
  109.8 1.0 copy-start.3
  111.5 15.8 %collective-permute-start.2 = (bf16[1,16,16,512]{3,2,1,0:T(8,128)(2,1)S(1)}, bf16[1,16,16,512]{3,2,1,0:T(8,128)(2,1)S(1)}, u32[]{:S(2)}, u32[]{:S(2)}) collective-permute-start(bf16[1,16,16,512]{3,2,1,0:T(8,128)(2,1)S(1)} %bitcast.87), channel_id=1, source_target_pairs={{0,4},{4,8},{8,12},{12,16},{16,20},{20,24},{24,28},{28,32},{32,36}... | collective-permute-start | bytes 786440 | tf_op jit(solution)/shard_map/ppermute | solution.py:371
  114.5 14.0 %collective-permute-start.3 = (bf16[1,16,16,512]{3,2,1,0:T(8,128)(2,1)S(1)}, bf16[1,16,16,512]{3,2,1,0:T(8,128)(2,1)S(1)}, u32[]{:S(2)}, u32[]{:S(2)}) collective-permute-start(bf16[1,16,16,512]{3,2,1,0:T(8,128)(2,1)S(1)} %bitcast.86), channel_id=1, source_target_pairs={{4,0},{8,4},{12,8},{16,12},{20,16},{24,20},{28,24},{32,28},{36,32}... | collective-permute-start | bytes 786440 | tf_op jit(solution)/shard_map/ppermute | solution.py:373

commit v12 on v8

--- a/solution.py
+++ b/solution.py
@@ -30,8 +30,43 @@
     return (p // 16, p // 2 % 8, p % 2, lax.axis_index("xh"), lax.axis_index("core"))
 
 
+def attend_rows(kv_ref, q_ref, top_ref, total_ref, acc_ref, first_row, row_rows, first):
+    heads, q_rows, _ = top_ref.shape
+    q_tile = q_rows // 2
+    key_width = heads * HEAD
+    score_scale = HEAD ** (-0.5)
+    rows = pl.ds(pl.multiple_of(first_row, row_rows), row_rows)
+    for head in range(heads):
+        keys = kv_ref[rows, head * HEAD : (head + 1) * HEAD]
+        values = kv_ref[rows, key_width + head * HEAD : key_width + (head + 1) * HEAD]
+        for start in range(0, q_rows, q_tile):
+            tile = slice(start, start + q_tile)
+            columns = slice(head * HEAD, (head + 1) * HEAD)
+            scores = lax.dot_general(
+                q_ref[tile, columns], keys, (((1,), (1,)), ((), ())),
+                preferred_element_type=jnp.float32,
+            ) * score_scale
+            top = jnp.max(scores, axis=1, keepdims=True)
+            if not first:
+                old_top = top_ref[head, tile]
+                top = jnp.maximum(top, old_top)
+                rescale = jnp.exp(old_top - top)
+            weights = jnp.exp(scores - top)
+            row_sum = jnp.sum(weights, axis=1, keepdims=True)
+            mixed = jnp.dot(
+                weights.astype(jnp.bfloat16), values, preferred_element_type=jnp.float32
+            )
+            if not first:
+                row_sum = row_sum + rescale * total_ref[head, tile]
+                mixed = mixed + rescale * acc_ref[tile, columns]
+            top_ref[head, tile] = top
+            total_ref[head, tile] = row_sum
+            acc_ref[tile, columns] = mixed
+
+
 def gather_kernel(
-    row_size, x_ref, out_ref, send_a, recv_a, send_b, recv_b, send_c, recv_c, local_sem
+    row_size, x_ref, q_ref, heads_ref, out_ref, top_ref, total_ref, acc_ref,
+    send_a, recv_a, send_b, recv_b, send_c, recv_c, local_sem,
 ):
     me = lax.axis_index(SLAB)
     block = x_ref.shape[0]
@@ -92,6 +127,10 @@
 
     for other_y in (left_y, right_y):
         across(other_y, own_y).start()
+    attend = functools.partial(
+        attend_rows, out_ref, q_ref, top_ref, total_ref, acc_ref, row_rows=row_rows
+    )
+    attend(own_y * row_rows, first=True)
     for other_y in (left_y, right_y):
         across(other_y, own_y).wait_send()
         across(other_y, other_y).wait_recv()
@@ -111,22 +150,34 @@
     far_y = lax.rem(own_y + 2, y_count)
     forward(right_y, left_y, 0).start()
     forward(left_y, right_y, 1).start()
+    attend(left_y * row_rows, first=False)
+    attend(right_y * row_rows, first=False)
     forward(right_y, left_y, 0).wait_send()
     forward(left_y, right_y, 1).wait_send()
     forward(right_y, far_y, 0).wait_recv()
     forward(left_y, far_y, 1).wait_recv()
-
-
-def slab_gather(x, count, row_size):
+    attend(far_y * row_rows, first=False)
+    heads = top_ref.shape[0]
+    for head in range(heads):
+        columns = slice(head * HEAD, (head + 1) * HEAD)
+        heads_ref[:, columns] = (acc_ref[:, columns] / total_ref[head]).astype(heads_ref.dtype)
+
+
+def gather_attend(x, queries, count, row_size, heads):
     rows, width = x.shape
+    q_rows = queries.shape[0]
     y_count = count // row_size
     assert y_count == 4
     return pl.pallas_call(
         functools.partial(gather_kernel, row_size),
-        out_shape=jax.ShapeDtypeStruct((count * rows, width), x.dtype),
-        in_specs=[pl.BlockSpec(memory_space=pltpu.VMEM)],
+        out_shape=jax.ShapeDtypeStruct(queries.shape, jnp.bfloat16),
+        in_specs=[pl.BlockSpec(memory_space=pltpu.VMEM)] * 2,
         out_specs=pl.BlockSpec(memory_space=pltpu.VMEM),
         scratch_shapes=[
+            pltpu.VMEM((count * rows, width), x.dtype),
+            pltpu.VMEM((heads, q_rows, 1), jnp.float32),
+            pltpu.VMEM((heads, q_rows, 1), jnp.float32),
+            pltpu.VMEM(queries.shape, jnp.float32),
             pltpu.SemaphoreType.DMA((row_size,)),
             pltpu.SemaphoreType.DMA((row_size,)),
             pltpu.SemaphoreType.DMA((y_count,)),
@@ -136,7 +187,7 @@
             pltpu.SemaphoreType.DMA(()),
         ],
         compiler_params=pltpu.CompilerParams(collective_id=0, has_side_effects=True),
-    )(x)
+    )(x, queries)
 
 
 def head_peer(q):
@@ -300,37 +351,6 @@
         compiler_params=pltpu.CompilerParams(collective_id=1, has_side_effects=True),
     )(g)
     return summed.reshape(rows, width)
-
-
-def attention_kernel(heads, q_tile, q_ref, kv_ref, out_ref):
-    key_width = heads * HEAD
-    score_scale = HEAD ** (-0.5)
-    for head in range(heads):
-        keys = kv_ref[:, head * HEAD : (head + 1) * HEAD]
-        values = kv_ref[:, key_width + head * HEAD : key_width + (head + 1) * HEAD]
-        for first in range(0, q_ref.shape[0], q_tile):
-            queries = q_ref[first : first + q_tile, head * HEAD : (head + 1) * HEAD]
-            scores = lax.dot_general(
-                queries, keys, (((1,), (1,)), ((), ())), preferred_element_type=jnp.float32
-            ) * score_scale
-            top = jnp.max(scores, axis=1, keepdims=True)
-            weights = jnp.exp(scores - top)
-            row_sum = jnp.sum(weights, axis=1, keepdims=True)
-            mixed = jnp.dot(
-                weights.astype(jnp.bfloat16), values, preferred_element_type=jnp.float32
-            )
-            out_ref[first : first + q_tile, head * HEAD : (head + 1) * HEAD] = (
-                mixed / row_sum
-            ).astype(out_ref.dtype)
-
-
-def attention(queries, kv, heads, q_tile=256):
-    return pl.pallas_call(
-        functools.partial(attention_kernel, heads, q_tile),
-        out_shape=jax.ShapeDtypeStruct(queries.shape, jnp.bfloat16),
-        in_specs=[pl.BlockSpec(memory_space=pltpu.VMEM)] * 2,
-        out_specs=pl.BlockSpec(memory_space=pltpu.VMEM),
-    )(queries, kv)
 
 
 def padded_2(cells, sides, width):
@@ -461,8 +481,13 @@
     )
     key_width = heads_dev * HEAD
     pieces = jnp.concatenate([own_keys.reshape(local_rows, key_width), own_values], axis=1)
-    pieces = slab_gather(pieces, lax.psum(1, SLAB), lax.psum(1, ("z", "xl")))
-    heads_out = attention(queries.reshape(tok_rows, key_width), pieces, heads_dev)
+    heads_out = gather_attend(
+        pieces,
+        queries.reshape(tok_rows, key_width),
+        lax.psum(1, SLAB),
+        lax.psum(1, ("z", "xl")),
+        heads_dev,
+    )
     partial_value = jnp.dot(heads_out, w_out, preferred_element_type=jnp.float32)
     head_total = head_sum(partial_value, lax.psum(1, FFN)).astype(jnp.float32)
     attended = head_total.astype(jnp.bfloat16)

time: 167 us -> 163 us (0.976)
  Pallas kernels: 98.8 us -> 92.3 us
  local copies, waits for them, and re-layouts: 6.95 us -> 8.77 us
    pallas_call x2 -> x1, Pallas kernels: 53 us -> 46.4 us  [gather_attend(): pl.pallas_call(functools.partial(gather_kernel, row_size), out_shape=jax....]
where the time goes in v12:
time: 163 us; the launch traced here: 161 us
  Pallas kernels  92.3 us (57%)
  waiting for transfers between devices  21.8 us (13%)
  other arithmetic  17.7 us (11%)
  starting transfers between devices  11.7 us (7%)
  local copies, waits for them, and re-layouts  8.77 us (5%)
  matrix products  8.09 us (5%)
    pallas_call x1, Pallas kernels, gather_attend(): pl.pallas_call(functools.partial(gather_kernel, row_size), out_shape=jax....  46.4 us
    pallas_call x1, Pallas kernels, slab_scatter(): pl.pallas_call(functools.partial(scatter_kernel, row_size), out_shape=jax...  28.1 us
    ppermute x2, waiting for transfers between devices, padded_2(): lax.ppermute(tail, axis, [(i, (i + 1) % count) for i in range(ends)])  20.1 us
    pallas_call x1, Pallas kernels, head_sum(): pl.pallas_call(functools.partial(head_sum_kernel, count), out_shape=jax.S...  17.7 us
    ppermute x2, starting transfers between devices, padded_2(): lax.ppermute(head, axis, [((i + 1) % count, i) for i in range(ends)])  6.04 us
    ppermute x2, starting transfers between devices, padded_2(): lax.ppermute(tail, axis, [(i, (i + 1) % count) for i in range(ends)])  5.67 us
    convert_element_type x1, other arithmetic, per_device(): depth_conv(grad_pad, w_depth[::-1], CZ).astype(jnp.bfloat16)  3.84 us
    add x1, other arithmetic, depth_conv(): result = result + window.astype(jnp.float32) * weights[offset]  3.82 us
  transfers between devices with their start and end apart: 4, of which 4 were waited for; matrix products, arithmetic and copies ran while one was open for 0% of the time, Pallas kernels for 0%

profile of v12, /device:TPU:2, one launch (start us, length us, event | category | flops | bytes accessed | tf_op | source)
XLA Modules:
  0.0 161.4 jit_solution(9016866691578036584)
XLA Ops:
  1.1 1.2 convert_reduce_fusion
  2.3 1.3 fusion.15
  3.6 1.3 fusion.17
  6.0 3.2 %fusion.63 = (f32[64]{0:T(128)S(1)}, f32[64,512]{1,0:T(8,128)S(1)}) fusion(bf16[64,4096]{1,0:T(8,128)(2,1)S(1)} %reshape.616, bf16[4096,512]{1,0:T(8,128)(2,1)} %param.15), kind=kOutput, calls=%fused_computation.139 | convolution fusion | flops 268468160 | bytes 4849920 | tf_op jit(solution)/shard_map/dot_general | solution.py:466
  12.5 46.4 %shard_map.148 = bf16[512,128]{1,0:T(8,128)(2,1)} custom-call(bf16[64,256]{1,0:T(8,128)(2,1)} %pad_maximum_fusion.7.x_ref, bf16[512,128]{1,0:T(8,128)(2,1)} %copy.25.q_ref), custom_call_target="tpu_custom_call" | custom-call | tf_op jit(solution)/shard_map/pallas_call | solution.py:171
  58.9 2.0 %convolution_convert_fusion.3 = bf16[512,512]{1,0:T(8,128)(2,1)} fusion(bf16[512,128]{1,0:T(8,128)(2,1)} %shard_map.148, bf16[128,512]{1,0:T(8,128)(2,1)S(1)} %copy-done.7), kind=kOutput, calls=%fused_computation.26 | convolution fusion | flops 67371008 | bytes 786432 | tf_op jit(solution)/shard_map/dot_general | solution.py:491
  60.9 17.7 %shard_map.149 = bf16[4,128,512]{2,1,0:T(8,128)(2,1)} custom-call(bf16[4,128,512]{2,1,0:T(8,128)(2,1)} %bitcast.80), custom_call_target="tpu_custom_call" | custom-call | tf_op jit(solution)/shard_map/pallas_call | solution.py:245
  78.6 1.3 fusion.27
  80.0 1.3 multiply_reduce_fusion
  81.9 2.5 %collective-permute-start = (bf16[1,16,16,512]{3,2,1,0:T(8,128)(2,1)S(1)}, bf16[1,16,16,512]{3,2,1,0:T(8,128)(2,1)S(1)}, u32[]{:S(2)}, u32[]{:S(2)}) collective-permute-start(bf16[1,16,16,512]{3,2,1,0:T(8,128)(2,1)S(1)} %bitcast.85), channel_id=1, source_target_pairs={{0,4},{4,8},{8,12},{12,16},{16,20},{20,24},{24,28},{28,32},{32,36}... | collective-permute-start | bytes 786440 | tf_op jit(solution)/shard_map/ppermute | solution.py:364
  84.4 3.4 %collective-permute-start.1 = (bf16[1,16,16,512]{3,2,1,0:T(8,128)(2,1)S(1)}, bf16[1,16,16,512]{3,2,1,0:T(8,128)(2,1)S(1)}, u32[]{:S(2)}, u32[]{:S(2)}) collective-permute-start(bf16[1,16,16,512]{3,2,1,0:T(8,128)(2,1)S(1)} %bitcast.84), channel_id=1, source_target_pairs={{4,0},{8,4},{12,8},{16,12},{20,16},{24,20},{28,24},{32,28},{36,32}... | collective-permute-start | bytes 786440 | tf_op jit(solution)/shard_map/ppermute | solution.py:366
  87.9 10.5 %collective-permute-done = bf16[1,16,16,512]{3,2,1,0:T(8,128)(2,1)S(1)} collective-permute-done((bf16[1,16,16,512]{3,2,1,0:T(8,128)(2,1)S(1)}, bf16[1,16,16,512]{3,2,1,0:T(8,128)(2,1)S(1)}, u32[]{:S(2)}, u32[]{:S(2)}) %collective-permute-start) | collective-permute-done | bytes 262176 | tf_op jit(solution)/shard_map/ppermute | solution.py:364
  99.6 3.8 %multiply_add_fusion = f32[2,16,16,512]{3,2,1,0:T(8,128)S(1)} fusion(bf16[2,16,16,512]{3,2,1,0:T(8,128)(2,1)S(1)} %bitcast.78, bf16[4,18,18,512]{3,2,1,0:T(8,128)(2,1)S(1)} %fusion.10, bf16[1,16,16,512]{3,2,1,0:T(8,128)(2,1)S(1)} %collective-permute-done.1, bf16[1,16,16,512]{3,2,1,0:T(8,128)(2,1)S(1)} %collective-permute-done, f32[512]{0:T(512)S(1)} %bitcast.100, ...), kind=kLoop, calls=%fused_computation.46 | loop fusion | flops 21495808 | bytes 14735360 | tf_op jit(solution)/shard_map/add | solution.py:442
  103.7 0.8 copy-done.3
  105.1 3.2 %collective-permute-start.2 = (bf16[1,16,16,512]{3,2,1,0:T(8,128)(2,1)S(1)}, bf16[1,16,16,512]{3,2,1,0:T(8,128)(2,1)S(1)}, u32[]{:S(2)}, u32[]{:S(2)}) collective-permute-start(bf16[1,16,16,512]{3,2,1,0:T(8,128)(2,1)S(1)} %bitcast.87), channel_id=1, source_target_pairs={{0,4},{4,8},{8,12},{12,16},{16,20},{20,24},{24,28},{28,32},{32,36}... | collective-permute-start | bytes 786440 | tf_op jit(solution)/shard_map/ppermute | solution.py:364
  108.3 2.7 %collective-permute-start.3 = (bf16[1,16,16,512]{3,2,1,0:T(8,128)(2,1)S(1)}, bf16[1,16,16,512]{3,2,1,0:T(8,128)(2,1)S(1)}, u32[]{:S(2)}, u32[]{:S(2)}) collective-permute-start(bf16[1,16,16,512]{3,2,1,0:T(8,128)(2,1)S(1)} %bitcast.86), channel_id=1, source_target_pairs={{4,0},{8,4},{12,8},{16,12},{20,16},{24,20},{28,24},{32,28},{36,32}... | collective-permute-start | bytes 786440 | tf_op jit(solution)/shard_map/ppermute | solution.py:366
  111.4 9.6 %collective-permute-done.2 = bf16[1,16,16,512]{3,2,1,0:T(8,128)(2,1)S(1)} collective-permute-done((bf16[1,16,16,512]{3,2,1,0:T(8,128)(2,1)S(1)}, bf16[1,16,16,512]{3,2,1,0:T(8,128)(2,1)S(1)}, u32[]{:S(2)}, u32[]{:S(2)}) %collective-permute-start.2) | collective-permute-done | bytes 262176 | tf_op jit(solution)/shard_map/ppermute | solution.py:364
  121.0 1.2 collective-permute-done.3
  123.0 3.8 %add_convert_fusion = bf16[2,16,16,512]{3,2,1,0:T(8,128)(2,1)S(1)} fusion(bf16[2,16,16,512]{3,2,1,0:T(8,128)(2,1)S(1)} %bitcast.73, bf16[4,18,18,512]{3,2,1,0:T(8,128)(2,1)S(1)} %select_maximum_fusion, bf16[1,16,16,512]{3,2,1,0:T(8,128)(2,1)S(1)} %collective-permute-done.3, bf16[1,16,16,512]{3,2,1,0:T(8,128)(2,1)S(1)} %collective-permute-done.2, ...), kind=kLoop, calls=%fused_computation.45 | loop fusion | flops 21757952 | bytes 14211072 | tf_op jit(solution)/shard_map/convert_element_type | solution.py:517
  127.6 1.3 copy.26
  128.9 2.2 %convert_element_type.374.g_ref = bf16[64,16,512]{2,1,0:T(8,128)(2,1)} reshape(bf16[512,1024]{1,0:T(8,128)(2,1)} %copy.26) | data formatting | bytes 2097152 | tf_op jit(solution)/shard_map/convert_element_type | solution.py:335
  131.1 28.1 %shard_map.150 = f32[16,512]{1,0:T(8,128)} custom-call(bf16[64,16,512]{2,1,0:T(8,128)(2,1)} %convert_element_type.374.g_ref), custom_call_target="tpu_custom_call" | custom-call | tf_op jit(solution)/shard_map/pallas_call | solution.py:336
  159.2 0.8 reshape.625
  160.6 0.8 copy.30
  (69 shorter events, 9.9 us)
Async XLA Ops:
  0.6 103.1 %copy-start = (bf16[512,512]{1,0:T(8,128)(2,1)S(1)}, bf16[512,512]{1,0:T(8,128)(2,1)}, u32[]{:S(2)}) copy-start(bf16[512,512]{1,0:T(8,128)(2,1)} %param.25) | copy-start | bytes 1572868
  5.9 3.5 %copy-start.5 = (bf16[512,128]{1,0:T(8,128)(2,1)S(1)}, bf16[512,128]{1,0:T(8,128)(2,1)}, u32[]{:S(2)}) copy-start(bf16[512,128]{1,0:T(8,128)(2,1)} %param.18) | copy-start | bytes 393220
  5.9 3.5 %copy-start.9 = (f32[512]{0:T(512)S(1)}, f32[512]{0:T(512)}, u32[]{:S(2)}) copy-start(f32[512]{0:T(512)} %param.16) | copy-start | bytes 6148
  6.0 4.2 %copy-start.6 = (bf16[512,128]{1,0:T(8,128)(2,1)S(1)}, bf16[512,128]{1,0:T(8,128)(2,1)}, u32[]{:S(2)}) copy-start(bf16[512,128]{1,0:T(8,128)(2,1)} %param.19) | copy-start | bytes 393220
  6.0 4.4 %copy-start.4 = (bf16[512,128]{1,0:T(8,128)(2,1)S(1)}, bf16[512,128]{1,0:T(8,128)(2,1)}, u32[]{:S(2)}) copy-start(bf16[512,128]{1,0:T(8,128)(2,1)} %param.17) | copy-start | bytes 393220
  9.2 49.7 %copy-start.7 = (bf16[128,512]{1,0:T(8,128)(2,1)S(1)}, bf16[128,512]{1,0:T(8,128)(2,1)}, u32[]{:S(2)}) copy-start(bf16[128,512]{1,0:T(8,128)(2,1)} %param.20) | copy-start | bytes 393220
  10.4 68.2 %copy-start.1 = (bf16[512,512]{1,0:T(8,128)(2,1)S(1)}, bf16[512,512]{1,0:T(8,128)(2,1)}, u32[]{:S(2)}) copy-start(bf16[512,512]{1,0:T(8,128)(2,1)} %param.13) | copy-start | bytes 1572868
  12.5 68.8 %copy-start.10 = (bf16[512,512]{1,0:T(8,128)(2,1)S(1)}, bf16[512,512]{1,0:T(8,128)(2,1)}, u32[]{:S(2)}) copy-start(bf16[512,512]{1,0:T(8,128)(2,1)} %param.22) | copy-start | bytes 1572868
  12.5 68.8 %copy-start.11 = (f32[512]{0:T(512)S(1)}, f32[512]{0:T(512)}, u32[]{:S(2)}) copy-start(f32[512]{0:T(512)} %param.21) | copy-start | bytes 6148
  78.6 2.7 %copy-start.2 = (bf16[4,128,512]{2,1,0:T(8,128)(2,1)S(1)}, bf16[4,128,512]{2,1,0:T(8,128)(2,1)}, u32[]{:S(2)}) copy-start(bf16[4,128,512]{2,1,0:T(8,128)(2,1)} %shard_map.149) | copy-start | bytes 1572868
  81.3 6.5 %copy-start.8 = (f32[27,512]{1,0:T(8,128)S(1)}, f32[27,512]{1,0:T(8,128)}, u32[]{:S(2)}) copy-start(f32[27,512]{1,0:T(8,128)} %param.23) | copy-start | bytes 165892
  81.9 16.4 %collective-permute-start = (bf16[1,16,16,512]{3,2,1,0:T(8,128)(2,1)S(1)}, bf16[1,16,16,512]{3,2,1,0:T(8,128)(2,1)S(1)}, u32[]{:S(2)}, u32[]{:S(2)}) collective-permute-start(bf16[1,16,16,512]{3,2,1,0:T(8,128)(2,1)S(1)} %bitcast.85), channel_id=1, source_target_pairs={{0,4},{4,8},{8,12},{12,16},{16,20},{20,24},{24,28},{28,32},{32,36}... | collective-permute-start | bytes 786440 | tf_op jit(solution)/shard_map/ppermute | solution.py:364
  84.4 14.4 %collective-permute-start.1 = (bf16[1,16,16,512]{3,2,1,0:T(8,128)(2,1)S(1)}, bf16[1,16,16,512]{3,2,1,0:T(8,128)(2,1)S(1)}, u32[]{:S(2)}, u32[]{:S(2)}) collective-permute-start(bf16[1,16,16,512]{3,2,1,0:T(8,128)(2,1)S(1)} %bitcast.84), channel_id=1, source_target_pairs={{4,0},{8,4},{12,8},{16,12},{20,16},{24,20},{28,24},{32,28},{36,32}... | collective-permute-start | bytes 786440 | tf_op jit(solution)/shard_map/ppermute | solution.py:366
  103.4 1.0 copy-start.3
  105.1 16.0 %collective-permute-start.2 = (bf16[1,16,16,512]{3,2,1,0:T(8,128)(2,1)S(1)}, bf16[1,16,16,512]{3,2,1,0:T(8,128)(2,1)S(1)}, u32[]{:S(2)}, u32[]{:S(2)}) collective-permute-start(bf16[1,16,16,512]{3,2,1,0:T(8,128)(2,1)S(1)} %bitcast.87), channel_id=1, source_target_pairs={{0,4},{4,8},{8,12},{12,16},{16,20},{20,24},{24,28},{28,32},{32,36}... | collective-permute-start | bytes 786440 | tf_op jit(solution)/shard_map/ppermute | solution.py:364
  108.3 14.0 %collective-permute-start.3 = (bf16[1,16,16,512]{3,2,1,0:T(8,128)(2,1)S(1)}, bf16[1,16,16,512]{3,2,1,0:T(8,128)(2,1)S(1)}, u32[]{:S(2)}, u32[]{:S(2)}) collective-permute-start(bf16[1,16,16,512]{3,2,1,0:T(8,128)(2,1)S(1)} %bitcast.86), channel_id=1, source_target_pairs={{4,0},{8,4},{12,8},{16,12},{20,16},{24,20},{28,24},{32,28},{36,32}... | collective-permute-start | bytes 786440 | tf_op jit(solution)/shard_map/ppermute | solution.py:366

commit v13 on v12

--- a/solution.py
+++ b/solution.py
@@ -353,23 +353,6 @@
     return summed.reshape(rows, width)
 
 
-def padded_2(cells, sides, width):
-    for axis, dim in sides:
-        count = lax.psum(1, axis)
-        ends = count - 1
-        head = lax.slice_in_dim(cells, 0, width, axis=dim)
-        tail = lax.slice_in_dim(cells, cells.shape[dim] - width, cells.shape[dim], axis=dim)
-        cells = jnp.concatenate(
-            [
-                lax.ppermute(tail, axis, [(i, (i + 1) % count) for i in range(ends)]),
-                cells,
-                lax.ppermute(head, axis, [((i + 1) % count, i) for i in range(ends)]),
-            ],
-            axis=dim,
-        )
-    return cells
-
-
 def layer_norm(values, scale_gain):
     values = values.astype(jnp.float32)
     centered = values - jnp.mean(values, axis=-1, keepdims=True)
@@ -441,6 +424,28 @@
         ]
         result = result + window.astype(jnp.float32) * weights[offset]
     return result
+
+
+def conv_with_halos(cells, weights):
+    count = lax.psum(1, SLAB)
+    ends = count - 1
+    planes = cells.shape[0]
+    below = lax.ppermute(cells[planes - 1], SLAB, [(i, i + 1) for i in range(ends)])
+    above = lax.ppermute(cells[0], SLAB, [(i + 1, i) for i in range(ends)])
+    own = depth_conv(jnp.pad(cells, ((1, 1), (1, 1), (1, 1), (0, 0))), weights, planes)
+    height, width_x = cells.shape[1], cells.shape[2]
+
+    def plane_terms(plane, first):
+        padded = jnp.pad(plane, ((1, 1), (1, 1), (0, 0))).astype(jnp.float32)
+        total = jnp.zeros(plane.shape, jnp.float32)
+        for offset in range(9):
+            shift_y, shift_x = offset // 3, offset % 3
+            window = padded[shift_y : shift_y + height, shift_x : shift_x + width_x]
+            total = total + window * weights[first + offset]
+        return total
+
+    own = own.at[0].add(plane_terms(below, 0))
+    return own.at[planes - 1].add(plane_terms(above, 18))
 
 
 def per_device(
@@ -499,9 +504,7 @@
         .astype(jnp.bfloat16)
         .reshape(CZ, GY, GX, channels)
     )
-    pre_wide = padded_2(pre, ((SLAB, 0),), 1)
-    pre_pad = jnp.pad(pre_wide, ((0, 0), (1, 1), (1, 1), (0, 0)))
-    mixed = depth_conv(pre_pad, w_depth, CZ).reshape(tok_rows, channels)
+    mixed = conv_with_halos(pre, w_depth).reshape(tok_rows, channels)
     normal_cdf = 0.5 * (1.0 + lax.erf(mixed * ROOT_HALF))
     normal_pdf = jnp.exp(-0.5 * mixed * mixed) * NORMAL_SCALE
     activated = (mixed * normal_cdf).astype(jnp.bfloat16)
@@ -511,10 +514,10 @@
         .astype(jnp.bfloat16)
         .reshape(CZ, GY, GX, channels)
     )
-    grad_wide = padded_2(grad_mixed, ((SLAB, 0),), 1)
-    grad_pad = jnp.pad(grad_wide, ((0, 0), (1, 1), (1, 1), (0, 0)))
     grad_pre = (
-        depth_conv(grad_pad, w_depth[::-1], CZ).astype(jnp.bfloat16).reshape(tok_rows, channels)
+        conv_with_halos(grad_mixed, w_depth[::-1])
+        .astype(jnp.bfloat16)
+        .reshape(tok_rows, channels)
     )
     up_full = jnp.einsum("td,tc->dc", normed_ffn, grad_pre, preferred_element_type=jnp.float32)
     down_full = jnp.einsum("td,tc->dc", grad_out, activated, preferred_element_type=jnp.float32)

time: 163 us -> 156 us (0.957)
  waiting for transfers between devices: 21.8 us -> 14.4 us
    ppermute x4, waiting for transfers between devices: 21.8 us -> 14.4 us  [the longest x2 7.42 us: conv_with_halos(): lax.ppermute(cells[planes - 1], SLAB, [(i, i + 1) for i in range(ends)])]
    convert_element_type x1 -> x5, other arithmetic: 3.84 us -> 0.48 us  [the longest x4 0.4 us: plane_terms(): padded = jnp.pad(plane, ((1, 1), (1, 1), (0, 0))).astype(jnp.float32)]
    add x1 -> x2, other arithmetic: 3.82 us -> 6.97 us  [depth_conv(): result = result + window.astype(jnp.float32) * weights[offset]]
    scatter-add x0 -> x4, other arithmetic: none -> 1.8 us  [the longest x2 0.9 us: conv_with_halos(): return own.at[planes - 1].add(plane_terms(above, 18))]
  transfers between devices with their start and end apart: 4 -> 4, of which waited for: 4 -> 3; matrix products, arithmetic and copies ran while one was open for 0% -> 6% of each run, Pallas kernels for 0% -> 0%
where the time goes in v13:
time: 156 us; the launch traced here: 155 us
  Pallas kernels  93.5 us (60%)
  other arithmetic  17.7 us (11%)
  waiting for transfers between devices  14.4 us (9%)
  starting transfers between devices  11.7 us (8%)
  local copies, waits for them, and re-layouts  8.77 us (6%)
  matrix products  8.06 us (5%)
    pallas_call x1, Pallas kernels, gather_attend(): pl.pallas_call(functools.partial(gather_kernel, row_size), out_shape=jax....  46.4 us
    pallas_call x1, Pallas kernels, slab_scatter(): pl.pallas_call(functools.partial(scatter_kernel, row_size), out_shape=jax...  29.3 us
    pallas_call x1, Pallas kernels, head_sum(): pl.pallas_call(functools.partial(head_sum_kernel, count), out_shape=jax.S...  17.7 us
    ppermute x2, waiting for transfers between devices, conv_with_halos(): lax.ppermute(cells[planes - 1], SLAB, [(i, i + 1) for i in range(ends)])  7.42 us
    ppermute x2, waiting for transfers between devices, conv_with_halos(): above = lax.ppermute(cells[0], SLAB, [(i + 1, i) for i in range(ends)])  6.99 us
    add x2, other arithmetic, depth_conv(): result = result + window.astype(jnp.float32) * weights[offset]  6.97 us
    ppermute x2, starting transfers between devices, conv_with_halos(): above = lax.ppermute(cells[0], SLAB, [(i + 1, i) for i in range(ends)])  6.13 us
    ppermute x2, starting transfers between devices, conv_with_halos(): lax.ppermute(cells[planes - 1], SLAB, [(i, i + 1) for i in range(ends)])  5.58 us
  transfers between devices with their start and end apart: 4, of which 3 were waited for; matrix products, arithmetic and copies ran while one was open for 6% of the time, Pallas kernels for 0%

profile of v13, /device:TPU:2, one launch (start us, length us, event | category | flops | bytes accessed | tf_op | source)
XLA Modules:
  0.0 155.3 jit_solution(12692479331421895625)
XLA Ops:
  1.1 1.2 convert_reduce_fusion
  2.3 1.3 fusion.4
  3.6 1.3 fusion.6
  6.0 3.2 %fusion.96 = (f32[64]{0:T(128)S(1)}, f32[64,512]{1,0:T(8,128)S(1)}) fusion(bf16[64,4096]{1,0:T(8,128)(2,1)S(1)} %reshape.796, bf16[4096,512]{1,0:T(8,128)(2,1)} %param.23), kind=kOutput, calls=%fused_computation.254 | convolution fusion | flops 268468160 | bytes 4849920 | tf_op jit(solution)/shard_map/dot_general | solution.py:471
  11.1 0.8 copy.25.q_ref
  12.5 46.4 %shard_map.148 = bf16[512,128]{1,0:T(8,128)(2,1)} custom-call(bf16[64,256]{1,0:T(8,128)(2,1)} %pad_maximum_fusion.3.x_ref, bf16[512,128]{1,0:T(8,128)(2,1)} %copy.25.q_ref), custom_call_target="tpu_custom_call" | custom-call | tf_op jit(solution)/shard_map/pallas_call | solution.py:171
  58.9 2.0 %convolution_convert_fusion.3 = bf16[512,512]{1,0:T(8,128)(2,1)} fusion(bf16[512,128]{1,0:T(8,128)(2,1)} %shard_map.148, bf16[128,512]{1,0:T(8,128)(2,1)S(1)} %copy-done.7), kind=kOutput, calls=%fused_computation.61 | convolution fusion | flops 67371008 | bytes 786432 | tf_op jit(solution)/shard_map/dot_general | solution.py:496
  60.9 17.7 %shard_map.149 = bf16[4,128,512]{2,1,0:T(8,128)(2,1)} custom-call(bf16[4,128,512]{2,1,0:T(8,128)(2,1)} %bitcast.102), custom_call_target="tpu_custom_call" | custom-call | tf_op jit(solution)/shard_map/pallas_call | solution.py:245
  78.6 1.3 fusion.16
  80.0 1.3 multiply_reduce_fusion
  81.9 2.5 %collective-permute-start = (bf16[16,16,512]{2,1,0:T(8,128)(2,1)S(1)}, bf16[16,16,512]{2,1,0:T(8,128)(2,1)S(1)}, u32[]{:S(2)}, u32[]{:S(2)}) collective-permute-start(bf16[16,16,512]{2,1,0:T(8,128)(2,1)S(1)} %bitcast.107), channel_id=1, source_target_pairs={{0,4},{4,8},{8,12},{12,16},{16,20},{20,24},{24,28},{28,32},{32,36}... | collective-permute-start | bytes 786440 | tf_op jit(solution)/shard_map/ppermute | solution.py:433
  84.4 3.4 %collective-permute-start.1 = (bf16[16,16,512]{2,1,0:T(8,128)(2,1)S(1)}, bf16[16,16,512]{2,1,0:T(8,128)(2,1)S(1)}, u32[]{:S(2)}, u32[]{:S(2)}) collective-permute-start(bf16[16,16,512]{2,1,0:T(8,128)(2,1)S(1)} %bitcast.106), channel_id=1, source_target_pairs={{4,0},{8,4},{12,8},{16,12},{20,16},{24,20},{28,24},{32,28},{36,32}... | collective-permute-start | bytes 786440 | tf_op jit(solution)/shard_map/ppermute | solution.py:434
  87.9 3.6 %multiply_add_fusion.1 = f32[2,16,16,512]{3,2,1,0:T(8,128)S(1)} fusion(bf16[2,16,16,512]{3,2,1,0:T(8,128)(2,1)S(1)} %bitcast.100, f32[512]{0:T(512)S(1)} %bitcast.174, f32[512]{0:T(512)S(1)} %bitcast.178, f32[512]{0:T(512)S(1)} %bitcast.146, f32[512]{0:T(512)S(1)} %bitcast.150, f32[512]{0:T(512)S(1)} %bitcast.154, f32[512]{0:T(512)S(1)} %bitcast.158, ...), kind=kLoop, calls=%fused_computation.81 | loop fusion | flops 20971520 | bytes 1628160 | tf_op jit(solution)/shard_map/add | solution.py:425
  91.5 6.9 %collective-permute-done = bf16[16,16,512]{2,1,0:T(8,128)(2,1)S(1)} collective-permute-done((bf16[16,16,512]{2,1,0:T(8,128)(2,1)S(1)}, bf16[16,16,512]{2,1,0:T(8,128)(2,1)S(1)}, u32[]{:S(2)}, u32[]{:S(2)}) %collective-permute-start) | collective-permute-done | bytes 262176 | tf_op jit(solution)/shard_map/ppermute | solution.py:433
  99.8 0.8 copy-done.3
  101.1 3.1 %collective-permute-start.2 = (bf16[16,16,512]{2,1,0:T(8,128)(2,1)S(1)}, bf16[16,16,512]{2,1,0:T(8,128)(2,1)S(1)}, u32[]{:S(2)}, u32[]{:S(2)}) collective-permute-start(bf16[16,16,512]{2,1,0:T(8,128)(2,1)S(1)} %bitcast.109), channel_id=1, source_target_pairs={{0,4},{4,8},{8,12},{12,16},{16,20},{20,24},{24,28},{28,32},{32,36}... | collective-permute-start | bytes 786440 | tf_op jit(solution)/shard_map/ppermute | solution.py:433
  104.2 3.4 %multiply_add_fusion = f32[2,16,16,512]{3,2,1,0:T(8,128)S(1)} fusion(bf16[2,16,16,512]{3,2,1,0:T(8,128)(2,1)S(1)} %bitcast.99, f32[512]{0:T(512)S(1)} %bitcast.176, f32[512]{0:T(512)S(1)} %bitcast.180, f32[512]{0:T(512)S(1)} %bitcast.148, f32[512]{0:T(512)S(1)} %bitcast.152, f32[512]{0:T(512)S(1)} %bitcast.156, f32[512]{0:T(512)S(1)} %bitcast.160, ...), kind=kLoop, calls=%fused_computation.80 | loop fusion | flops 20971520 | bytes 1628160 | tf_op jit(solution)/shard_map/add | solution.py:425
  107.6 2.8 %collective-permute-start.3 = (bf16[16,16,512]{2,1,0:T(8,128)(2,1)S(1)}, bf16[16,16,512]{2,1,0:T(8,128)(2,1)S(1)}, u32[]{:S(2)}, u32[]{:S(2)}) collective-permute-start(bf16[16,16,512]{2,1,0:T(8,128)(2,1)S(1)} %bitcast.108), channel_id=1, source_target_pairs={{4,0},{8,4},{12,8},{16,12},{20,16},{24,20},{28,24},{32,28},{36,32}... | collective-permute-start | bytes 786440 | tf_op jit(solution)/shard_map/ppermute | solution.py:434
  111.9 7.0 %collective-permute-done.3 = bf16[16,16,512]{2,1,0:T(8,128)(2,1)S(1)} collective-permute-done((bf16[16,16,512]{2,1,0:T(8,128)(2,1)S(1)}, bf16[16,16,512]{2,1,0:T(8,128)(2,1)S(1)}, u32[]{:S(2)}, u32[]{:S(2)}) %collective-permute-start.3) | collective-permute-done | bytes 262176 | tf_op jit(solution)/shard_map/ppermute | solution.py:434
  120.3 1.3 copy.26
  121.6 2.2 %convert_element_type.395.g_ref = bf16[64,16,512]{2,1,0:T(8,128)(2,1)} reshape(bf16[512,1024]{1,0:T(8,128)(2,1)} %copy.26) | data formatting | bytes 2097152 | tf_op jit(solution)/shard_map/convert_element_type | solution.py:335
  123.8 29.3 %shard_map.150 = f32[16,512]{1,0:T(8,128)} custom-call(bf16[64,16,512]{2,1,0:T(8,128)(2,1)} %convert_element_type.395.g_ref), custom_call_target="tpu_custom_call" | custom-call | tf_op jit(solution)/shard_map/pallas_call | solution.py:336
  153.1 0.8 reshape.809
  154.5 0.8 copy.34
  (76 shorter events, 9.9 us)
Async XLA Ops:
  0.6 99.1 %copy-start = (bf16[512,512]{1,0:T(8,128)(2,1)S(1)}, bf16[512,512]{1,0:T(8,128)(2,1)}, u32[]{:S(2)}) copy-start(bf16[512,512]{1,0:T(8,128)(2,1)} %param.33) | copy-start | bytes 1572868
  5.9 3.5 %copy-start.5 = (bf16[512,128]{1,0:T(8,128)(2,1)S(1)}, bf16[512,128]{1,0:T(8,128)(2,1)}, u32[]{:S(2)}) copy-start(bf16[512,128]{1,0:T(8,128)(2,1)} %param.26) | copy-start | bytes 393220
  5.9 3.5 %copy-start.9 = (f32[512]{0:T(512)S(1)}, f32[512]{0:T(512)}, u32[]{:S(2)}) copy-start(f32[512]{0:T(512)} %param.24) | copy-start | bytes 6148
  6.0 4.2 %copy-start.6 = (bf16[512,128]{1,0:T(8,128)(2,1)S(1)}, bf16[512,128]{1,0:T(8,128)(2,1)}, u32[]{:S(2)}) copy-start(bf16[512,128]{1,0:T(8,128)(2,1)} %param.27) | copy-start | bytes 393220
  6.0 4.4 %copy-start.4 = (bf16[512,128]{1,0:T(8,128)(2,1)S(1)}, bf16[512,128]{1,0:T(8,128)(2,1)}, u32[]{:S(2)}) copy-start(bf16[512,128]{1,0:T(8,128)(2,1)} %param.25) | copy-start | bytes 393220
  9.2 49.7 %copy-start.7 = (bf16[128,512]{1,0:T(8,128)(2,1)S(1)}, bf16[128,512]{1,0:T(8,128)(2,1)}, u32[]{:S(2)}) copy-start(bf16[128,512]{1,0:T(8,128)(2,1)} %param.28) | copy-start | bytes 393220
  10.4 68.2 %copy-start.1 = (bf16[512,512]{1,0:T(8,128)(2,1)S(1)}, bf16[512,512]{1,0:T(8,128)(2,1)}, u32[]{:S(2)}) copy-start(bf16[512,512]{1,0:T(8,128)(2,1)} %param.21) | copy-start | bytes 1572868
  12.5 68.8 %copy-start.10 = (bf16[512,512]{1,0:T(8,128)(2,1)S(1)}, bf16[512,512]{1,0:T(8,128)(2,1)}, u32[]{:S(2)}) copy-start(bf16[512,512]{1,0:T(8,128)(2,1)} %param.30) | copy-start | bytes 1572868
  12.5 68.8 %copy-start.11 = (f32[512]{0:T(512)S(1)}, f32[512]{0:T(512)}, u32[]{:S(2)}) copy-start(f32[512]{0:T(512)} %param.29) | copy-start | bytes 6148
  78.6 2.7 %copy-start.2 = (bf16[4,128,512]{2,1,0:T(8,128)(2,1)S(1)}, bf16[4,128,512]{2,1,0:T(8,128)(2,1)}, u32[]{:S(2)}) copy-start(bf16[4,128,512]{2,1,0:T(8,128)(2,1)} %shard_map.149) | copy-start | bytes 1572868
  81.3 6.5 %copy-start.8 = (f32[27,512]{1,0:T(8,128)S(1)}, f32[27,512]{1,0:T(8,128)}, u32[]{:S(2)}) copy-start(f32[27,512]{1,0:T(8,128)} %param.31) | copy-start | bytes 165892
  81.9 16.4 %collective-permute-start = (bf16[16,16,512]{2,1,0:T(8,128)(2,1)S(1)}, bf16[16,16,512]{2,1,0:T(8,128)(2,1)S(1)}, u32[]{:S(2)}, u32[]{:S(2)}) collective-permute-start(bf16[16,16,512]{2,1,0:T(8,128)(2,1)S(1)} %bitcast.107), channel_id=1, source_target_pairs={{0,4},{4,8},{8,12},{12,16},{16,20},{20,24},{24,28},{28,32},{32,36}... | collective-permute-start | bytes 786440 | tf_op jit(solution)/shard_map/ppermute | solution.py:433
  84.4 14.5 %collective-permute-start.1 = (bf16[16,16,512]{2,1,0:T(8,128)(2,1)S(1)}, bf16[16,16,512]{2,1,0:T(8,128)(2,1)S(1)}, u32[]{:S(2)}, u32[]{:S(2)}) collective-permute-start(bf16[16,16,512]{2,1,0:T(8,128)(2,1)S(1)} %bitcast.106), channel_id=1, source_target_pairs={{4,0},{8,4},{12,8},{16,12},{20,16},{24,20},{28,24},{32,28},{36,32}... | collective-permute-start | bytes 786440 | tf_op jit(solution)/shard_map/ppermute | solution.py:434
  99.5 1.0 copy-start.3
  101.1 10.2 %collective-permute-start.2 = (bf16[16,16,512]{2,1,0:T(8,128)(2,1)S(1)}, bf16[16,16,512]{2,1,0:T(8,128)(2,1)S(1)}, u32[]{:S(2)}, u32[]{:S(2)}) collective-permute-start(bf16[16,16,512]{2,1,0:T(8,128)(2,1)S(1)} %bitcast.109), channel_id=1, source_target_pairs={{0,4},{4,8},{8,12},{12,16},{16,20},{20,24},{24,28},{28,32},{32,36}... | collective-permute-start | bytes 786440 | tf_op jit(solution)/shard_map/ppermute | solution.py:433
  107.6 11.3 %collective-permute-start.3 = (bf16[16,16,512]{2,1,0:T(8,128)(2,1)S(1)}, bf16[16,16,512]{2,1,0:T(8,128)(2,1)S(1)}, u32[]{:S(2)}, u32[]{:S(2)}) collective-permute-start(bf16[16,16,512]{2,1,0:T(8,128)(2,1)S(1)} %bitcast.108), channel_id=1, source_target_pairs={{4,0},{8,4},{12,8},{16,12},{20,16},{24,20},{28,24},{32,28},{36,32}... | collective-permute-start | bytes 786440 | tf_op jit(solution)/shard_map/ppermute | solution.py:434

commit v14 on v13

--- a/solution.py
+++ b/solution.py
@@ -327,7 +327,7 @@
     lax.fori_loop(1, row_size, finish_row, 0)
 
 
-def slab_scatter(g, count, row_size):
+def slab_scatter(g, count, row_size, collective):
     total_rows, width = g.shape
     rows = total_rows // count
     y_count = count // row_size
@@ -348,7 +348,7 @@
             pltpu.SemaphoreType.DMA((row_size,)),
             pltpu.SemaphoreType.DMA((row_size,)),
         ],
-        compiler_params=pltpu.CompilerParams(collective_id=1, has_side_effects=True),
+        compiler_params=pltpu.CompilerParams(collective_id=collective, has_side_effects=True),
     )(g)
     return summed.reshape(rows, width)
 
@@ -508,6 +508,7 @@
     normal_cdf = 0.5 * (1.0 + lax.erf(mixed * ROOT_HALF))
     normal_pdf = jnp.exp(-0.5 * mixed * mixed) * NORMAL_SCALE
     activated = (mixed * normal_cdf).astype(jnp.bfloat16)
+    down_full = jnp.einsum("td,tc->dc", grad_out, activated, preferred_element_type=jnp.float32)
     grad_act = jnp.einsum("td,cd->tc", grad_out, w_down, preferred_element_type=jnp.float32)
     grad_mixed = (
         (grad_act * (normal_cdf + mixed * normal_pdf))
@@ -520,13 +521,11 @@
         .reshape(tok_rows, channels)
     )
     up_full = jnp.einsum("td,tc->dc", normed_ffn, grad_pre, preferred_element_type=jnp.float32)
-    down_full = jnp.einsum("td,tc->dc", grad_out, activated, preferred_element_type=jnp.float32)
-    grads = slab_scatter(
-        jnp.concatenate([up_full, down_full], axis=1),
-        lax.psum(1, SLAB),
-        lax.psum(1, ("z", "xl")),
-    )
-    return (attended, grads[:, :channels], grads[:, channels:])
+    slab_count = lax.psum(1, SLAB)
+    row_size = lax.psum(1, ("z", "xl"))
+    grad_down = slab_scatter(down_full, slab_count, row_size, 1)
+    grad_up = slab_scatter(up_full, slab_count, row_size, 5)
+    return (attended, grad_up, grad_down)
 
 
 def solution(mesh):

time: 156 us -> 164 us (1.051)
  Pallas kernels: 93.5 us -> 104 us
  waiting for transfers between devices: 14.4 us -> 6.89 us
  other arithmetic: 17.7 us -> 19.5 us
    pallas_call x1 -> x2, Pallas kernels: 29.3 us -> 40 us  [slab_scatter(): pl.pallas_call(functools.partial(scatter_kernel, row_size), out_shape=jax...]
    ppermute x2, waiting for transfers between devices: 6.99 us -> 0.01 us  [conv_with_halos(): above = lax.ppermute(cells[0], SLAB, [(i + 1, i) for i in range(ends)])]
    convert_element_type x1, local copies, waits for them, and re-layouts: 2.2 us -> 0.21 us  [slab_scatter(): g.astype(jnp.bfloat16).reshape(count, tile_rows, rows * width // tile_rows)]
    convert_element_type x4, other arithmetic: 0.4 us -> 2.35 us  [plane_terms(): padded = jnp.pad(plane, ((1, 1), (1, 1), (0, 0))).astype(jnp.float32)]
    reshape x0 -> x2, local copies, waits for them, and re-layouts: none -> 1.93 us  [slab_scatter(): g.astype(jnp.bfloat16).reshape(count, tile_rows, rows * width // tile_rows)]
    reshape x1 -> x2, local copies, waits for them, and re-layouts: 0.77 us -> 2.66 us  [slab_scatter(): return summed.reshape(rows, width)]
  transfers between devices with their start and end apart: 4 -> 4, of which waited for: 3 -> 1; matrix products, arithmetic and copies ran while one was open for 6% -> 7% of each run, Pallas kernels for 0% -> 15%
where the time goes in v14:
time: 164 us; the launch traced here: 162 us
  Pallas kernels  104 us (63%)
  other arithmetic  19.5 us (12%)
  starting transfers between devices  12.3 us (8%)
  matrix products  9.13 us (6%)
  local copies, waits for them, and re-layouts  8.91 us (5%)
  waiting for transfers between devices  6.89 us (4%)
    pallas_call x1, Pallas kernels, gather_attend(): pl.pallas_call(functools.partial(gather_kernel, row_size), out_shape=jax....  46.3 us
    pallas_call x2, Pallas kernels, slab_scatter(): pl.pallas_call(functools.partial(scatter_kernel, row_size), out_shape=jax...  40 us
    pallas_call x1, Pallas kernels, head_sum(): pl.pallas_call(functools.partial(head_sum_kernel, count), out_shape=jax.S...  17.7 us
    add x2, other arithmetic, depth_conv(): result = result + window.astype(jnp.float32) * weights[offset]  6.96 us
    ppermute x2, waiting for transfers between devices, conv_with_halos(): lax.ppermute(cells[planes - 1], SLAB, [(i, i + 1) for i in range(ends)])  6.89 us
    ppermute x2, starting transfers between devices, conv_with_halos(): above = lax.ppermute(cells[0], SLAB, [(i + 1, i) for i in range(ends)])  6.7 us
    ppermute x2, starting transfers between devices, conv_with_halos(): lax.ppermute(cells[planes - 1], SLAB, [(i, i + 1) for i in range(ends)])  5.64 us
  transfers between devices with their start and end apart: 4, of which 1 were waited for; matrix products, arithmetic and copies ran while one was open for 7% of the time, Pallas kernels for 15%

profile of v14, /device:TPU:2, one launch (start us, length us, event | category | flops | bytes accessed | tf_op | source)
XLA Modules:
  0.0 162.1 jit_solution(826401885291646799)
XLA Ops:
  1.1 1.2 convert_reduce_fusion
  2.3 1.3 fusion.4
  3.6 1.3 fusion.6
  6.0 3.2 %fusion.95 = (f32[64]{0:T(128)S(1)}, f32[64,512]{1,0:T(8,128)S(1)}) fusion(bf16[64,4096]{1,0:T(8,128)(2,1)S(1)} %reshape.802, bf16[4096,512]{1,0:T(8,128)(2,1)} %param.23), kind=kOutput, calls=%fused_computation.252 | convolution fusion | flops 268468160 | bytes 4849920 | tf_op jit(solution)/shard_map/dot_general | solution.py:471
  12.5 46.3 %shard_map.148 = bf16[512,128]{1,0:T(8,128)(2,1)} custom-call(bf16[64,256]{1,0:T(8,128)(2,1)} %pad_maximum_fusion.2.x_ref, bf16[512,128]{1,0:T(8,128)(2,1)} %copy.25.q_ref), custom_call_target="tpu_custom_call" | custom-call | tf_op jit(solution)/shard_map/pallas_call | solution.py:171
  58.8 2.0 %convolution_convert_fusion.3 = bf16[512,512]{1,0:T(8,128)(2,1)} fusion(bf16[512,128]{1,0:T(8,128)(2,1)} %shard_map.148, bf16[128,512]{1,0:T(8,128)(2,1)S(1)} %copy-done.7), kind=kOutput, calls=%fused_computation.61 | convolution fusion | flops 67371008 | bytes 786432 | tf_op jit(solution)/shard_map/dot_general | solution.py:496
  60.8 17.7 %shard_map.149 = bf16[4,128,512]{2,1,0:T(8,128)(2,1)} custom-call(bf16[4,128,512]{2,1,0:T(8,128)(2,1)} %bitcast.102), custom_call_target="tpu_custom_call" | custom-call | tf_op jit(solution)/shard_map/pallas_call | solution.py:245
  78.6 1.3 fusion.16
  79.8 1.3 multiply_reduce_fusion
  81.2 1.6 convolution_convert_fusion.2
  82.8 2.5 %collective-permute-start = (bf16[16,16,512]{2,1,0:T(8,128)(2,1)S(1)}, bf16[16,16,512]{2,1,0:T(8,128)(2,1)S(1)}, u32[]{:S(2)}, u32[]{:S(2)}) collective-permute-start(bf16[16,16,512]{2,1,0:T(8,128)(2,1)S(1)} %bitcast.108), channel_id=1, source_target_pairs={{0,4},{4,8},{8,12},{12,16},{16,20},{20,24},{24,28},{28,32},{32,36}... | collective-permute-start | bytes 786440 | tf_op jit(solution)/shard_map/ppermute | solution.py:433
  85.3 3.3 %collective-permute-start.1 = (bf16[16,16,512]{2,1,0:T(8,128)(2,1)S(1)}, bf16[16,16,512]{2,1,0:T(8,128)(2,1)S(1)}, u32[]{:S(2)}, u32[]{:S(2)}) collective-permute-start(bf16[16,16,512]{2,1,0:T(8,128)(2,1)S(1)} %bitcast.106), channel_id=1, source_target_pairs={{4,0},{8,4},{12,8},{16,12},{20,16},{24,20},{28,24},{32,28},{36,32}... | collective-permute-start | bytes 786440 | tf_op jit(solution)/shard_map/ppermute | solution.py:434
  88.7 3.6 %multiply_add_fusion.1 = f32[2,16,16,512]{3,2,1,0:T(8,128)S(1)} fusion(bf16[2,16,16,512]{3,2,1,0:T(8,128)(2,1)S(1)} %bitcast.100, f32[512]{0:T(512)S(1)} %bitcast.173, f32[512]{0:T(512)S(1)} %bitcast.177, f32[512]{0:T(512)S(1)} %bitcast.145, f32[512]{0:T(512)S(1)} %bitcast.149, f32[512]{0:T(512)S(1)} %bitcast.153, f32[512]{0:T(512)S(1)} %bitcast.157, ...), kind=kLoop, calls=%fused_computation.80 | loop fusion | flops 20971520 | bytes 1628160 | tf_op jit(solution)/shard_map/add | solution.py:425
  92.3 6.9 %collective-permute-done = bf16[16,16,512]{2,1,0:T(8,128)(2,1)S(1)} collective-permute-done((bf16[16,16,512]{2,1,0:T(8,128)(2,1)S(1)}, bf16[16,16,512]{2,1,0:T(8,128)(2,1)S(1)}, u32[]{:S(2)}, u32[]{:S(2)}) %collective-permute-start) | collective-permute-done | bytes 262176 | tf_op jit(solution)/shard_map/ppermute | solution.py:433
  102.2 3.1 %collective-permute-start.2 = (bf16[16,16,512]{2,1,0:T(8,128)(2,1)}, bf16[16,16,512]{2,1,0:T(8,128)(2,1)}, u32[]{:S(2)}, u32[]{:S(2)}) collective-permute-start(bf16[16,16,512]{2,1,0:T(8,128)(2,1)} %bitcast.39), channel_id=1, source_target_pairs={{0,4},{4,8},{8,12},{12,16},{16,20},{20,24},{24,28},{28,32},{32,36}... | collective-permute-start | bytes 786440 | tf_op jit(solution)/shard_map/ppermute | solution.py:433
  105.3 3.4 %multiply_add_fusion = f32[2,16,16,512]{3,2,1,0:T(8,128)S(1)} fusion(bf16[2,16,16,512]{3,2,1,0:T(8,128)(2,1)S(1)} %bitcast.99, f32[512]{0:T(512)S(1)} %bitcast.175, f32[512]{0:T(512)S(1)} %bitcast.179, f32[512]{0:T(512)S(1)} %bitcast.147, f32[512]{0:T(512)S(1)} %bitcast.151, f32[512]{0:T(512)S(1)} %bitcast.155, f32[512]{0:T(512)S(1)} %bitcast.159, ...), kind=kLoop, calls=%fused_computation.79 | loop fusion | flops 20971520 | bytes 1628160 | tf_op jit(solution)/shard_map/add | solution.py:425
  108.7 3.4 %collective-permute-start.3 = (bf16[16,16,512]{2,1,0:T(8,128)(2,1)S(1)}, bf16[16,16,512]{2,1,0:T(8,128)(2,1)}, u32[]{:S(2)}, u32[]{:S(2)}) collective-permute-start(bf16[16,16,512]{2,1,0:T(8,128)(2,1)S(1)} %bitcast.107), channel_id=1, source_target_pairs={{4,0},{8,4},{12,8},{16,12},{20,16},{24,20},{28,24},{32,28},{36,32}... | collective-permute-start | bytes 786440 | tf_op jit(solution)/shard_map/ppermute | solution.py:434
  112.8 1.0 reshape.817.g_ref
  113.8 23.7 %shard_map.151 = f32[16,256]{1,0:T(8,128)} custom-call(bf16[64,16,256]{2,1,0:T(8,128)(2,1)} %reshape.817.g_ref), custom_call_target="tpu_custom_call" | custom-call | tf_op jit(solution)/shard_map/pallas_call | solution.py:336
  137.4 1.3 reshape.818
  138.8 1.0 pad_convert_fusion.1
  140.3 1.1 pad_convert_fusion
  143.6 16.4 %shard_map.150 = f32[16,256]{1,0:T(8,128)} custom-call(bf16[64,16,256]{2,1,0:T(8,128)(2,1)} %reshape.815.g_ref), custom_call_target="tpu_custom_call" | custom-call | tf_op jit(solution)/shard_map/pallas_call | solution.py:336
  160.0 1.3 reshape.816
  (77 shorter events, 11.7 us)
Async XLA Ops:
  0.6 100.0 %copy-start = (bf16[512,512]{1,0:T(8,128)(2,1)S(1)}, bf16[512,512]{1,0:T(8,128)(2,1)}, u32[]{:S(2)}) copy-start(bf16[512,512]{1,0:T(8,128)(2,1)} %param.33) | copy-start | bytes 1572868
  4.9 4.5 %copy-start.5 = (bf16[512,128]{1,0:T(8,128)(2,1)S(1)}, bf16[512,128]{1,0:T(8,128)(2,1)}, u32[]{:S(2)}) copy-start(bf16[512,128]{1,0:T(8,128)(2,1)} %param.26) | copy-start | bytes 393220
  4.9 4.5 %copy-start.9 = (f32[512]{0:T(512)S(1)}, f32[512]{0:T(512)}, u32[]{:S(2)}) copy-start(f32[512]{0:T(512)} %param.24) | copy-start | bytes 6148
  5.2 5.0 %copy-start.6 = (bf16[512,128]{1,0:T(8,128)(2,1)S(1)}, bf16[512,128]{1,0:T(8,128)(2,1)}, u32[]{:S(2)}) copy-start(bf16[512,128]{1,0:T(8,128)(2,1)} %param.27) | copy-start | bytes 393220
  5.2 5.2 %copy-start.4 = (bf16[512,128]{1,0:T(8,128)(2,1)S(1)}, bf16[512,128]{1,0:T(8,128)(2,1)}, u32[]{:S(2)}) copy-start(bf16[512,128]{1,0:T(8,128)(2,1)} %param.25) | copy-start | bytes 393220
  6.0 52.9 %copy-start.7 = (bf16[128,512]{1,0:T(8,128)(2,1)S(1)}, bf16[128,512]{1,0:T(8,128)(2,1)}, u32[]{:S(2)}) copy-start(bf16[128,512]{1,0:T(8,128)(2,1)} %param.28) | copy-start | bytes 393220
  6.0 72.6 %copy-start.1 = (bf16[512,512]{1,0:T(8,128)(2,1)S(1)}, bf16[512,512]{1,0:T(8,128)(2,1)}, u32[]{:S(2)}) copy-start(bf16[512,512]{1,0:T(8,128)(2,1)} %param.21) | copy-start | bytes 1572868
  9.2 72.0 %copy-start.10 = (bf16[512,512]{1,0:T(8,128)(2,1)S(1)}, bf16[512,512]{1,0:T(8,128)(2,1)}, u32[]{:S(2)}) copy-start(bf16[512,512]{1,0:T(8,128)(2,1)} %param.30) | copy-start | bytes 1572868
  9.2 72.0 %copy-start.11 = (f32[512]{0:T(512)S(1)}, f32[512]{0:T(512)}, u32[]{:S(2)}) copy-start(f32[512]{0:T(512)} %param.29) | copy-start | bytes 6148
  11.1 77.6 %copy-start.8 = (f32[27,512]{1,0:T(8,128)S(1)}, f32[27,512]{1,0:T(8,128)}, u32[]{:S(2)}) copy-start(f32[27,512]{1,0:T(8,128)} %param.31) | copy-start | bytes 165892
  82.8 16.4 %collective-permute-start = (bf16[16,16,512]{2,1,0:T(8,128)(2,1)S(1)}, bf16[16,16,512]{2,1,0:T(8,128)(2,1)S(1)}, u32[]{:S(2)}, u32[]{:S(2)}) collective-permute-start(bf16[16,16,512]{2,1,0:T(8,128)(2,1)S(1)} %bitcast.108), channel_id=1, source_target_pairs={{0,4},{4,8},{8,12},{12,16},{16,20},{20,24},{24,28},{28,32},{32,36}... | collective-permute-start | bytes 786440 | tf_op jit(solution)/shard_map/ppermute | solution.py:433
  85.3 14.5 %collective-permute-start.1 = (bf16[16,16,512]{2,1,0:T(8,128)(2,1)S(1)}, bf16[16,16,512]{2,1,0:T(8,128)(2,1)S(1)}, u32[]{:S(2)}, u32[]{:S(2)}) collective-permute-start(bf16[16,16,512]{2,1,0:T(8,128)(2,1)S(1)} %bitcast.106), channel_id=1, source_target_pairs={{4,0},{8,4},{12,8},{16,12},{20,16},{24,20},{28,24},{32,28},{36,32}... | collective-permute-start | bytes 786440 | tf_op jit(solution)/shard_map/ppermute | solution.py:434
  99.9 1.0 copy-start.3
  102.2 36.5 %collective-permute-start.2 = (bf16[16,16,512]{2,1,0:T(8,128)(2,1)}, bf16[16,16,512]{2,1,0:T(8,128)(2,1)}, u32[]{:S(2)}, u32[]{:S(2)}) collective-permute-start(bf16[16,16,512]{2,1,0:T(8,128)(2,1)} %bitcast.39), channel_id=1, source_target_pairs={{0,4},{4,8},{8,12},{12,16},{16,20},{20,24},{24,28},{28,32},{32,36}... | collective-permute-start | bytes 786440 | tf_op jit(solution)/shard_map/ppermute | solution.py:433
  108.7 31.6 %collective-permute-start.3 = (bf16[16,16,512]{2,1,0:T(8,128)(2,1)S(1)}, bf16[16,16,512]{2,1,0:T(8,128)(2,1)}, u32[]{:S(2)}, u32[]{:S(2)}) collective-permute-start(bf16[16,16,512]{2,1,0:T(8,128)(2,1)S(1)} %bitcast.107), channel_id=1, source_target_pairs={{4,0},{8,4},{12,8},{16,12},{20,16},{24,20},{28,24},{32,28},{36,32}... | collective-permute-start | bytes 786440 | tf_op jit(solution)/shard_map/ppermute | solution.py:434
  140.3 1.7 %copy-start.2 = (bf16[4,128,512]{2,1,0:T(8,128)(2,1)S(1)}, bf16[4,128,512]{2,1,0:T(8,128)(2,1)}, u32[]{:S(2)}) copy-start(bf16[4,128,512]{2,1,0:T(8,128)(2,1)} %shard_map.149) | copy-start | bytes 1572868

commit v15 on v13

--- a/solution.py
+++ b/solution.py
@@ -508,7 +508,9 @@
     normal_cdf = 0.5 * (1.0 + lax.erf(mixed * ROOT_HALF))
     normal_pdf = jnp.exp(-0.5 * mixed * mixed) * NORMAL_SCALE
     activated = (mixed * normal_cdf).astype(jnp.bfloat16)
-    grad_act = jnp.einsum("td,cd->tc", grad_out, w_down, preferred_element_type=jnp.float32)
+    grad_act = lax.optimization_barrier(
+        jnp.einsum("td,cd->tc", grad_out, w_down, preferred_element_type=jnp.float32)
+    )
     grad_mixed = (
         (grad_act * (normal_cdf + mixed * normal_pdf))
         .astype(jnp.bfloat16)

time: 156 us -> 155 us (level)
  no operation moved by 1% of the time
where the time goes in v15:
time: 155 us; the launch traced here: 154 us
  Pallas kernels  93.5 us (60%)
  other arithmetic  18 us (12%)
  waiting for transfers between devices  13.9 us (9%)
  starting transfers between devices  11.8 us (8%)
  local copies, waits for them, and re-layouts  7.99 us (5%)
  matrix products  7.98 us (5%)
    pallas_call x1, Pallas kernels, gather_attend(): pl.pallas_call(functools.partial(gather_kernel, row_size), out_shape=jax....  46.4 us
    pallas_call x1, Pallas kernels, slab_scatter(): pl.pallas_call(functools.partial(scatter_kernel, row_size), out_shape=jax...  29.3 us
    pallas_call x1, Pallas kernels, head_sum(): pl.pallas_call(functools.partial(head_sum_kernel, count), out_shape=jax.S...  17.7 us
    ppermute x2, waiting for transfers between devices, conv_with_halos(): above = lax.ppermute(cells[0], SLAB, [(i + 1, i) for i in range(ends)])  6.98 us
    add x2, other arithmetic, depth_conv(): result = result + window.astype(jnp.float32) * weights[offset]  6.97 us
    ppermute x2, waiting for transfers between devices, conv_with_halos(): lax.ppermute(cells[planes - 1], SLAB, [(i, i + 1) for i in range(ends)])  6.93 us
    ppermute x2, starting transfers between devices, conv_with_halos(): above = lax.ppermute(cells[0], SLAB, [(i + 1, i) for i in range(ends)])  6.13 us
    ppermute x2, starting transfers between devices, conv_with_halos(): lax.ppermute(cells[planes - 1], SLAB, [(i, i + 1) for i in range(ends)])  5.71 us
  transfers between devices with their start and end apart: 4, of which 3 were waited for; matrix products, arithmetic and copies ran while one was open for 6% of the time, Pallas kernels for 0%

profile of v15, /device:TPU:2, one launch (start us, length us, event | category | flops | bytes accessed | tf_op | source)
XLA Modules:
  0.0 154.4 jit_solution(17050509999208170658)
XLA Ops:
  1.1 1.2 convert_reduce_fusion
  2.3 1.3 fusion.3
  3.6 1.3 fusion.5
  6.0 3.2 %fusion.96 = (f32[64]{0:T(128)S(1)}, f32[64,512]{1,0:T(8,128)S(1)}) fusion(bf16[64,4096]{1,0:T(8,128)(2,1)S(1)} %reshape.796, bf16[4096,512]{1,0:T(8,128)(2,1)} %param.23), kind=kOutput, calls=%fused_computation.254 | convolution fusion | flops 268468160 | bytes 4849920 | tf_op jit(solution)/shard_map/dot_general | solution.py:471
  11.1 0.8 copy.25.q_ref
  12.5 46.4 %shard_map.148 = bf16[512,128]{1,0:T(8,128)(2,1)} custom-call(bf16[64,256]{1,0:T(8,128)(2,1)} %pad_maximum_fusion.3.x_ref, bf16[512,128]{1,0:T(8,128)(2,1)} %copy.25.q_ref), custom_call_target="tpu_custom_call" | custom-call | tf_op jit(solution)/shard_map/pallas_call | solution.py:171
  58.9 2.0 %convolution_convert_fusion.3 = bf16[512,512]{1,0:T(8,128)(2,1)} fusion(bf16[512,128]{1,0:T(8,128)(2,1)} %shard_map.148, bf16[128,512]{1,0:T(8,128)(2,1)S(1)} %copy-done.7), kind=kOutput, calls=%fused_computation.59 | convolution fusion | flops 67371008 | bytes 786432 | tf_op jit(solution)/shard_map/dot_general | solution.py:496
  60.9 17.7 %shard_map.149 = bf16[4,128,512]{2,1,0:T(8,128)(2,1)} custom-call(bf16[4,128,512]{2,1,0:T(8,128)(2,1)} %bitcast.105), custom_call_target="tpu_custom_call" | custom-call | tf_op jit(solution)/shard_map/pallas_call | solution.py:245
  78.6 1.3 fusion.17
  80.0 1.3 multiply_reduce_fusion
  81.9 2.6 %collective-permute-start = (bf16[16,16,512]{2,1,0:T(8,128)(2,1)S(1)}, bf16[16,16,512]{2,1,0:T(8,128)(2,1)S(1)}, u32[]{:S(2)}, u32[]{:S(2)}) collective-permute-start(bf16[16,16,512]{2,1,0:T(8,128)(2,1)S(1)} %bitcast.110), channel_id=1, source_target_pairs={{0,4},{4,8},{8,12},{12,16},{16,20},{20,24},{24,28},{28,32},{32,36}... | collective-permute-start | bytes 786440 | tf_op jit(solution)/shard_map/ppermute | solution.py:433
  84.6 3.4 %collective-permute-start.1 = (bf16[16,16,512]{2,1,0:T(8,128)(2,1)S(1)}, bf16[16,16,512]{2,1,0:T(8,128)(2,1)S(1)}, u32[]{:S(2)}, u32[]{:S(2)}) collective-permute-start(bf16[16,16,512]{2,1,0:T(8,128)(2,1)S(1)} %bitcast.109), channel_id=1, source_target_pairs={{4,0},{8,4},{12,8},{16,12},{20,16},{24,20},{28,24},{32,28},{36,32}... | collective-permute-start | bytes 786440 | tf_op jit(solution)/shard_map/ppermute | solution.py:434
  88.0 3.6 %multiply_add_fusion.1 = f32[2,16,16,512]{3,2,1,0:T(8,128)S(1)} fusion(bf16[2,16,16,512]{3,2,1,0:T(8,128)(2,1)S(1)} %bitcast.103, f32[512]{0:T(512)S(1)} %bitcast.177, f32[512]{0:T(512)S(1)} %bitcast.181, f32[512]{0:T(512)S(1)} %bitcast.149, f32[512]{0:T(512)S(1)} %bitcast.153, f32[512]{0:T(512)S(1)} %bitcast.157, f32[512]{0:T(512)S(1)} %bitcast.161, ...), kind=kLoop, calls=%fused_computation.81 | loop fusion | flops 20971520 | bytes 1628160 | tf_op jit(solution)/shard_map/add | solution.py:425
  92.1 6.4 %collective-permute-done = bf16[16,16,512]{2,1,0:T(8,128)(2,1)S(1)} collective-permute-done((bf16[16,16,512]{2,1,0:T(8,128)(2,1)S(1)}, bf16[16,16,512]{2,1,0:T(8,128)(2,1)S(1)}, u32[]{:S(2)}, u32[]{:S(2)}) %collective-permute-start) | collective-permute-done | bytes 262176 | tf_op jit(solution)/shard_map/ppermute | solution.py:433
  100.2 3.1 %collective-permute-start.2 = (bf16[16,16,512]{2,1,0:T(8,128)(2,1)S(1)}, bf16[16,16,512]{2,1,0:T(8,128)(2,1)S(1)}, u32[]{:S(2)}, u32[]{:S(2)}) collective-permute-start(bf16[16,16,512]{2,1,0:T(8,128)(2,1)S(1)} %bitcast.112), channel_id=1, source_target_pairs={{0,4},{4,8},{8,12},{12,16},{16,20},{20,24},{24,28},{28,32},{32,36}... | collective-permute-start | bytes 786440 | tf_op jit(solution)/shard_map/ppermute | solution.py:433
  103.3 3.4 %multiply_add_fusion = f32[2,16,16,512]{3,2,1,0:T(8,128)S(1)} fusion(bf16[2,16,16,512]{3,2,1,0:T(8,128)(2,1)S(1)} %bitcast.102, f32[512]{0:T(512)S(1)} %bitcast.179, f32[512]{0:T(512)S(1)} %bitcast.183, f32[512]{0:T(512)S(1)} %bitcast.151, f32[512]{0:T(512)S(1)} %bitcast.155, f32[512]{0:T(512)S(1)} %bitcast.159, f32[512]{0:T(512)S(1)} %bitcast.163, ...), kind=kLoop, calls=%fused_computation.80 | loop fusion | flops 20971520 | bytes 1628160 | tf_op jit(solution)/shard_map/add | solution.py:425
  106.7 2.8 %collective-permute-start.3 = (bf16[16,16,512]{2,1,0:T(8,128)(2,1)S(1)}, bf16[16,16,512]{2,1,0:T(8,128)(2,1)S(1)}, u32[]{:S(2)}, u32[]{:S(2)}) collective-permute-start(bf16[16,16,512]{2,1,0:T(8,128)(2,1)S(1)} %bitcast.111), channel_id=1, source_target_pairs={{4,0},{8,4},{12,8},{16,12},{20,16},{24,20},{28,24},{32,28},{36,32}... | collective-permute-start | bytes 786440 | tf_op jit(solution)/shard_map/ppermute | solution.py:434
  111.0 7.0 %collective-permute-done.3 = bf16[16,16,512]{2,1,0:T(8,128)(2,1)S(1)} collective-permute-done((bf16[16,16,512]{2,1,0:T(8,128)(2,1)S(1)}, bf16[16,16,512]{2,1,0:T(8,128)(2,1)S(1)}, u32[]{:S(2)}, u32[]{:S(2)}) %collective-permute-start.3) | collective-permute-done | bytes 262176 | tf_op jit(solution)/shard_map/ppermute | solution.py:434
  118.6 0.6 convolution_convert_fusion.1
  119.3 1.3 copy.26
  120.7 2.2 %convert_element_type.395.g_ref = bf16[64,16,512]{2,1,0:T(8,128)(2,1)} reshape(bf16[512,1024]{1,0:T(8,128)(2,1)} %copy.26) | data formatting | bytes 2097152 | tf_op jit(solution)/shard_map/convert_element_type | solution.py:335
  122.9 29.3 %shard_map.150 = f32[16,512]{1,0:T(8,128)} custom-call(bf16[64,16,512]{2,1,0:T(8,128)(2,1)} %convert_element_type.395.g_ref), custom_call_target="tpu_custom_call" | custom-call | tf_op jit(solution)/shard_map/pallas_call | solution.py:336
  152.2 0.8 reshape.809
  153.6 0.8 copy.34
  (76 shorter events, 9.4 us)
Async XLA Ops:
  0.6 91.0 %copy-start = (bf16[512,512]{1,0:T(8,128)(2,1)S(1)}, bf16[512,512]{1,0:T(8,128)(2,1)}, u32[]{:S(2)}) copy-start(bf16[512,512]{1,0:T(8,128)(2,1)} %param.33) | copy-start | bytes 1572868
  5.9 3.5 %copy-start.5 = (bf16[512,128]{1,0:T(8,128)(2,1)S(1)}, bf16[512,128]{1,0:T(8,128)(2,1)}, u32[]{:S(2)}) copy-start(bf16[512,128]{1,0:T(8,128)(2,1)} %param.26) | copy-start | bytes 393220
  5.9 3.5 %copy-start.9 = (f32[512]{0:T(512)S(1)}, f32[512]{0:T(512)}, u32[]{:S(2)}) copy-start(f32[512]{0:T(512)} %param.24) | copy-start | bytes 6148
  6.0 4.2 %copy-start.6 = (bf16[512,128]{1,0:T(8,128)(2,1)S(1)}, bf16[512,128]{1,0:T(8,128)(2,1)}, u32[]{:S(2)}) copy-start(bf16[512,128]{1,0:T(8,128)(2,1)} %param.27) | copy-start | bytes 393220
  6.0 4.4 %copy-start.4 = (bf16[512,128]{1,0:T(8,128)(2,1)S(1)}, bf16[512,128]{1,0:T(8,128)(2,1)}, u32[]{:S(2)}) copy-start(bf16[512,128]{1,0:T(8,128)(2,1)} %param.25) | copy-start | bytes 393220
  9.2 49.7 %copy-start.7 = (bf16[128,512]{1,0:T(8,128)(2,1)S(1)}, bf16[128,512]{1,0:T(8,128)(2,1)}, u32[]{:S(2)}) copy-start(bf16[128,512]{1,0:T(8,128)(2,1)} %param.28) | copy-start | bytes 393220
  10.4 68.2 %copy-start.1 = (bf16[512,512]{1,0:T(8,128)(2,1)S(1)}, bf16[512,512]{1,0:T(8,128)(2,1)}, u32[]{:S(2)}) copy-start(bf16[512,512]{1,0:T(8,128)(2,1)} %param.21) | copy-start | bytes 1572868
  12.5 68.8 %copy-start.10 = (bf16[512,512]{1,0:T(8,128)(2,1)S(1)}, bf16[512,512]{1,0:T(8,128)(2,1)}, u32[]{:S(2)}) copy-start(bf16[512,512]{1,0:T(8,128)(2,1)} %param.30) | copy-start | bytes 1572868
  12.5 68.8 %copy-start.11 = (f32[512]{0:T(512)S(1)}, f32[512]{0:T(512)}, u32[]{:S(2)}) copy-start(f32[512]{0:T(512)} %param.29) | copy-start | bytes 6148
  78.6 2.7 %copy-start.2 = (bf16[4,128,512]{2,1,0:T(8,128)(2,1)S(1)}, bf16[4,128,512]{2,1,0:T(8,128)(2,1)}, u32[]{:S(2)}) copy-start(bf16[4,128,512]{2,1,0:T(8,128)(2,1)} %shard_map.149) | copy-start | bytes 1572868
  81.3 6.6 %copy-start.8 = (f32[27,512]{1,0:T(8,128)S(1)}, f32[27,512]{1,0:T(8,128)}, u32[]{:S(2)}) copy-start(f32[27,512]{1,0:T(8,128)} %param.31) | copy-start | bytes 165892
  81.9 9.7 %copy-start.3 = (bf16[512,512]{1,0:T(8,128)(2,1)S(1)}, bf16[512,512]{1,0:T(8,128)(2,1)}, u32[]{:S(2)}) copy-start(bf16[512,512]{1,0:T(8,128)(2,1)} %param.32) | copy-start | bytes 1572868
  81.9 16.6 %collective-permute-start = (bf16[16,16,512]{2,1,0:T(8,128)(2,1)S(1)}, bf16[16,16,512]{2,1,0:T(8,128)(2,1)S(1)}, u32[]{:S(2)}, u32[]{:S(2)}) collective-permute-start(bf16[16,16,512]{2,1,0:T(8,128)(2,1)S(1)} %bitcast.110), channel_id=1, source_target_pairs={{0,4},{4,8},{8,12},{12,16},{16,20},{20,24},{24,28},{28,32},{32,36}... | collective-permute-start | bytes 786440 | tf_op jit(solution)/shard_map/ppermute | solution.py:433
  84.6 14.5 %collective-permute-start.1 = (bf16[16,16,512]{2,1,0:T(8,128)(2,1)S(1)}, bf16[16,16,512]{2,1,0:T(8,128)(2,1)S(1)}, u32[]{:S(2)}, u32[]{:S(2)}) collective-permute-start(bf16[16,16,512]{2,1,0:T(8,128)(2,1)S(1)} %bitcast.109), channel_id=1, source_target_pairs={{4,0},{8,4},{12,8},{16,12},{20,16},{24,20},{28,24},{32,28},{36,32}... | collective-permute-start | bytes 786440 | tf_op jit(solution)/shard_map/ppermute | solution.py:434
  100.2 10.2 %collective-permute-start.2 = (bf16[16,16,512]{2,1,0:T(8,128)(2,1)S(1)}, bf16[16,16,512]{2,1,0:T(8,128)(2,1)S(1)}, u32[]{:S(2)}, u32[]{:S(2)}) collective-permute-start(bf16[16,16,512]{2,1,0:T(8,128)(2,1)S(1)} %bitcast.112), channel_id=1, source_target_pairs={{0,4},{4,8},{8,12},{12,16},{16,20},{20,24},{24,28},{28,32},{32,36}... | collective-permute-start | bytes 786440 | tf_op jit(solution)/shard_map/ppermute | solution.py:433
  106.7 11.3 %collective-permute-start.3 = (bf16[16,16,512]{2,1,0:T(8,128)(2,1)S(1)}, bf16[16,16,512]{2,1,0:T(8,128)(2,1)S(1)}, u32[]{:S(2)}, u32[]{:S(2)}) collective-permute-start(bf16[16,16,512]{2,1,0:T(8,128)(2,1)S(1)} %bitcast.111), channel_id=1, source_target_pairs={{4,0},{8,4},{12,8},{16,12},{20,16},{24,20},{28,24},{32,28},{36,32}... | collective-permute-start | bytes 786440 | tf_op jit(solution)/shard_map/ppermute | solution.py:434

commit v16 on v15

--- a/solution.py
+++ b/solution.py
@@ -273,30 +273,51 @@
         return carry
 
     lax.fori_loop(1, row_size, greet, 0)
-    others = [lax.rem(own_y + j, y_count) for j in range(1, y_count)]
-    for other_y in others:
+    left_y = lax.rem(own_y + y_count - 1, y_count)
+    right_y = lax.rem(own_y + 1, y_count)
+    far_y = lax.rem(own_y + 2, y_count)
+    for other_y in (left_y, right_y):
         pl.semaphore_signal(
             barrier, inc=1, device_id=peer_id(other_y * row_size + spot), device_id_type=MESH
         )
-    pl.semaphore_wait(barrier, row_size + y_count - 2)
-
-    def across(target_y, source_y):
-        return pltpu.make_async_remote_copy(
-            src_ref=g_ref.at[pl.ds(target_y * row_size, row_size)],
-            dst_ref=slots_y.at[source_y],
-            send_sem=send_a.at[target_y],
-            recv_sem=recv_a.at[source_y],
+    pl.semaphore_wait(barrier, row_size + 1)
+    half = row_size // 2
+
+    def hop(src, dst, index, target_y):
+        return pltpu.make_async_remote_copy(
+            src_ref=src,
+            dst_ref=dst,
+            send_sem=send_a.at[index],
+            recv_sem=recv_a.at[index],
             device_id=peer_id(target_y * row_size + spot),
             device_id_type=MESH,
         )
 
-    for other_y in others:
-        across(other_y, own_y).start()
+    def rows_of(row_y, first, count):
+        return g_ref.at[pl.ds(row_y * row_size + first, count)]
+
+    near_right = hop(rows_of(right_y, 0, row_size), slots_y.at[0], 0, right_y)
+    near_left = hop(rows_of(left_y, 0, row_size), slots_y.at[1], 1, left_y)
+    low, high = pl.ds(0, half), pl.ds(half, half)
+    pass_right = hop(rows_of(far_y, 0, half), slots_y.at[2, low], 2, right_y)
+    pass_left = hop(rows_of(far_y, half, half), slots_y.at[2, high], 3, left_y)
+    for copy in (pass_right, pass_left, near_right, near_left):
+        copy.start()
+    pass_right.wait_recv()
+    on_right = hop(slots_y.at[2, low], slots_y.at[3, low], 4, right_y)
+    on_right.start()
+    pass_left.wait_recv()
+    on_left = hop(slots_y.at[2, high], slots_y.at[3, high], 5, left_y)
+    on_left.start()
     total = g_ref[pl.ds(own_y * row_size, row_size)].astype(jnp.float32)
-    for other_y in others:
-        across(other_y, own_y).wait_send()
-        across(other_y, other_y).wait_recv()
-        total = total + slots_y[other_y].astype(jnp.float32)
+    for copy in (near_right, near_left):
+        copy.wait_recv()
+    total = total + slots_y[0].astype(jnp.float32) + slots_y[1].astype(jnp.float32)
+    for copy in (on_right, on_left):
+        copy.wait_recv()
+    total = total + slots_y[3].astype(jnp.float32)
+    for copy in (pass_right, pass_left, near_right, near_left, on_right, on_left):
+        copy.wait_send()
     totals[...] = total
     sums[...] = total.astype(sums.dtype)
 
@@ -331,6 +352,7 @@
     total_rows, width = g.shape
     rows = total_rows // count
     y_count = count // row_size
+    assert y_count == 4
     tile_rows = 16
     g = g.astype(jnp.bfloat16).reshape(count, tile_rows, rows * width // tile_rows)
     summed = pl.pallas_call(
@@ -343,8 +365,8 @@
             pltpu.VMEM((row_size,) + g.shape[1:], jnp.float32),
             pltpu.VMEM((row_size,) + g.shape[1:], g.dtype),
             pltpu.VMEM((row_size,) + g.shape[1:], g.dtype),
-            pltpu.SemaphoreType.DMA((y_count,)),
-            pltpu.SemaphoreType.DMA((y_count,)),
+            pltpu.SemaphoreType.DMA((6,)),
+            pltpu.SemaphoreType.DMA((6,)),
             pltpu.SemaphoreType.DMA((row_size,)),
             pltpu.SemaphoreType.DMA((row_size,)),
         ],

time: 155 us -> 155 us (level)
  no operation moved by 1% of the time
where the time goes in v16:
time: 155 us
  Pallas kernels  93.7 us (60%)
  other arithmetic  18 us (12%)
  waiting for transfers between devices  13.9 us (9%)
  starting transfers between devices  11.8 us (8%)
  local copies, waits for them, and re-layouts  7.99 us (5%)
  matrix products  7.98 us (5%)
    pallas_call x1, Pallas kernels, gather_attend(): pl.pallas_call(functools.partial(gather_kernel, row_size), out_shape=jax....  46.4 us
    pallas_call x1, Pallas kernels, slab_scatter(): pl.pallas_call(functools.partial(scatter_kernel, row_size), out_shape=jax...  29.5 us
    pallas_call x1, Pallas kernels, head_sum(): pl.pallas_call(functools.partial(head_sum_kernel, count), out_shape=jax.S...  17.7 us
    ppermute x2, waiting for transfers between devices, conv_with_halos(): above = lax.ppermute(cells[0], SLAB, [(i + 1, i) for i in range(ends)])  6.98 us
    add x2, other arithmetic, depth_conv(): result = result + window.astype(jnp.float32) * weights[offset]  6.97 us
    ppermute x2, waiting for transfers between devices, conv_with_halos(): lax.ppermute(cells[planes - 1], SLAB, [(i, i + 1) for i in range(ends)])  6.93 us
    ppermute x2, starting transfers between devices, conv_with_halos(): above = lax.ppermute(cells[0], SLAB, [(i + 1, i) for i in range(ends)])  6.13 us
    ppermute x2, starting transfers between devices, conv_with_halos(): lax.ppermute(cells[planes - 1], SLAB, [(i, i + 1) for i in range(ends)])  5.71 us
  transfers between devices with their start and end apart: 4, of which 3 were waited for; matrix products, arithmetic and copies ran while one was open for 6% of the time, Pallas kernels for 0%

profile of v16, /device:TPU:2, one launch (start us, length us, event | category | flops | bytes accessed | tf_op | source)
XLA Modules:
  0.0 154.6 jit_solution(14677413197488093944)
XLA Ops:
  1.1 1.2 convert_reduce_fusion
  2.3 1.3 fusion.3
  3.6 1.3 fusion.5
  6.0 3.2 %fusion.96 = (f32[64]{0:T(128)S(1)}, f32[64,512]{1,0:T(8,128)S(1)}) fusion(bf16[64,4096]{1,0:T(8,128)(2,1)S(1)} %reshape.796, bf16[4096,512]{1,0:T(8,128)(2,1)} %param.23), kind=kOutput, calls=%fused_computation.254 | convolution fusion | flops 268468160 | bytes 4849920 | tf_op jit(solution)/shard_map/dot_general | solution.py:493
  11.1 0.8 copy.25.q_ref
  12.5 46.4 %shard_map.148 = bf16[512,128]{1,0:T(8,128)(2,1)} custom-call(bf16[64,256]{1,0:T(8,128)(2,1)} %pad_maximum_fusion.3.x_ref, bf16[512,128]{1,0:T(8,128)(2,1)} %copy.25.q_ref), custom_call_target="tpu_custom_call" | custom-call | tf_op jit(solution)/shard_map/pallas_call | solution.py:171
  58.9 2.0 %convolution_convert_fusion.3 = bf16[512,512]{1,0:T(8,128)(2,1)} fusion(bf16[512,128]{1,0:T(8,128)(2,1)} %shard_map.148, bf16[128,512]{1,0:T(8,128)(2,1)S(1)} %copy-done.7), kind=kOutput, calls=%fused_computation.59 | convolution fusion | flops 67371008 | bytes 786432 | tf_op jit(solution)/shard_map/dot_general | solution.py:518
  60.9 17.7 %shard_map.149 = bf16[4,128,512]{2,1,0:T(8,128)(2,1)} custom-call(bf16[4,128,512]{2,1,0:T(8,128)(2,1)} %bitcast.105), custom_call_target="tpu_custom_call" | custom-call | tf_op jit(solution)/shard_map/pallas_call | solution.py:245
  78.6 1.3 fusion.17
  80.0 1.3 multiply_reduce_fusion
  81.9 2.6 %collective-permute-start = (bf16[16,16,512]{2,1,0:T(8,128)(2,1)S(1)}, bf16[16,16,512]{2,1,0:T(8,128)(2,1)S(1)}, u32[]{:S(2)}, u32[]{:S(2)}) collective-permute-start(bf16[16,16,512]{2,1,0:T(8,128)(2,1)S(1)} %bitcast.110), channel_id=1, source_target_pairs={{0,4},{4,8},{8,12},{12,16},{16,20},{20,24},{24,28},{28,32},{32,36}... | collective-permute-start | bytes 786440 | tf_op jit(solution)/shard_map/ppermute | solution.py:455
  84.6 3.4 %collective-permute-start.1 = (bf16[16,16,512]{2,1,0:T(8,128)(2,1)S(1)}, bf16[16,16,512]{2,1,0:T(8,128)(2,1)S(1)}, u32[]{:S(2)}, u32[]{:S(2)}) collective-permute-start(bf16[16,16,512]{2,1,0:T(8,128)(2,1)S(1)} %bitcast.109), channel_id=1, source_target_pairs={{4,0},{8,4},{12,8},{16,12},{20,16},{24,20},{28,24},{32,28},{36,32}... | collective-permute-start | bytes 786440 | tf_op jit(solution)/shard_map/ppermute | solution.py:456
  88.0 3.6 %multiply_add_fusion.1 = f32[2,16,16,512]{3,2,1,0:T(8,128)S(1)} fusion(bf16[2,16,16,512]{3,2,1,0:T(8,128)(2,1)S(1)} %bitcast.103, f32[512]{0:T(512)S(1)} %bitcast.177, f32[512]{0:T(512)S(1)} %bitcast.181, f32[512]{0:T(512)S(1)} %bitcast.149, f32[512]{0:T(512)S(1)} %bitcast.153, f32[512]{0:T(512)S(1)} %bitcast.157, f32[512]{0:T(512)S(1)} %bitcast.161, ...), kind=kLoop, calls=%fused_computation.81 | loop fusion | flops 20971520 | bytes 1628160 | tf_op jit(solution)/shard_map/add | solution.py:447
  92.1 6.4 %collective-permute-done = bf16[16,16,512]{2,1,0:T(8,128)(2,1)S(1)} collective-permute-done((bf16[16,16,512]{2,1,0:T(8,128)(2,1)S(1)}, bf16[16,16,512]{2,1,0:T(8,128)(2,1)S(1)}, u32[]{:S(2)}, u32[]{:S(2)}) %collective-permute-start) | collective-permute-done | bytes 262176 | tf_op jit(solution)/shard_map/ppermute | solution.py:455
  100.2 3.1 %collective-permute-start.2 = (bf16[16,16,512]{2,1,0:T(8,128)(2,1)S(1)}, bf16[16,16,512]{2,1,0:T(8,128)(2,1)S(1)}, u32[]{:S(2)}, u32[]{:S(2)}) collective-permute-start(bf16[16,16,512]{2,1,0:T(8,128)(2,1)S(1)} %bitcast.112), channel_id=1, source_target_pairs={{0,4},{4,8},{8,12},{12,16},{16,20},{20,24},{24,28},{28,32},{32,36}... | collective-permute-start | bytes 786440 | tf_op jit(solution)/shard_map/ppermute | solution.py:455
  103.3 3.4 %multiply_add_fusion = f32[2,16,16,512]{3,2,1,0:T(8,128)S(1)} fusion(bf16[2,16,16,512]{3,2,1,0:T(8,128)(2,1)S(1)} %bitcast.102, f32[512]{0:T(512)S(1)} %bitcast.179, f32[512]{0:T(512)S(1)} %bitcast.183, f32[512]{0:T(512)S(1)} %bitcast.151, f32[512]{0:T(512)S(1)} %bitcast.155, f32[512]{0:T(512)S(1)} %bitcast.159, f32[512]{0:T(512)S(1)} %bitcast.163, ...), kind=kLoop, calls=%fused_computation.80 | loop fusion | flops 20971520 | bytes 1628160 | tf_op jit(solution)/shard_map/add | solution.py:447
  106.7 2.8 %collective-permute-start.3 = (bf16[16,16,512]{2,1,0:T(8,128)(2,1)S(1)}, bf16[16,16,512]{2,1,0:T(8,128)(2,1)S(1)}, u32[]{:S(2)}, u32[]{:S(2)}) collective-permute-start(bf16[16,16,512]{2,1,0:T(8,128)(2,1)S(1)} %bitcast.111), channel_id=1, source_target_pairs={{4,0},{8,4},{12,8},{16,12},{20,16},{24,20},{28,24},{32,28},{36,32}... | collective-permute-start | bytes 786440 | tf_op jit(solution)/shard_map/ppermute | solution.py:456
  111.0 7.0 %collective-permute-done.3 = bf16[16,16,512]{2,1,0:T(8,128)(2,1)S(1)} collective-permute-done((bf16[16,16,512]{2,1,0:T(8,128)(2,1)S(1)}, bf16[16,16,512]{2,1,0:T(8,128)(2,1)S(1)}, u32[]{:S(2)}, u32[]{:S(2)}) %collective-permute-start.3) | collective-permute-done | bytes 262176 | tf_op jit(solution)/shard_map/ppermute | solution.py:456
  118.6 0.6 convolution_convert_fusion.1
  119.3 1.3 copy.26
  120.7 2.2 %convert_element_type.395.g_ref = bf16[64,16,512]{2,1,0:T(8,128)(2,1)} reshape(bf16[512,1024]{1,0:T(8,128)(2,1)} %copy.26) | data formatting | bytes 2097152 | tf_op jit(solution)/shard_map/convert_element_type | solution.py:357
  122.9 29.5 %shard_map.150 = f32[16,512]{1,0:T(8,128)} custom-call(bf16[64,16,512]{2,1,0:T(8,128)(2,1)} %convert_element_type.395.g_ref), custom_call_target="tpu_custom_call" | custom-call | tf_op jit(solution)/shard_map/pallas_call | solution.py:358
  152.4 0.8 reshape.809
  153.8 0.8 copy.34
  (76 shorter events, 9.4 us)
Async XLA Ops:
  0.6 91.0 %copy-start = (bf16[512,512]{1,0:T(8,128)(2,1)S(1)}, bf16[512,512]{1,0:T(8,128)(2,1)}, u32[]{:S(2)}) copy-start(bf16[512,512]{1,0:T(8,128)(2,1)} %param.33) | copy-start | bytes 1572868
  5.9 3.5 %copy-start.5 = (bf16[512,128]{1,0:T(8,128)(2,1)S(1)}, bf16[512,128]{1,0:T(8,128)(2,1)}, u32[]{:S(2)}) copy-start(bf16[512,128]{1,0:T(8,128)(2,1)} %param.26) | copy-start | bytes 393220
  5.9 3.5 %copy-start.9 = (f32[512]{0:T(512)S(1)}, f32[512]{0:T(512)}, u32[]{:S(2)}) copy-start(f32[512]{0:T(512)} %param.24) | copy-start | bytes 6148
  6.0 4.2 %copy-start.6 = (bf16[512,128]{1,0:T(8,128)(2,1)S(1)}, bf16[512,128]{1,0:T(8,128)(2,1)}, u32[]{:S(2)}) copy-start(bf16[512,128]{1,0:T(8,128)(2,1)} %param.27) | copy-start | bytes 393220
  6.0 4.4 %copy-start.4 = (bf16[512,128]{1,0:T(8,128)(2,1)S(1)}, bf16[512,128]{1,0:T(8,128)(2,1)}, u32[]{:S(2)}) copy-start(bf16[512,128]{1,0:T(8,128)(2,1)} %param.25) | copy-start | bytes 393220
  9.2 49.7 %copy-start.7 = (bf16[128,512]{1,0:T(8,128)(2,1)S(1)}, bf16[128,512]{1,0:T(8,128)(2,1)}, u32[]{:S(2)}) copy-start(bf16[128,512]{1,0:T(8,128)(2,1)} %param.28) | copy-start | bytes 393220
  10.4 68.2 %copy-start.1 = (bf16[512,512]{1,0:T(8,128)(2,1)S(1)}, bf16[512,512]{1,0:T(8,128)(2,1)}, u32[]{:S(2)}) copy-start(bf16[512,512]{1,0:T(8,128)(2,1)} %param.21) | copy-start | bytes 1572868
  12.5 68.8 %copy-start.10 = (bf16[512,512]{1,0:T(8,128)(2,1)S(1)}, bf16[512,512]{1,0:T(8,128)(2,1)}, u32[]{:S(2)}) copy-start(bf16[512,512]{1,0:T(8,128)(2,1)} %param.30) | copy-start | bytes 1572868
  12.5 68.8 %copy-start.11 = (f32[512]{0:T(512)S(1)}, f32[512]{0:T(512)}, u32[]{:S(2)}) copy-start(f32[512]{0:T(512)} %param.29) | copy-start | bytes 6148
  78.6 2.7 %copy-start.2 = (bf16[4,128,512]{2,1,0:T(8,128)(2,1)S(1)}, bf16[4,128,512]{2,1,0:T(8,128)(2,1)}, u32[]{:S(2)}) copy-start(bf16[4,128,512]{2,1,0:T(8,128)(2,1)} %shard_map.149) | copy-start | bytes 1572868
  81.3 6.6 %copy-start.8 = (f32[27,512]{1,0:T(8,128)S(1)}, f32[27,512]{1,0:T(8,128)}, u32[]{:S(2)}) copy-start(f32[27,512]{1,0:T(8,128)} %param.31) | copy-start | bytes 165892
  81.9 9.7 %copy-start.3 = (bf16[512,512]{1,0:T(8,128)(2,1)S(1)}, bf16[512,512]{1,0:T(8,128)(2,1)}, u32[]{:S(2)}) copy-start(bf16[512,512]{1,0:T(8,128)(2,1)} %param.32) | copy-start | bytes 1572868
  81.9 16.6 %collective-permute-start = (bf16[16,16,512]{2,1,0:T(8,128)(2,1)S(1)}, bf16[16,16,512]{2,1,0:T(8,128)(2,1)S(1)}, u32[]{:S(2)}, u32[]{:S(2)}) collective-permute-start(bf16[16,16,512]{2,1,0:T(8,128)(2,1)S(1)} %bitcast.110), channel_id=1, source_target_pairs={{0,4},{4,8},{8,12},{12,16},{16,20},{20,24},{24,28},{28,32},{32,36}... | collective-permute-start | bytes 786440 | tf_op jit(solution)/shard_map/ppermute | solution.py:455
  84.6 14.5 %collective-permute-start.1 = (bf16[16,16,512]{2,1,0:T(8,128)(2,1)S(1)}, bf16[16,16,512]{2,1,0:T(8,128)(2,1)S(1)}, u32[]{:S(2)}, u32[]{:S(2)}) collective-permute-start(bf16[16,16,512]{2,1,0:T(8,128)(2,1)S(1)} %bitcast.109), channel_id=1, source_target_pairs={{4,0},{8,4},{12,8},{16,12},{20,16},{24,20},{28,24},{32,28},{36,32}... | collective-permute-start | bytes 786440 | tf_op jit(solution)/shard_map/ppermute | solution.py:456
  100.2 10.2 %collective-permute-start.2 = (bf16[16,16,512]{2,1,0:T(8,128)(2,1)S(1)}, bf16[16,16,512]{2,1,0:T(8,128)(2,1)S(1)}, u32[]{:S(2)}, u32[]{:S(2)}) collective-permute-start(bf16[16,16,512]{2,1,0:T(8,128)(2,1)S(1)} %bitcast.112), channel_id=1, source_target_pairs={{0,4},{4,8},{8,12},{12,16},{16,20},{20,24},{24,28},{28,32},{32,36}... | collective-permute-start | bytes 786440 | tf_op jit(solution)/shard_map/ppermute | solution.py:455
  106.7 11.3 %collective-permute-start.3 = (bf16[16,16,512]{2,1,0:T(8,128)(2,1)S(1)}, bf16[16,16,512]{2,1,0:T(8,128)(2,1)S(1)}, u32[]{:S(2)}, u32[]{:S(2)}) collective-permute-start(bf16[16,16,512]{2,1,0:T(8,128)(2,1)S(1)} %bitcast.111), channel_id=1, source_target_pairs={{4,0},{8,4},{12,8},{16,12},{20,16},{24,20},{28,24},{32,28},{36,32}... | collective-permute-start | bytes 786440 | tf_op jit(solution)/shard_map/ppermute | solution.py:456

commit v17 on v15

--- a/solution.py
+++ b/solution.py
@@ -327,12 +327,13 @@
     lax.fori_loop(1, row_size, finish_row, 0)
 
 
-def slab_scatter(g, count, row_size):
-    total_rows, width = g.shape
+def slab_scatter(blocks, count, row_size):
+    total_rows, width = blocks[0].shape
     rows = total_rows // count
     y_count = count // row_size
-    tile_rows = 16
-    g = g.astype(jnp.bfloat16).reshape(count, tile_rows, rows * width // tile_rows)
+    g = jnp.concatenate(
+        [block.astype(jnp.bfloat16).reshape(count, rows, width) for block in blocks], axis=1
+    )
     summed = pl.pallas_call(
         functools.partial(scatter_kernel, row_size),
         out_shape=jax.ShapeDtypeStruct(g.shape[1:], jnp.float32),
@@ -350,7 +351,7 @@
         ],
         compiler_params=pltpu.CompilerParams(collective_id=1, has_side_effects=True),
     )(g)
-    return summed.reshape(rows, width)
+    return [summed[i * rows : (i + 1) * rows] for i in range(len(blocks))]
 
 
 def layer_norm(values, scale_gain):
@@ -523,12 +524,10 @@
     )
     up_full = jnp.einsum("td,tc->dc", normed_ffn, grad_pre, preferred_element_type=jnp.float32)
     down_full = jnp.einsum("td,tc->dc", grad_out, activated, preferred_element_type=jnp.float32)
-    grads = slab_scatter(
-        jnp.concatenate([up_full, down_full], axis=1),
-        lax.psum(1, SLAB),
-        lax.psum(1, ("z", "xl")),
-    )
-    return (attended, grads[:, :channels], grads[:, channels:])
+    grad_up, grad_down = slab_scatter(
+        [up_full, down_full], lax.psum(1, SLAB), lax.psum(1, ("z", "xl"))
+    )
+    return (attended, grad_up, grad_down)
 
 
 def solution(mesh):

time: 155 us -> 152 us (0.981)
  local copies, waits for them, and re-layouts: 7.99 us -> 4.43 us
    convert_element_type x1 -> x0, local copies, waits for them, and re-layouts: 2.2 us -> none  [slab_scatter(): g.astype(jnp.bfloat16).reshape(count, tile_rows, rows * width // tile_rows)]
where the time goes in v17:
time: 152 us
  Pallas kernels  93.5 us (62%)
  other arithmetic  19.1 us (13%)
  waiting for transfers between devices  13.9 us (9%)
  starting transfers between devices  11.8 us (8%)
  matrix products  8.04 us (5%)
  local copies, waits for them, and re-layouts  4.43 us (3%)
    pallas_call x1, Pallas kernels, gather_attend(): pl.pallas_call(functools.partial(gather_kernel, row_size), out_shape=jax....  46.4 us
    pallas_call x1, Pallas kernels, slab_scatter(): pl.pallas_call(functools.partial(scatter_kernel, row_size), out_shape=jax...  29.3 us
    pallas_call x1, Pallas kernels, head_sum(): pl.pallas_call(functools.partial(head_sum_kernel, count), out_shape=jax.S...  17.7 us
    ppermute x2, waiting for transfers between devices, conv_with_halos(): above = lax.ppermute(cells[0], SLAB, [(i + 1, i) for i in range(ends)])  6.98 us
    add x2, other arithmetic, depth_conv(): result = result + window.astype(jnp.float32) * weights[offset]  6.97 us
    ppermute x2, waiting for transfers between devices, conv_with_halos(): lax.ppermute(cells[planes - 1], SLAB, [(i, i + 1) for i in range(ends)])  6.9 us
    ppermute x2, starting transfers between devices, conv_with_halos(): above = lax.ppermute(cells[0], SLAB, [(i + 1, i) for i in range(ends)])  6.13 us
    ppermute x2, starting transfers between devices, conv_with_halos(): lax.ppermute(cells[planes - 1], SLAB, [(i, i + 1) for i in range(ends)])  5.71 us
  transfers between devices with their start and end apart: 4, of which 3 were waited for; matrix products, arithmetic and copies ran while one was open for 6% of the time, Pallas kernels for 0%

profile of v17, /device:TPU:2, one launch (start us, length us, event | category | flops | bytes accessed | tf_op | source)
XLA Modules:
  0.0 151.9 jit_solution(9797207107398967726)
XLA Ops:
  1.1 1.2 convert_reduce_fusion
  2.3 1.3 fusion.4
  3.6 1.3 fusion.6
  6.0 3.2 %fusion.97 = (f32[64]{0:T(128)S(1)}, f32[64,512]{1,0:T(8,128)S(1)}) fusion(bf16[64,4096]{1,0:T(8,128)(2,1)S(1)} %reshape.796, bf16[4096,512]{1,0:T(8,128)(2,1)} %param.23), kind=kOutput, calls=%fused_computation.255 | convolution fusion | flops 268468160 | bytes 4849920 | tf_op jit(solution)/shard_map/dot_general | solution.py:472
  11.1 0.8 copy.23.q_ref
  11.9 0.6 pad_maximum_fusion.3.x_ref
  12.5 46.4 %shard_map.148 = bf16[512,128]{1,0:T(8,128)(2,1)} custom-call(bf16[64,256]{1,0:T(8,128)(2,1)} %pad_maximum_fusion.3.x_ref, bf16[512,128]{1,0:T(8,128)(2,1)} %copy.23.q_ref), custom_call_target="tpu_custom_call" | custom-call | tf_op jit(solution)/shard_map/pallas_call | solution.py:171
  58.9 2.0 %convolution_convert_fusion.3 = bf16[512,512]{1,0:T(8,128)(2,1)} fusion(bf16[512,128]{1,0:T(8,128)(2,1)} %shard_map.148, bf16[128,512]{1,0:T(8,128)(2,1)S(1)} %copy-done.7), kind=kOutput, calls=%fused_computation.59 | convolution fusion | flops 67371008 | bytes 786432 | tf_op jit(solution)/shard_map/dot_general | solution.py:497
  60.9 17.7 %shard_map.149 = bf16[4,128,512]{2,1,0:T(8,128)(2,1)} custom-call(bf16[4,128,512]{2,1,0:T(8,128)(2,1)} %bitcast.109), custom_call_target="tpu_custom_call" | custom-call | tf_op jit(solution)/shard_map/pallas_call | solution.py:245
  78.6 1.3 fusion.18
  80.0 1.3 multiply_reduce_fusion
  81.9 2.6 %collective-permute-start = (bf16[16,16,512]{2,1,0:T(8,128)(2,1)S(1)}, bf16[16,16,512]{2,1,0:T(8,128)(2,1)S(1)}, u32[]{:S(2)}, u32[]{:S(2)}) collective-permute-start(bf16[16,16,512]{2,1,0:T(8,128)(2,1)S(1)} %bitcast.114), channel_id=1, source_target_pairs={{0,4},{4,8},{8,12},{12,16},{16,20},{20,24},{24,28},{28,32},{32,36}... | collective-permute-start | bytes 786440 | tf_op jit(solution)/shard_map/ppermute | solution.py:434
  84.6 3.4 %collective-permute-start.1 = (bf16[16,16,512]{2,1,0:T(8,128)(2,1)S(1)}, bf16[16,16,512]{2,1,0:T(8,128)(2,1)S(1)}, u32[]{:S(2)}, u32[]{:S(2)}) collective-permute-start(bf16[16,16,512]{2,1,0:T(8,128)(2,1)S(1)} %bitcast.113), channel_id=1, source_target_pairs={{4,0},{8,4},{12,8},{16,12},{20,16},{24,20},{28,24},{32,28},{36,32}... | collective-permute-start | bytes 786440 | tf_op jit(solution)/shard_map/ppermute | solution.py:435
  88.0 3.6 %multiply_add_fusion.1 = f32[2,16,16,512]{3,2,1,0:T(8,128)S(1)} fusion(bf16[2,16,16,512]{3,2,1,0:T(8,128)(2,1)S(1)} %bitcast.107, f32[512]{0:T(512)S(1)} %bitcast.181, f32[512]{0:T(512)S(1)} %bitcast.185, f32[512]{0:T(512)S(1)} %bitcast.153, f32[512]{0:T(512)S(1)} %bitcast.157, f32[512]{0:T(512)S(1)} %bitcast.161, f32[512]{0:T(512)S(1)} %bitcast.165, ...), kind=kLoop, calls=%fused_computation.82 | loop fusion | flops 20971520 | bytes 1628160 | tf_op jit(solution)/shard_map/add | solution.py:426
  92.1 6.4 %collective-permute-done = bf16[16,16,512]{2,1,0:T(8,128)(2,1)S(1)} collective-permute-done((bf16[16,16,512]{2,1,0:T(8,128)(2,1)S(1)}, bf16[16,16,512]{2,1,0:T(8,128)(2,1)S(1)}, u32[]{:S(2)}, u32[]{:S(2)}) %collective-permute-start) | collective-permute-done | bytes 262176 | tf_op jit(solution)/shard_map/ppermute | solution.py:434
  100.2 3.1 %collective-permute-start.2 = (bf16[16,16,512]{2,1,0:T(8,128)(2,1)S(1)}, bf16[16,16,512]{2,1,0:T(8,128)(2,1)S(1)}, u32[]{:S(2)}, u32[]{:S(2)}) collective-permute-start(bf16[16,16,512]{2,1,0:T(8,128)(2,1)S(1)} %bitcast.116), channel_id=1, source_target_pairs={{0,4},{4,8},{8,12},{12,16},{16,20},{20,24},{24,28},{28,32},{32,36}... | collective-permute-start | bytes 786440 | tf_op jit(solution)/shard_map/ppermute | solution.py:434
  103.3 3.4 %multiply_add_fusion = f32[2,16,16,512]{3,2,1,0:T(8,128)S(1)} fusion(bf16[2,16,16,512]{3,2,1,0:T(8,128)(2,1)S(1)} %bitcast.106, f32[512]{0:T(512)S(1)} %bitcast.183, f32[512]{0:T(512)S(1)} %bitcast.187, f32[512]{0:T(512)S(1)} %bitcast.155, f32[512]{0:T(512)S(1)} %bitcast.159, f32[512]{0:T(512)S(1)} %bitcast.163, f32[512]{0:T(512)S(1)} %bitcast.167, ...), kind=kLoop, calls=%fused_computation.81 | loop fusion | flops 20971520 | bytes 1628160 | tf_op jit(solution)/shard_map/add | solution.py:426
  106.7 2.8 %collective-permute-start.3 = (bf16[16,16,512]{2,1,0:T(8,128)(2,1)S(1)}, bf16[16,16,512]{2,1,0:T(8,128)(2,1)S(1)}, u32[]{:S(2)}, u32[]{:S(2)}) collective-permute-start(bf16[16,16,512]{2,1,0:T(8,128)(2,1)S(1)} %bitcast.115), channel_id=1, source_target_pairs={{4,0},{8,4},{12,8},{16,12},{20,16},{24,20},{28,24},{32,28},{36,32}... | collective-permute-start | bytes 786440 | tf_op jit(solution)/shard_map/ppermute | solution.py:435
  111.0 7.0 %collective-permute-done.3 = bf16[16,16,512]{2,1,0:T(8,128)(2,1)S(1)} collective-permute-done((bf16[16,16,512]{2,1,0:T(8,128)(2,1)S(1)}, bf16[16,16,512]{2,1,0:T(8,128)(2,1)S(1)}, u32[]{:S(2)}, u32[]{:S(2)}) %collective-permute-start.3) | collective-permute-done | bytes 262176 | tf_op jit(solution)/shard_map/ppermute | solution.py:435
  118.6 0.7 fusion.2
  119.3 1.1 pad_maximum_fusion.g_ref
  120.4 29.3 %shard_map.150 = f32[16,512]{1,0:T(8,128)} custom-call(bf16[64,16,512]{2,1,0:T(8,128)(2,1)} %pad_maximum_fusion.g_ref), custom_call_target="tpu_custom_call" | custom-call | tf_op jit(solution)/shard_map/pallas_call | solution.py:337
  149.8 1.3 fusion.96
  151.1 0.8 copy.31
  (73 shorter events, 8.1 us)
Async XLA Ops:
  0.6 91.0 %copy-start = (bf16[512,512]{1,0:T(8,128)(2,1)S(1)}, bf16[512,512]{1,0:T(8,128)(2,1)}, u32[]{:S(2)}) copy-start(bf16[512,512]{1,0:T(8,128)(2,1)} %param.33) | copy-start | bytes 1572868
  5.9 3.5 %copy-start.5 = (bf16[512,128]{1,0:T(8,128)(2,1)S(1)}, bf16[512,128]{1,0:T(8,128)(2,1)}, u32[]{:S(2)}) copy-start(bf16[512,128]{1,0:T(8,128)(2,1)} %param.26) | copy-start | bytes 393220
  5.9 3.5 %copy-start.9 = (f32[512]{0:T(512)S(1)}, f32[512]{0:T(512)}, u32[]{:S(2)}) copy-start(f32[512]{0:T(512)} %param.24) | copy-start | bytes 6148
  6.0 4.2 %copy-start.6 = (bf16[512,128]{1,0:T(8,128)(2,1)S(1)}, bf16[512,128]{1,0:T(8,128)(2,1)}, u32[]{:S(2)}) copy-start(bf16[512,128]{1,0:T(8,128)(2,1)} %param.27) | copy-start | bytes 393220
  6.0 4.4 %copy-start.4 = (bf16[512,128]{1,0:T(8,128)(2,1)S(1)}, bf16[512,128]{1,0:T(8,128)(2,1)}, u32[]{:S(2)}) copy-start(bf16[512,128]{1,0:T(8,128)(2,1)} %param.25) | copy-start | bytes 393220
  9.2 49.7 %copy-start.7 = (bf16[128,512]{1,0:T(8,128)(2,1)S(1)}, bf16[128,512]{1,0:T(8,128)(2,1)}, u32[]{:S(2)}) copy-start(bf16[128,512]{1,0:T(8,128)(2,1)} %param.28) | copy-start | bytes 393220
  10.4 68.2 %copy-start.1 = (bf16[512,512]{1,0:T(8,128)(2,1)S(1)}, bf16[512,512]{1,0:T(8,128)(2,1)}, u32[]{:S(2)}) copy-start(bf16[512,512]{1,0:T(8,128)(2,1)} %param.21) | copy-start | bytes 1572868
  12.5 68.8 %copy-start.10 = (bf16[512,512]{1,0:T(8,128)(2,1)S(1)}, bf16[512,512]{1,0:T(8,128)(2,1)}, u32[]{:S(2)}) copy-start(bf16[512,512]{1,0:T(8,128)(2,1)} %param.30) | copy-start | bytes 1572868
  12.5 68.8 %copy-start.11 = (f32[512]{0:T(512)S(1)}, f32[512]{0:T(512)}, u32[]{:S(2)}) copy-start(f32[512]{0:T(512)} %param.29) | copy-start | bytes 6148
  78.6 2.7 %copy-start.2 = (bf16[4,128,512]{2,1,0:T(8,128)(2,1)S(1)}, bf16[4,128,512]{2,1,0:T(8,128)(2,1)}, u32[]{:S(2)}) copy-start(bf16[4,128,512]{2,1,0:T(8,128)(2,1)} %shard_map.149) | copy-start | bytes 1572868
  81.3 6.6 %copy-start.8 = (f32[27,512]{1,0:T(8,128)S(1)}, f32[27,512]{1,0:T(8,128)}, u32[]{:S(2)}) copy-start(f32[27,512]{1,0:T(8,128)} %param.31) | copy-start | bytes 165892
  81.9 9.7 %copy-start.3 = (bf16[512,512]{1,0:T(8,128)(2,1)S(1)}, bf16[512,512]{1,0:T(8,128)(2,1)}, u32[]{:S(2)}) copy-start(bf16[512,512]{1,0:T(8,128)(2,1)} %param.32) | copy-start | bytes 1572868
  81.9 16.6 %collective-permute-start = (bf16[16,16,512]{2,1,0:T(8,128)(2,1)S(1)}, bf16[16,16,512]{2,1,0:T(8,128)(2,1)S(1)}, u32[]{:S(2)}, u32[]{:S(2)}) collective-permute-start(bf16[16,16,512]{2,1,0:T(8,128)(2,1)S(1)} %bitcast.114), channel_id=1, source_target_pairs={{0,4},{4,8},{8,12},{12,16},{16,20},{20,24},{24,28},{28,32},{32,36}... | collective-permute-start | bytes 786440 | tf_op jit(solution)/shard_map/ppermute | solution.py:434
  84.6 14.5 %collective-permute-start.1 = (bf16[16,16,512]{2,1,0:T(8,128)(2,1)S(1)}, bf16[16,16,512]{2,1,0:T(8,128)(2,1)S(1)}, u32[]{:S(2)}, u32[]{:S(2)}) collective-permute-start(bf16[16,16,512]{2,1,0:T(8,128)(2,1)S(1)} %bitcast.113), channel_id=1, source_target_pairs={{4,0},{8,4},{12,8},{16,12},{20,16},{24,20},{28,24},{32,28},{36,32}... | collective-permute-start | bytes 786440 | tf_op jit(solution)/shard_map/ppermute | solution.py:435
  100.2 10.2 %collective-permute-start.2 = (bf16[16,16,512]{2,1,0:T(8,128)(2,1)S(1)}, bf16[16,16,512]{2,1,0:T(8,128)(2,1)S(1)}, u32[]{:S(2)}, u32[]{:S(2)}) collective-permute-start(bf16[16,16,512]{2,1,0:T(8,128)(2,1)S(1)} %bitcast.116), channel_id=1, source_target_pairs={{0,4},{4,8},{8,12},{12,16},{16,20},{20,24},{24,28},{28,32},{32,36}... | collective-permute-start | bytes 786440 | tf_op jit(solution)/shard_map/ppermute | solution.py:434
  106.7 11.3 %collective-permute-start.3 = (bf16[16,16,512]{2,1,0:T(8,128)(2,1)S(1)}, bf16[16,16,512]{2,1,0:T(8,128)(2,1)S(1)}, u32[]{:S(2)}, u32[]{:S(2)}) collective-permute-start(bf16[16,16,512]{2,1,0:T(8,128)(2,1)S(1)} %bitcast.115), channel_id=1, source_target_pairs={{4,0},{8,4},{12,8},{16,12},{20,16},{24,20},{28,24},{32,28},{36,32}... | collective-permute-start | bytes 786440 | tf_op jit(solution)/shard_map/ppermute | solution.py:435

commit v18 on v17

--- a/solution.py
+++ b/solution.py
@@ -260,7 +260,8 @@
 
 
 def scatter_kernel(
-    row_size, g_ref, out_ref, slots_y, totals, sums, slots_row, send_a, recv_a, send_b, recv_b
+    row_size, g_ref, up_ref, down_ref, slots_y, totals, sums, slots_row,
+    send_a, recv_a, send_b, recv_b,
 ):
     me = lax.axis_index(SLAB)
     own_y, spot = me // row_size, me % row_size
@@ -315,13 +316,17 @@
         return carry
 
     lax.fori_loop(1, row_size, start_row, 0)
-    out_ref[...] = totals[spot]
+    rows = up_ref.shape[0]
+    up_ref[...] = totals[spot, :rows]
+    down_ref[...] = totals[spot, rows:]
 
     def finish_row(k, carry):
         other = lax.rem(spot + k, row_size)
         along_row(other, spot).wait_send()
         along_row(other, other).wait_recv()
-        out_ref[...] += slots_row[other].astype(jnp.float32)
+        arrived = slots_row[other].astype(jnp.float32)
+        up_ref[...] += arrived[:rows]
+        down_ref[...] += arrived[rows:]
         return carry
 
     lax.fori_loop(1, row_size, finish_row, 0)
@@ -336,9 +341,9 @@
     )
     summed = pl.pallas_call(
         functools.partial(scatter_kernel, row_size),
-        out_shape=jax.ShapeDtypeStruct(g.shape[1:], jnp.float32),
+        out_shape=[jax.ShapeDtypeStruct((rows, width), jnp.float32)] * len(blocks),
         in_specs=[pl.BlockSpec(memory_space=pltpu.VMEM)],
-        out_specs=pl.BlockSpec(memory_space=pltpu.VMEM),
+        out_specs=[pl.BlockSpec(memory_space=pltpu.VMEM)] * len(blocks),
         scratch_shapes=[
             pltpu.VMEM((y_count, row_size) + g.shape[1:], g.dtype),
             pltpu.VMEM((row_size,) + g.shape[1:], jnp.float32),
@@ -351,7 +356,7 @@
         ],
         compiler_params=pltpu.CompilerParams(collective_id=1, has_side_effects=True),
     )(g)
-    return [summed[i * rows : (i + 1) * rows] for i in range(len(blocks))]
+    return summed
 
 
 def layer_norm(values, scale_gain):

time: 152 us -> 154 us (1.013)
    unnamed x25 -> x27, local copies, waits for them, and re-layouts: 0.86 us -> 3.51 us
where the time goes in v18:
time: 154 us; the launch traced here: 153 us
  Pallas kernels  93.5 us (61%)
  other arithmetic  19.1 us (12%)
  waiting for transfers between devices  13.9 us (9%)
  starting transfers between devices  11.8 us (8%)
  matrix products  8.04 us (5%)
  local copies, waits for them, and re-layouts  5.73 us (4%)
    pallas_call x1, Pallas kernels, gather_attend(): pl.pallas_call(functools.partial(gather_kernel, row_size), out_shape=jax....  46.4 us
    pallas_call x1, Pallas kernels, slab_scatter(): pl.pallas_call(functools.partial(scatter_kernel, row_size), out_shape=[ja...  29.3 us
    pallas_call x1, Pallas kernels, head_sum(): pl.pallas_call(functools.partial(head_sum_kernel, count), out_shape=jax.S...  17.7 us
    ppermute x2, waiting for transfers between devices, conv_with_halos(): above = lax.ppermute(cells[0], SLAB, [(i + 1, i) for i in range(ends)])  6.98 us
    add x2, other arithmetic, depth_conv(): result = result + window.astype(jnp.float32) * weights[offset]  6.97 us
    ppermute x2, waiting for transfers between devices, conv_with_halos(): lax.ppermute(cells[planes - 1], SLAB, [(i, i + 1) for i in range(ends)])  6.9 us
    ppermute x2, starting transfers between devices, conv_with_halos(): above = lax.ppermute(cells[0], SLAB, [(i + 1, i) for i in range(ends)])  6.13 us
    ppermute x2, starting transfers between devices, conv_with_halos(): lax.ppermute(cells[planes - 1], SLAB, [(i, i + 1) for i in range(ends)])  5.71 us
  transfers between devices with their start and end apart: 4, of which 3 were waited for; matrix products, arithmetic and copies ran while one was open for 6% of the time, Pallas kernels for 0%

profile of v18, /device:TPU:2, one launch (start us, length us, event | category | flops | bytes accessed | tf_op | source)
XLA Modules:
  0.0 153.2 jit_solution(17719804126249887469)
XLA Ops:
  1.1 1.2 convert_reduce_fusion
  2.3 1.3 fusion.4
  3.6 1.3 fusion.6
  6.0 3.2 %fusion.96 = (f32[64]{0:T(128)S(1)}, f32[64,512]{1,0:T(8,128)S(1)}) fusion(bf16[64,4096]{1,0:T(8,128)(2,1)S(1)} %reshape.796, bf16[4096,512]{1,0:T(8,128)(2,1)} %param.23), kind=kOutput, calls=%fused_computation.254 | convolution fusion | flops 268468160 | bytes 4849920 | tf_op jit(solution)/shard_map/dot_general | solution.py:477
  11.1 0.8 copy.23.q_ref
  12.5 46.4 %shard_map.148 = bf16[512,128]{1,0:T(8,128)(2,1)} custom-call(bf16[64,256]{1,0:T(8,128)(2,1)} %pad_maximum_fusion.3.x_ref, bf16[512,128]{1,0:T(8,128)(2,1)} %copy.23.q_ref), custom_call_target="tpu_custom_call" | custom-call | tf_op jit(solution)/shard_map/pallas_call | solution.py:171
  58.9 2.0 %convolution_convert_fusion.3 = bf16[512,512]{1,0:T(8,128)(2,1)} fusion(bf16[512,128]{1,0:T(8,128)(2,1)} %shard_map.148, bf16[128,512]{1,0:T(8,128)(2,1)S(1)} %copy-done.7), kind=kOutput, calls=%fused_computation.59 | convolution fusion | flops 67371008 | bytes 786432 | tf_op jit(solution)/shard_map/dot_general | solution.py:502
  60.9 17.7 %shard_map.149 = bf16[4,128,512]{2,1,0:T(8,128)(2,1)} custom-call(bf16[4,128,512]{2,1,0:T(8,128)(2,1)} %bitcast.109), custom_call_target="tpu_custom_call" | custom-call | tf_op jit(solution)/shard_map/pallas_call | solution.py:245
  78.6 1.3 fusion.18
  80.0 1.3 multiply_reduce_fusion
  81.9 2.6 %collective-permute-start = (bf16[16,16,512]{2,1,0:T(8,128)(2,1)S(1)}, bf16[16,16,512]{2,1,0:T(8,128)(2,1)S(1)}, u32[]{:S(2)}, u32[]{:S(2)}) collective-permute-start(bf16[16,16,512]{2,1,0:T(8,128)(2,1)S(1)} %bitcast.114), channel_id=1, source_target_pairs={{0,4},{4,8},{8,12},{12,16},{16,20},{20,24},{24,28},{28,32},{32,36}... | collective-permute-start | bytes 786440 | tf_op jit(solution)/shard_map/ppermute | solution.py:439
  84.6 3.4 %collective-permute-start.1 = (bf16[16,16,512]{2,1,0:T(8,128)(2,1)S(1)}, bf16[16,16,512]{2,1,0:T(8,128)(2,1)S(1)}, u32[]{:S(2)}, u32[]{:S(2)}) collective-permute-start(bf16[16,16,512]{2,1,0:T(8,128)(2,1)S(1)} %bitcast.113), channel_id=1, source_target_pairs={{4,0},{8,4},{12,8},{16,12},{20,16},{24,20},{28,24},{32,28},{36,32}... | collective-permute-start | bytes 786440 | tf_op jit(solution)/shard_map/ppermute | solution.py:440
  88.0 3.6 %multiply_add_fusion.1 = f32[2,16,16,512]{3,2,1,0:T(8,128)S(1)} fusion(bf16[2,16,16,512]{3,2,1,0:T(8,128)(2,1)S(1)} %bitcast.107, f32[512]{0:T(512)S(1)} %bitcast.181, f32[512]{0:T(512)S(1)} %bitcast.185, f32[512]{0:T(512)S(1)} %bitcast.153, f32[512]{0:T(512)S(1)} %bitcast.157, f32[512]{0:T(512)S(1)} %bitcast.161, f32[512]{0:T(512)S(1)} %bitcast.165, ...), kind=kLoop, calls=%fused_computation.82 | loop fusion | flops 20971520 | bytes 1628160 | tf_op jit(solution)/shard_map/add | solution.py:431
  92.1 6.4 %collective-permute-done = bf16[16,16,512]{2,1,0:T(8,128)(2,1)S(1)} collective-permute-done((bf16[16,16,512]{2,1,0:T(8,128)(2,1)S(1)}, bf16[16,16,512]{2,1,0:T(8,128)(2,1)S(1)}, u32[]{:S(2)}, u32[]{:S(2)}) %collective-permute-start) | collective-permute-done | bytes 262176 | tf_op jit(solution)/shard_map/ppermute | solution.py:439
  100.2 3.1 %collective-permute-start.2 = (bf16[16,16,512]{2,1,0:T(8,128)(2,1)S(1)}, bf16[16,16,512]{2,1,0:T(8,128)(2,1)S(1)}, u32[]{:S(2)}, u32[]{:S(2)}) collective-permute-start(bf16[16,16,512]{2,1,0:T(8,128)(2,1)S(1)} %bitcast.116), channel_id=1, source_target_pairs={{0,4},{4,8},{8,12},{12,16},{16,20},{20,24},{24,28},{28,32},{32,36}... | collective-permute-start | bytes 786440 | tf_op jit(solution)/shard_map/ppermute | solution.py:439
  103.3 3.4 %multiply_add_fusion = f32[2,16,16,512]{3,2,1,0:T(8,128)S(1)} fusion(bf16[2,16,16,512]{3,2,1,0:T(8,128)(2,1)S(1)} %bitcast.106, f32[512]{0:T(512)S(1)} %bitcast.183, f32[512]{0:T(512)S(1)} %bitcast.187, f32[512]{0:T(512)S(1)} %bitcast.155, f32[512]{0:T(512)S(1)} %bitcast.159, f32[512]{0:T(512)S(1)} %bitcast.163, f32[512]{0:T(512)S(1)} %bitcast.167, ...), kind=kLoop, calls=%fused_computation.81 | loop fusion | flops 20971520 | bytes 1628160 | tf_op jit(solution)/shard_map/add | solution.py:431
  106.7 2.8 %collective-permute-start.3 = (bf16[16,16,512]{2,1,0:T(8,128)(2,1)S(1)}, bf16[16,16,512]{2,1,0:T(8,128)(2,1)S(1)}, u32[]{:S(2)}, u32[]{:S(2)}) collective-permute-start(bf16[16,16,512]{2,1,0:T(8,128)(2,1)S(1)} %bitcast.115), channel_id=1, source_target_pairs={{4,0},{8,4},{12,8},{16,12},{20,16},{24,20},{28,24},{32,28},{36,32}... | collective-permute-start | bytes 786440 | tf_op jit(solution)/shard_map/ppermute | solution.py:440
  111.0 7.0 %collective-permute-done.3 = bf16[16,16,512]{2,1,0:T(8,128)(2,1)S(1)} collective-permute-done((bf16[16,16,512]{2,1,0:T(8,128)(2,1)S(1)}, bf16[16,16,512]{2,1,0:T(8,128)(2,1)S(1)}, u32[]{:S(2)}, u32[]{:S(2)}) %collective-permute-start.3) | collective-permute-done | bytes 262176 | tf_op jit(solution)/shard_map/ppermute | solution.py:440
  118.6 0.7 fusion.2
  119.3 1.1 pad_maximum_fusion.g_ref
  120.4 29.3 %shard_map.150 = (f32[8,512]{1,0:T(8,128)}, f32[8,512]{1,0:T(8,128)}) custom-call(bf16[64,16,512]{2,1,0:T(8,128)(2,1)} %pad_maximum_fusion.g_ref), custom_call_target="tpu_custom_call" | custom-call | tf_op jit(solution)/shard_map/pallas_call | solution.py:342
  149.8 0.8 copy.33
  150.6 1.3 copy.34
  151.9 1.3 copy.35
  (74 shorter events, 8.7 us)
Async XLA Ops:
  0.6 91.0 %copy-start = (bf16[512,512]{1,0:T(8,128)(2,1)S(1)}, bf16[512,512]{1,0:T(8,128)(2,1)}, u32[]{:S(2)}) copy-start(bf16[512,512]{1,0:T(8,128)(2,1)} %param.33) | copy-start | bytes 1572868
  5.9 3.5 %copy-start.5 = (bf16[512,128]{1,0:T(8,128)(2,1)S(1)}, bf16[512,128]{1,0:T(8,128)(2,1)}, u32[]{:S(2)}) copy-start(bf16[512,128]{1,0:T(8,128)(2,1)} %param.26) | copy-start | bytes 393220
  5.9 3.5 %copy-start.9 = (f32[512]{0:T(512)S(1)}, f32[512]{0:T(512)}, u32[]{:S(2)}) copy-start(f32[512]{0:T(512)} %param.24) | copy-start | bytes 6148
  6.0 4.2 %copy-start.6 = (bf16[512,128]{1,0:T(8,128)(2,1)S(1)}, bf16[512,128]{1,0:T(8,128)(2,1)}, u32[]{:S(2)}) copy-start(bf16[512,128]{1,0:T(8,128)(2,1)} %param.27) | copy-start | bytes 393220
  6.0 4.4 %copy-start.4 = (bf16[512,128]{1,0:T(8,128)(2,1)S(1)}, bf16[512,128]{1,0:T(8,128)(2,1)}, u32[]{:S(2)}) copy-start(bf16[512,128]{1,0:T(8,128)(2,1)} %param.25) | copy-start | bytes 393220
  9.2 49.7 %copy-start.7 = (bf16[128,512]{1,0:T(8,128)(2,1)S(1)}, bf16[128,512]{1,0:T(8,128)(2,1)}, u32[]{:S(2)}) copy-start(bf16[128,512]{1,0:T(8,128)(2,1)} %param.28) | copy-start | bytes 393220
  10.4 68.2 %copy-start.1 = (bf16[512,512]{1,0:T(8,128)(2,1)S(1)}, bf16[512,512]{1,0:T(8,128)(2,1)}, u32[]{:S(2)}) copy-start(bf16[512,512]{1,0:T(8,128)(2,1)} %param.21) | copy-start | bytes 1572868
  12.5 68.8 %copy-start.10 = (bf16[512,512]{1,0:T(8,128)(2,1)S(1)}, bf16[512,512]{1,0:T(8,128)(2,1)}, u32[]{:S(2)}) copy-start(bf16[512,512]{1,0:T(8,128)(2,1)} %param.30) | copy-start | bytes 1572868
  12.5 68.8 %copy-start.11 = (f32[512]{0:T(512)S(1)}, f32[512]{0:T(512)}, u32[]{:S(2)}) copy-start(f32[512]{0:T(512)} %param.29) | copy-start | bytes 6148
  78.6 2.7 %copy-start.2 = (bf16[4,128,512]{2,1,0:T(8,128)(2,1)S(1)}, bf16[4,128,512]{2,1,0:T(8,128)(2,1)}, u32[]{:S(2)}) copy-start(bf16[4,128,512]{2,1,0:T(8,128)(2,1)} %shard_map.149) | copy-start | bytes 1572868
  81.3 6.6 %copy-start.8 = (f32[27,512]{1,0:T(8,128)S(1)}, f32[27,512]{1,0:T(8,128)}, u32[]{:S(2)}) copy-start(f32[27,512]{1,0:T(8,128)} %param.31) | copy-start | bytes 165892
  81.9 9.7 %copy-start.3 = (bf16[512,512]{1,0:T(8,128)(2,1)S(1)}, bf16[512,512]{1,0:T(8,128)(2,1)}, u32[]{:S(2)}) copy-start(bf16[512,512]{1,0:T(8,128)(2,1)} %param.32) | copy-start | bytes 1572868
  81.9 16.6 %collective-permute-start = (bf16[16,16,512]{2,1,0:T(8,128)(2,1)S(1)}, bf16[16,16,512]{2,1,0:T(8,128)(2,1)S(1)}, u32[]{:S(2)}, u32[]{:S(2)}) collective-permute-start(bf16[16,16,512]{2,1,0:T(8,128)(2,1)S(1)} %bitcast.114), channel_id=1, source_target_pairs={{0,4},{4,8},{8,12},{12,16},{16,20},{20,24},{24,28},{28,32},{32,36}... | collective-permute-start | bytes 786440 | tf_op jit(solution)/shard_map/ppermute | solution.py:439
  84.6 14.5 %collective-permute-start.1 = (bf16[16,16,512]{2,1,0:T(8,128)(2,1)S(1)}, bf16[16,16,512]{2,1,0:T(8,128)(2,1)S(1)}, u32[]{:S(2)}, u32[]{:S(2)}) collective-permute-start(bf16[16,16,512]{2,1,0:T(8,128)(2,1)S(1)} %bitcast.113), channel_id=1, source_target_pairs={{4,0},{8,4},{12,8},{16,12},{20,16},{24,20},{28,24},{32,28},{36,32}... | collective-permute-start | bytes 786440 | tf_op jit(solution)/shard_map/ppermute | solution.py:440
  100.2 10.2 %collective-permute-start.2 = (bf16[16,16,512]{2,1,0:T(8,128)(2,1)S(1)}, bf16[16,16,512]{2,1,0:T(8,128)(2,1)S(1)}, u32[]{:S(2)}, u32[]{:S(2)}) collective-permute-start(bf16[16,16,512]{2,1,0:T(8,128)(2,1)S(1)} %bitcast.116), channel_id=1, source_target_pairs={{0,4},{4,8},{8,12},{12,16},{16,20},{20,24},{24,28},{28,32},{32,36}... | collective-permute-start | bytes 786440 | tf_op jit(solution)/shard_map/ppermute | solution.py:439
  106.7 11.3 %collective-permute-start.3 = (bf16[16,16,512]{2,1,0:T(8,128)(2,1)S(1)}, bf16[16,16,512]{2,1,0:T(8,128)(2,1)S(1)}, u32[]{:S(2)}, u32[]{:S(2)}) collective-permute-start(bf16[16,16,512]{2,1,0:T(8,128)(2,1)S(1)} %bitcast.115), channel_id=1, source_target_pairs={{4,0},{8,4},{12,8},{16,12},{20,16},{24,20},{28,24},{32,28},{36,32}... | collective-permute-start | bytes 786440 | tf_op jit(solution)/shard_map/ppermute | solution.py:440

commit v19 on v17

--- a/solution.py
+++ b/solution.py
@@ -472,10 +472,14 @@
     reduced = jnp.dot(patches, w_reduce, preferred_element_type=jnp.float32)
     key_input = layer_norm(reduced, gain_keys).astype(jnp.bfloat16)
     tok_cos, tok_sin = token_tables(slab_index * CZ, CZ, HEAD)
-    queries = jnp.dot(normed, w_query, preferred_element_type=jnp.float32).reshape(
-        tok_rows, heads_dev, HEAD
-    )
-    queries = rotate(queries, tok_cos, tok_sin).astype(jnp.bfloat16)
+    queries = jnp.dot(normed, w_query, preferred_element_type=jnp.float32)
+    queries = jnp.concatenate(
+        [
+            rotate(queries[:, head * HEAD : (head + 1) * HEAD], tok_cos[:, 0], tok_sin[:, 0])
+            for head in range(heads_dev)
+        ],
+        axis=1,
+    ).astype(jnp.bfloat16)
     local_rows = key_input.shape[0]
     own_cos, own_sin = key_tables(slab_index * local_rows, local_rows, HEAD)
     own_keys = jnp.dot(key_input, w_key, preferred_element_type=jnp.float32).reshape(
@@ -489,7 +493,7 @@
     pieces = jnp.concatenate([own_keys.reshape(local_rows, key_width), own_values], axis=1)
     heads_out = gather_attend(
         pieces,
-        queries.reshape(tok_rows, key_width),
+        queries,
         lax.psum(1, SLAB),
         lax.psum(1, ("z", "xl")),
         heads_dev,

time: 152 us -> 154 us (1.013)
  other arithmetic: 19.1 us -> 20.9 us
where the time goes in v19:
time: 154 us; the launch traced here: 153 us
  Pallas kernels  93.6 us (61%)
  other arithmetic  20.9 us (14%)
  waiting for transfers between devices  13.9 us (9%)
  starting transfers between devices  11.8 us (8%)
  matrix products  8.03 us (5%)
  local copies, waits for them, and re-layouts  3.67 us (2%)
    pallas_call x1, Pallas kernels, gather_attend(): pl.pallas_call(functools.partial(gather_kernel, row_size), out_shape=jax....  46.5 us
    pallas_call x1, Pallas kernels, slab_scatter(): pl.pallas_call(functools.partial(scatter_kernel, row_size), out_shape=jax...  29.3 us
    pallas_call x1, Pallas kernels, head_sum(): pl.pallas_call(functools.partial(head_sum_kernel, count), out_shape=jax.S...  17.7 us
    add x2, other arithmetic, depth_conv(): result = result + window.astype(jnp.float32) * weights[offset]  6.97 us
    ppermute x2, waiting for transfers between devices, conv_with_halos(): above = lax.ppermute(cells[0], SLAB, [(i + 1, i) for i in range(ends)])  6.93 us
    ppermute x2, waiting for transfers between devices, conv_with_halos(): lax.ppermute(cells[planes - 1], SLAB, [(i, i + 1) for i in range(ends)])  6.93 us
    ppermute x2, starting transfers between devices, conv_with_halos(): above = lax.ppermute(cells[0], SLAB, [(i + 1, i) for i in range(ends)])  6.07 us
    ppermute x2, starting transfers between devices, conv_with_halos(): lax.ppermute(cells[planes - 1], SLAB, [(i, i + 1) for i in range(ends)])  5.77 us
  transfers between devices with their start and end apart: 4, of which 3 were waited for; matrix products, arithmetic and copies ran while one was open for 6% of the time, Pallas kernels for 0%

profile of v19, /device:TPU:2, one launch (start us, length us, event | category | flops | bytes accessed | tf_op | source)
XLA Modules:
  0.0 153.0 jit_solution(9512453547061746441)
XLA Ops:
  1.1 1.2 convert_reduce_fusion
  2.3 1.3 fusion.4
  3.6 1.3 fusion.6
  6.0 3.2 %fusion.97 = (f32[64]{0:T(128)S(1)}, f32[64,512]{1,0:T(8,128)S(1)}) fusion(bf16[64,4096]{1,0:T(8,128)(2,1)S(1)} %reshape.628, bf16[4096,512]{1,0:T(8,128)(2,1)} %param.23), kind=kOutput, calls=%fused_computation.257 | convolution fusion | flops 268468160 | bytes 4849920 | tf_op jit(solution)/shard_map/dot_general | solution.py:472
  11.3 1.4 subtract_convert_fusion.1
  12.7 0.8 pad_maximum_fusion.1.q_ref
  13.5 46.5 %shard_map.148 = bf16[512,128]{1,0:T(8,128)(2,1)} custom-call(bf16[64,256]{1,0:T(8,128)(2,1)} %pad_maximum_fusion.3.x_ref, bf16[512,128]{1,0:T(8,128)(2,1)} %pad_maximum_fusion.1.q_ref), custom_call_target="tpu_custom_call" | custom-call | tf_op jit(solution)/shard_map/pallas_call | solution.py:171
  60.1 2.0 %convolution_convert_fusion.3 = bf16[512,512]{1,0:T(8,128)(2,1)} fusion(bf16[512,128]{1,0:T(8,128)(2,1)} %shard_map.148, bf16[128,512]{1,0:T(8,128)(2,1)S(1)} %copy-done.7), kind=kOutput, calls=%fused_computation.59 | convolution fusion | flops 67371008 | bytes 786432 | tf_op jit(solution)/shard_map/dot_general | solution.py:501
  62.1 17.7 %shard_map.149 = bf16[4,128,512]{2,1,0:T(8,128)(2,1)} custom-call(bf16[4,128,512]{2,1,0:T(8,128)(2,1)} %bitcast.107), custom_call_target="tpu_custom_call" | custom-call | tf_op jit(solution)/shard_map/pallas_call | solution.py:245
  79.8 1.3 fusion.18
  81.1 1.3 multiply_reduce_fusion
  83.1 2.7 %collective-permute-start = (bf16[16,16,512]{2,1,0:T(8,128)(2,1)S(1)}, bf16[16,16,512]{2,1,0:T(8,128)(2,1)S(1)}, u32[]{:S(2)}, u32[]{:S(2)}) collective-permute-start(bf16[16,16,512]{2,1,0:T(8,128)(2,1)S(1)} %bitcast.110), channel_id=1, source_target_pairs={{0,4},{4,8},{8,12},{12,16},{16,20},{20,24},{24,28},{28,32},{32,36}... | collective-permute-start | bytes 786440 | tf_op jit(solution)/shard_map/ppermute | solution.py:434
  85.8 3.3 %collective-permute-start.1 = (bf16[16,16,512]{2,1,0:T(8,128)(2,1)S(1)}, bf16[16,16,512]{2,1,0:T(8,128)(2,1)S(1)}, u32[]{:S(2)}, u32[]{:S(2)}) collective-permute-start(bf16[16,16,512]{2,1,0:T(8,128)(2,1)S(1)} %bitcast.109), channel_id=1, source_target_pairs={{4,0},{8,4},{12,8},{16,12},{20,16},{24,20},{28,24},{32,28},{36,32}... | collective-permute-start | bytes 786440 | tf_op jit(solution)/shard_map/ppermute | solution.py:435
  89.2 3.6 %multiply_add_fusion.1 = f32[2,16,16,512]{3,2,1,0:T(8,128)S(1)} fusion(bf16[2,16,16,512]{3,2,1,0:T(8,128)(2,1)S(1)} %bitcast.105, f32[512]{0:T(512)S(1)} %bitcast.177, f32[512]{0:T(512)S(1)} %bitcast.181, f32[512]{0:T(512)S(1)} %bitcast.149, f32[512]{0:T(512)S(1)} %bitcast.153, f32[512]{0:T(512)S(1)} %bitcast.157, f32[512]{0:T(512)S(1)} %bitcast.161, ...), kind=kLoop, calls=%fused_computation.82 | loop fusion | flops 20971520 | bytes 1628160 | tf_op jit(solution)/shard_map/add | solution.py:426
  93.3 6.4 %collective-permute-done = bf16[16,16,512]{2,1,0:T(8,128)(2,1)S(1)} collective-permute-done((bf16[16,16,512]{2,1,0:T(8,128)(2,1)S(1)}, bf16[16,16,512]{2,1,0:T(8,128)(2,1)S(1)}, u32[]{:S(2)}, u32[]{:S(2)}) %collective-permute-start) | collective-permute-done | bytes 262176 | tf_op jit(solution)/shard_map/ppermute | solution.py:434
  101.3 3.1 %collective-permute-start.2 = (bf16[16,16,512]{2,1,0:T(8,128)(2,1)S(1)}, bf16[16,16,512]{2,1,0:T(8,128)(2,1)S(1)}, u32[]{:S(2)}, u32[]{:S(2)}) collective-permute-start(bf16[16,16,512]{2,1,0:T(8,128)(2,1)S(1)} %bitcast.112), channel_id=1, source_target_pairs={{0,4},{4,8},{8,12},{12,16},{16,20},{20,24},{24,28},{28,32},{32,36}... | collective-permute-start | bytes 786440 | tf_op jit(solution)/shard_map/ppermute | solution.py:434
  104.5 3.4 %multiply_add_fusion = f32[2,16,16,512]{3,2,1,0:T(8,128)S(1)} fusion(bf16[2,16,16,512]{3,2,1,0:T(8,128)(2,1)S(1)} %bitcast.104, f32[512]{0:T(512)S(1)} %bitcast.179, f32[512]{0:T(512)S(1)} %bitcast.183, f32[512]{0:T(512)S(1)} %bitcast.151, f32[512]{0:T(512)S(1)} %bitcast.155, f32[512]{0:T(512)S(1)} %bitcast.159, f32[512]{0:T(512)S(1)} %bitcast.163, ...), kind=kLoop, calls=%fused_computation.81 | loop fusion | flops 20971520 | bytes 1628160 | tf_op jit(solution)/shard_map/add | solution.py:426
  107.8 2.7 %collective-permute-start.3 = (bf16[16,16,512]{2,1,0:T(8,128)(2,1)S(1)}, bf16[16,16,512]{2,1,0:T(8,128)(2,1)S(1)}, u32[]{:S(2)}, u32[]{:S(2)}) collective-permute-start(bf16[16,16,512]{2,1,0:T(8,128)(2,1)S(1)} %bitcast.111), channel_id=1, source_target_pairs={{4,0},{8,4},{12,8},{16,12},{20,16},{24,20},{28,24},{32,28},{36,32}... | collective-permute-start | bytes 786440 | tf_op jit(solution)/shard_map/ppermute | solution.py:435
  112.2 6.9 %collective-permute-done.3 = bf16[16,16,512]{2,1,0:T(8,128)(2,1)S(1)} collective-permute-done((bf16[16,16,512]{2,1,0:T(8,128)(2,1)S(1)}, bf16[16,16,512]{2,1,0:T(8,128)(2,1)S(1)}, u32[]{:S(2)}, u32[]{:S(2)}) %collective-permute-start.3) | collective-permute-done | bytes 262176 | tf_op jit(solution)/shard_map/ppermute | solution.py:435
  119.8 0.7 fusion.2
  120.4 1.1 pad_maximum_fusion.g_ref
  121.6 29.3 %shard_map.150 = f32[16,512]{1,0:T(8,128)} custom-call(bf16[64,16,512]{2,1,0:T(8,128)(2,1)} %pad_maximum_fusion.g_ref), custom_call_target="tpu_custom_call" | custom-call | tf_op jit(solution)/shard_map/pallas_call | solution.py:337
  150.9 1.3 fusion.96
  152.2 0.8 copy.41
  (71 shorter events, 8.4 us)
Async XLA Ops:
  0.6 92.1 %copy-start = (bf16[512,512]{1,0:T(8,128)(2,1)S(1)}, bf16[512,512]{1,0:T(8,128)(2,1)}, u32[]{:S(2)}) copy-start(bf16[512,512]{1,0:T(8,128)(2,1)} %param.33) | copy-start | bytes 1572868
  5.9 3.5 %copy-start.5 = (bf16[512,128]{1,0:T(8,128)(2,1)S(1)}, bf16[512,128]{1,0:T(8,128)(2,1)}, u32[]{:S(2)}) copy-start(bf16[512,128]{1,0:T(8,128)(2,1)} %param.26) | copy-start | bytes 393220
  5.9 3.5 %copy-start.9 = (f32[512]{0:T(512)S(1)}, f32[512]{0:T(512)}, u32[]{:S(2)}) copy-start(f32[512]{0:T(512)} %param.24) | copy-start | bytes 6148
  6.0 4.2 %copy-start.6 = (bf16[512,128]{1,0:T(8,128)(2,1)S(1)}, bf16[512,128]{1,0:T(8,128)(2,1)}, u32[]{:S(2)}) copy-start(bf16[512,128]{1,0:T(8,128)(2,1)} %param.27) | copy-start | bytes 393220
  6.0 4.4 %copy-start.4 = (bf16[512,128]{1,0:T(8,128)(2,1)S(1)}, bf16[512,128]{1,0:T(8,128)(2,1)}, u32[]{:S(2)}) copy-start(bf16[512,128]{1,0:T(8,128)(2,1)} %param.25) | copy-start | bytes 393220
  9.7 50.3 %copy-start.7 = (bf16[128,512]{1,0:T(8,128)(2,1)S(1)}, bf16[128,512]{1,0:T(8,128)(2,1)}, u32[]{:S(2)}) copy-start(bf16[128,512]{1,0:T(8,128)(2,1)} %param.28) | copy-start | bytes 393220
  11.3 68.5 %copy-start.1 = (bf16[512,512]{1,0:T(8,128)(2,1)S(1)}, bf16[512,512]{1,0:T(8,128)(2,1)}, u32[]{:S(2)}) copy-start(bf16[512,512]{1,0:T(8,128)(2,1)} %param.21) | copy-start | bytes 1572868
  13.5 69.0 %copy-start.10 = (bf16[512,512]{1,0:T(8,128)(2,1)S(1)}, bf16[512,512]{1,0:T(8,128)(2,1)}, u32[]{:S(2)}) copy-start(bf16[512,512]{1,0:T(8,128)(2,1)} %param.30) | copy-start | bytes 1572868
  13.5 69.0 %copy-start.11 = (f32[512]{0:T(512)S(1)}, f32[512]{0:T(512)}, u32[]{:S(2)}) copy-start(f32[512]{0:T(512)} %param.29) | copy-start | bytes 6148
  79.8 2.7 %copy-start.2 = (bf16[4,128,512]{2,1,0:T(8,128)(2,1)S(1)}, bf16[4,128,512]{2,1,0:T(8,128)(2,1)}, u32[]{:S(2)}) copy-start(bf16[4,128,512]{2,1,0:T(8,128)(2,1)} %shard_map.149) | copy-start | bytes 1572868
  82.5 6.6 %copy-start.8 = (f32[27,512]{1,0:T(8,128)S(1)}, f32[27,512]{1,0:T(8,128)}, u32[]{:S(2)}) copy-start(f32[27,512]{1,0:T(8,128)} %param.31) | copy-start | bytes 165892
  83.0 9.7 %copy-start.3 = (bf16[512,512]{1,0:T(8,128)(2,1)S(1)}, bf16[512,512]{1,0:T(8,128)(2,1)}, u32[]{:S(2)}) copy-start(bf16[512,512]{1,0:T(8,128)(2,1)} %param.32) | copy-start | bytes 1572868
  83.1 16.6 %collective-permute-start = (bf16[16,16,512]{2,1,0:T(8,128)(2,1)S(1)}, bf16[16,16,512]{2,1,0:T(8,128)(2,1)S(1)}, u32[]{:S(2)}, u32[]{:S(2)}) collective-permute-start(bf16[16,16,512]{2,1,0:T(8,128)(2,1)S(1)} %bitcast.110), channel_id=1, source_target_pairs={{0,4},{4,8},{8,12},{12,16},{16,20},{20,24},{24,28},{28,32},{32,36}... | collective-permute-start | bytes 786440 | tf_op jit(solution)/shard_map/ppermute | solution.py:434
  85.8 14.5 %collective-permute-start.1 = (bf16[16,16,512]{2,1,0:T(8,128)(2,1)S(1)}, bf16[16,16,512]{2,1,0:T(8,128)(2,1)S(1)}, u32[]{:S(2)}, u32[]{:S(2)}) collective-permute-start(bf16[16,16,512]{2,1,0:T(8,128)(2,1)S(1)} %bitcast.109), channel_id=1, source_target_pairs={{4,0},{8,4},{12,8},{16,12},{20,16},{24,20},{28,24},{32,28},{36,32}... | collective-permute-start | bytes 786440 | tf_op jit(solution)/shard_map/ppermute | solution.py:435
  101.3 10.3 %collective-permute-start.2 = (bf16[16,16,512]{2,1,0:T(8,128)(2,1)S(1)}, bf16[16,16,512]{2,1,0:T(8,128)(2,1)S(1)}, u32[]{:S(2)}, u32[]{:S(2)}) collective-permute-start(bf16[16,16,512]{2,1,0:T(8,128)(2,1)S(1)} %bitcast.112), channel_id=1, source_target_pairs={{0,4},{4,8},{8,12},{12,16},{16,20},{20,24},{24,28},{28,32},{32,36}... | collective-permute-start | bytes 786440 | tf_op jit(solution)/shard_map/ppermute | solution.py:434
  107.8 11.3 %collective-permute-start.3 = (bf16[16,16,512]{2,1,0:T(8,128)(2,1)S(1)}, bf16[16,16,512]{2,1,0:T(8,128)(2,1)S(1)}, u32[]{:S(2)}, u32[]{:S(2)}) collective-permute-start(bf16[16,16,512]{2,1,0:T(8,128)(2,1)S(1)} %bitcast.111), channel_id=1, source_target_pairs={{4,0},{8,4},{12,8},{16,12},{20,16},{24,20},{28,24},{32,28},{36,32}... | collective-permute-start | bytes 786440 | tf_op jit(solution)/shard_map/ppermute | solution.py:435

commit v20 on v17

--- a/solution.py
+++ b/solution.py
@@ -32,7 +32,7 @@
 
 def attend_rows(kv_ref, q_ref, top_ref, total_ref, acc_ref, first_row, row_rows, first):
     heads, q_rows, _ = top_ref.shape
-    q_tile = q_rows // 2
+    q_tile = q_rows
     key_width = heads * HEAD
     score_scale = HEAD ** (-0.5)
     rows = pl.ds(pl.multiple_of(first_row, row_rows), row_rows)

time: 152 us -> 153 us (level)
  no operation moved by 1% of the time
where the time goes in v20:
time: 153 us; the launch traced here: 152 us
  Pallas kernels  94 us (61%)
  other arithmetic  19.1 us (12%)
  waiting for transfers between devices  13.9 us (9%)
  starting transfers between devices  11.8 us (8%)
  matrix products  8.05 us (5%)
  local copies, waits for them, and re-layouts  4.43 us (3%)
    pallas_call x1, Pallas kernels, gather_attend(): pl.pallas_call(functools.partial(gather_kernel, row_size), out_shape=jax....  46.9 us
    pallas_call x1, Pallas kernels, slab_scatter(): pl.pallas_call(functools.partial(scatter_kernel, row_size), out_shape=jax...  29.3 us
    pallas_call x1, Pallas kernels, head_sum(): pl.pallas_call(functools.partial(head_sum_kernel, count), out_shape=jax.S...  17.7 us
    ppermute x2, waiting for transfers between devices, conv_with_halos(): above = lax.ppermute(cells[0], SLAB, [(i + 1, i) for i in range(ends)])  6.97 us
    add x2, other arithmetic, depth_conv(): result = result + window.astype(jnp.float32) * weights[offset]  6.97 us
    ppermute x2, waiting for transfers between devices, conv_with_halos(): lax.ppermute(cells[planes - 1], SLAB, [(i, i + 1) for i in range(ends)])  6.92 us
    ppermute x2, starting transfers between devices, conv_with_halos(): above = lax.ppermute(cells[0], SLAB, [(i + 1, i) for i in range(ends)])  6.1 us
    ppermute x2, starting transfers between devices, conv_with_halos(): lax.ppermute(cells[planes - 1], SLAB, [(i, i + 1) for i in range(ends)])  5.74 us
  transfers between devices with their start and end apart: 4, of which 3 were waited for; matrix products, arithmetic and copies ran while one was open for 6% of the time, Pallas kernels for 0%

profile of v20, /device:TPU:2, one launch (start us, length us, event | category | flops | bytes accessed | tf_op | source)
XLA Modules:
  0.0 152.4 jit_solution(1298675656114897247)
XLA Ops:
  1.1 1.2 convert_reduce_fusion
  2.3 1.3 fusion.4
  3.6 1.3 fusion.6
  6.0 3.2 %fusion.97 = (f32[64]{0:T(128)S(1)}, f32[64,512]{1,0:T(8,128)S(1)}) fusion(bf16[64,4096]{1,0:T(8,128)(2,1)S(1)} %reshape.796, bf16[4096,512]{1,0:T(8,128)(2,1)} %param.23), kind=kOutput, calls=%fused_computation.255 | convolution fusion | flops 268468160 | bytes 4849920 | tf_op jit(solution)/shard_map/dot_general | solution.py:472
  11.1 0.8 copy.23.q_ref
  11.9 0.6 pad_maximum_fusion.3.x_ref
  12.5 46.9 %shard_map.148 = bf16[512,128]{1,0:T(8,128)(2,1)} custom-call(bf16[64,256]{1,0:T(8,128)(2,1)} %pad_maximum_fusion.3.x_ref, bf16[512,128]{1,0:T(8,128)(2,1)} %copy.23.q_ref), custom_call_target="tpu_custom_call" | custom-call | tf_op jit(solution)/shard_map/pallas_call | solution.py:171
  59.4 2.0 %convolution_convert_fusion.3 = bf16[512,512]{1,0:T(8,128)(2,1)} fusion(bf16[512,128]{1,0:T(8,128)(2,1)} %shard_map.148, bf16[128,512]{1,0:T(8,128)(2,1)S(1)} %copy-done.7), kind=kOutput, calls=%fused_computation.59 | convolution fusion | flops 67371008 | bytes 786432 | tf_op jit(solution)/shard_map/dot_general | solution.py:497
  61.4 17.7 %shard_map.149 = bf16[4,128,512]{2,1,0:T(8,128)(2,1)} custom-call(bf16[4,128,512]{2,1,0:T(8,128)(2,1)} %bitcast.109), custom_call_target="tpu_custom_call" | custom-call | tf_op jit(solution)/shard_map/pallas_call | solution.py:245
  79.2 1.3 fusion.18
  80.5 1.3 multiply_reduce_fusion
  82.5 2.6 %collective-permute-start = (bf16[16,16,512]{2,1,0:T(8,128)(2,1)S(1)}, bf16[16,16,512]{2,1,0:T(8,128)(2,1)S(1)}, u32[]{:S(2)}, u32[]{:S(2)}) collective-permute-start(bf16[16,16,512]{2,1,0:T(8,128)(2,1)S(1)} %bitcast.114), channel_id=1, source_target_pairs={{0,4},{4,8},{8,12},{12,16},{16,20},{20,24},{24,28},{28,32},{32,36}... | collective-permute-start | bytes 786440 | tf_op jit(solution)/shard_map/ppermute | solution.py:434
  85.1 3.3 %collective-permute-start.1 = (bf16[16,16,512]{2,1,0:T(8,128)(2,1)S(1)}, bf16[16,16,512]{2,1,0:T(8,128)(2,1)S(1)}, u32[]{:S(2)}, u32[]{:S(2)}) collective-permute-start(bf16[16,16,512]{2,1,0:T(8,128)(2,1)S(1)} %bitcast.113), channel_id=1, source_target_pairs={{4,0},{8,4},{12,8},{16,12},{20,16},{24,20},{28,24},{32,28},{36,32}... | collective-permute-start | bytes 786440 | tf_op jit(solution)/shard_map/ppermute | solution.py:435
  88.5 3.6 %multiply_add_fusion.1 = f32[2,16,16,512]{3,2,1,0:T(8,128)S(1)} fusion(bf16[2,16,16,512]{3,2,1,0:T(8,128)(2,1)S(1)} %bitcast.107, f32[512]{0:T(512)S(1)} %bitcast.181, f32[512]{0:T(512)S(1)} %bitcast.185, f32[512]{0:T(512)S(1)} %bitcast.153, f32[512]{0:T(512)S(1)} %bitcast.157, f32[512]{0:T(512)S(1)} %bitcast.161, f32[512]{0:T(512)S(1)} %bitcast.165, ...), kind=kLoop, calls=%fused_computation.82 | loop fusion | flops 20971520 | bytes 1628160 | tf_op jit(solution)/shard_map/add | solution.py:426
  92.6 6.4 %collective-permute-done = bf16[16,16,512]{2,1,0:T(8,128)(2,1)S(1)} collective-permute-done((bf16[16,16,512]{2,1,0:T(8,128)(2,1)S(1)}, bf16[16,16,512]{2,1,0:T(8,128)(2,1)S(1)}, u32[]{:S(2)}, u32[]{:S(2)}) %collective-permute-start) | collective-permute-done | bytes 262176 | tf_op jit(solution)/shard_map/ppermute | solution.py:434
  100.7 3.1 %collective-permute-start.2 = (bf16[16,16,512]{2,1,0:T(8,128)(2,1)S(1)}, bf16[16,16,512]{2,1,0:T(8,128)(2,1)S(1)}, u32[]{:S(2)}, u32[]{:S(2)}) collective-permute-start(bf16[16,16,512]{2,1,0:T(8,128)(2,1)S(1)} %bitcast.116), channel_id=1, source_target_pairs={{0,4},{4,8},{8,12},{12,16},{16,20},{20,24},{24,28},{28,32},{32,36}... | collective-permute-start | bytes 786440 | tf_op jit(solution)/shard_map/ppermute | solution.py:434
  103.8 3.4 %multiply_add_fusion = f32[2,16,16,512]{3,2,1,0:T(8,128)S(1)} fusion(bf16[2,16,16,512]{3,2,1,0:T(8,128)(2,1)S(1)} %bitcast.106, f32[512]{0:T(512)S(1)} %bitcast.183, f32[512]{0:T(512)S(1)} %bitcast.187, f32[512]{0:T(512)S(1)} %bitcast.155, f32[512]{0:T(512)S(1)} %bitcast.159, f32[512]{0:T(512)S(1)} %bitcast.163, f32[512]{0:T(512)S(1)} %bitcast.167, ...), kind=kLoop, calls=%fused_computation.81 | loop fusion | flops 20971520 | bytes 1628160 | tf_op jit(solution)/shard_map/add | solution.py:426
  107.2 2.8 %collective-permute-start.3 = (bf16[16,16,512]{2,1,0:T(8,128)(2,1)S(1)}, bf16[16,16,512]{2,1,0:T(8,128)(2,1)S(1)}, u32[]{:S(2)}, u32[]{:S(2)}) collective-permute-start(bf16[16,16,512]{2,1,0:T(8,128)(2,1)S(1)} %bitcast.115), channel_id=1, source_target_pairs={{4,0},{8,4},{12,8},{16,12},{20,16},{24,20},{28,24},{32,28},{36,32}... | collective-permute-start | bytes 786440 | tf_op jit(solution)/shard_map/ppermute | solution.py:435
  111.5 7.0 %collective-permute-done.3 = bf16[16,16,512]{2,1,0:T(8,128)(2,1)S(1)} collective-permute-done((bf16[16,16,512]{2,1,0:T(8,128)(2,1)S(1)}, bf16[16,16,512]{2,1,0:T(8,128)(2,1)S(1)}, u32[]{:S(2)}, u32[]{:S(2)}) %collective-permute-start.3) | collective-permute-done | bytes 262176 | tf_op jit(solution)/shard_map/ppermute | solution.py:435
  119.2 0.7 fusion.2
  119.9 1.1 pad_maximum_fusion.g_ref
  121.0 29.3 %shard_map.150 = f32[16,512]{1,0:T(8,128)} custom-call(bf16[64,16,512]{2,1,0:T(8,128)(2,1)} %pad_maximum_fusion.g_ref), custom_call_target="tpu_custom_call" | custom-call | tf_op jit(solution)/shard_map/pallas_call | solution.py:337
  150.3 1.3 fusion.96
  151.6 0.8 copy.31
  (73 shorter events, 8.1 us)
Async XLA Ops:
  0.6 91.5 %copy-start = (bf16[512,512]{1,0:T(8,128)(2,1)S(1)}, bf16[512,512]{1,0:T(8,128)(2,1)}, u32[]{:S(2)}) copy-start(bf16[512,512]{1,0:T(8,128)(2,1)} %param.33) | copy-start | bytes 1572868
  5.9 3.5 %copy-start.5 = (bf16[512,128]{1,0:T(8,128)(2,1)S(1)}, bf16[512,128]{1,0:T(8,128)(2,1)}, u32[]{:S(2)}) copy-start(bf16[512,128]{1,0:T(8,128)(2,1)} %param.26) | copy-start | bytes 393220
  5.9 3.5 %copy-start.9 = (f32[512]{0:T(512)S(1)}, f32[512]{0:T(512)}, u32[]{:S(2)}) copy-start(f32[512]{0:T(512)} %param.24) | copy-start | bytes 6148
  6.0 4.2 %copy-start.6 = (bf16[512,128]{1,0:T(8,128)(2,1)S(1)}, bf16[512,128]{1,0:T(8,128)(2,1)}, u32[]{:S(2)}) copy-start(bf16[512,128]{1,0:T(8,128)(2,1)} %param.27) | copy-start | bytes 393220
  6.0 4.4 %copy-start.4 = (bf16[512,128]{1,0:T(8,128)(2,1)S(1)}, bf16[512,128]{1,0:T(8,128)(2,1)}, u32[]{:S(2)}) copy-start(bf16[512,128]{1,0:T(8,128)(2,1)} %param.25) | copy-start | bytes 393220
  9.2 50.2 %copy-start.7 = (bf16[128,512]{1,0:T(8,128)(2,1)S(1)}, bf16[128,512]{1,0:T(8,128)(2,1)}, u32[]{:S(2)}) copy-start(bf16[128,512]{1,0:T(8,128)(2,1)} %param.28) | copy-start | bytes 393220
  10.4 68.8 %copy-start.1 = (bf16[512,512]{1,0:T(8,128)(2,1)S(1)}, bf16[512,512]{1,0:T(8,128)(2,1)}, u32[]{:S(2)}) copy-start(bf16[512,512]{1,0:T(8,128)(2,1)} %param.21) | copy-start | bytes 1572868
  12.5 69.4 %copy-start.10 = (bf16[512,512]{1,0:T(8,128)(2,1)S(1)}, bf16[512,512]{1,0:T(8,128)(2,1)}, u32[]{:S(2)}) copy-start(bf16[512,512]{1,0:T(8,128)(2,1)} %param.30) | copy-start | bytes 1572868
  12.5 69.4 %copy-start.11 = (f32[512]{0:T(512)S(1)}, f32[512]{0:T(512)}, u32[]{:S(2)}) copy-start(f32[512]{0:T(512)} %param.29) | copy-start | bytes 6148
  79.2 2.7 %copy-start.2 = (bf16[4,128,512]{2,1,0:T(8,128)(2,1)S(1)}, bf16[4,128,512]{2,1,0:T(8,128)(2,1)}, u32[]{:S(2)}) copy-start(bf16[4,128,512]{2,1,0:T(8,128)(2,1)} %shard_map.149) | copy-start | bytes 1572868
  81.8 6.6 %copy-start.8 = (f32[27,512]{1,0:T(8,128)S(1)}, f32[27,512]{1,0:T(8,128)}, u32[]{:S(2)}) copy-start(f32[27,512]{1,0:T(8,128)} %param.31) | copy-start | bytes 165892
  82.4 9.7 %copy-start.3 = (bf16[512,512]{1,0:T(8,128)(2,1)S(1)}, bf16[512,512]{1,0:T(8,128)(2,1)}, u32[]{:S(2)}) copy-start(bf16[512,512]{1,0:T(8,128)(2,1)} %param.32) | copy-start | bytes 1572868
  82.5 16.6 %collective-permute-start = (bf16[16,16,512]{2,1,0:T(8,128)(2,1)S(1)}, bf16[16,16,512]{2,1,0:T(8,128)(2,1)S(1)}, u32[]{:S(2)}, u32[]{:S(2)}) collective-permute-start(bf16[16,16,512]{2,1,0:T(8,128)(2,1)S(1)} %bitcast.114), channel_id=1, source_target_pairs={{0,4},{4,8},{8,12},{12,16},{16,20},{20,24},{24,28},{28,32},{32,36}... | collective-permute-start | bytes 786440 | tf_op jit(solution)/shard_map/ppermute | solution.py:434
  85.1 14.5 %collective-permute-start.1 = (bf16[16,16,512]{2,1,0:T(8,128)(2,1)S(1)}, bf16[16,16,512]{2,1,0:T(8,128)(2,1)S(1)}, u32[]{:S(2)}, u32[]{:S(2)}) collective-permute-start(bf16[16,16,512]{2,1,0:T(8,128)(2,1)S(1)} %bitcast.113), channel_id=1, source_target_pairs={{4,0},{8,4},{12,8},{16,12},{20,16},{24,20},{28,24},{32,28},{36,32}... | collective-permute-start | bytes 786440 | tf_op jit(solution)/shard_map/ppermute | solution.py:435
  100.7 10.3 %collective-permute-start.2 = (bf16[16,16,512]{2,1,0:T(8,128)(2,1)S(1)}, bf16[16,16,512]{2,1,0:T(8,128)(2,1)S(1)}, u32[]{:S(2)}, u32[]{:S(2)}) collective-permute-start(bf16[16,16,512]{2,1,0:T(8,128)(2,1)S(1)} %bitcast.116), channel_id=1, source_target_pairs={{0,4},{4,8},{8,12},{12,16},{16,20},{20,24},{24,28},{28,32},{32,36}... | collective-permute-start | bytes 786440 | tf_op jit(solution)/shard_map/ppermute | solution.py:434
  107.2 11.3 %collective-permute-start.3 = (bf16[16,16,512]{2,1,0:T(8,128)(2,1)S(1)}, bf16[16,16,512]{2,1,0:T(8,128)(2,1)S(1)}, u32[]{:S(2)}, u32[]{:S(2)}) collective-permute-start(bf16[16,16,512]{2,1,0:T(8,128)(2,1)S(1)} %bitcast.115), channel_id=1, source_target_pairs={{4,0},{8,4},{12,8},{16,12},{20,16},{24,20},{28,24},{32,28},{36,32}... | collective-permute-start | bytes 786440 | tf_op jit(solution)/shard_map/ppermute | solution.py:435

commit v21 on v19

--- a/solution.py
+++ b/solution.py
@@ -32,7 +32,7 @@
 
 def attend_rows(kv_ref, q_ref, top_ref, total_ref, acc_ref, first_row, row_rows, first):
     heads, q_rows, _ = top_ref.shape
-    q_tile = q_rows // 2
+    q_tile = q_rows
     key_width = heads * HEAD
     score_scale = HEAD ** (-0.5)
     rows = pl.ds(pl.multiple_of(first_row, row_rows), row_rows)

time: 154 us -> 154 us (level)
  no operation moved by 1% of the time
where the time goes in v21:
time: 154 us
  Pallas kernels  94.1 us (61%)
  other arithmetic  20.9 us (14%)
  waiting for transfers between devices  13.8 us (9%)
  starting transfers between devices  11.8 us (8%)
  matrix products  8.03 us (5%)
  local copies, waits for them, and re-layouts  3.67 us (2%)
    pallas_call x1, Pallas kernels, gather_attend(): pl.pallas_call(functools.partial(gather_kernel, row_size), out_shape=jax....  47.1 us
    pallas_call x1, Pallas kernels, slab_scatter(): pl.pallas_call(functools.partial(scatter_kernel, row_size), out_shape=jax...  29.3 us
    pallas_call x1, Pallas kernels, head_sum(): pl.pallas_call(functools.partial(head_sum_kernel, count), out_shape=jax.S...  17.7 us
    add x2, other arithmetic, depth_conv(): result = result + window.astype(jnp.float32) * weights[offset]  6.97 us
    ppermute x2, waiting for transfers between devices, conv_with_halos(): above = lax.ppermute(cells[0], SLAB, [(i + 1, i) for i in range(ends)])  6.94 us
    ppermute x2, waiting for transfers between devices, conv_with_halos(): lax.ppermute(cells[planes - 1], SLAB, [(i, i + 1) for i in range(ends)])  6.91 us
    ppermute x2, starting transfers between devices, conv_with_halos(): above = lax.ppermute(cells[0], SLAB, [(i + 1, i) for i in range(ends)])  6.13 us
    ppermute x2, starting transfers between devices, conv_with_halos(): lax.ppermute(cells[planes - 1], SLAB, [(i, i + 1) for i in range(ends)])  5.71 us
  transfers between devices with their start and end apart: 4, of which 3 were waited for; matrix products, arithmetic and copies ran while one was open for 6% of the time, Pallas kernels for 0%

profile of v21, /device:TPU:2, one launch (start us, length us, event | category | flops | bytes accessed | tf_op | source)
XLA Modules:
  0.0 153.6 jit_solution(11614223757830309110)
XLA Ops:
  1.1 1.2 convert_reduce_fusion
  2.3 1.3 fusion.4
  3.6 1.3 fusion.6
  6.0 3.2 %fusion.97 = (f32[64]{0:T(128)S(1)}, f32[64,512]{1,0:T(8,128)S(1)}) fusion(bf16[64,4096]{1,0:T(8,128)(2,1)S(1)} %reshape.628, bf16[4096,512]{1,0:T(8,128)(2,1)} %param.23), kind=kOutput, calls=%fused_computation.257 | convolution fusion | flops 268468160 | bytes 4849920 | tf_op jit(solution)/shard_map/dot_general | solution.py:472
  11.3 1.4 subtract_convert_fusion.1
  12.7 0.8 pad_maximum_fusion.1.q_ref
  13.5 47.1 %shard_map.148 = bf16[512,128]{1,0:T(8,128)(2,1)} custom-call(bf16[64,256]{1,0:T(8,128)(2,1)} %pad_maximum_fusion.3.x_ref, bf16[512,128]{1,0:T(8,128)(2,1)} %pad_maximum_fusion.1.q_ref), custom_call_target="tpu_custom_call" | custom-call | tf_op jit(solution)/shard_map/pallas_call | solution.py:171
  60.6 2.0 %convolution_convert_fusion.3 = bf16[512,512]{1,0:T(8,128)(2,1)} fusion(bf16[512,128]{1,0:T(8,128)(2,1)} %shard_map.148, bf16[128,512]{1,0:T(8,128)(2,1)S(1)} %copy-done.7), kind=kOutput, calls=%fused_computation.59 | convolution fusion | flops 67371008 | bytes 786432 | tf_op jit(solution)/shard_map/dot_general | solution.py:501
  62.6 17.7 %shard_map.149 = bf16[4,128,512]{2,1,0:T(8,128)(2,1)} custom-call(bf16[4,128,512]{2,1,0:T(8,128)(2,1)} %bitcast.107), custom_call_target="tpu_custom_call" | custom-call | tf_op jit(solution)/shard_map/pallas_call | solution.py:245
  80.3 1.3 fusion.18
  81.7 1.3 multiply_reduce_fusion
  83.6 2.6 %collective-permute-start = (bf16[16,16,512]{2,1,0:T(8,128)(2,1)S(1)}, bf16[16,16,512]{2,1,0:T(8,128)(2,1)S(1)}, u32[]{:S(2)}, u32[]{:S(2)}) collective-permute-start(bf16[16,16,512]{2,1,0:T(8,128)(2,1)S(1)} %bitcast.110), channel_id=1, source_target_pairs={{0,4},{4,8},{8,12},{12,16},{16,20},{20,24},{24,28},{28,32},{32,36}... | collective-permute-start | bytes 786440 | tf_op jit(solution)/shard_map/ppermute | solution.py:434
  86.3 3.4 %collective-permute-start.1 = (bf16[16,16,512]{2,1,0:T(8,128)(2,1)S(1)}, bf16[16,16,512]{2,1,0:T(8,128)(2,1)S(1)}, u32[]{:S(2)}, u32[]{:S(2)}) collective-permute-start(bf16[16,16,512]{2,1,0:T(8,128)(2,1)S(1)} %bitcast.109), channel_id=1, source_target_pairs={{4,0},{8,4},{12,8},{16,12},{20,16},{24,20},{28,24},{32,28},{36,32}... | collective-permute-start | bytes 786440 | tf_op jit(solution)/shard_map/ppermute | solution.py:435
  89.7 3.6 %multiply_add_fusion.1 = f32[2,16,16,512]{3,2,1,0:T(8,128)S(1)} fusion(bf16[2,16,16,512]{3,2,1,0:T(8,128)(2,1)S(1)} %bitcast.105, f32[512]{0:T(512)S(1)} %bitcast.177, f32[512]{0:T(512)S(1)} %bitcast.181, f32[512]{0:T(512)S(1)} %bitcast.149, f32[512]{0:T(512)S(1)} %bitcast.153, f32[512]{0:T(512)S(1)} %bitcast.157, f32[512]{0:T(512)S(1)} %bitcast.161, ...), kind=kLoop, calls=%fused_computation.82 | loop fusion | flops 20971520 | bytes 1628160 | tf_op jit(solution)/shard_map/add | solution.py:426
  93.8 6.4 %collective-permute-done = bf16[16,16,512]{2,1,0:T(8,128)(2,1)S(1)} collective-permute-done((bf16[16,16,512]{2,1,0:T(8,128)(2,1)S(1)}, bf16[16,16,512]{2,1,0:T(8,128)(2,1)S(1)}, u32[]{:S(2)}, u32[]{:S(2)}) %collective-permute-start) | collective-permute-done | bytes 262176 | tf_op jit(solution)/shard_map/ppermute | solution.py:434
  101.9 3.1 %collective-permute-start.2 = (bf16[16,16,512]{2,1,0:T(8,128)(2,1)S(1)}, bf16[16,16,512]{2,1,0:T(8,128)(2,1)S(1)}, u32[]{:S(2)}, u32[]{:S(2)}) collective-permute-start(bf16[16,16,512]{2,1,0:T(8,128)(2,1)S(1)} %bitcast.112), channel_id=1, source_target_pairs={{0,4},{4,8},{8,12},{12,16},{16,20},{20,24},{24,28},{28,32},{32,36}... | collective-permute-start | bytes 786440 | tf_op jit(solution)/shard_map/ppermute | solution.py:434
  105.0 3.4 %multiply_add_fusion = f32[2,16,16,512]{3,2,1,0:T(8,128)S(1)} fusion(bf16[2,16,16,512]{3,2,1,0:T(8,128)(2,1)S(1)} %bitcast.104, f32[512]{0:T(512)S(1)} %bitcast.179, f32[512]{0:T(512)S(1)} %bitcast.183, f32[512]{0:T(512)S(1)} %bitcast.151, f32[512]{0:T(512)S(1)} %bitcast.155, f32[512]{0:T(512)S(1)} %bitcast.159, f32[512]{0:T(512)S(1)} %bitcast.163, ...), kind=kLoop, calls=%fused_computation.81 | loop fusion | flops 20971520 | bytes 1628160 | tf_op jit(solution)/shard_map/add | solution.py:426
  108.4 2.8 %collective-permute-start.3 = (bf16[16,16,512]{2,1,0:T(8,128)(2,1)S(1)}, bf16[16,16,512]{2,1,0:T(8,128)(2,1)S(1)}, u32[]{:S(2)}, u32[]{:S(2)}) collective-permute-start(bf16[16,16,512]{2,1,0:T(8,128)(2,1)S(1)} %bitcast.111), channel_id=1, source_target_pairs={{4,0},{8,4},{12,8},{16,12},{20,16},{24,20},{28,24},{32,28},{36,32}... | collective-permute-start | bytes 786440 | tf_op jit(solution)/shard_map/ppermute | solution.py:435
  112.7 6.9 %collective-permute-done.3 = bf16[16,16,512]{2,1,0:T(8,128)(2,1)S(1)} collective-permute-done((bf16[16,16,512]{2,1,0:T(8,128)(2,1)S(1)}, bf16[16,16,512]{2,1,0:T(8,128)(2,1)S(1)}, u32[]{:S(2)}, u32[]{:S(2)}) %collective-permute-start.3) | collective-permute-done | bytes 262176 | tf_op jit(solution)/shard_map/ppermute | solution.py:435
  120.3 0.7 fusion.2
  121.0 1.1 pad_maximum_fusion.g_ref
  122.1 29.3 %shard_map.150 = f32[16,512]{1,0:T(8,128)} custom-call(bf16[64,16,512]{2,1,0:T(8,128)(2,1)} %pad_maximum_fusion.g_ref), custom_call_target="tpu_custom_call" | custom-call | tf_op jit(solution)/shard_map/pallas_call | solution.py:337
  151.4 1.3 fusion.96
  152.8 0.8 copy.41
  (71 shorter events, 8.4 us)
Async XLA Ops:
  0.6 92.7 %copy-start = (bf16[512,512]{1,0:T(8,128)(2,1)S(1)}, bf16[512,512]{1,0:T(8,128)(2,1)}, u32[]{:S(2)}) copy-start(bf16[512,512]{1,0:T(8,128)(2,1)} %param.33) | copy-start | bytes 1572868
  5.9 3.5 %copy-start.5 = (bf16[512,128]{1,0:T(8,128)(2,1)S(1)}, bf16[512,128]{1,0:T(8,128)(2,1)}, u32[]{:S(2)}) copy-start(bf16[512,128]{1,0:T(8,128)(2,1)} %param.26) | copy-start | bytes 393220
  5.9 3.5 %copy-start.9 = (f32[512]{0:T(512)S(1)}, f32[512]{0:T(512)}, u32[]{:S(2)}) copy-start(f32[512]{0:T(512)} %param.24) | copy-start | bytes 6148
  6.0 4.2 %copy-start.6 = (bf16[512,128]{1,0:T(8,128)(2,1)S(1)}, bf16[512,128]{1,0:T(8,128)(2,1)}, u32[]{:S(2)}) copy-start(bf16[512,128]{1,0:T(8,128)(2,1)} %param.27) | copy-start | bytes 393220
  6.0 4.4 %copy-start.4 = (bf16[512,128]{1,0:T(8,128)(2,1)S(1)}, bf16[512,128]{1,0:T(8,128)(2,1)}, u32[]{:S(2)}) copy-start(bf16[512,128]{1,0:T(8,128)(2,1)} %param.25) | copy-start | bytes 393220
  9.7 50.9 %copy-start.7 = (bf16[128,512]{1,0:T(8,128)(2,1)S(1)}, bf16[128,512]{1,0:T(8,128)(2,1)}, u32[]{:S(2)}) copy-start(bf16[128,512]{1,0:T(8,128)(2,1)} %param.28) | copy-start | bytes 393220
  11.3 69.0 %copy-start.1 = (bf16[512,512]{1,0:T(8,128)(2,1)S(1)}, bf16[512,512]{1,0:T(8,128)(2,1)}, u32[]{:S(2)}) copy-start(bf16[512,512]{1,0:T(8,128)(2,1)} %param.21) | copy-start | bytes 1572868
  13.5 69.5 %copy-start.10 = (bf16[512,512]{1,0:T(8,128)(2,1)S(1)}, bf16[512,512]{1,0:T(8,128)(2,1)}, u32[]{:S(2)}) copy-start(bf16[512,512]{1,0:T(8,128)(2,1)} %param.30) | copy-start | bytes 1572868
  13.5 69.5 %copy-start.11 = (f32[512]{0:T(512)S(1)}, f32[512]{0:T(512)}, u32[]{:S(2)}) copy-start(f32[512]{0:T(512)} %param.29) | copy-start | bytes 6148
  80.3 2.7 %copy-start.2 = (bf16[4,128,512]{2,1,0:T(8,128)(2,1)S(1)}, bf16[4,128,512]{2,1,0:T(8,128)(2,1)}, u32[]{:S(2)}) copy-start(bf16[4,128,512]{2,1,0:T(8,128)(2,1)} %shard_map.149) | copy-start | bytes 1572868
  83.0 6.6 %copy-start.8 = (f32[27,512]{1,0:T(8,128)S(1)}, f32[27,512]{1,0:T(8,128)}, u32[]{:S(2)}) copy-start(f32[27,512]{1,0:T(8,128)} %param.31) | copy-start | bytes 165892
  83.6 9.7 %copy-start.3 = (bf16[512,512]{1,0:T(8,128)(2,1)S(1)}, bf16[512,512]{1,0:T(8,128)(2,1)}, u32[]{:S(2)}) copy-start(bf16[512,512]{1,0:T(8,128)(2,1)} %param.32) | copy-start | bytes 1572868
  83.6 16.6 %collective-permute-start = (bf16[16,16,512]{2,1,0:T(8,128)(2,1)S(1)}, bf16[16,16,512]{2,1,0:T(8,128)(2,1)S(1)}, u32[]{:S(2)}, u32[]{:S(2)}) collective-permute-start(bf16[16,16,512]{2,1,0:T(8,128)(2,1)S(1)} %bitcast.110), channel_id=1, source_target_pairs={{0,4},{4,8},{8,12},{12,16},{16,20},{20,24},{24,28},{28,32},{32,36}... | collective-permute-start | bytes 786440 | tf_op jit(solution)/shard_map/ppermute | solution.py:434
  86.3 14.5 %collective-permute-start.1 = (bf16[16,16,512]{2,1,0:T(8,128)(2,1)S(1)}, bf16[16,16,512]{2,1,0:T(8,128)(2,1)S(1)}, u32[]{:S(2)}, u32[]{:S(2)}) collective-permute-start(bf16[16,16,512]{2,1,0:T(8,128)(2,1)S(1)} %bitcast.109), channel_id=1, source_target_pairs={{4,0},{8,4},{12,8},{16,12},{20,16},{24,20},{28,24},{32,28},{36,32}... | collective-permute-start | bytes 786440 | tf_op jit(solution)/shard_map/ppermute | solution.py:435
  101.9 10.3 %collective-permute-start.2 = (bf16[16,16,512]{2,1,0:T(8,128)(2,1)S(1)}, bf16[16,16,512]{2,1,0:T(8,128)(2,1)S(1)}, u32[]{:S(2)}, u32[]{:S(2)}) collective-permute-start(bf16[16,16,512]{2,1,0:T(8,128)(2,1)S(1)} %bitcast.112), channel_id=1, source_target_pairs={{0,4},{4,8},{8,12},{12,16},{16,20},{20,24},{24,28},{28,32},{32,36}... | collective-permute-start | bytes 786440 | tf_op jit(solution)/shard_map/ppermute | solution.py:434
  108.4 11.3 %collective-permute-start.3 = (bf16[16,16,512]{2,1,0:T(8,128)(2,1)S(1)}, bf16[16,16,512]{2,1,0:T(8,128)(2,1)S(1)}, u32[]{:S(2)}, u32[]{:S(2)}) collective-permute-start(bf16[16,16,512]{2,1,0:T(8,128)(2,1)S(1)} %bitcast.111), channel_id=1, source_target_pairs={{4,0},{8,4},{12,8},{16,12},{20,16},{24,20},{28,24},{32,28},{36,32}... | collective-permute-start | bytes 786440 | tf_op jit(solution)/shard_map/ppermute | solution.py:435
